TPU v7x, 256 devices: a whole 4x4x8 slice. The times are simulated.
256 devices in a mesh: ex: 16 (over z, y_lo), par: 16 (over y_hi, x, core).
Axes of the slice: x: 4, y: 4 (y_hi: 2, y_lo: 2; y = y_hi * 2 + y_lo), z: 8, core: 2. Of those that a mesh axis runs over, the one named last changes fastest.
Arguments:
- gradients: bfloat16 [1024, 65536], P('ex', 'par'), may hold values from -6 to 6
- inverse_gram: bfloat16 [16384, 16384], P('par', 'ex'), may hold values from -1 to 3
- hash_words: int32 [4], replicated, may hold values from 1 to 2147483646
Outputs:
- scores: float32 [1024, 1024], P('par', 'ex')
All inputs are finite; a program needn't handle non-finite values.
Results may differ from a plain program's by a relative error of at most 0.0003.
Values may be sent and summed in bfloat16 or wider, within the bound.
No kernel may reach another device: no remote copies, remote signals or barrier semaphores. Data moves between devices by JAX's collectives and lax.ppermute only.
A program may use at most 64 MiB of HBM per device.

v0:
```python
import math

import jax
import jax.numpy as jnp
from jax import lax
from jax.sharding import PartitionSpec as P

FEATURES = 16384


def shifted(values, amount):
    return lax.shift_right_logical(values, jnp.full(values.shape, amount, jnp.int32))


def hash_table(hash_words, row_start, row_count, col_start, col_count):
    row_ids = lax.broadcasted_iota(jnp.int32, (row_count, col_count), 0) + row_start
    col_ids = lax.broadcasted_iota(jnp.int32, (row_count, col_count), 1) + col_start
    mixed = row_ids * FEATURES + col_ids
    mixed = mixed * (hash_words[0] | 1) + hash_words[1]
    mixed = mixed ^ shifted(mixed, 15)
    mixed = mixed * (hash_words[2] | 1)
    mixed = mixed ^ shifted(mixed, 13)
    mixed = mixed * (hash_words[3] | 1)
    mixed = mixed ^ shifted(mixed, 16)
    top_bit = shifted(mixed, 31)
    return ((1 - 2 * top_bit).astype(jnp.float32) * FEATURES ** (-0.5)).astype(jnp.bfloat16)


def per_device(gradients, inverse_gram, hash_words):
    ex_rows, param_width = gradients.shape
    feat_par = inverse_gram.shape[0]
    par_index = lax.axis_index("par")
    row_start = par_index * param_width
    col_width = math.gcd(feat_par * lax.axis_size("par"), 1024)

    def column_block(col_start):
        sign_table = hash_table(hash_words, row_start, param_width, col_start, col_width)
        return lax.dot_general(
            sign_table, gradients, (((0,), (1,)), ((), ())), preferred_element_type=jnp.float32
        )

    col_starts = (
        jnp.arange(feat_par * lax.axis_size("par") // col_width, dtype=jnp.int32) * col_width
    )
    projected = lax.psum_scatter(
        lax.map(column_block, col_starts).reshape(feat_par * lax.axis_size("par"), ex_rows),
        "par",
        scatter_dimension=0,
        tiled=True,
    )
    features = projected.T.astype(jnp.bfloat16)
    partials = jnp.dot(
        lax.all_gather(features, "ex", axis=0, tiled=True),
        inverse_gram,
        preferred_element_type=jnp.float32,
    )
    conditioned = lax.psum_scatter(partials, "par", scatter_dimension=0, tiled=True).astype(
        jnp.bfloat16
    )
    feature_rows = lax.all_gather(features, "par", axis=1, tiled=True)
    pairs = lax.dot_general(
        lax.all_gather(conditioned, "ex", axis=1, tiled=True),
        feature_rows,
        (((1,), (1,)), ((), ())),
        preferred_element_type=jnp.float32,
    )
    return pairs * FEATURES ** (-0.5)


def solution(mesh):
    return jax.shard_map(
        per_device,
        mesh=mesh,
        in_specs=(P("ex", "par"), P("par", "ex"), P()),
        out_specs=P("par", "ex"),
        check_vma=False,
    )
```

profile of v0, /device:TPU:22, one launch (start us, length us, event | category | flops | bytes accessed | tf_op | source)
XLA Modules:
  0.0 734.3 jit_solution(12569676455765907485)
XLA Ops:
  6.5 1.5 fusion.20
  9.9 322.3 %while.11 = (s32[]{:T(128)}, f32[16,1024,64]{1,0,2:T(8,128)}, s32[]{:T(128)}, s32[16]{0:T(128)S(1)}, s32[]{:T(128)}, /*index=5*/s32[4]{0:T(128)}, s32[]{:T(128)}...) while((s32[]{:T(128)}, f32[16,1024,64]{1,0,2:T(8,128)}, s32[]{:T(128)}, ...), condition=%wide.region_1.2_spmd, body=%wide.region_0.1_spmd.sunk | while | flops 608183296 | bytes 1876125 | solution.py:46
  11.3 1.3 slice.26
  12.6 11.1 %fusion.32 = f32[1,1024,64]{1,2,0:T(8,128)S(1)} fusion(bf16[64,4096]{1,0:T(8,128)(2,1)} %get-tuple-element.179, s32[]{:T(128)} %get-tuple-element.178, s32[]{:T(128)} %get-tuple-element.177, s32[]{:T(128)} %bitcast.24, s32[]{:T(128)} %get-tuple-element.175, s32[1024]{0:T(1024)S(1)} %iota_add_fusion.2, s32[4096]{0:T(1024)S(1)} %add_multiply_fusion.2), kind=kOutput, calls=%fused_computation.12.clone.1 | convolution fusion | flops 608174080 | bytes 806928 | tf_op jit(solution)/shard_map/while/body/eval_jaxpr/dot_general | solution.py:38
  24.0 6.1 dynamic_update_slice.6
  30.7 0.7 iota_add_fusion.2
  31.5 1.3 slice.26
  32.8 11.1 %fusion.32 = f32[1,1024,64]{1,2,0:T(8,128)S(1)} fusion(bf16[64,4096]{1,0:T(8,128)(2,1)} %get-tuple-element.179, s32[]{:T(128)} %get-tuple-element.178, s32[]{:T(128)} %get-tuple-element.177, s32[]{:T(128)} %bitcast.24, s32[]{:T(128)} %get-tuple-element.175, s32[1024]{0:T(1024)S(1)} %iota_add_fusion.2, s32[4096]{0:T(1024)S(1)} %add_multiply_fusion.2), kind=kOutput, calls=%fused_computation.12.clone.1 | convolution fusion | flops 608174080 | bytes 806928 | tf_op jit(solution)/shard_map/while/body/eval_jaxpr/dot_general | solution.py:38
  44.1 6.1 dynamic_update_slice.6
  50.9 0.7 iota_add_fusion.2
  51.6 1.3 slice.26
  52.9 11.1 %fusion.32 = f32[1,1024,64]{1,2,0:T(8,128)S(1)} fusion(bf16[64,4096]{1,0:T(8,128)(2,1)} %get-tuple-element.179, s32[]{:T(128)} %get-tuple-element.178, s32[]{:T(128)} %get-tuple-element.177, s32[]{:T(128)} %bitcast.24, s32[]{:T(128)} %get-tuple-element.175, s32[1024]{0:T(1024)S(1)} %iota_add_fusion.2, s32[4096]{0:T(1024)S(1)} %add_multiply_fusion.2), kind=kOutput, calls=%fused_computation.12.clone.1 | convolution fusion | flops 608174080 | bytes 806928 | tf_op jit(solution)/shard_map/while/body/eval_jaxpr/dot_general | solution.py:38
  64.3 6.1 dynamic_update_slice.6
  71.0 0.7 iota_add_fusion.2
  71.7 1.3 slice.26
  73.1 11.1 %fusion.32 = f32[1,1024,64]{1,2,0:T(8,128)S(1)} fusion(bf16[64,4096]{1,0:T(8,128)(2,1)} %get-tuple-element.179, s32[]{:T(128)} %get-tuple-element.178, s32[]{:T(128)} %get-tuple-element.177, s32[]{:T(128)} %bitcast.24, s32[]{:T(128)} %get-tuple-element.175, s32[1024]{0:T(1024)S(1)} %iota_add_fusion.2, s32[4096]{0:T(1024)S(1)} %add_multiply_fusion.2), kind=kOutput, calls=%fused_computation.12.clone.1 | convolution fusion | flops 608174080 | bytes 806928 | tf_op jit(solution)/shard_map/while/body/eval_jaxpr/dot_general | solution.py:38
  84.4 6.1 dynamic_update_slice.6
  91.2 0.7 iota_add_fusion.2
  91.9 1.3 slice.26
  93.2 11.1 %fusion.32 = f32[1,1024,64]{1,2,0:T(8,128)S(1)} fusion(bf16[64,4096]{1,0:T(8,128)(2,1)} %get-tuple-element.179, s32[]{:T(128)} %get-tuple-element.178, s32[]{:T(128)} %get-tuple-element.177, s32[]{:T(128)} %bitcast.24, s32[]{:T(128)} %get-tuple-element.175, s32[1024]{0:T(1024)S(1)} %iota_add_fusion.2, s32[4096]{0:T(1024)S(1)} %add_multiply_fusion.2), kind=kOutput, calls=%fused_computation.12.clone.1 | convolution fusion | flops 608174080 | bytes 806928 | tf_op jit(solution)/shard_map/while/body/eval_jaxpr/dot_general | solution.py:38
  104.5 6.1 dynamic_update_slice.6
  112.0 1.3 slice.26
  113.3 11.1 %fusion.32 = f32[1,1024,64]{1,2,0:T(8,128)S(1)} fusion(bf16[64,4096]{1,0:T(8,128)(2,1)} %get-tuple-element.179, s32[]{:T(128)} %get-tuple-element.178, s32[]{:T(128)} %get-tuple-element.177, s32[]{:T(128)} %bitcast.24, s32[]{:T(128)} %get-tuple-element.175, s32[1024]{0:T(1024)S(1)} %iota_add_fusion.2, s32[4096]{0:T(1024)S(1)} %add_multiply_fusion.2), kind=kOutput, calls=%fused_computation.12.clone.1 | convolution fusion | flops 608174080 | bytes 806928 | tf_op jit(solution)/shard_map/while/body/eval_jaxpr/dot_general | solution.py:38
  124.7 6.1 dynamic_update_slice.6
  132.2 1.3 slice.26
  133.5 11.1 %fusion.32 = f32[1,1024,64]{1,2,0:T(8,128)S(1)} fusion(bf16[64,4096]{1,0:T(8,128)(2,1)} %get-tuple-element.179, s32[]{:T(128)} %get-tuple-element.178, s32[]{:T(128)} %get-tuple-element.177, s32[]{:T(128)} %bitcast.24, s32[]{:T(128)} %get-tuple-element.175, s32[1024]{0:T(1024)S(1)} %iota_add_fusion.2, s32[4096]{0:T(1024)S(1)} %add_multiply_fusion.2), kind=kOutput, calls=%fused_computation.12.clone.1 | convolution fusion | flops 608174080 | bytes 806928 | tf_op jit(solution)/shard_map/while/body/eval_jaxpr/dot_general | solution.py:38
  144.8 6.1 dynamic_update_slice.6
  152.3 1.3 slice.26
  153.6 11.1 %fusion.32 = f32[1,1024,64]{1,2,0:T(8,128)S(1)} fusion(bf16[64,4096]{1,0:T(8,128)(2,1)} %get-tuple-element.179, s32[]{:T(128)} %get-tuple-element.178, s32[]{:T(128)} %get-tuple-element.177, s32[]{:T(128)} %bitcast.24, s32[]{:T(128)} %get-tuple-element.175, s32[1024]{0:T(1024)S(1)} %iota_add_fusion.2, s32[4096]{0:T(1024)S(1)} %add_multiply_fusion.2), kind=kOutput, calls=%fused_computation.12.clone.1 | convolution fusion | flops 608174080 | bytes 806928 | tf_op jit(solution)/shard_map/while/body/eval_jaxpr/dot_general | solution.py:38
  165.0 6.1 dynamic_update_slice.6
  172.5 1.3 slice.26
  173.8 11.1 %fusion.32 = f32[1,1024,64]{1,2,0:T(8,128)S(1)} fusion(bf16[64,4096]{1,0:T(8,128)(2,1)} %get-tuple-element.179, s32[]{:T(128)} %get-tuple-element.178, s32[]{:T(128)} %get-tuple-element.177, s32[]{:T(128)} %bitcast.24, s32[]{:T(128)} %get-tuple-element.175, s32[1024]{0:T(1024)S(1)} %iota_add_fusion.2, s32[4096]{0:T(1024)S(1)} %add_multiply_fusion.2), kind=kOutput, calls=%fused_computation.12.clone.1 | convolution fusion | flops 608174080 | bytes 806928 | tf_op jit(solution)/shard_map/while/body/eval_jaxpr/dot_general | solution.py:38
  185.1 6.1 dynamic_update_slice.6
  192.6 1.3 slice.26
  193.9 11.1 %fusion.32 = f32[1,1024,64]{1,2,0:T(8,128)S(1)} fusion(bf16[64,4096]{1,0:T(8,128)(2,1)} %get-tuple-element.179, s32[]{:T(128)} %get-tuple-element.178, s32[]{:T(128)} %get-tuple-element.177, s32[]{:T(128)} %bitcast.24, s32[]{:T(128)} %get-tuple-element.175, s32[1024]{0:T(1024)S(1)} %iota_add_fusion.2, s32[4096]{0:T(1024)S(1)} %add_multiply_fusion.2), kind=kOutput, calls=%fused_computation.12.clone.1 | convolution fusion | flops 608174080 | bytes 806928 | tf_op jit(solution)/shard_map/while/body/eval_jaxpr/dot_general | solution.py:38
  205.3 6.1 dynamic_update_slice.6
  212.7 1.3 slice.26
  214.1 11.1 %fusion.32 = f32[1,1024,64]{1,2,0:T(8,128)S(1)} fusion(bf16[64,4096]{1,0:T(8,128)(2,1)} %get-tuple-element.179, s32[]{:T(128)} %get-tuple-element.178, s32[]{:T(128)} %get-tuple-element.177, s32[]{:T(128)} %bitcast.24, s32[]{:T(128)} %get-tuple-element.175, s32[1024]{0:T(1024)S(1)} %iota_add_fusion.2, s32[4096]{0:T(1024)S(1)} %add_multiply_fusion.2), kind=kOutput, calls=%fused_computation.12.clone.1 | convolution fusion | flops 608174080 | bytes 806928 | tf_op jit(solution)/shard_map/while/body/eval_jaxpr/dot_general | solution.py:38
  225.4 6.1 dynamic_update_slice.6
  232.9 1.3 slice.26
  234.2 11.1 %fusion.32 = f32[1,1024,64]{1,2,0:T(8,128)S(1)} fusion(bf16[64,4096]{1,0:T(8,128)(2,1)} %get-tuple-element.179, s32[]{:T(128)} %get-tuple-element.178, s32[]{:T(128)} %get-tuple-element.177, s32[]{:T(128)} %bitcast.24, s32[]{:T(128)} %get-tuple-element.175, s32[1024]{0:T(1024)S(1)} %iota_add_fusion.2, s32[4096]{0:T(1024)S(1)} %add_multiply_fusion.2), kind=kOutput, calls=%fused_computation.12.clone.1 | convolution fusion | flops 608174080 | bytes 806928 | tf_op jit(solution)/shard_map/while/body/eval_jaxpr/dot_general | solution.py:38
  245.5 6.1 dynamic_update_slice.6
  253.0 1.3 slice.26
  254.4 11.1 %fusion.32 = f32[1,1024,64]{1,2,0:T(8,128)S(1)} fusion(bf16[64,4096]{1,0:T(8,128)(2,1)} %get-tuple-element.179, s32[]{:T(128)} %get-tuple-element.178, s32[]{:T(128)} %get-tuple-element.177, s32[]{:T(128)} %bitcast.24, s32[]{:T(128)} %get-tuple-element.175, s32[1024]{0:T(1024)S(1)} %iota_add_fusion.2, s32[4096]{0:T(1024)S(1)} %add_multiply_fusion.2), kind=kOutput, calls=%fused_computation.12.clone.1 | convolution fusion | flops 608174080 | bytes 806928 | tf_op jit(solution)/shard_map/while/body/eval_jaxpr/dot_general | solution.py:38
  265.7 6.1 dynamic_update_slice.6
  273.2 1.3 slice.26
  274.5 11.1 %fusion.32 = f32[1,1024,64]{1,2,0:T(8,128)S(1)} fusion(bf16[64,4096]{1,0:T(8,128)(2,1)} %get-tuple-element.179, s32[]{:T(128)} %get-tuple-element.178, s32[]{:T(128)} %get-tuple-element.177, s32[]{:T(128)} %bitcast.24, s32[]{:T(128)} %get-tuple-element.175, s32[1024]{0:T(1024)S(1)} %iota_add_fusion.2, s32[4096]{0:T(1024)S(1)} %add_multiply_fusion.2), kind=kOutput, calls=%fused_computation.12.clone.1 | convolution fusion | flops 608174080 | bytes 806928 | tf_op jit(solution)/shard_map/while/body/eval_jaxpr/dot_general | solution.py:38
  285.8 6.1 dynamic_update_slice.6
  293.3 1.3 slice.26
  294.6 11.1 %fusion.32 = f32[1,1024,64]{1,2,0:T(8,128)S(1)} fusion(bf16[64,4096]{1,0:T(8,128)(2,1)} %get-tuple-element.179, s32[]{:T(128)} %get-tuple-element.178, s32[]{:T(128)} %get-tuple-element.177, s32[]{:T(128)} %bitcast.24, s32[]{:T(128)} %get-tuple-element.175, s32[1024]{0:T(1024)S(1)} %iota_add_fusion.2, s32[4096]{0:T(1024)S(1)} %add_multiply_fusion.2), kind=kOutput, calls=%fused_computation.12.clone.1 | convolution fusion | flops 608174080 | bytes 806928 | tf_op jit(solution)/shard_map/while/body/eval_jaxpr/dot_general | solution.py:38
  306.0 6.1 dynamic_update_slice.6
  313.5 1.3 slice.26
  314.8 11.1 %fusion.32 = f32[1,1024,64]{1,2,0:T(8,128)S(1)} fusion(bf16[64,4096]{1,0:T(8,128)(2,1)} %get-tuple-element.179, s32[]{:T(128)} %get-tuple-element.178, s32[]{:T(128)} %get-tuple-element.177, s32[]{:T(128)} %bitcast.24, s32[]{:T(128)} %get-tuple-element.175, s32[1024]{0:T(1024)S(1)} %iota_add_fusion.2, s32[4096]{0:T(1024)S(1)} %add_multiply_fusion.2), kind=kOutput, calls=%fused_computation.12.clone.1 | convolution fusion | flops 608174080 | bytes 806928 | tf_op jit(solution)/shard_map/while/body/eval_jaxpr/dot_general | solution.py:38
  326.1 6.1 dynamic_update_slice.6
  332.2 6.7 copy.7
  339.0 88.0 %reduce-scatter.3.cloned.1.call-done = f32[1024,64]{0,1:T(8,128)} async-done(((f32[16384,64]{0,1:T(8,128)}), f32[1024,64]{0,1:T(8,128)}) %reduce-scatter.3.cloned.1.call-update) | async-done | bytes 262160 | tf_op jit(solution)/shard_map/reduce_scatter | solution.py:45
  427.0 1.6 convert_bitcast_fusion
  428.7 75.2 %all-gather.4.cloned.1.call-done = bf16[1024,1024]{1,0:T(8,128)(2,1)} async-done(((bf16[64,1024]{1,0:T(8,128)(2,1)}), bf16[1024,1024]{1,0:T(8,128)(2,1)}) %all-gather.4.cloned.1.call-update) | async-done | bytes 2097168 | tf_op jit(solution)/shard_map/all_gather | solution.py:53
  503.9 5.9 fusion.21
  510.4 82.5 %reduce-scatter.5.cloned.1.call-done = f32[64,1024]{1,0:T(8,128)} async-done(((f32[1024,1024]{1,0:T(8,128)}), f32[64,1024]{1,0:T(8,128)}) %reduce-scatter.5.cloned.1.call-update) | async-done | bytes 262160 | tf_op jit(solution)/shard_map/reduce_scatter | solution.py:57
  592.9 1.6 convert_element_type.19
  594.5 53.6 %all-gather.8.cloned.1.call-done = bf16[64,16384]{1,0:T(8,128)(2,1)} async-done(((bf16[64,1024]{1,0:T(8,128)(2,1)}), bf16[64,16384]{1,0:T(8,128)(2,1)}) %all-gather.8.cloned.1.call-update) | async-done | bytes 2097168 | tf_op jit(solution)/shard_map/all_gather | solution.py:60
  648.1 76.2 %all-gather.6.cloned.1.call-done = bf16[64,16384]{1,0:T(8,128)(2,1)} async-done(((bf16[64,1024]{1,0:T(8,128)(2,1)}), bf16[64,16384]{1,0:T(8,128)(2,1)}) %all-gather.6.cloned.1.call-update) | async-done | bytes 2097168 | tf_op jit(solution)/shard_map/all_gather | solution.py:62
  724.3 3.5 convolution_multiply_fusion
  (74 shorter events, 24.1 us)
Async XLA Ops:
  6.5 497.4 %copy-start = (bf16[1024,1024]{1,0:T(8,128)(2,1)S(1)}, bf16[1024,1024]{1,0:T(8,128)(2,1)}, u32[]{:S(2)}) copy-start(bf16[1024,1024]{1,0:T(8,128)(2,1)} %param.6) | copy-start | bytes 6291460
  6.5 420.5 %reduce-scatter.3.cloned.1.call-start = ((), (), s32[]{:S(2)}) async-start(), calls=%async_computation.2 | async-start | bytes 4456448 | tf_op jit(solution)/shard_map/reduce_scatter | solution.py:45
  338.9 165.0 %all-gather.4.cloned.1.call-start = ((), (), s32[]{:S(2)}) async-start(), calls=%async_computation.3 | async-start | bytes 2228224 | tf_op jit(solution)/shard_map/all_gather | solution.py:53
  428.7 164.2 %reduce-scatter.5.cloned.1.call-start = ((), (), s32[]{:S(2)}) async-start(), calls=%async_computation.4 | async-start | bytes 4456448 | tf_op jit(solution)/shard_map/reduce_scatter | solution.py:57
  509.8 138.3 %all-gather.8.cloned.1.call-start = ((), (), s32[]{:S(2)}) async-start(), calls=%async_computation.6 | async-start | bytes 2228224 | tf_op jit(solution)/shard_map/all_gather | solution.py:60
  510.4 213.9 %all-gather.6.cloned.1.call-start = ((), (), s32[]{:S(2)}) async-start(), calls=%async_computation.5 | async-start | bytes 2228224 | tf_op jit(solution)/shard_map/all_gather | solution.py:62
Sparse Core Ops, SparseCore 0:
  339.1 87.9 reduce-scatter.2
  428.9 74.9 all-gather.3
  509.9 82.9 reduce-scatter.4
  595.5 52.5 all-gather.7
  649.7 74.4 all-gather.5
where the time goes:
time: 739 us; the launch traced here: 734 us
  waiting for transfers between devices  376 us (51%)
  matrix products  186 us (25%)
  local copies, waits for them, and re-layouts  142 us (19%)
  between operations  15 us (2%)
  other arithmetic  14.4 us (2%)
    dot_general x16, matrix products, column_block(): lax.dot_general(sign_table, gradients, (((0,), (1,)), ((), ())), preferre...  177 us
    dynamic_update_slice x32, local copies, waits for them, and re-layouts, per_device(): lax.map(column_block, col_starts)  102 us
    reduce_scatter x1, waiting for transfers between devices, per_device(): lax.psum_scatter(lax.map(column_block, col_starts).reshape(feat_par * lax...  88 us
    reduce_scatter x1, waiting for transfers between devices, per_device(): lax.psum_scatter(partials, 'par', scatter_dimension=0, tiled=True)  82.5 us
    all_gather x1, waiting for transfers between devices, per_device(): lax.all_gather(conditioned, 'ex', axis=1, tiled=True)  76.2 us
    all_gather x1, waiting for transfers between devices, per_device(): lax.all_gather(features, 'ex', axis=0, tiled=True)  75.2 us
    all_gather x1, waiting for transfers between devices, per_device(): feature_rows = lax.all_gather(features, 'par', axis=1, tiled=True)  53.6 us
    slice x16, local copies, waits for them, and re-layouts, hash_table(): mixed = mixed * (hash_words[0] | 1) + hash_words[1]  21.1 us
  transfers between devices with their start and end apart: 5, of which 5 were waited for; matrix products, arithmetic and copies ran while one was open for 0% of the time, Pallas kernels for 0%

commit v1 on v0

v1 whole, which is shorter than its diff:
```python
import jax
import jax.numpy as jnp
from jax import lax
from jax.experimental import pallas as pl
from jax.experimental.pallas import tpu as pltpu
from jax.sharding import Mesh
from jax.sharding import PartitionSpec as P

FEATURES = 16384
SCALE = FEATURES ** (-0.5)
BF16 = jnp.bfloat16
F32 = jnp.float32

EX = ("zh", "zl", "yl")
CHIPS = ("yh", "x")
PAR = ("yh", "x", "c")


def shifted(values, amount):
    return lax.shift_right_logical(values, jnp.full(values.shape, amount, jnp.int32))


def signs(hash_words, row_start, rows, cols):
    m0 = hash_words[0] | 1
    row_ids = lax.broadcasted_iota(jnp.int32, (rows, cols.shape[1]), 0)
    mixed = row_ids * (FEATURES * m0) + (cols * m0 + (row_start * (FEATURES * m0) + hash_words[1]))
    mixed = mixed ^ shifted(mixed, 15)
    mixed = mixed * (hash_words[2] | 1)
    mixed = mixed ^ shifted(mixed, 13)
    mixed = mixed * (hash_words[3] | 1)
    return jnp.where(mixed < 0, BF16(-1), BF16(1))


def project_kernel(words, mine, next_y, next_z, diag_a, diag_b, *rest):
    other = rest[:5]
    out, examples, total = rest[5:]
    step = pl.program_id(0)
    half = pl.num_programs(0) // 2
    me = lax.axis_index("zl") * 2 + lax.axis_index("yl")
    core = lax.axis_index("c")
    chip = lax.axis_index("yh") * 4 + lax.axis_index("x")
    slice_id = lax.axis_index("yl") * 4 + lax.axis_index("zl") * 2 + core
    rows, depth = mine.shape

    def fill(own, y, z, da, db):
        def at(flip, offset=0):
            return pl.multiple_of((me ^ flip) * rows + offset, 32)

        examples[pl.ds(at(0), rows), :] = own[...]
        examples[pl.ds(at(1), rows), :] = y[...]
        examples[pl.ds(at(2), rows), :] = z[...]
        examples[pl.ds(at(3), rows // 2), :] = da[...]
        examples[pl.ds(at(3, rows // 2), rows // 2), :] = db[...]

    @pl.when(step == 0)
    def _():
        total[...] = jnp.zeros_like(total)

    @pl.when(step < half)
    def _():
        fill(mine, next_y, next_z, diag_a, diag_b)

    @pl.when(step >= half)
    def _():
        fill(*other)

    which = jnp.where(step < half, core, 1 - core)
    inner = jnp.where(step < half, step, step - half)
    row_start = (chip * 2 + which) * (half * depth) + inner * depth
    wide = 512
    held = examples[...]

    def chunk(index, carry):
        lane = lax.broadcasted_iota(jnp.int32, (1, wide), 1)
        cols = lane + (lane >> 8) * (2048 - 256) + (index * (wide // 256) * 2048 + slice_id * 256)
        table = signs(words, row_start, depth, cols)
        at = pl.ds(pl.multiple_of(index * wide, wide), wide)
        total[:, at] += jnp.dot(held, table, preferred_element_type=F32)
        return carry

    lax.fori_loop(0, total.shape[1] // wide, chunk, 0, unroll=2)

    @pl.when(step == 2 * half - 1)
    def _():
        for block in range(8):
            out[block] = total[:, block * 256 : (block + 1) * 256] * SCALE


def project(words, own, other, depth=512):
    rows, params = own[0].shape
    half = params // depth

    def spec(array, second):
        if second:
            return pl.BlockSpec((array.shape[0], depth), lambda k: (0, jnp.maximum(k - half, 0)))
        return pl.BlockSpec((array.shape[0], depth), lambda k: (0, jnp.minimum(k, half - 1)))

    return pl.pallas_call(
        project_kernel,
        out_shape=jax.ShapeDtypeStruct((8, 4 * rows, 256), F32),
        grid=(2 * half,),
        in_specs=[pl.BlockSpec(memory_space=pltpu.SMEM)]
        + [spec(a, False) for a in own]
        + [spec(a, True) for a in other],
        out_specs=pl.BlockSpec((8, 4 * rows, 256), lambda k: (0, 0, 0)),
        scratch_shapes=[pltpu.VMEM((4 * rows, depth), BF16), pltpu.VMEM((4 * rows, 2048), F32)],
        compiler_params=pltpu.CompilerParams(vmem_limit_bytes=24 << 20),
        cost_estimate=pl.CostEstimate(flops=2 * 256 * 8192 * 2048, bytes_accessed=5 << 20, transcendentals=0),
    )(words, *own, *other)


def sum_kernel(parts, out):
    total = parts[0]
    for index in range(1, parts.shape[0]):
        total += parts[index]
    out[...] = total.astype(out.dtype)


def sum_parts(parts):
    return pl.pallas_call(
        sum_kernel,
        out_shape=jax.ShapeDtypeStruct(parts.shape[1:], BF16),
        compiler_params=pltpu.CompilerParams(vmem_limit_bytes=16 << 20),
    )(parts)


def condition_kernel(pieces, low, high, out):
    group = pl.program_id(0)
    total = None
    for yl in range(2):
        tile = (low, high)[yl]
        for zl in range(2):
            for core in range(2):
                start = (zl * 2 + core) * 256
                term = jnp.dot(
                    pieces[0, zl, yl, core], tile[start : start + 256, :], preferred_element_type=F32
                )
                total = term if total is None else total + term
    out[...] = total


def condition(pieces, low, high):
    rows = pieces.shape[4]
    return pl.pallas_call(
        condition_kernel,
        out_shape=jax.ShapeDtypeStruct((4 * rows, low.shape[1]), F32),
        grid=(4,),
        in_specs=[
            pl.BlockSpec((1,) + pieces.shape[1:], lambda g: (g, 0, 0, 0, 0, 0)),
            pl.BlockSpec(low.shape, lambda g: (0, 0)),
            pl.BlockSpec(high.shape, lambda g: (0, 0)),
        ],
        out_specs=pl.BlockSpec((rows, low.shape[1]), lambda g: (g, 0)),
        compiler_params=pltpu.CompilerParams(vmem_limit_bytes=24 << 20),
        cost_estimate=pl.CostEstimate(flops=2 * 512 * 2048 * 1024, bytes_accessed=7 << 20, transcendentals=0),
    )(pieces, low, high)


def pair_kernel(parts, features, out):
    total = parts[0]
    for index in range(1, parts.shape[0]):
        total += parts[index]
    rows = total.astype(BF16)
    for zh in range(4):
        pairs = None
        for zl in range(2):
            for core in range(2):
                start = (zl * 2 + core) * 256
                term = lax.dot_general(
                    rows[:, start : start + 256],
                    features[zh * 2 + zl, core],
                    (((1,), (1,)), ((), ())),
                    preferred_element_type=F32,
                )
                pairs = term if pairs is None else pairs + term
        for block in range(4):
            piece = pairs[:, block * 64 : (block + 1) * 64]
            out[zh * 4 + block, :, :64] = piece[:32]
            out[zh * 4 + block, :, 64:] = piece[32:]


def pair(parts, features):
    return pl.pallas_call(
        pair_kernel,
        out_shape=jax.ShapeDtypeStruct((16, 32, 128), F32),
        compiler_params=pltpu.CompilerParams(vmem_limit_bytes=24 << 20),
    )(parts, features)


def finish_kernel(parts, out):
    total = parts[0]
    for index in range(1, parts.shape[0]):
        total += parts[index]
    total = total * SCALE
    out[:32] = total[:, :64]
    out[32:] = total[:, 64:]


def finish(parts):
    return pl.pallas_call(
        finish_kernel,
        out_shape=jax.ShapeDtypeStruct((64, 64), F32),
    )(parts)


def swap(value, axis):
    return lax.ppermute(value, axis, [(0, 1), (1, 0)])


def per_device(gradients, inverse_gram, hash_words):
    core = lax.axis_index("c")
    half = gradients.shape[0] // 2
    next_y = swap(gradients, "yl")
    next_z = swap(gradients, "zl")
    own = [gradients, next_y, next_z, swap(next_y[:half], "zl"), swap(next_z[half:], "yl")]
    other = [swap(a, "c") for a in own]
    other_tile = swap(inverse_gram, "c")

    partial = project(hash_words, own, other)
    piece = sum_parts(lax.all_to_all(partial, CHIPS, 0, 0, tiled=True))

    by_core = jnp.transpose(piece.reshape(2, 2, 64, 256), (1, 0, 2, 3)).reshape(2, 128, 256)
    by_core = lax.all_to_all(by_core, "c", 0, 0, tiled=True)
    gathered = lax.all_gather(by_core, EX, axis=0).reshape(4, 2, 2, 2, 128, 256)

    route = []
    for z in range(8):
        for yl in range(2):
            for chip in range(8):
                for c in range(2):
                    route.append((((z * 2 + yl) * 8 + chip) * 2 + c, ((chip * 2 + yl) * 8 + z) * 2 + c))
    turned = lax.ppermute(piece, EX + PAR, route)
    features = lax.all_gather(turned, PAR, axis=0).reshape(8, 2, 256, 256)

    low = jnp.where(core == 0, inverse_gram, other_tile)
    high = jnp.where(core == 0, other_tile, inverse_gram)
    conditioned = condition(gathered, low, high)
    parts = lax.all_to_all(conditioned.reshape(8, 64, 1024), CHIPS, 0, 0, tiled=True)
    return finish(lax.all_to_all(pair(parts, features), EX, 0, 0, tiled=True))


def solution(mesh):
    fine = Mesh(mesh.devices.reshape(4, 2, 2, 2, 4, 2), EX + PAR)
    return jax.shard_map(
        per_device,
        mesh=fine,
        in_specs=(P(EX, PAR), P(PAR, EX), P()),
        out_specs=P(PAR, EX),
        check_vma=False,
    )
```

time: 739 us -> 272 us (0.37)
  waiting for transfers between devices: 376 us -> 125 us
  matrix products: 186 us -> 0 us
  local copies, waits for them, and re-layouts: 142 us -> 8.45 us
  blocking collectives: 0 us -> 57.1 us
  Pallas kernels: 0 us -> 37.9 us
  starting transfers between devices: 0.17 us -> 24.8 us
  other arithmetic: 14.4 us -> 3.9 us
    dot_general x18 -> x0, matrix products: 186 us -> none  [the longest x16 177 us: column_block(): lax.dot_general(sign_table, gradients, (((0,), (1,)), ((), ())), preferre...]
    reduce_scatter x2 -> x0, waiting for transfers between devices: 170 us -> none  [the longest x1 88 us: per_device(): lax.psum_scatter(lax.map(column_block, col_starts).reshape(feat_par * lax...]
    all_gather x3 -> x2, waiting for transfers between devices: 205 us -> 93.3 us  [the longest x1 47.4 us: per_device(): gathered = lax.all_gather(by_core, EX, axis=0).reshape(4, 2, 2, 2, 128, 256)]
    dynamic_update_slice x32 -> x0, local copies, waits for them, and re-layouts: 102 us -> none  [per_device(): lax.map(column_block, col_starts)]
    all_to_all x0 -> x3, blocking collectives: none -> 57.1 us  [the longest x1 31.5 us: per_device(): piece = sum_parts(lax.all_to_all(partial, CHIPS, 0, 0, tiled=True))]
    pallas_call x0 -> x5, Pallas kernels: none -> 37.9 us  [the longest x1 32.4 us: project(): pl.pallas_call(project_kernel, out_shape=jax.ShapeDtypeStruct((8, 4 * row...]
    ppermute x0 -> x11, waiting for transfers between devices: none -> 31.7 us  [the longest x10 17.3 us: swap(): return lax.ppermute(value, axis, [(0, 1), (1, 0)])]
    slice x17 -> x2, local copies, waits for them, and re-layouts: 22.6 us -> 0.04 us  [the longest x1 0.02 us: per_device(): next_y[:half]]
  transfers between devices with their start and end apart: 5 -> 14, of which waited for: 5 -> 7; matrix products, arithmetic and copies ran while one was open for 0% -> 1% of each run, Pallas kernels for 0% -> 1%
where the time goes in v1:
time: 272 us; the launch traced here: 271 us
  waiting for transfers between devices  125 us (46%)
  blocking collectives  57.1 us (21%)
  Pallas kernels  37.9 us (14%)
  starting transfers between devices  24.8 us (9%)
  between operations  13.5 us (5%)
  local copies, waits for them, and re-layouts  8.45 us (3%)
  other arithmetic  3.9 us (1%)
    all_gather x1, waiting for transfers between devices, per_device(): gathered = lax.all_gather(by_core, EX, axis=0).reshape(4, 2, 2, 2, 128, 256)  47.4 us
    all_gather x1, waiting for transfers between devices, per_device(): features = lax.all_gather(turned, PAR, axis=0).reshape(8, 2, 256, 256)  45.8 us
    pallas_call x1, Pallas kernels, project(): pl.pallas_call(project_kernel, out_shape=jax.ShapeDtypeStruct((8, 4 * row...  32.4 us
    all_to_all x1, blocking collectives, per_device(): piece = sum_parts(lax.all_to_all(partial, CHIPS, 0, 0, tiled=True))  31.5 us
    all_to_all x1, blocking collectives, per_device(): return finish(lax.all_to_all(pair(parts, features), EX, 0, 0, tiled=True))  20.9 us
    ppermute x10, waiting for transfers between devices, swap(): return lax.ppermute(value, axis, [(0, 1), (1, 0)])  17.3 us
    ppermute x1, waiting for transfers between devices, per_device(): turned = lax.ppermute(piece, EX + PAR, route)  14.4 us
    ppermute x1, starting transfers between devices, per_device(): turned = lax.ppermute(piece, EX + PAR, route)  10.5 us
  transfers between devices with their start and end apart: 14, of which 7 were waited for; matrix products, arithmetic and copies ran while one was open for 1% of the time, Pallas kernels for 1%

profile of v1, /device:TPU:22, one launch (start us, length us, event | category | flops | bytes accessed | tf_op | source)
XLA Modules:
  0.0 270.6 jit_solution(1706134937891358689)
XLA Ops:
  6.5 0.0 all-gather.5.cloned.1.call-start
  6.5 1.3 collective-permute-start
  7.8 1.9 collective-permute-start.1
  9.7 0.0 collective-permute-start.4
  9.7 10.7 %collective-permute-done.next_y = bf16[64,4096]{1,0:T(8,128)(2,1)S(1)} collective-permute-done((bf16[64,4096]{1,0:T(8,128)(2,1)}, bf16[64,4096]{1,0:T(8,128)(2,1)S(1)}, u32[]{:S(2)}, u32[]{:S(2)}) %collective-permute-start) | collective-permute-done | bytes 524320 | tf_op jit(solution)/shard_map/ppermute | solution.py:207
  20.4 2.0 collective-permute-start.2
  22.4 0.0 collective-permute-done.1.next_z
  22.5 1.4 collective-permute-start.3
  23.8 0.0 collective-permute-start.5
  23.8 0.5 collective-permute-start.6
  24.3 3.5 %collective-permute-done.2.diag_a = bf16[32,4096]{1,0:T(8,128)(2,1)S(1)} collective-permute-done((bf16[32,4096]{1,0:T(8,128)(2,1)S(1)}, bf16[32,4096]{1,0:T(8,128)(2,1)S(1)}, u32[]{:S(2)}, u32[]{:S(2)}) %collective-permute-start.2) | collective-permute-done | bytes 262176 | tf_op jit(solution)/shard_map/ppermute | solution.py:207
  27.9 0.0 collective-permute-start.7
  27.9 1.6 collective-permute-done.3.diag_b
  29.4 0.0 collective-permute-start.8
  29.4 0.0 collective-permute-done.4.rest_0_
  29.5 0.0 collective-permute-done.7.rest_3_
  29.5 1.5 collective-permute-done.8.rest_4_
  31.0 0.0 collective-permute-done.5.rest_1_
  31.0 0.0 collective-permute-done.6.rest_2_
  31.0 0.0 copy-start.4
  31.0 1.0 copy-done.4
  32.0 0.0 copy-start.5
  32.0 0.7 copy-done.5
  32.7 32.4 %shard_map.37 = f32[8,256,256]{2,1,0:T(8,128)S(1)} custom-call(s32[4]{0:T(128)S(1)} %copy-done.5, bf16[64,4096]{1,0:T(8,128)(2,1)S(1)} %copy-done.4, bf16[64,4096]{1,0:T(8,128)(2,1)S(1)} %collective-permute-done.next_y, bf16[64,4096]{1,0:T(8,128)(2,1)S(1)} %collective-permute-done.1.next_z, bf16[32,4096]{1,0:T(8,128)(2,1)S(1)} %collective-permute-done.2.diag_a, ...), custom_call_target="tpu_custom_call" | custom-call | flops 8589934592 | bytes 5242880 | tf_op jit(solution)/shard_map/pallas_call | solution.py:98
  65.1 31.5 %all_to_all.20.parts = f32[8,256,256]{2,1,0:T(8,128)S(1)} all-to-all(f32[8,256,256]{2,1,0:T(8,128)S(1)} %shard_map.37), channel_id=1, replica_groups=mesh['zh'=4,'zl'=2,'yl'=2,'yh'=2,'x'=4,'c'=2] {'yh','x'}, dimensions={0} | all-to-all | bytes 4194304 | tf_op jit(solution)/shard_map/all_to_all | solution.py:220
  96.7 0.0 copy-start.6
  96.7 0.1 shard_map.38
  96.8 4.7 %all_to_all.21 = bf16[2,128,256]{2,1,0:T(8,128)(2,1)} all-to-all(bf16[2,128,256]{2,1,0:T(8,128)(2,1)S(1)} %bitcast.11), channel_id=1, replica_groups=mesh['zh'=4,'zl'=2,'yl'=2,'yh'=2,'x'=4,'c'=2] {'c'}, dimensions={0} | all-to-all | bytes 262144 | tf_op jit(solution)/shard_map/all_to_all | solution.py:223
  101.4 0.0 all-gather.5.cloned.1.call-update
  101.5 0.0 all-gather.7.cloned.1.call-start
  101.5 0.0 copy-done.6
  101.5 0.2 collective-permute-start.9
  101.8 10.5 %collective-permute-start.10 = (bf16[256,256]{1,0:T(8,128)(2,1)S(1)}, bf16[256,256]{1,0:T(8,128)(2,1)S(1)}, u32[]{:S(2)}, u32[]{:S(2)}) collective-permute-start(bf16[256,256]{1,0:T(8,128)(2,1)S(1)} %shard_map.38), channel_id=1, source_target_pairs={{0,0},{1,1},{2,32},{3,33},{4,64},{5,65},{6,96},{7,97},{8,128},{9,1... | collective-permute-start | bytes 393224 | tf_op jit(solution)/shard_map/ppermute | solution.py:232
  112.2 14.4 %collective-permute-done.10 = bf16[256,256]{1,0:T(8,128)(2,1)S(1)} collective-permute-done((bf16[256,256]{1,0:T(8,128)(2,1)S(1)}, bf16[256,256]{1,0:T(8,128)(2,1)S(1)}, u32[]{:S(2)}, u32[]{:S(2)}) %collective-permute-start.10) | collective-permute-done | bytes 131104 | tf_op jit(solution)/shard_map/ppermute | solution.py:232
  126.7 0.0 copy-start.7
  126.7 0.6 copy-done.7
  127.3 0.0 all-gather.7.cloned.1.call-update
  127.3 0.0 collective-permute-done.9
  127.4 3.9 %broadcast_select_fusion = (bf16[1024,1024]{1,0:T(8,128)(2,1)S(1)}, bf16[1024,1024]{1,0:T(8,128)(2,1)}) fusion(bf16[1024,1024]{1,0:T(8,128)(2,1)} %collective-permute-done.9, bf16[1024,1024]{1,0:T(8,128)(2,1)} %param.4, pred[]{:T(512)S(6)} %eq.4), kind=kLoop, calls=%fused_computation | loop fusion | flops 2097152 | bytes 8388609 | tf_op jit(solution)/shard_map/jit(_where)/select_n | solution.py:236
  131.3 47.4 %all-gather.5.cloned.1.call-done = bf16[32,128,256]{2,1,0:T(8,128)(2,1)} async-done(((bf16[2,128,256]{2,1,0:T(8,128)(2,1)}), bf16[32,128,256]{2,1,0:T(8,128)(2,1)}) %all-gather.5.cloned.1.call-update) | async-done | bytes 2097168 | tf_op jit(solution)/shard_map/all_gather | solution.py:224
  178.7 0.0 copy-start.1
  178.7 1.6 copy-done.1
  180.3 0.0 copy-start.3
  180.3 1.6 copy-done.3
  181.9 2.9 %shard_map.39 = f32[512,1024]{1,0:T(8,128)S(1)} custom-call(bf16[4,2,2,2,128,256]{5,4,3,2,1,0:T(8,128)(2,1)S(1)} %bitcast.9, bf16[1024,1024]{1,0:T(8,128)(2,1)S(1)} %copy-done.1, bf16[1024,1024]{1,0:T(8,128)(2,1)S(1)} %get-tuple-element.5.high), custom_call_target="tpu_custom_call" | custom-call | flops 2147483648 | bytes 7340032 | tf_op jit(solution)/shard_map/pallas_call | solution.py:144
  184.8 0.0 copy-start
  184.8 1.3 copy-done
  186.1 6.9 %all-to-all-start.2 = ((f32[8,64,1024]{2,1,0:T(8,128)}), f32[8,64,1024]{2,1,0:T(8,128)S(1)}, u32[]{:S(2)}, u32[]{:S(2)}) async-start(f32[8,64,1024]{2,1,0:T(8,128)} %bitcast.7), calls=%async_computation.2 | async-start | bytes 4194304 | tf_op jit(solution)/shard_map/all_to_all | solution.py:238
  193.0 45.8 %all-gather.7.cloned.1.call-done = bf16[4096,256]{1,0:T(8,128)(2,1)} async-done(((bf16[256,256]{1,0:T(8,128)(2,1)}), bf16[4096,256]{1,0:T(8,128)(2,1)}) %all-gather.7.cloned.1.call-update) | async-done | bytes 2097168 | tf_op jit(solution)/shard_map/all_gather | solution.py:233
  238.8 0.0 all-to-all-done.2.parts
  238.8 0.0 copy-start.2
  238.8 1.6 copy-done.2
  240.4 0.8 shard_map.40
  241.2 20.9 %all_to_all.22.parts = f32[16,32,128]{2,1,0:T(8,128)} all-to-all(f32[16,32,128]{2,1,0:T(8,128)S(1)} %shard_map.40), channel_id=1, replica_groups=mesh['zh'=4,'zl'=2,'yl'=2,'yh'=2,'x'=4,'c'=2] {'zh','zl','yl'}, dimensions={0} | all-to-all | bytes 524288 | tf_op jit(solution)/shard_map/all_to_all | solution.py:239
  262.2 1.7 shard_map.41
  (3 shorter events, 0.0 us)
Async XLA Ops:
  6.5 172.2 %all-gather.5.cloned.1.call-start = ((), (), s32[]{:S(2)}) async-start(), calls=%async_computation.4 | async-start | bytes 2228224 | tf_op jit(solution)/shard_map/all_gather | solution.py:224
  6.5 13.9 %collective-permute-start = (bf16[64,4096]{1,0:T(8,128)(2,1)}, bf16[64,4096]{1,0:T(8,128)(2,1)S(1)}, u32[]{:S(2)}, u32[]{:S(2)}) collective-permute-start(bf16[64,4096]{1,0:T(8,128)(2,1)} %mine.1), channel_id=1, source_target_pairs={{0,16},{16,0},{1,17},{17,1},{2,18},{18,2},{3,19},{19,3},{4,20},{20... | collective-permute-start | bytes 1572872 | tf_op jit(solution)/shard_map/ppermute | solution.py:207
  7.8 14.6 %collective-permute-start.1 = (bf16[64,4096]{1,0:T(8,128)(2,1)}, bf16[64,4096]{1,0:T(8,128)(2,1)S(1)}, u32[]{:S(2)}, u32[]{:S(2)}) collective-permute-start(bf16[64,4096]{1,0:T(8,128)(2,1)} %mine.1), channel_id=1, source_target_pairs={{0,32},{32,0},{1,33},{33,1},{2,34},{34,2},{3,35},{35,3},{4,36},{36... | collective-permute-start | bytes 1572872 | tf_op jit(solution)/shard_map/ppermute | solution.py:207
  9.7 19.7 %collective-permute-start.4 = (bf16[64,4096]{1,0:T(8,128)(2,1)}, bf16[64,4096]{1,0:T(8,128)(2,1)S(1)}, u32[]{:S(2)}, u32[]{:S(2)}) collective-permute-start(bf16[64,4096]{1,0:T(8,128)(2,1)} %mine.1), channel_id=1, source_target_pairs={{0,1},{1,0},{2,3},{3,2},{4,5},{5,4},{6,7},{7,6},{8,9},{9,8},{10,11... | collective-permute-start | bytes 1572872 | tf_op jit(solution)/shard_map/ppermute | solution.py:207
  20.4 7.4 %collective-permute-start.2 = (bf16[32,4096]{1,0:T(8,128)(2,1)S(1)}, bf16[32,4096]{1,0:T(8,128)(2,1)S(1)}, u32[]{:S(2)}, u32[]{:S(2)}) collective-permute-start(bf16[32,4096]{1,0:T(8,128)(2,1)S(1)} %slice.8), channel_id=1, source_target_pairs={{0,32},{32,0},{1,33},{33,1},{2,34},{34,2},{3,35},{35,3},{4,36},{36... | collective-permute-start | bytes 786440 | tf_op jit(solution)/shard_map/ppermute | solution.py:207
  22.5 7.0 %collective-permute-start.3 = (bf16[32,4096]{1,0:T(8,128)(2,1)S(1)}, bf16[32,4096]{1,0:T(8,128)(2,1)S(1)}, u32[]{:S(2)}, u32[]{:S(2)}) collective-permute-start(bf16[32,4096]{1,0:T(8,128)(2,1)S(1)} %slice.9), channel_id=1, source_target_pairs={{0,16},{16,0},{1,17},{17,1},{2,18},{18,2},{3,19},{19,3},{4,20},{20... | collective-permute-start | bytes 786440 | tf_op jit(solution)/shard_map/ppermute | solution.py:207
  23.8 7.2 %collective-permute-start.5 = (bf16[64,4096]{1,0:T(8,128)(2,1)S(1)}, bf16[64,4096]{1,0:T(8,128)(2,1)S(1)}, u32[]{:S(2)}, u32[]{:S(2)}) collective-permute-start(bf16[64,4096]{1,0:T(8,128)(2,1)S(1)} %collective-permute-done.next_y), channel_id=1, source_target_pairs={{0,1},{1,0},{2,3},{3,2},{4,5},{5,4},{6,7},{7,6},{8,9},{9,8},{10,11... | collective-permute-start | bytes 1572872 | tf_op jit(solution)/shard_map/ppermute | solution.py:207
  23.8 7.2 %collective-permute-start.6 = (bf16[64,4096]{1,0:T(8,128)(2,1)S(1)}, bf16[64,4096]{1,0:T(8,128)(2,1)S(1)}, u32[]{:S(2)}, u32[]{:S(2)}) collective-permute-start(bf16[64,4096]{1,0:T(8,128)(2,1)S(1)} %collective-permute-done.1.next_z), channel_id=1, source_target_pairs={{0,1},{1,0},{2,3},{3,2},{4,5},{5,4},{6,7},{7,6},{8,9},{9,8},{10,11... | collective-permute-start | bytes 1572872 | tf_op jit(solution)/shard_map/ppermute | solution.py:207
  27.9 1.6 collective-permute-start.7
  29.4 1.5 collective-permute-start.8
  31.0 1.0 copy-start.4
  32.0 0.7 copy-start.5
  96.7 4.9 %copy-start.6 = (bf16[1024,1024]{1,0:T(8,128)(2,1)S(1)}, bf16[1024,1024]{1,0:T(8,128)(2,1)}, u32[]{:S(2)}) copy-start(bf16[1024,1024]{1,0:T(8,128)(2,1)} %param.4) | copy-start | bytes 6291460
  101.5 137.3 %all-gather.7.cloned.1.call-start = ((), (), s32[]{:S(2)}) async-start(), calls=%async_computation.5 | async-start | bytes 2228224 | tf_op jit(solution)/shard_map/all_gather | solution.py:233
  101.5 25.8 %collective-permute-start.9 = (bf16[1024,1024]{1,0:T(8,128)(2,1)S(1)}, bf16[1024,1024]{1,0:T(8,128)(2,1)}, u32[]{:S(2)}, u32[]{:S(2)}) collective-permute-start(bf16[1024,1024]{1,0:T(8,128)(2,1)S(1)} %copy-done.6), channel_id=1, source_target_pairs={{0,1},{1,0},{2,3},{3,2},{4,5},{5,4},{6,7},{7,6},{8,9},{9,8},{10,11... | collective-permute-start | bytes 6291464 | tf_op jit(solution)/shard_map/ppermute | solution.py:207
  101.8 24.9 %collective-permute-start.10 = (bf16[256,256]{1,0:T(8,128)(2,1)S(1)}, bf16[256,256]{1,0:T(8,128)(2,1)S(1)}, u32[]{:S(2)}, u32[]{:S(2)}) collective-permute-start(bf16[256,256]{1,0:T(8,128)(2,1)S(1)} %shard_map.38), channel_id=1, source_target_pairs={{0,0},{1,1},{2,32},{3,33},{4,64},{5,65},{6,96},{7,97},{8,128},{9,1... | collective-permute-start | bytes 393224 | tf_op jit(solution)/shard_map/ppermute | solution.py:232
  126.7 0.7 copy-start.7
  178.7 1.6 copy-start.1
  180.3 1.6 copy-start.3
  184.8 1.3 copy-start
  186.1 52.8 %all-to-all-start.2 = ((f32[8,64,1024]{2,1,0:T(8,128)}), f32[8,64,1024]{2,1,0:T(8,128)S(1)}, u32[]{:S(2)}, u32[]{:S(2)}) async-start(f32[8,64,1024]{2,1,0:T(8,128)} %bitcast.7), calls=%async_computation.2 | async-start | bytes 4194304 | tf_op jit(solution)/shard_map/all_to_all | solution.py:238
  238.8 1.6 copy-start.2
Sparse Core Ops, SparseCore 0:
  101.6 77.0 all-gather.4
  181.4 57.3 all-gather.6

commit v2 on v1

v2 whole, which is shorter than its diff:
```python
import functools

import jax
import jax.numpy as jnp
from jax import lax
from jax.experimental import pallas as pl
from jax.experimental.pallas import tpu as pltpu
from jax.sharding import Mesh
from jax.sharding import PartitionSpec as P

FEATURES = 16384
SCALE = FEATURES ** (-0.5)
BF16 = jnp.bfloat16
F32 = jnp.float32

EX = ("zh", "zl", "yl")
CHIPS = ("yh", "x")
PAR = ("yh", "x", "c")


def shifted(values, amount):
    return lax.shift_right_logical(values, jnp.full(values.shape, amount, jnp.int32))


def signs(hash_words, row_start, rows, cols):
    m0 = hash_words[0] | 1
    row_ids = lax.broadcasted_iota(jnp.int32, (rows, cols.shape[1]), 0)
    mixed = row_ids * (FEATURES * m0) + (cols * m0 + (row_start * (FEATURES * m0) + hash_words[1]))
    mixed = mixed ^ shifted(mixed, 15)
    mixed = mixed * (hash_words[2] | 1)
    mixed = mixed ^ shifted(mixed, 13)
    mixed = mixed * (hash_words[3] | 1)
    return jnp.where(mixed < 0, BF16(-1), BF16(1))


def project_kernel(part, width, words, mine, next_y, next_z, diag_a, diag_b, *rest):
    other = rest[:5]
    out, examples, total = rest[5:]
    step = pl.program_id(0)
    half = pl.num_programs(0) // 2
    me = lax.axis_index("zl") * 2 + lax.axis_index("yl")
    core = lax.axis_index("c")
    chip = lax.axis_index("yh") * 4 + lax.axis_index("x")
    slice_id = lax.axis_index("yl") * 4 + lax.axis_index("zl") * 2 + core
    rows, depth = mine.shape

    def fill(own, y, z, da, db):
        def at(flip, offset=0):
            return pl.multiple_of((me ^ flip) * rows + offset, 32)

        examples[pl.ds(at(0), rows), :] = own[...]
        examples[pl.ds(at(1), rows), :] = y[...]
        examples[pl.ds(at(2), rows), :] = z[...]
        examples[pl.ds(at(3), rows // 2), :] = da[...]
        examples[pl.ds(at(3, rows // 2), rows // 2), :] = db[...]

    @pl.when(step == 0)
    def _():
        total[...] = jnp.zeros_like(total)

    @pl.when(step < half)
    def _():
        fill(mine, next_y, next_z, diag_a, diag_b)

    @pl.when(step >= half)
    def _():
        fill(*other)

    which = jnp.where(step < half, core, 1 - core)
    inner = jnp.where(step < half, step, step - half)
    row_start = (chip * 2 + which) * (half * depth) + inner * depth
    wide = 512
    held = examples[...]

    def chunk(index, carry):
        lane = lax.broadcasted_iota(jnp.int32, (1, wide), 1)
        group, within = lane // width, lane % width
        cols = (group + index * (wide // width)) * 2048 + within + (slice_id * 256 + part * width)
        table = signs(words, row_start, depth, cols)
        at = pl.ds(pl.multiple_of(index * wide, wide), wide)
        total[:, at] += jnp.dot(held, table, preferred_element_type=F32)
        return carry

    lax.fori_loop(0, total.shape[1] // wide, chunk, 0, unroll=2)

    @pl.when(step == 2 * half - 1)
    def _():
        for block in range(8):
            out[block] = total[:, block * width : (block + 1) * width] * SCALE


def project(part, width, words, own, other, depth=512):
    rows, params = own[0].shape
    half = params // depth

    def spec(array, second):
        if second:
            return pl.BlockSpec((array.shape[0], depth), lambda k: (0, jnp.maximum(k - half, 0)))
        return pl.BlockSpec((array.shape[0], depth), lambda k: (0, jnp.minimum(k, half - 1)))

    return pl.pallas_call(
        functools.partial(project_kernel, part, width),
        out_shape=jax.ShapeDtypeStruct((8, 4 * rows, width), F32),
        grid=(2 * half,),
        in_specs=[pl.BlockSpec(memory_space=pltpu.SMEM)]
        + [spec(a, False) for a in own]
        + [spec(a, True) for a in other],
        out_specs=pl.BlockSpec((8, 4 * rows, width), lambda k: (0, 0, 0)),
        scratch_shapes=[pltpu.VMEM((4 * rows, depth), BF16), pltpu.VMEM((4 * rows, 8 * width), F32)],
        compiler_params=pltpu.CompilerParams(vmem_limit_bytes=24 << 20),
        cost_estimate=pl.CostEstimate(flops=2 * 256 * 8192 * 8 * width, bytes_accessed=5 << 20, transcendentals=0),
    )(words, *own, *other)


def sum_kernel(*refs):
    parts, (whole, keep, send) = refs[:-3], refs[-3:]
    core = lax.axis_index("c")
    width = parts[0].shape[2]
    for run, part in enumerate(parts):
        at = slice(run * width, (run + 1) * width)
        total = part[0]
        for index in range(1, part.shape[0]):
            total += part[index]
        whole[:, at] = total.astype(BF16)
    for block in range(2):
        for target, which in ((keep, core), (send, 1 - core)):
            start = pl.multiple_of(block * 128 + which * 64, 64)
            target[block * 64 : (block + 1) * 64, :] = whole[pl.ds(start, 64), :]


def sum_parts(parts):
    rows = parts[0].shape[1]
    features = sum(p.shape[2] for p in parts)
    shapes = [(rows, features), (rows // 2, features), (rows // 2, features)]
    return pl.pallas_call(
        sum_kernel,
        out_shape=[jax.ShapeDtypeStruct(shape, BF16) for shape in shapes],
        compiler_params=pltpu.CompilerParams(vmem_limit_bytes=16 << 20),
    )(*parts)


def condition_kernel(pieces, mine, other, out):
    core = lax.axis_index("c")
    yl = lax.axis_index("yl")

    def run(near, far):
        total = None
        for zl in range(2):
            for flips in range(4):
                tile = (near, far)[flips // 2]
                start = pl.multiple_of((zl * 2 + (core ^ (flips % 2))) * 256, 256)
                term = jnp.dot(pieces[zl, flips], tile[pl.ds(start, 256), :], preferred_element_type=F32)
                total = term if total is None else total + term
        out[...] = total

    @pl.when(yl == core)
    def _():
        run(mine, other)

    @pl.when(yl != core)
    def _():
        run(other, mine)


def condition(pieces, mine, other):
    rows = pieces.shape[2]
    return pl.pallas_call(
        condition_kernel,
        out_shape=jax.ShapeDtypeStruct((4 * rows, mine.shape[1]), F32),
        grid=(4,),
        in_specs=[
            pl.BlockSpec((2,) + pieces.shape[1:], lambda g: (g, 0, 0, 0)),
            pl.BlockSpec(mine.shape, lambda g: (0, 0)),
            pl.BlockSpec(other.shape, lambda g: (0, 0)),
        ],
        out_specs=pl.BlockSpec((rows, mine.shape[1]), lambda g: (g, 0)),
        compiler_params=pltpu.CompilerParams(vmem_limit_bytes=24 << 20),
        cost_estimate=pl.CostEstimate(flops=2 * 512 * 2048 * 1024, bytes_accessed=7 << 20, transcendentals=0),
    )(pieces, mine, other)


def pair_kernel(parts, *refs):
    features, (out, rows, pairs) = refs[:8], refs[8:]
    yh, x, core = (lax.axis_index(name) for name in PAR)
    total = parts[0]
    for index in range(1, parts.shape[0]):
        total += parts[index]
    rows[...] = total.astype(BF16)
    pairs[...] = jnp.zeros_like(pairs)
    for shift in range(4):
        for flip_core in range(2):
            for flip_yh in range(2):
                z = (yh ^ flip_yh) * 4 + ((x + 4 - shift) & 3)
                start = pl.multiple_of(((z & 1) * 2 + (core ^ flip_core)) * 256, 256)
                at = pl.ds(pl.multiple_of((z >> 1) * 256, 256), 256)
                pairs[:, at] += lax.dot_general(
                    rows[:, pl.ds(start, 256)],
                    features[shift * 2 + flip_core][flip_yh],
                    (((1,), (1,)), ((), ())),
                    preferred_element_type=F32,
                )
    for block in range(16):
        piece = pairs[:, block * 64 : (block + 1) * 64]
        out[block, :, :64] = piece[:32]
        out[block, :, 64:] = piece[32:]


def pair(parts, features):
    return pl.pallas_call(
        pair_kernel,
        out_shape=jax.ShapeDtypeStruct((16, 32, 128), F32),
        scratch_shapes=[pltpu.VMEM((64, 1024), BF16), pltpu.VMEM((64, 1024), F32)],
        compiler_params=pltpu.CompilerParams(vmem_limit_bytes=24 << 20),
    )(parts, *features)


def finish_kernel(parts, out):
    total = parts[0]
    for index in range(1, parts.shape[0]):
        total += parts[index]
    total = total * SCALE
    out[:32] = total[:, :64]
    out[32:] = total[:, 64:]


def finish(parts):
    return pl.pallas_call(
        finish_kernel,
        out_shape=jax.ShapeDtypeStruct((64, 64), F32),
    )(parts)


def swap(value, axis):
    return lax.ppermute(value, axis, [(0, 1), (1, 0)])


def shift_x(value, by):
    return lax.ppermute(value, "x", [(i, (i + by) % 4) for i in range(4)])


def per_device(gradients, inverse_gram, hash_words):
    half = gradients.shape[0] // 2
    next_y = swap(gradients, "yl")
    next_z = swap(gradients, "zl")
    own = [gradients, next_y, next_z, swap(next_y[:half], "zl"), swap(next_z[half:], "yl")]
    other = [swap(a, "c") for a in own]
    other_tile = swap(inverse_gram, "c")

    runs = []
    for part in range(2):
        partial = project(part, 128, hash_words, own, other)
        runs.append(lax.all_to_all(partial, CHIPS, 0, 0, tiled=True))
    whole, keep, send = sum_parts(runs)

    received = swap(send, "c")
    mine = jnp.stack([keep, received, swap(keep, "yl"), swap(received, "yl")])
    gathered = lax.all_gather(mine, ("zh", "zl"), axis=0)

    route = []
    for z in range(8):
        for yl in range(2):
            for chip in range(8):
                for c in range(2):
                    route.append((((z * 2 + yl) * 8 + chip) * 2 + c, ((chip * 2 + yl) * 8 + z) * 2 + c))
    turned = lax.ppermute(whole, EX + PAR, route)
    turned = jnp.stack([turned, swap(turned, "yh")])
    features = []
    for by in range(4):
        shifted_x = shift_x(turned, by) if by else turned
        features += [shifted_x, swap(shifted_x, "c")]

    gathered, features = lax.optimization_barrier((gathered, features))
    conditioned = condition(gathered, inverse_gram, other_tile)
    parts = lax.all_to_all(conditioned.reshape(8, 64, 1024), CHIPS, 0, 0, tiled=True)
    return finish(lax.all_to_all(pair(parts, features), EX, 0, 0, tiled=True))


def solution(mesh):
    fine = Mesh(mesh.devices.reshape(4, 2, 2, 2, 4, 2), EX + PAR)
    return jax.shard_map(
        per_device,
        mesh=fine,
        in_specs=(P(EX, PAR), P(PAR, EX), P()),
        out_specs=P(PAR, EX),
        check_vma=False,
    )
```

time: 272 us -> 231 us (0.85)
  waiting for transfers between devices: 125 us -> 53.7 us
  blocking collectives: 57.1 us -> 69.8 us
  local copies, waits for them, and re-layouts: 8.45 us -> 15.2 us
  starting transfers between devices: 24.8 us -> 31.5 us
  Pallas kernels: 37.9 us -> 43.1 us
  other arithmetic: 3.9 us -> 0.77 us
    all_gather x2 -> x1, waiting for transfers between devices: 93.3 us -> 0.14 us  [per_device(): gathered = lax.all_gather(mine, ('zh', 'zl'), axis=0)]
    all_to_all x2, blocking collectives: 36.2 us -> 51.6 us  [the longest x1 31.5 us: per_device(): lax.all_to_all(conditioned.reshape(8, 64, 1024), CHIPS, 0, 0, tiled=True)]
    ppermute x10 -> x18, waiting for transfers between devices: 17.3 us -> 28.3 us  [swap(): return lax.ppermute(value, axis, [(0, 1), (1, 0)])]
    ppermute x1 -> x4, waiting for transfers between devices: 14.4 us -> 25.3 us  [the longest x1 15 us: per_device(): turned = lax.ppermute(whole, EX + PAR, route)]
    unnamed x16 -> x46, local copies, waits for them, and re-layouts: 8.41 us -> 15.1 us
    select_n x1 -> x0, other arithmetic: 3.9 us -> none  [per_device(): high = jnp.where(core == 0, other_tile, inverse_gram)]
    ppermute x1 -> x4, starting transfers between devices: 10.5 us -> 14.3 us  [the longest x1 11 us: per_device(): turned = lax.ppermute(whole, EX + PAR, route)]
    pallas_call x2 -> x3, Pallas kernels: 32.5 us -> 36 us  [the longest x2 35.9 us: project(): pl.pallas_call(functools.partial(project_kernel, part, width), out_shape=...]
  transfers between devices with their start and end apart: 14 -> 24, of which waited for: 7 -> 14; matrix products, arithmetic and copies ran while one was open for 1% -> 0% of each run, Pallas kernels for 1% -> 8%
where the time goes in v2:
time: 231 us; the launch traced here: 228 us
  blocking collectives  69.8 us (30%)
  waiting for transfers between devices  53.7 us (23%)
  Pallas kernels  43.1 us (19%)
  starting transfers between devices  31.5 us (14%)
  local copies, waits for them, and re-layouts  15.2 us (7%)
  between operations  13.6 us (6%)
    pallas_call x2, Pallas kernels, project(): pl.pallas_call(functools.partial(project_kernel, part, width), out_shape=...  35.9 us
    all_to_all x1, blocking collectives, per_device(): lax.all_to_all(conditioned.reshape(8, 64, 1024), CHIPS, 0, 0, tiled=True)  31.5 us
    ppermute x18, waiting for transfers between devices, swap(): return lax.ppermute(value, axis, [(0, 1), (1, 0)])  28.3 us
    all_to_all x1, blocking collectives, per_device(): runs.append(lax.all_to_all(partial, CHIPS, 0, 0, tiled=True))  20.1 us
    all_to_all x1, blocking collectives, per_device(): return finish(lax.all_to_all(pair(parts, features), EX, 0, 0, tiled=True))  18.1 us
    unnamed x46, local copies, waits for them, and re-layouts  15.1 us
    ppermute x1, waiting for transfers between devices, per_device(): turned = lax.ppermute(whole, EX + PAR, route)  15 us
    ppermute x1, starting transfers between devices, per_device(): turned = lax.ppermute(whole, EX + PAR, route)  11 us
  transfers between devices with their start and end apart: 24, of which 14 were waited for; matrix products, arithmetic and copies ran while one was open for 0% of the time, Pallas kernels for 8%

profile of v2, /device:TPU:22, one launch (start us, length us, event | category | flops | bytes accessed | tf_op | source)
XLA Modules:
  0.0 227.6 jit_solution(16250613945016222626)
XLA Ops:
  6.5 1.9 collective-permute-start.1
  8.5 1.3 collective-permute-start
  9.7 0.0 collective-permute-start.4
  9.7 10.8 %collective-permute-done.1.next_z = bf16[64,4096]{1,0:T(8,128)(2,1)S(1)} collective-permute-done((bf16[64,4096]{1,0:T(8,128)(2,1)}, bf16[64,4096]{1,0:T(8,128)(2,1)S(1)}, u32[]{:S(2)}, u32[]{:S(2)}) %collective-permute-start.1) | collective-permute-done | bytes 524320 | tf_op jit(solution)/shard_map/ppermute | solution.py:234
  20.6 1.4 collective-permute-start.3
  22.0 0.1 collective-permute-done.next_y
  22.1 1.8 collective-permute-start.2
  23.8 0.0 collective-permute-start.6
  23.8 0.5 collective-permute-start.5
  24.3 3.7 %collective-permute-done.3.diag_b = bf16[32,4096]{1,0:T(8,128)(2,1)S(1)} collective-permute-done((bf16[32,4096]{1,0:T(8,128)(2,1)S(1)}, bf16[32,4096]{1,0:T(8,128)(2,1)S(1)}, u32[]{:S(2)}, u32[]{:S(2)}) %collective-permute-start.3) | collective-permute-done | bytes 262176 | tf_op jit(solution)/shard_map/ppermute | solution.py:234
  28.1 0.0 collective-permute-start.8
  28.1 1.1 collective-permute-done.2.diag_a
  29.2 0.0 collective-permute-start.7
  29.2 0.0 collective-permute-done.4.rest_0_
  29.2 0.4 collective-permute-done.8.rest_4_
  29.6 1.1 collective-permute-done.7.rest_3_
  30.7 0.0 collective-permute-done.5.rest_1_
  30.7 1.0 copy-done.9
  31.8 0.7 copy-done.21
  32.4 18.4 %shard_map.37 = f32[8,256,128]{2,1,0:T(8,128)} custom-call(s32[4]{0:T(128)S(1)} %copy-done.21, bf16[64,4096]{1,0:T(8,128)(2,1)S(1)} %copy-done.9, bf16[64,4096]{1,0:T(8,128)(2,1)S(1)} %collective-permute-done.next_y, bf16[64,4096]{1,0:T(8,128)(2,1)S(1)} %collective-permute-done.1.next_z, bf16[32,4096]{1,0:T(8,128)(2,1)S(1)} %collective-permute-done.2.diag_a, ...), custom_call_target="tpu_custom_call" | custom-call | flops 4294967296 | bytes 5242880 | tf_op jit(solution)/shard_map/pallas_call | solution.py:101
  50.8 0.8 copy-done.11
  51.6 0.8 copy-done.13
  52.4 0.7 copy-done.15
  53.2 0.7 copy-done.17
  53.9 0.7 copy-done.19
  54.6 7.3 %all-to-all-start = ((f32[8,256,128]{2,1,0:T(8,128)}), f32[8,256,128]{2,1,0:T(8,128)S(1)}, u32[]{:S(2)}, u32[]{:S(2)}) async-start(f32[8,256,128]{2,1,0:T(8,128)} %shard_map.37), calls=%async_computation | async-start | bytes 2097152 | tf_op jit(solution)/shard_map/all_to_all | solution.py:252
  61.9 1.0 copy-done.12
  63.0 1.0 copy-done.14
  64.0 0.9 copy-done.16
  65.0 0.9 copy-done.18
  65.9 0.9 copy-done.20
  66.9 17.4 %shard_map.38 = f32[8,256,128]{2,1,0:T(8,128)S(1)} custom-call(s32[4]{0:T(128)S(1)} %copy-done.22, bf16[64,4096]{1,0:T(8,128)(2,1)S(1)} %copy-done.10, bf16[64,4096]{1,0:T(8,128)(2,1)S(1)} %collective-permute-done.next_y, bf16[64,4096]{1,0:T(8,128)(2,1)S(1)} %collective-permute-done.1.next_z, bf16[32,4096]{1,0:T(8,128)(2,1)S(1)} %copy-done.16, ...), custom_call_target="tpu_custom_call" | custom-call | flops 4294967296 | bytes 5242880 | tf_op jit(solution)/shard_map/pallas_call | solution.py:101
  84.3 1.0 copy-done.2
  85.3 20.1 %all_to_all.20.refs_1_ = f32[8,256,128]{2,1,0:T(8,128)S(1)} all-to-all(f32[8,256,128]{2,1,0:T(8,128)} %copy-done.2), channel_id=1, replica_groups=mesh['zh'=4,'zl'=2,'yl'=2,'yh'=2,'x'=4,'c'=2] {'yh','x'}, dimensions={0} | all-to-all | bytes 2097152 | tf_op jit(solution)/shard_map/all_to_all | solution.py:252
  105.4 0.1 shard_map.39
  105.5 0.1 collective-permute-start.9
  105.6 1.2 collective-permute-start.10
  106.8 0.0 collective-permute-done.9
  106.9 1.1 collective-permute-start.11
  108.0 2.6 %collective-permute-done.10 = bf16[128,256]{1,0:T(8,128)(2,1)S(1)} collective-permute-done((bf16[128,256]{1,0:T(8,128)(2,1)S(1)}, bf16[128,256]{1,0:T(8,128)(2,1)S(1)}, u32[]{:S(2)}, u32[]{:S(2)}) %collective-permute-start.10) | collective-permute-done | bytes 65568 | tf_op jit(solution)/shard_map/ppermute | solution.py:234
  110.6 0.9 collective-permute-done.11
  111.6 0.7 pad_maximum_fusion
  112.3 0.0 all-gather.3.cloned.1.call-update
  112.3 0.1 collective-permute-start.21
  112.4 11.0 %collective-permute-start.12 = (bf16[256,256]{1,0:T(8,128)(2,1)S(1)}, bf16[256,256]{1,0:T(8,128)(2,1)S(1)}, u32[]{:S(2)}, u32[]{:S(2)}) collective-permute-start(bf16[256,256]{1,0:T(8,128)(2,1)S(1)} %get-tuple-element.19), channel_id=1, source_target_pairs={{0,0},{1,1},{2,32},{3,33},{4,64},{5,65},{6,96},{7,97},{8,128},{9,1... | collective-permute-start | bytes 393224 | tf_op jit(solution)/shard_map/ppermute | solution.py:265
  123.4 15.0 %collective-permute-done.12 = bf16[256,256]{1,0:T(8,128)(2,1)S(1)} collective-permute-done((bf16[256,256]{1,0:T(8,128)(2,1)S(1)}, bf16[256,256]{1,0:T(8,128)(2,1)S(1)}, u32[]{:S(2)}, u32[]{:S(2)}) %collective-permute-start.12) | collective-permute-done | bytes 131104 | tf_op jit(solution)/shard_map/ppermute | solution.py:265
  138.5 6.5 %collective-permute-done.13 = bf16[256,256]{1,0:T(8,128)(2,1)S(1)} collective-permute-done((bf16[256,256]{1,0:T(8,128)(2,1)S(1)}, bf16[256,256]{1,0:T(8,128)(2,1)S(1)}, u32[]{:S(2)}, u32[]{:S(2)}) %collective-permute-start.13) | collective-permute-done | bytes 131104 | tf_op jit(solution)/shard_map/ppermute | solution.py:234
  145.0 0.1 collective-permute-start.19
  145.1 0.3 collective-permute-start.17
  145.3 2.9 %collective-permute-start.15 = (bf16[2,256,256]{2,1,0:T(8,128)(2,1)S(1)}, bf16[2,256,256]{2,1,0:T(8,128)(2,1)S(1)}, u32[]{:S(2)}, u32[]{:S(2)}) collective-permute-start(bf16[2,256,256]{2,1,0:T(8,128)(2,1)S(1)} %pad_maximum_fusion.1.refs_0_), channel_id=1, source_target_pairs={{0,2},{2,4},{4,6},{6,0},{1,3},{3,5},{5,7},{7,1},{8,10},{10,12},{12... | collective-permute-start | bytes 786440 | tf_op jit(solution)/shard_map/ppermute | solution.py:238
  148.3 10.2 %collective-permute-done.19.refs_6_ = bf16[2,256,256]{2,1,0:T(8,128)(2,1)S(1)} collective-permute-done((bf16[2,256,256]{2,1,0:T(8,128)(2,1)S(1)}, bf16[2,256,256]{2,1,0:T(8,128)(2,1)S(1)}, u32[]{:S(2)}, u32[]{:S(2)}) %collective-permute-start.19) | collective-permute-done | bytes 262176 | tf_op jit(solution)/shard_map/ppermute | solution.py:238
  158.4 0.5 collective-permute-start.18
  159.0 0.1 collective-permute-done.15.refs_2_
  159.1 0.9 collective-permute-done.20.refs_7_
  160.0 0.7 copy-done.3
  160.7 0.7 copy-done.5
  161.4 0.7 copy-done.7
  162.1 0.1 all-gather.3.cloned.1.call-done
  162.3 1.6 copy-done.1
  163.9 4.5 %shard_map.40 = f32[512,1024]{1,0:T(8,128)S(1)} custom-call(bf16[8,4,128,256]{3,2,1,0:T(8,128)(2,1)S(1)} %bitcast.9, bf16[1024,1024]{1,0:T(8,128)(2,1)S(1)} %copy-done, bf16[1024,1024]{1,0:T(8,128)(2,1)} %collective-permute-done.21.other), custom_call_target="tpu_custom_call" | custom-call | flops 2147483648 | bytes 7340032 | tf_op jit(solution)/shard_map/pallas_call | solution.py:167
  168.5 31.5 %all_to_all.21.parts = f32[8,64,1024]{2,1,0:T(8,128)S(1)} all-to-all(f32[8,64,1024]{2,1,0:T(8,128)S(1)} %bitcast.8), channel_id=1, replica_groups=mesh['zh'=4,'zl'=2,'yl'=2,'yh'=2,'x'=4,'c'=2] {'yh','x'}, dimensions={0} | all-to-all | bytes 4194304 | tf_op jit(solution)/shard_map/all_to_all | solution.py:274
  200.0 0.9 shard_map.41
  200.9 18.1 %all_to_all.22.parts = f32[16,32,128]{2,1,0:T(8,128)} all-to-all(f32[16,32,128]{2,1,0:T(8,128)S(1)} %shard_map.41), channel_id=1, replica_groups=mesh['zh'=4,'zl'=2,'yl'=2,'yh'=2,'x'=4,'c'=2] {'zh','zl','yl'}, dimensions={0} | all-to-all | bytes 524288 | tf_op jit(solution)/shard_map/all_to_all | solution.py:275
  219.1 1.7 shard_map.42
  (44 shorter events, 0.1 us)
Async XLA Ops:
  6.5 14.0 %collective-permute-start.1 = (bf16[64,4096]{1,0:T(8,128)(2,1)}, bf16[64,4096]{1,0:T(8,128)(2,1)S(1)}, u32[]{:S(2)}, u32[]{:S(2)}) collective-permute-start(bf16[64,4096]{1,0:T(8,128)(2,1)} %mine.4), channel_id=1, source_target_pairs={{0,32},{32,0},{1,33},{33,1},{2,34},{34,2},{3,35},{35,3},{4,36},{36... | collective-permute-start | bytes 1572872 | tf_op jit(solution)/shard_map/ppermute | solution.py:234
  8.5 13.6 %collective-permute-start = (bf16[64,4096]{1,0:T(8,128)(2,1)}, bf16[64,4096]{1,0:T(8,128)(2,1)S(1)}, u32[]{:S(2)}, u32[]{:S(2)}) collective-permute-start(bf16[64,4096]{1,0:T(8,128)(2,1)} %mine.4), channel_id=1, source_target_pairs={{0,16},{16,0},{1,17},{17,1},{2,18},{18,2},{3,19},{19,3},{4,20},{20... | collective-permute-start | bytes 1572872 | tf_op jit(solution)/shard_map/ppermute | solution.py:234
  9.7 19.4 %collective-permute-start.4 = (bf16[64,4096]{1,0:T(8,128)(2,1)}, bf16[64,4096]{1,0:T(8,128)(2,1)S(1)}, u32[]{:S(2)}, u32[]{:S(2)}) collective-permute-start(bf16[64,4096]{1,0:T(8,128)(2,1)} %mine.4), channel_id=1, source_target_pairs={{0,1},{1,0},{2,3},{3,2},{4,5},{5,4},{6,7},{7,6},{8,9},{9,8},{10,11... | collective-permute-start | bytes 1572872 | tf_op jit(solution)/shard_map/ppermute | solution.py:234
  20.6 7.5 %collective-permute-start.3 = (bf16[32,4096]{1,0:T(8,128)(2,1)S(1)}, bf16[32,4096]{1,0:T(8,128)(2,1)S(1)}, u32[]{:S(2)}, u32[]{:S(2)}) collective-permute-start(bf16[32,4096]{1,0:T(8,128)(2,1)S(1)} %slice.9), channel_id=1, source_target_pairs={{0,16},{16,0},{1,17},{17,1},{2,18},{18,2},{3,19},{19,3},{4,20},{20... | collective-permute-start | bytes 786440 | tf_op jit(solution)/shard_map/ppermute | solution.py:234
  22.1 7.1 %collective-permute-start.2 = (bf16[32,4096]{1,0:T(8,128)(2,1)S(1)}, bf16[32,4096]{1,0:T(8,128)(2,1)S(1)}, u32[]{:S(2)}, u32[]{:S(2)}) collective-permute-start(bf16[32,4096]{1,0:T(8,128)(2,1)S(1)} %slice.8), channel_id=1, source_target_pairs={{0,32},{32,0},{1,33},{33,1},{2,34},{34,2},{3,35},{35,3},{4,36},{36... | collective-permute-start | bytes 786440 | tf_op jit(solution)/shard_map/ppermute | solution.py:234
  23.8 5.8 %collective-permute-start.6 = (bf16[64,4096]{1,0:T(8,128)(2,1)S(1)}, bf16[64,4096]{1,0:T(8,128)(2,1)S(1)}, u32[]{:S(2)}, u32[]{:S(2)}) collective-permute-start(bf16[64,4096]{1,0:T(8,128)(2,1)S(1)} %collective-permute-done.1.next_z), channel_id=1, source_target_pairs={{0,1},{1,0},{2,3},{3,2},{4,5},{5,4},{6,7},{7,6},{8,9},{9,8},{10,11... | collective-permute-start | bytes 1572872 | tf_op jit(solution)/shard_map/ppermute | solution.py:234
  23.8 6.9 %collective-permute-start.5 = (bf16[64,4096]{1,0:T(8,128)(2,1)S(1)}, bf16[64,4096]{1,0:T(8,128)(2,1)S(1)}, u32[]{:S(2)}, u32[]{:S(2)}) collective-permute-start(bf16[64,4096]{1,0:T(8,128)(2,1)S(1)} %collective-permute-done.next_y), channel_id=1, source_target_pairs={{0,1},{1,0},{2,3},{3,2},{4,5},{5,4},{6,7},{7,6},{8,9},{9,8},{10,11... | collective-permute-start | bytes 1572872 | tf_op jit(solution)/shard_map/ppermute | solution.py:234
  28.1 1.5 collective-permute-start.8
  29.2 1.5 collective-permute-start.7
  30.7 1.0 copy-start.9
  31.8 0.7 copy-start.21
  50.8 0.8 copy-start.11
  51.6 0.8 copy-start.13
  52.4 0.7 copy-start.15
  53.2 0.7 copy-start.17
  53.9 0.7 copy-start.19
  54.6 7.3 %copy-start.10 = (bf16[64,4096]{1,0:T(8,128)(2,1)S(1)}, bf16[64,4096]{1,0:T(8,128)(2,1)}, u32[]{:S(2)}) copy-start(bf16[64,4096]{1,0:T(8,128)(2,1)} %mine.4) | copy-start | bytes 1572868
  54.6 7.3 %copy-start.22 = (s32[4]{0:T(128)S(1)}, s32[4]{0:T(128)}, u32[]{:S(2)}) copy-start(s32[4]{0:T(128)} %words.3) | copy-start | bytes 52
  54.6 30.7 %all-to-all-start = ((f32[8,256,128]{2,1,0:T(8,128)}), f32[8,256,128]{2,1,0:T(8,128)S(1)}, u32[]{:S(2)}, u32[]{:S(2)}) async-start(f32[8,256,128]{2,1,0:T(8,128)} %shard_map.37), calls=%async_computation | async-start | bytes 2097152 | tf_op jit(solution)/shard_map/all_to_all | solution.py:252
  61.9 100.4 %all-gather.3.cloned.1.call-start = ((), (), s32[]{:S(2)}) async-start(), calls=%async_computation.4 | async-start | bytes 2359296 | tf_op jit(solution)/shard_map/all_gather | solution.py:257
  61.9 1.0 copy-start.12
  63.0 1.0 copy-start.14
  64.0 0.9 copy-start.16
  65.0 0.9 copy-start.18
  65.9 0.9 copy-start.20
  84.3 1.0 copy-start.2
  85.3 27.0 %copy-start = (bf16[1024,1024]{1,0:T(8,128)(2,1)S(1)}, bf16[1024,1024]{1,0:T(8,128)(2,1)}, u32[]{:S(2)}) copy-start(bf16[1024,1024]{1,0:T(8,128)(2,1)} %mine.5) | copy-start | bytes 6291460
  105.5 1.3 collective-permute-start.9
  105.6 5.0 %collective-permute-start.10 = (bf16[128,256]{1,0:T(8,128)(2,1)S(1)}, bf16[128,256]{1,0:T(8,128)(2,1)S(1)}, u32[]{:S(2)}, u32[]{:S(2)}) collective-permute-start(bf16[128,256]{1,0:T(8,128)(2,1)S(1)} %get-tuple-element.17), channel_id=1, source_target_pairs={{0,16},{16,0},{1,17},{17,1},{2,18},{18,2},{3,19},{19,3},{4,20},{20... | collective-permute-start | bytes 196616 | tf_op jit(solution)/shard_map/ppermute | solution.py:234
  106.9 4.7 %collective-permute-start.11 = (bf16[128,256]{1,0:T(8,128)(2,1)S(1)}, bf16[128,256]{1,0:T(8,128)(2,1)S(1)}, u32[]{:S(2)}, u32[]{:S(2)}) collective-permute-start(bf16[128,256]{1,0:T(8,128)(2,1)S(1)} %collective-permute-done.9), channel_id=1, source_target_pairs={{0,16},{16,0},{1,17},{17,1},{2,18},{18,2},{3,19},{19,3},{4,20},{20... | collective-permute-start | bytes 196616 | tf_op jit(solution)/shard_map/ppermute | solution.py:234
  112.3 50.0 %collective-permute-start.21 = (bf16[1024,1024]{1,0:T(8,128)(2,1)S(1)}, bf16[1024,1024]{1,0:T(8,128)(2,1)}, u32[]{:S(2)}, u32[]{:S(2)}) collective-permute-start(bf16[1024,1024]{1,0:T(8,128)(2,1)S(1)} %copy-done), channel_id=1, source_target_pairs={{0,1},{1,0},{2,3},{3,2},{4,5},{5,4},{6,7},{7,6},{8,9},{9,8},{10,11... | collective-permute-start | bytes 6291464 | tf_op jit(solution)/shard_map/ppermute | solution.py:234
  112.4 26.0 %collective-permute-start.12 = (bf16[256,256]{1,0:T(8,128)(2,1)S(1)}, bf16[256,256]{1,0:T(8,128)(2,1)S(1)}, u32[]{:S(2)}, u32[]{:S(2)}) collective-permute-start(bf16[256,256]{1,0:T(8,128)(2,1)S(1)} %get-tuple-element.19), channel_id=1, source_target_pairs={{0,0},{1,1},{2,32},{3,33},{4,64},{5,65},{6,96},{7,97},{8,128},{9,1... | collective-permute-start | bytes 393224 | tf_op jit(solution)/shard_map/ppermute | solution.py:265
  138.5 6.5 %collective-permute-start.13 = (bf16[256,256]{1,0:T(8,128)(2,1)S(1)}, bf16[256,256]{1,0:T(8,128)(2,1)S(1)}, u32[]{:S(2)}, u32[]{:S(2)}) collective-permute-start(bf16[256,256]{1,0:T(8,128)(2,1)S(1)} %collective-permute-done.12), channel_id=1, source_target_pairs={{0,8},{8,0},{1,9},{9,1},{2,10},{10,2},{3,11},{11,3},{4,12},{12,4},... | collective-permute-start | bytes 393224 | tf_op jit(solution)/shard_map/ppermute | solution.py:234
  145.0 13.5 %collective-permute-start.19 = (bf16[2,256,256]{2,1,0:T(8,128)(2,1)S(1)}, bf16[2,256,256]{2,1,0:T(8,128)(2,1)S(1)}, u32[]{:S(2)}, u32[]{:S(2)}) collective-permute-start(bf16[2,256,256]{2,1,0:T(8,128)(2,1)S(1)} %pad_maximum_fusion.1.refs_0_), channel_id=1, source_target_pairs={{0,6},{2,0},{4,2},{6,4},{1,7},{3,1},{5,3},{7,5},{8,14},{10,8},{12,... | collective-permute-start | bytes 786440 | tf_op jit(solution)/shard_map/ppermute | solution.py:238
  145.1 13.4 %collective-permute-start.17 = (bf16[2,256,256]{2,1,0:T(8,128)(2,1)S(1)}, bf16[2,256,256]{2,1,0:T(8,128)(2,1)S(1)}, u32[]{:S(2)}, u32[]{:S(2)}) collective-permute-start(bf16[2,256,256]{2,1,0:T(8,128)(2,1)S(1)} %pad_maximum_fusion.1.refs_0_), channel_id=1, source_target_pairs={{0,4},{2,6},{4,0},{6,2},{1,5},{3,7},{5,1},{7,3},{8,12},{10,14},{12... | collective-permute-start | bytes 786440 | tf_op jit(solution)/shard_map/ppermute | solution.py:238
  145.3 13.7 %collective-permute-start.15 = (bf16[2,256,256]{2,1,0:T(8,128)(2,1)S(1)}, bf16[2,256,256]{2,1,0:T(8,128)(2,1)S(1)}, u32[]{:S(2)}, u32[]{:S(2)}) collective-permute-start(bf16[2,256,256]{2,1,0:T(8,128)(2,1)S(1)} %pad_maximum_fusion.1.refs_0_), channel_id=1, source_target_pairs={{0,2},{2,4},{4,6},{6,0},{1,3},{3,5},{5,7},{7,1},{8,10},{10,12},{12... | collective-permute-start | bytes 786440 | tf_op jit(solution)/shard_map/ppermute | solution.py:238
  148.3 10.8 %collective-permute-start.14 = (bf16[2,256,256]{2,1,0:T(8,128)(2,1)S(1)}, bf16[2,256,256]{2,1,0:T(8,128)(2,1)S(1)}, u32[]{:S(2)}, u32[]{:S(2)}) collective-permute-start(bf16[2,256,256]{2,1,0:T(8,128)(2,1)S(1)} %pad_maximum_fusion.1.refs_0_), channel_id=1, source_target_pairs={{0,1},{1,0},{2,3},{3,2},{4,5},{5,4},{6,7},{7,6},{8,9},{9,8},{10,11... | collective-permute-start | bytes 786440 | tf_op jit(solution)/shard_map/ppermute | solution.py:234
  158.4 1.5 collective-permute-start.20
  158.4 2.2 collective-permute-start.18
  159.1 2.4 %collective-permute-start.16 = (bf16[2,256,256]{2,1,0:T(8,128)(2,1)S(1)}, bf16[2,256,256]{2,1,0:T(8,128)(2,1)S(1)}, u32[]{:S(2)}, u32[]{:S(2)}) collective-permute-start(bf16[2,256,256]{2,1,0:T(8,128)(2,1)S(1)} %collective-permute-done.15.refs_2_), channel_id=1, source_target_pairs={{0,1},{1,0},{2,3},{3,2},{4,5},{5,4},{6,7},{7,6},{8,9},{9,8},{10,11... | collective-permute-start | bytes 786440 | tf_op jit(solution)/shard_map/ppermute | solution.py:234
  160.0 0.7 copy-start.3
  160.7 0.7 copy-start.5
  161.4 0.7 copy-start.7
  162.3 1.6 copy-start.1
  168.4 31.6 %copy-start.4 = (bf16[2,256,256]{2,1,0:T(8,128)(2,1)S(1)}, bf16[2,256,256]{2,1,0:T(8,128)(2,1)}, u32[]{:S(2)}) copy-start(bf16[2,256,256]{2,1,0:T(8,128)(2,1)} %copy-done.3) | copy-start | bytes 786436
  168.4 31.6 %copy-start.6 = (bf16[2,256,256]{2,1,0:T(8,128)(2,1)S(1)}, bf16[2,256,256]{2,1,0:T(8,128)(2,1)}, u32[]{:S(2)}) copy-start(bf16[2,256,256]{2,1,0:T(8,128)(2,1)} %copy-done.5) | copy-start | bytes 786436
  168.4 31.6 %copy-start.8 = (bf16[2,256,256]{2,1,0:T(8,128)(2,1)S(1)}, bf16[2,256,256]{2,1,0:T(8,128)(2,1)}, u32[]{:S(2)}) copy-start(bf16[2,256,256]{2,1,0:T(8,128)(2,1)} %copy-done.7) | copy-start | bytes 786436
Sparse Core Ops, SparseCore 0:
  112.4 49.7 all-gather.2

commit v3 on v2

v3 whole, which is shorter than its diff:
```python
import functools

import jax
import jax.numpy as jnp
from jax import lax
from jax.experimental import pallas as pl
from jax.experimental.pallas import tpu as pltpu
from jax.sharding import Mesh
from jax.sharding import PartitionSpec as P

FEATURES = 16384
SCALE = FEATURES ** (-0.5)
BF16 = jnp.bfloat16
F32 = jnp.float32

EX = ("zh", "zl", "yl")
CHIPS = ("yh", "x")
PAR = ("yh", "x", "c")
FEATURES_PER_CHIP = FEATURES // 8


def shifted(values, amount):
    return lax.shift_right_logical(values, jnp.full(values.shape, amount, jnp.int32))


def signs(hash_words, row_start, rows, cols):
    m0 = hash_words[0] | 1
    row_ids = lax.broadcasted_iota(jnp.int32, (rows, cols.shape[1]), 0)
    mixed = row_ids * (FEATURES * m0) + (cols * m0 + (row_start * (FEATURES * m0) + hash_words[1]))
    mixed = mixed ^ shifted(mixed, 15)
    mixed = mixed * (hash_words[2] | 1)
    mixed = mixed ^ shifted(mixed, 13)
    mixed = mixed * (hash_words[3] | 1)
    return jnp.where(mixed < 0, BF16(-1), BF16(1))


def columns(first, count, part, width):
    slice_id = lax.axis_index("yl") * 4 + lax.axis_index("zl") * 2 + lax.axis_index("c")
    column = lax.broadcasted_iota(jnp.int32, (1, count), 1)
    group, within = column // width, column % width
    return (group + first // width) * FEATURES_PER_CHIP + within + (slice_id * 256 + part * width)


def first_parameter(block, depth, params):
    per_core = params // 2 // depth
    core = lax.axis_index("c")
    chip = lax.axis_index("yh") * 4 + lax.axis_index("x")
    which = jnp.where(block < per_core, core, 1 - core)
    inner = jnp.where(block < per_core, block, block - per_core)
    return (chip * 2 + which) * (params // 2) + inner * depth


def table_kernel(part, width, first, params, words, out):
    depth, wide = out.shape
    row_start = first_parameter(pl.program_id(0) + first, depth, params)
    rows = 32

    def chunk(index, carry):
        start = pl.multiple_of(index * rows, rows)
        cols = columns(0, wide, part, width)
        out[pl.ds(start, rows), :] = signs(words, row_start + start, rows, cols)
        return carry

    lax.fori_loop(0, depth // rows, chunk, 0)


def table(part, width, first, count, depth, params, words):
    return pl.pallas_call(
        functools.partial(table_kernel, part, width, first, params),
        out_shape=jax.ShapeDtypeStruct((count * depth, 8 * width), BF16),
        grid=(count,),
        in_specs=[pl.BlockSpec(memory_space=pltpu.SMEM)],
        out_specs=pl.BlockSpec((depth, 8 * width), lambda k: (k, 0)),
        compiler_params=pltpu.CompilerParams(vmem_limit_bytes=60 << 20),
        cost_estimate=pl.CostEstimate(
            flops=1200 * count * depth * 8 * width,
            bytes_accessed=2 * count * depth * 8 * width,
            transcendentals=0,
        ),
    )(words)


def load_examples(blocks, examples, arrived):
    me = lax.axis_index("zl") * 2 + lax.axis_index("yl")
    half = len(blocks) // 2
    params = blocks[0].shape[1]
    rows = blocks[0].shape[0]
    copies = []
    for index, block in enumerate(blocks):
        kind = index % half
        start = (me ^ min(kind, 3)) * rows + (rows // 2 if kind == 4 else 0)
        target = examples.at[
            pl.ds(pl.multiple_of(start, 32), block.shape[0]),
            (index // half) * params : (index // half + 1) * params,
        ]
        copies.append(pltpu.make_async_copy(block, target, arrived.at[index]))
    for copy in copies:
        copy.start()
    for copy in copies:
        copy.wait()


def write_run(out, total, width):
    for block in range(8):
        out[block] = total[:, block * width : (block + 1) * width] * SCALE


def ready_kernel(split, width, first, second, *refs):
    blocks, (out, examples, total, arrived) = refs[:-4], refs[-4:]
    step = pl.program_id(0)
    depth = first.shape[0]

    @pl.when(step == 0)
    def _():
        load_examples(blocks, examples, arrived)
        total[...] = jnp.zeros_like(total)

    held = examples[:, pl.ds(pl.multiple_of(step * depth, depth), depth)]

    @pl.when(step < split)
    def _():
        total[...] += jnp.dot(held, first[...], preferred_element_type=F32)

    @pl.when(step >= split)
    def _():
        total[...] += jnp.dot(held, second[...], preferred_element_type=F32)

    @pl.when(step == pl.num_programs(0) - 1)
    def _():
        write_run(out, total, width)


def hash_kernel(part, width, words, *refs):
    blocks, (out, examples, total, arrived) = refs[:-4], refs[-4:]
    step = pl.program_id(0)
    params = examples.shape[1]
    depth = params // pl.num_programs(0)
    wide = 512

    @pl.when(step == 0)
    def _():
        load_examples(blocks, examples, arrived)
        total[...] = jnp.zeros_like(total)

    held = examples[:, pl.ds(pl.multiple_of(step * depth, depth), depth)]
    row_start = first_parameter(step, depth, params)
    for first in range(0, 8 * width, wide):
        made = signs(words, row_start, depth, columns(first, wide, part, width))
        total[:, first : first + wide] += jnp.dot(held, made, preferred_element_type=F32)

    @pl.when(step == pl.num_programs(0) - 1)
    def _():
        write_run(out, total, width)


def project(kernel, leading, specs, steps, width, blocks):
    rows, params = 4 * blocks[0].shape[0], 2 * blocks[0].shape[1]
    return pl.pallas_call(
        kernel,
        out_shape=jax.ShapeDtypeStruct((8, rows, width), F32),
        grid=(steps,),
        in_specs=specs + [pl.BlockSpec(memory_space=pltpu.HBM)] * len(blocks),
        out_specs=pl.BlockSpec((8, rows, width), lambda k: (0, 0, 0)),
        scratch_shapes=[
            pltpu.VMEM((rows, params), BF16),
            pltpu.VMEM((rows, 8 * width), F32),
            pltpu.SemaphoreType.DMA((len(blocks),)),
        ],
        compiler_params=pltpu.CompilerParams(vmem_limit_bytes=60 << 20),
        cost_estimate=pl.CostEstimate(
            flops=2 * rows * params * 8 * width, bytes_accessed=16 << 20, transcendentals=0
        ),
    )(*leading, *blocks)


def sum_kernel(part, *earlier_and_outs):
    earlier, (whole, keep, send) = earlier_and_outs[:-3], earlier_and_outs[-3:]
    core = lax.axis_index("c")
    width = part.shape[2]
    total = part[0]
    for index in range(1, part.shape[0]):
        total += part[index]
    total = total.astype(BF16)
    for index, value in enumerate(earlier):
        whole[:, index * width : (index + 1) * width] = value[...]
    whole[:, len(earlier) * width :] = total
    mine = slice(len(earlier) * width, (len(earlier) + 1) * width)
    for block in range(2):
        for target, which in ((keep, core), (send, 1 - core)):
            start = pl.multiple_of(block * 128 + which * 64, 64)
            target[block * 64 : (block + 1) * 64, :] = whole[pl.ds(start, 64), mine]


def sum_parts(part, *earlier):
    _, rows, width = part.shape
    shapes = [(rows, width * (1 + len(earlier))), (rows // 2, width), (rows // 2, width)]
    return pl.pallas_call(
        sum_kernel,
        out_shape=[jax.ShapeDtypeStruct(shape, BF16) for shape in shapes],
        compiler_params=pltpu.CompilerParams(vmem_limit_bytes=8 << 20),
    )(part, *earlier)


def condition_kernel(low, high, mine, other, out):
    core = lax.axis_index("c")
    yl = lax.axis_index("yl")

    def run(near, far):
        total = None
        for zl in range(2):
            for flips in range(4):
                tile = (near, far)[flips // 2]
                start = pl.multiple_of((zl * 2 + (core ^ (flips % 2))) * 256, 256)
                piece = jnp.concatenate([low[zl, flips], high[zl, flips]], axis=1)
                term = jnp.dot(piece, tile[pl.ds(start, 256), :], preferred_element_type=F32)
                total = term if total is None else total + term
        out[...] = total

    @pl.when(yl == core)
    def _():
        run(mine, other)

    @pl.when(yl != core)
    def _():
        run(other, mine)


def condition(low, high, mine, other):
    rows = low.shape[2]
    return pl.pallas_call(
        condition_kernel,
        out_shape=jax.ShapeDtypeStruct((4 * rows, mine.shape[1]), F32),
        grid=(4,),
        in_specs=[
            pl.BlockSpec((2,) + low.shape[1:], lambda g: (g, 0, 0, 0)),
            pl.BlockSpec((2,) + high.shape[1:], lambda g: (g, 0, 0, 0)),
            pl.BlockSpec(mine.shape, lambda g: (0, 0)),
            pl.BlockSpec(other.shape, lambda g: (0, 0)),
        ],
        out_specs=pl.BlockSpec((rows, mine.shape[1]), lambda g: (g, 0)),
        compiler_params=pltpu.CompilerParams(vmem_limit_bytes=24 << 20),
        cost_estimate=pl.CostEstimate(flops=2 * 512 * 2048 * 1024, bytes_accessed=7 << 20, transcendentals=0),
    )(low, high, mine, other)


def pair_kernel(parts, *refs):
    away, (out, rows, pairs, features, arrived) = refs[:8], refs[8:]
    copies = [pltpu.make_async_copy(a, features.at[i], arrived.at[i]) for i, a in enumerate(away)]
    for copy in copies:
        copy.start()
    yh, x, core = (lax.axis_index(name) for name in PAR)
    total = parts[0]
    for index in range(1, parts.shape[0]):
        total += parts[index]
    rows[...] = total.astype(BF16)
    pairs[...] = jnp.zeros_like(pairs)
    for copy in copies:
        copy.wait()
    for shift in range(4):
        for flip_core in range(2):
            for flip_yh in range(2):
                z = (yh ^ flip_yh) * 4 + ((x + 4 - shift) & 3)
                start = pl.multiple_of(((z & 1) * 2 + (core ^ flip_core)) * 256, 256)
                at = pl.ds(pl.multiple_of((z >> 1) * 256, 256), 256)
                pairs[:, at] += lax.dot_general(
                    rows[:, pl.ds(start, 256)],
                    features[shift * 2 + flip_core, flip_yh],
                    (((1,), (1,)), ((), ())),
                    preferred_element_type=F32,
                )
    for block in range(16):
        piece = pairs[:, block * 64 : (block + 1) * 64]
        out[block, :, :64] = piece[:32]
        out[block, :, 64:] = piece[32:]


def pair(parts, features):
    return pl.pallas_call(
        pair_kernel,
        out_shape=jax.ShapeDtypeStruct((16, 32, 128), F32),
        in_specs=[pl.BlockSpec(memory_space=pltpu.VMEM)] + [pl.BlockSpec(memory_space=pltpu.HBM)] * 8,
        scratch_shapes=[
            pltpu.VMEM((64, 1024), BF16),
            pltpu.VMEM((64, 1024), F32),
            pltpu.VMEM((8, 2, 256, 256), BF16),
            pltpu.SemaphoreType.DMA((8,)),
        ],
        compiler_params=pltpu.CompilerParams(vmem_limit_bytes=60 << 20),
    )(parts, *features)


def finish_kernel(parts, out):
    total = parts[0]
    for index in range(1, parts.shape[0]):
        total += parts[index]
    total = total * SCALE
    out[:32] = total[:, :64]
    out[32:] = total[:, 64:]


def finish(parts):
    return pl.pallas_call(
        finish_kernel,
        out_shape=jax.ShapeDtypeStruct((64, 64), F32),
    )(parts)


def swap(value, axis):
    return lax.ppermute(value, axis, [(0, 1), (1, 0)])


def shift_x(value, by):
    return lax.ppermute(value, "x", [(i, (i + by) % 4) for i in range(4)])


def per_device(gradients, inverse_gram, hash_words):
    half = gradients.shape[0] // 2
    next_y = swap(gradients, "yl")
    next_z = swap(gradients, "zl")
    own = [gradients, next_y, next_z, swap(next_y[:half], "zl"), swap(next_z[half:], "yl")]
    other = [swap(a, "c") for a in own]
    other_tile = swap(inverse_gram, "c")

    blocks = own + other
    width, depth, params = 128, 1024, 2 * gradients.shape[1]
    split = 5
    words_spec = pl.BlockSpec(memory_space=pltpu.SMEM)

    first = table(0, width, 0, split, depth, params, hash_words)
    second = table(0, width, split, params // depth - split, depth, params, hash_words)
    table_specs = [
        pl.BlockSpec((depth, 8 * width), lambda k: (jnp.minimum(k, split - 1), 0)),
        pl.BlockSpec((depth, 8 * width), lambda k: (jnp.maximum(k - split, 0), 0)),
    ]
    partial = project(
        functools.partial(ready_kernel, split, width), [first, second], table_specs, params // depth, width, blocks
    )
    part = lax.all_to_all(partial, CHIPS, 0, 0, tiled=True)
    partial = project(functools.partial(hash_kernel, 1, width), [hash_words], [words_spec], 16, width, blocks)
    partial, part = lax.optimization_barrier((partial, part))
    next_part = lax.all_to_all(partial, CHIPS, 0, 0, tiled=True)

    def flips(keep, send):
        received = swap(send, "c")
        return jnp.stack([keep, received, swap(keep, "yl"), swap(received, "yl")])

    whole, keep, send = sum_parts(part)
    mine = flips(keep, send)
    low = lax.all_gather(mine, ("zh", "zl"), axis=0)
    next_part, mine = lax.optimization_barrier((next_part, mine))
    whole, keep, send = sum_parts(next_part, whole)
    mine, low = lax.optimization_barrier((flips(keep, send), low))
    high = lax.all_gather(mine, ("zh", "zl"), axis=0)

    route = []
    for z in range(8):
        for yl in range(2):
            for chip in range(8):
                for c in range(2):
                    route.append((((z * 2 + yl) * 8 + chip) * 2 + c, ((chip * 2 + yl) * 8 + z) * 2 + c))
    turned = lax.ppermute(whole, EX + PAR, route)
    turned = jnp.stack([turned, swap(turned, "yh")])
    features = []
    for by in range(4):
        shifted_x = shift_x(turned, by) if by else turned
        features += [shifted_x, swap(shifted_x, "c")]

    high, features = lax.optimization_barrier((high, features))
    conditioned = condition(low, high, inverse_gram, other_tile)
    parts = lax.all_to_all(conditioned.reshape(8, 64, 1024), CHIPS, 0, 0, tiled=True)
    return finish(lax.all_to_all(pair(parts, features), EX, 0, 0, tiled=True))


def solution(mesh):
    fine = Mesh(mesh.devices.reshape(4, 2, 2, 2, 4, 2), EX + PAR)
    return jax.shard_map(
        per_device,
        mesh=fine,
        in_specs=(P(EX, PAR), P(PAR, EX), P()),
        out_specs=P(PAR, EX),
        check_vma=False,
    )
```

time: 231 us -> 244 us (1.056)
  waiting for transfers between devices: 53.7 us -> 76.5 us
  blocking collectives: 69.8 us -> 47.1 us
  Pallas kernels: 43.1 us -> 63.7 us
  local copies, waits for them, and re-layouts: 15.2 us -> 5.83 us
    all_to_all x1 -> x0, blocking collectives: 20.1 us -> none  [per_device(): runs.append(lax.all_to_all(partial, CHIPS, 0, 0, tiled=True))]
    pallas_call x2 -> x4, Pallas kernels: 35.9 us -> 52.5 us  [the longest x2 33.8 us: project(): pl.pallas_call(kernel, out_shape=jax.ShapeDtypeStruct((8, rows, width), F...]
    all_gather x1 -> x2, waiting for transfers between devices: 0.14 us -> 15.3 us  [the longest x1 15.1 us: per_device(): low = lax.all_gather(mine, ('zh', 'zl'), axis=0)]
    all_to_all x1 -> x2, waiting for transfers between devices: 0.01 us -> 12.1 us  [the longest x1 12.1 us: per_device(): next_part = lax.all_to_all(partial, CHIPS, 0, 0, tiled=True)]
    unnamed x46 -> x38, local copies, waits for them, and re-layouts: 15.1 us -> 5.8 us
    ppermute x1, starting transfers between devices: 11 us -> 3.44 us  [per_device(): turned = lax.ppermute(whole, EX + PAR, route)]
    all_to_all x1 -> x2, starting transfers between devices: 7.31 us -> 14.4 us  [the longest x1 7.22 us: per_device(): next_part = lax.all_to_all(partial, CHIPS, 0, 0, tiled=True)]
    ppermute x18 -> x21, waiting for transfers between devices: 28.3 us -> 23.9 us  [swap(): return lax.ppermute(value, axis, [(0, 1), (1, 0)])]
  transfers between devices with their start and end apart: 24 -> 29, of which waited for: 14 -> 16; matrix products, arithmetic and copies ran while one was open for 0% -> 0% of each run, Pallas kernels for 8% -> 16%
where the time goes in v3:
time: 244 us; the launch traced here: 240 us
  waiting for transfers between devices  76.5 us (31%)
  Pallas kernels  63.7 us (26%)
  blocking collectives  47.1 us (19%)
  starting transfers between devices  31.5 us (13%)
  between operations  13.7 us (6%)
  local copies, waits for them, and re-layouts  5.83 us (2%)
    pallas_call x2, Pallas kernels, project(): pl.pallas_call(kernel, out_shape=jax.ShapeDtypeStruct((8, rows, width), F...  33.8 us
    all_to_all x1, blocking collectives, per_device(): lax.all_to_all(conditioned.reshape(8, 64, 1024), CHIPS, 0, 0, tiled=True)  31.6 us
    ppermute x21, waiting for transfers between devices, swap(): return lax.ppermute(value, axis, [(0, 1), (1, 0)])  23.9 us
    pallas_call x2, Pallas kernels, table(): pl.pallas_call(functools.partial(table_kernel, part, width, first, params...  18.8 us
    ppermute x1, waiting for transfers between devices, per_device(): turned = lax.ppermute(whole, EX + PAR, route)  15.6 us
    all_to_all x1, blocking collectives, per_device(): return finish(lax.all_to_all(pair(parts, features), EX, 0, 0, tiled=True))  15.5 us
    all_gather x1, waiting for transfers between devices, per_device(): low = lax.all_gather(mine, ('zh', 'zl'), axis=0)  15.1 us
    all_to_all x1, waiting for transfers between devices, per_device(): next_part = lax.all_to_all(partial, CHIPS, 0, 0, tiled=True)  12.1 us
  transfers between devices with their start and end apart: 29, of which 16 were waited for; matrix products, arithmetic and copies ran while one was open for 0% of the time, Pallas kernels for 16%

profile of v3, /device:TPU:22, one launch (start us, length us, event | category | flops | bytes accessed | tf_op | source)
XLA Modules:
  0.0 239.7 jit_solution(4095507212294460818)
XLA Ops:
  6.5 1.3 collective-permute-start
  7.8 1.9 collective-permute-start.1
  9.7 0.0 collective-permute-start.4
  9.7 10.7 %collective-permute-done.refs_1_ = bf16[64,4096]{1,0:T(8,128)(2,1)S(1)} collective-permute-done((bf16[64,4096]{1,0:T(8,128)(2,1)}, bf16[64,4096]{1,0:T(8,128)(2,1)S(1)}, u32[]{:S(2)}, u32[]{:S(2)}) %collective-permute-start) | collective-permute-done | bytes 524320 | tf_op jit(solution)/shard_map/ppermute | solution.py:309
  20.4 2.0 collective-permute-start.2
  22.5 1.4 collective-permute-start.3
  23.8 0.0 collective-permute-start.5
  23.8 0.5 collective-permute-start.6
  24.3 11.2 %shard_map.38.first = bf16[5120,1024]{1,0:T(8,128)(2,1)} custom-call(s32[4]{0:T(128)} %words.5), custom_call_target="tpu_custom_call" | custom-call | flops 6291456000 | bytes 10485760 | tf_op jit(solution)/shard_map/pallas_call | solution.py:68
  35.6 0.0 collective-permute-done.2.refs_3_
  35.6 0.1 collective-permute-start.7
  35.7 0.5 collective-permute-start.8
  36.2 7.5 %shard_map.39.second = bf16[3072,1024]{1,0:T(8,128)(2,1)} custom-call(s32[4]{0:T(128)} %words.5), custom_call_target="tpu_custom_call" | custom-call | flops 3774873600 | bytes 6291456 | tf_op jit(solution)/shard_map/pallas_call | solution.py:68
  43.8 0.7 copy-done.6
  44.6 0.1 copy-done.11
  44.6 0.1 copy-done.12
  44.7 0.2 copy-done.7
  44.9 0.8 copy-done.8
  45.7 14.6 %shard_map.40 = f32[8,256,128]{2,1,0:T(8,128)} custom-call(bf16[5120,1024]{1,0:T(8,128)(2,1)} %shard_map.38.first, bf16[3072,1024]{1,0:T(8,128)(2,1)} %shard_map.39.second, bf16[64,4096]{1,0:T(8,128)(2,1)} %refs_0_.3, bf16[64,4096]{1,0:T(8,128)(2,1)} %copy-done.3, bf16[64,4096]{1,0:T(8,128)(2,1)} %copy-done.4, bf16[32,4096]{1,0:T(8,128)(2,1)} %copy-done.9, ...), custom_call_target="tpu_custom_call" | custom-call | flops 4294967296 | bytes 16777216 | tf_op jit(solution)/shard_map/pallas_call | solution.py:158
  60.3 7.2 %all-to-all-start = ((f32[8,256,128]{2,1,0:T(8,128)}), f32[8,256,128]{2,1,0:T(8,128)S(1)}, u32[]{:S(2)}, u32[]{:S(2)}) async-start(f32[8,256,128]{2,1,0:T(8,128)} %shard_map.40), calls=%async_computation | async-start | bytes 2097152 | tf_op jit(solution)/shard_map/all_to_all | solution.py:338
  67.5 19.2 %shard_map.37 = f32[8,256,128]{2,1,0:T(8,128)} custom-call(s32[4]{0:T(128)} %words.5, bf16[64,4096]{1,0:T(8,128)(2,1)} %refs_0_.3, bf16[64,4096]{1,0:T(8,128)(2,1)} %copy-done.3, bf16[64,4096]{1,0:T(8,128)(2,1)} %copy-done.4, bf16[32,4096]{1,0:T(8,128)(2,1)} %copy-done.9, bf16[32,4096]{1,0:T(8,128)(2,1)} %copy-done.10, bf16[64,4096]{1,0:T(8,128)(2,1)} %copy-done.6, ...), custom_call_target="tpu_custom_call" | custom-call | flops 4294967296 | bytes 16777216 | tf_op jit(solution)/shard_map/pallas_call | solution.py:158
  86.7 0.0 copy-start
  86.7 0.1 shard_map.41
  86.8 0.1 collective-permute-start.9
  86.9 0.8 collective-permute-start.10
  87.7 0.4 collective-permute-done.9
  88.1 0.9 collective-permute-start.11
  89.0 1.9 collective-permute-done.10
  90.9 1.1 collective-permute-done.11
  92.0 0.7 pad_maximum_fusion.1
  92.7 0.0 all-gather.5.cloned.1.call-update
  92.7 7.2 %all-to-all-start.1 = ((f32[8,256,128]{2,1,0:T(8,128)}), f32[8,256,128]{2,1,0:T(8,128)S(1)}, u32[]{:S(2)}, u32[]{:S(2)}) async-start(f32[8,256,128]{2,1,0:T(8,128)} %shard_map.37), calls=%async_computation.1 | async-start | bytes 2097152 | tf_op jit(solution)/shard_map/all_to_all | solution.py:341
  99.9 0.1 collective-permute-start.24
  100.0 12.1 %all-to-all-done.1.part = f32[8,256,128]{2,1,0:T(8,128)S(1)} async-done(((f32[8,256,128]{2,1,0:T(8,128)}), f32[8,256,128]{2,1,0:T(8,128)S(1)}, u32[]{:S(2)}, u32[]{:S(2)}) %all-to-all-start.1) | async-done | bytes 1048608 | tf_op jit(solution)/shard_map/all_to_all | solution.py:341
  112.2 0.1 shard_map.42
  112.2 0.1 collective-permute-start.12
  112.3 0.9 collective-permute-start.13
  113.3 0.2 collective-permute-done.12
  113.5 0.9 collective-permute-start.14
  114.4 1.9 collective-permute-done.13
  116.4 1.1 collective-permute-done.14
  117.4 0.7 pad_maximum_fusion.2
  118.1 15.1 %all-gather.5.cloned.1.call-done = bf16[32,128,128]{2,1,0:T(8,128)(2,1)} async-done(((bf16[4,128,128]{2,1,0:T(8,128)(2,1)}), bf16[32,128,128]{2,1,0:T(8,128)(2,1)}) %all-gather.5.cloned.1.call-update) | async-done | bytes 1048592 | tf_op jit(solution)/shard_map/all_gather | solution.py:349
  133.2 0.0 all-gather.7.cloned.1.call-update
  133.3 3.4 %collective-permute-start.15 = (bf16[256,256]{1,0:T(8,128)(2,1)S(1)}, bf16[256,256]{1,0:T(8,128)(2,1)S(1)}, u32[]{:S(2)}, u32[]{:S(2)}) collective-permute-start(bf16[256,256]{1,0:T(8,128)(2,1)S(1)} %get-tuple-element.35), channel_id=1, source_target_pairs={{0,0},{1,1},{2,32},{3,33},{4,64},{5,65},{6,96},{7,97},{8,128},{9,1... | collective-permute-start | bytes 393224 | tf_op jit(solution)/shard_map/ppermute | solution.py:361
  136.7 15.6 %collective-permute-done.15 = bf16[256,256]{1,0:T(8,128)(2,1)S(1)} collective-permute-done((bf16[256,256]{1,0:T(8,128)(2,1)S(1)}, bf16[256,256]{1,0:T(8,128)(2,1)S(1)}, u32[]{:S(2)}, u32[]{:S(2)}) %collective-permute-start.15) | collective-permute-done | bytes 131104 | tf_op jit(solution)/shard_map/ppermute | solution.py:361
  152.3 6.5 %collective-permute-done.16 = bf16[256,256]{1,0:T(8,128)(2,1)S(1)} collective-permute-done((bf16[256,256]{1,0:T(8,128)(2,1)S(1)}, bf16[256,256]{1,0:T(8,128)(2,1)S(1)}, u32[]{:S(2)}, u32[]{:S(2)}) %collective-permute-start.16) | collective-permute-done | bytes 131104 | tf_op jit(solution)/shard_map/ppermute | solution.py:309
  158.8 0.1 collective-permute-start.18
  158.9 0.1 collective-permute-start.20
  159.0 1.9 collective-permute-start.22
  160.9 5.1 %collective-permute-done.18.refs_2_ = bf16[2,256,256]{2,1,0:T(8,128)(2,1)S(1)} collective-permute-done((bf16[2,256,256]{2,1,0:T(8,128)(2,1)S(1)}, bf16[2,256,256]{2,1,0:T(8,128)(2,1)S(1)}, u32[]{:S(2)}, u32[]{:S(2)}) %collective-permute-start.18) | collective-permute-done | bytes 262176 | tf_op jit(solution)/shard_map/ppermute | solution.py:313
  166.1 1.7 collective-permute-done.20.refs_4_
  167.8 2.7 %collective-permute-done.22.refs_6_ = bf16[2,256,256]{2,1,0:T(8,128)(2,1)S(1)} collective-permute-done((bf16[2,256,256]{2,1,0:T(8,128)(2,1)S(1)}, bf16[2,256,256]{2,1,0:T(8,128)(2,1)S(1)}, u32[]{:S(2)}, u32[]{:S(2)}) %collective-permute-start.22) | collective-permute-done | bytes 262176 | tf_op jit(solution)/shard_map/ppermute | solution.py:313
  170.5 0.7 copy-done.17
  171.3 0.7 copy-done.18
  172.0 0.2 collective-permute-done.23.refs_7_
  172.2 0.1 all-gather.7.cloned.1.call-done
  172.3 1.2 copy-done.1
  173.5 1.2 copy-done.2
  174.7 4.6 %shard_map.43 = f32[512,1024]{1,0:T(8,128)S(1)} custom-call(bf16[8,4,128,128]{3,2,1,0:T(8,128)(2,1)S(1)} %bitcast.14, bf16[8,4,128,128]{3,2,1,0:T(8,128)(2,1)S(1)} %bitcast.15, bf16[1024,1024]{1,0:T(8,128)(2,1)S(1)} %copy-done, bf16[1024,1024]{1,0:T(8,128)(2,1)} %collective-permute-done.24.other), custom_call_target="tpu_custom_call" | custom-call | flops 2147483648 | bytes 7340032 | tf_op jit(solution)/shard_map/pallas_call | solution.py:230
  179.4 31.6 %all_to_all.20.parts = f32[8,64,1024]{2,1,0:T(8,128)} all-to-all(f32[8,64,1024]{2,1,0:T(8,128)S(1)} %bitcast.13), channel_id=1, replica_groups=mesh['zh'=4,'zl'=2,'yl'=2,'yh'=2,'x'=4,'c'=2] {'yh','x'}, dimensions={0} | all-to-all | bytes 4194304 | tf_op jit(solution)/shard_map/all_to_all | solution.py:370
  211.0 4.8 %shard_map.44 = f32[16,32,128]{2,1,0:T(8,128)} custom-call(f32[8,64,1024]{2,1,0:T(8,128)} %all_to_all.20.parts, bf16[2,256,256]{2,1,0:T(8,128)(2,1)} %copy-done.5, bf16[2,256,256]{2,1,0:T(8,128)(2,1)} %copy-done.16, bf16[2,256,256]{2,1,0:T(8,128)(2,1)} %copy-done.13, bf16[2,256,256]{2,1,0:T(8,128)(2,1)} %copy-done.17, bf16[2,256,256]{2,1,0:T(8,128)(2,1)} %copy-done.14, ...), custom_call_target="tpu_custom_call" | custom-call | tf_op jit(solution)/shard_map/pallas_call | solution.py:278
  215.8 15.5 %all_to_all.21.parts = f32[16,32,128]{2,1,0:T(8,128)} all-to-all(f32[16,32,128]{2,1,0:T(8,128)} %shard_map.44), channel_id=1, replica_groups=mesh['zh'=4,'zl'=2,'yl'=2,'yh'=2,'x'=4,'c'=2] {'zh','zl','yl'}, dimensions={0} | all-to-all | bytes 524288 | tf_op jit(solution)/shard_map/all_to_all | solution.py:371
  231.3 1.7 shard_map.45
  (50 shorter events, 0.2 us)
Async XLA Ops:
  6.5 13.9 %collective-permute-start = (bf16[64,4096]{1,0:T(8,128)(2,1)}, bf16[64,4096]{1,0:T(8,128)(2,1)S(1)}, u32[]{:S(2)}, u32[]{:S(2)}) collective-permute-start(bf16[64,4096]{1,0:T(8,128)(2,1)} %refs_0_.3), channel_id=1, source_target_pairs={{0,16},{16,0},{1,17},{17,1},{2,18},{18,2},{3,19},{19,3},{4,20},{20... | collective-permute-start | bytes 1572872 | tf_op jit(solution)/shard_map/ppermute | solution.py:309
  7.8 14.6 %collective-permute-start.1 = (bf16[64,4096]{1,0:T(8,128)(2,1)}, bf16[64,4096]{1,0:T(8,128)(2,1)S(1)}, u32[]{:S(2)}, u32[]{:S(2)}) collective-permute-start(bf16[64,4096]{1,0:T(8,128)(2,1)} %refs_0_.3), channel_id=1, source_target_pairs={{0,32},{32,0},{1,33},{33,1},{2,34},{34,2},{3,35},{35,3},{4,36},{36... | collective-permute-start | bytes 1572872 | tf_op jit(solution)/shard_map/ppermute | solution.py:309
  9.7 34.0 %collective-permute-start.4 = (bf16[64,4096]{1,0:T(8,128)(2,1)}, bf16[64,4096]{1,0:T(8,128)(2,1)S(1)}, u32[]{:S(2)}, u32[]{:S(2)}) collective-permute-start(bf16[64,4096]{1,0:T(8,128)(2,1)} %refs_0_.3), channel_id=1, source_target_pairs={{0,1},{1,0},{2,3},{3,2},{4,5},{5,4},{6,7},{7,6},{8,9},{9,8},{10,11... | collective-permute-start | bytes 1572872 | tf_op jit(solution)/shard_map/ppermute | solution.py:309
  20.4 15.2 %copy-start.3 = (bf16[64,4096]{1,0:T(8,128)(2,1)}, bf16[64,4096]{1,0:T(8,128)(2,1)S(1)}, u32[]{:S(2)}) copy-start(bf16[64,4096]{1,0:T(8,128)(2,1)S(1)} %collective-permute-done.refs_1_) | copy-start | bytes 1572868
  20.4 15.2 %collective-permute-start.2 = (bf16[32,4096]{1,0:T(8,128)(2,1)S(1)}, bf16[32,4096]{1,0:T(8,128)(2,1)S(1)}, u32[]{:S(2)}, u32[]{:S(2)}) collective-permute-start(bf16[32,4096]{1,0:T(8,128)(2,1)S(1)} %slice.8), channel_id=1, source_target_pairs={{0,32},{32,0},{1,33},{33,1},{2,34},{34,2},{3,35},{35,3},{4,36},{36... | collective-permute-start | bytes 786440 | tf_op jit(solution)/shard_map/ppermute | solution.py:309
  22.4 13.2 %copy-start.4 = (bf16[64,4096]{1,0:T(8,128)(2,1)}, bf16[64,4096]{1,0:T(8,128)(2,1)S(1)}, u32[]{:S(2)}) copy-start(bf16[64,4096]{1,0:T(8,128)(2,1)S(1)} %collective-permute-done.1.refs_2_) | copy-start | bytes 1572868
  22.5 13.3 %collective-permute-start.3 = (bf16[32,4096]{1,0:T(8,128)(2,1)S(1)}, bf16[32,4096]{1,0:T(8,128)(2,1)S(1)}, u32[]{:S(2)}, u32[]{:S(2)}) collective-permute-start(bf16[32,4096]{1,0:T(8,128)(2,1)S(1)} %slice.9), channel_id=1, source_target_pairs={{0,16},{16,0},{1,17},{17,1},{2,18},{18,2},{3,19},{19,3},{4,20},{20... | collective-permute-start | bytes 786440 | tf_op jit(solution)/shard_map/ppermute | solution.py:309
  23.8 20.0 %collective-permute-start.5 = (bf16[64,4096]{1,0:T(8,128)(2,1)S(1)}, bf16[64,4096]{1,0:T(8,128)(2,1)S(1)}, u32[]{:S(2)}, u32[]{:S(2)}) collective-permute-start(bf16[64,4096]{1,0:T(8,128)(2,1)S(1)} %collective-permute-done.refs_1_), channel_id=1, source_target_pairs={{0,1},{1,0},{2,3},{3,2},{4,5},{5,4},{6,7},{7,6},{8,9},{9,8},{10,11... | collective-permute-start | bytes 1572872 | tf_op jit(solution)/shard_map/ppermute | solution.py:309
  23.8 20.0 %collective-permute-start.6 = (bf16[64,4096]{1,0:T(8,128)(2,1)S(1)}, bf16[64,4096]{1,0:T(8,128)(2,1)S(1)}, u32[]{:S(2)}, u32[]{:S(2)}) collective-permute-start(bf16[64,4096]{1,0:T(8,128)(2,1)S(1)} %collective-permute-done.1.refs_2_), channel_id=1, source_target_pairs={{0,1},{1,0},{2,3},{3,2},{4,5},{5,4},{6,7},{7,6},{8,9},{9,8},{10,11... | collective-permute-start | bytes 1572872 | tf_op jit(solution)/shard_map/ppermute | solution.py:309
  35.6 8.1 %copy-start.9 = (bf16[32,4096]{1,0:T(8,128)(2,1)}, bf16[32,4096]{1,0:T(8,128)(2,1)S(1)}, u32[]{:S(2)}) copy-start(bf16[32,4096]{1,0:T(8,128)(2,1)S(1)} %collective-permute-done.2.refs_3_) | copy-start | bytes 786436
  35.6 8.2 %collective-permute-start.7 = (bf16[32,4096]{1,0:T(8,128)(2,1)S(1)}, bf16[32,4096]{1,0:T(8,128)(2,1)S(1)}, u32[]{:S(2)}, u32[]{:S(2)}) collective-permute-start(bf16[32,4096]{1,0:T(8,128)(2,1)S(1)} %collective-permute-done.2.refs_3_), channel_id=1, source_target_pairs={{0,1},{1,0},{2,3},{3,2},{4,5},{5,4},{6,7},{7,6},{8,9},{9,8},{10,11... | collective-permute-start | bytes 786440 | tf_op jit(solution)/shard_map/ppermute | solution.py:309
  35.7 8.0 %copy-start.10 = (bf16[32,4096]{1,0:T(8,128)(2,1)}, bf16[32,4096]{1,0:T(8,128)(2,1)S(1)}, u32[]{:S(2)}) copy-start(bf16[32,4096]{1,0:T(8,128)(2,1)S(1)} %collective-permute-done.3.refs_4_) | copy-start | bytes 786436
  35.7 8.1 %collective-permute-start.8 = (bf16[32,4096]{1,0:T(8,128)(2,1)S(1)}, bf16[32,4096]{1,0:T(8,128)(2,1)S(1)}, u32[]{:S(2)}, u32[]{:S(2)}) collective-permute-start(bf16[32,4096]{1,0:T(8,128)(2,1)S(1)} %collective-permute-done.3.refs_4_), channel_id=1, source_target_pairs={{0,1},{1,0},{2,3},{3,2},{4,5},{5,4},{6,7},{7,6},{8,9},{9,8},{10,11... | collective-permute-start | bytes 786440 | tf_op jit(solution)/shard_map/ppermute | solution.py:309
  43.8 0.8 copy-start.6
  43.8 0.9 copy-start.11
  43.8 0.9 copy-start.12
  43.8 1.1 copy-start.7
  44.9 0.8 copy-start.8
  60.3 26.4 %all-to-all-start = ((f32[8,256,128]{2,1,0:T(8,128)}), f32[8,256,128]{2,1,0:T(8,128)S(1)}, u32[]{:S(2)}, u32[]{:S(2)}) async-start(f32[8,256,128]{2,1,0:T(8,128)} %shard_map.40), calls=%async_computation | async-start | bytes 2097152 | tf_op jit(solution)/shard_map/all_to_all | solution.py:338
  67.5 65.8 %all-gather.5.cloned.1.call-start = ((), (), s32[]{:S(2)}) async-start(), calls=%async_computation.4 | async-start | bytes 1179648 | tf_op jit(solution)/shard_map/all_gather | solution.py:349
  86.7 13.2 %copy-start = (bf16[1024,1024]{1,0:T(8,128)(2,1)S(1)}, bf16[1024,1024]{1,0:T(8,128)(2,1)}, u32[]{:S(2)}) copy-start(bf16[1024,1024]{1,0:T(8,128)(2,1)} %mine.1) | copy-start | bytes 6291460
  86.8 1.3 collective-permute-start.9
  86.9 4.1 %collective-permute-start.10 = (bf16[128,128]{1,0:T(8,128)(2,1)S(1)}, bf16[128,128]{1,0:T(8,128)(2,1)S(1)}, u32[]{:S(2)}, u32[]{:S(2)}) collective-permute-start(bf16[128,128]{1,0:T(8,128)(2,1)S(1)} %get-tuple-element.27), channel_id=1, source_target_pairs={{0,16},{16,0},{1,17},{17,1},{2,18},{18,2},{3,19},{19,3},{4,20},{20... | collective-permute-start | bytes 98312 | tf_op jit(solution)/shard_map/ppermute | solution.py:309
  88.1 3.9 %collective-permute-start.11 = (bf16[128,128]{1,0:T(8,128)(2,1)S(1)}, bf16[128,128]{1,0:T(8,128)(2,1)S(1)}, u32[]{:S(2)}, u32[]{:S(2)}) collective-permute-start(bf16[128,128]{1,0:T(8,128)(2,1)S(1)} %collective-permute-done.9), channel_id=1, source_target_pairs={{0,16},{16,0},{1,17},{17,1},{2,18},{18,2},{3,19},{19,3},{4,20},{20... | collective-permute-start | bytes 98312 | tf_op jit(solution)/shard_map/ppermute | solution.py:309
  92.7 19.5 %all-to-all-start.1 = ((f32[8,256,128]{2,1,0:T(8,128)}), f32[8,256,128]{2,1,0:T(8,128)S(1)}, u32[]{:S(2)}, u32[]{:S(2)}) async-start(f32[8,256,128]{2,1,0:T(8,128)} %shard_map.37), calls=%async_computation.1 | async-start | bytes 2097152 | tf_op jit(solution)/shard_map/all_to_all | solution.py:341
  99.9 72.4 %all-gather.7.cloned.1.call-start = ((), (), s32[]{:S(2)}) async-start(), calls=%async_computation.5 | async-start | bytes 1179648 | tf_op jit(solution)/shard_map/all_gather | solution.py:353
  99.9 72.4 %collective-permute-start.24 = (bf16[1024,1024]{1,0:T(8,128)(2,1)S(1)}, bf16[1024,1024]{1,0:T(8,128)(2,1)}, u32[]{:S(2)}, u32[]{:S(2)}) collective-permute-start(bf16[1024,1024]{1,0:T(8,128)(2,1)S(1)} %copy-done), channel_id=1, source_target_pairs={{0,1},{1,0},{2,3},{3,2},{4,5},{5,4},{6,7},{7,6},{8,9},{9,8},{10,11... | collective-permute-start | bytes 6291464 | tf_op jit(solution)/shard_map/ppermute | solution.py:309
  112.2 1.3 collective-permute-start.12
  112.3 4.1 %collective-permute-start.13 = (bf16[128,128]{1,0:T(8,128)(2,1)S(1)}, bf16[128,128]{1,0:T(8,128)(2,1)S(1)}, u32[]{:S(2)}, u32[]{:S(2)}) collective-permute-start(bf16[128,128]{1,0:T(8,128)(2,1)S(1)} %get-tuple-element.31), channel_id=1, source_target_pairs={{0,16},{16,0},{1,17},{17,1},{2,18},{18,2},{3,19},{19,3},{4,20},{20... | collective-permute-start | bytes 98312 | tf_op jit(solution)/shard_map/ppermute | solution.py:309
  113.5 3.9 %collective-permute-start.14 = (bf16[128,128]{1,0:T(8,128)(2,1)S(1)}, bf16[128,128]{1,0:T(8,128)(2,1)S(1)}, u32[]{:S(2)}, u32[]{:S(2)}) collective-permute-start(bf16[128,128]{1,0:T(8,128)(2,1)S(1)} %collective-permute-done.12), channel_id=1, source_target_pairs={{0,16},{16,0},{1,17},{17,1},{2,18},{18,2},{3,19},{19,3},{4,20},{20... | collective-permute-start | bytes 98312 | tf_op jit(solution)/shard_map/ppermute | solution.py:309
  133.3 19.1 %collective-permute-start.15 = (bf16[256,256]{1,0:T(8,128)(2,1)S(1)}, bf16[256,256]{1,0:T(8,128)(2,1)S(1)}, u32[]{:S(2)}, u32[]{:S(2)}) collective-permute-start(bf16[256,256]{1,0:T(8,128)(2,1)S(1)} %get-tuple-element.35), channel_id=1, source_target_pairs={{0,0},{1,1},{2,32},{3,33},{4,64},{5,65},{6,96},{7,97},{8,128},{9,1... | collective-permute-start | bytes 393224 | tf_op jit(solution)/shard_map/ppermute | solution.py:361
  152.3 6.5 %collective-permute-start.16 = (bf16[256,256]{1,0:T(8,128)(2,1)S(1)}, bf16[256,256]{1,0:T(8,128)(2,1)S(1)}, u32[]{:S(2)}, u32[]{:S(2)}) collective-permute-start(bf16[256,256]{1,0:T(8,128)(2,1)S(1)} %collective-permute-done.15), channel_id=1, source_target_pairs={{0,8},{8,0},{1,9},{9,1},{2,10},{10,2},{3,11},{11,3},{4,12},{12,4},... | collective-permute-start | bytes 393224 | tf_op jit(solution)/shard_map/ppermute | solution.py:309
  158.8 20.5 %copy-start.5 = (bf16[2,256,256]{2,1,0:T(8,128)(2,1)}, bf16[2,256,256]{2,1,0:T(8,128)(2,1)S(1)}, u32[]{:S(2)}) copy-start(bf16[2,256,256]{2,1,0:T(8,128)(2,1)S(1)} %pad_maximum_fusion.refs_0_) | copy-start | bytes 786436
  158.8 7.2 %collective-permute-start.18 = (bf16[2,256,256]{2,1,0:T(8,128)(2,1)S(1)}, bf16[2,256,256]{2,1,0:T(8,128)(2,1)S(1)}, u32[]{:S(2)}, u32[]{:S(2)}) collective-permute-start(bf16[2,256,256]{2,1,0:T(8,128)(2,1)S(1)} %pad_maximum_fusion.refs_0_), channel_id=1, source_target_pairs={{0,2},{2,4},{4,6},{6,0},{1,3},{3,5},{5,7},{7,1},{8,10},{10,12},{12... | collective-permute-start | bytes 786440 | tf_op jit(solution)/shard_map/ppermute | solution.py:313
  158.9 8.9 %collective-permute-start.20 = (bf16[2,256,256]{2,1,0:T(8,128)(2,1)S(1)}, bf16[2,256,256]{2,1,0:T(8,128)(2,1)S(1)}, u32[]{:S(2)}, u32[]{:S(2)}) collective-permute-start(bf16[2,256,256]{2,1,0:T(8,128)(2,1)S(1)} %pad_maximum_fusion.refs_0_), channel_id=1, source_target_pairs={{0,4},{2,6},{4,0},{6,2},{1,5},{3,7},{5,1},{7,3},{8,12},{10,14},{12... | collective-permute-start | bytes 786440 | tf_op jit(solution)/shard_map/ppermute | solution.py:313
  159.0 11.5 %collective-permute-start.22 = (bf16[2,256,256]{2,1,0:T(8,128)(2,1)S(1)}, bf16[2,256,256]{2,1,0:T(8,128)(2,1)S(1)}, u32[]{:S(2)}, u32[]{:S(2)}) collective-permute-start(bf16[2,256,256]{2,1,0:T(8,128)(2,1)S(1)} %pad_maximum_fusion.refs_0_), channel_id=1, source_target_pairs={{0,6},{2,0},{4,2},{6,4},{1,7},{3,1},{5,3},{7,5},{8,14},{10,8},{12,... | collective-permute-start | bytes 786440 | tf_op jit(solution)/shard_map/ppermute | solution.py:313
  160.9 9.5 %collective-permute-start.17 = (bf16[2,256,256]{2,1,0:T(8,128)(2,1)S(1)}, bf16[2,256,256]{2,1,0:T(8,128)(2,1)S(1)}, u32[]{:S(2)}, u32[]{:S(2)}) collective-permute-start(bf16[2,256,256]{2,1,0:T(8,128)(2,1)S(1)} %pad_maximum_fusion.refs_0_), channel_id=1, source_target_pairs={{0,1},{1,0},{2,3},{3,2},{4,5},{5,4},{6,7},{7,6},{8,9},{9,8},{10,11... | collective-permute-start | bytes 786440 | tf_op jit(solution)/shard_map/ppermute | solution.py:309
  166.1 13.3 %copy-start.13 = (bf16[2,256,256]{2,1,0:T(8,128)(2,1)}, bf16[2,256,256]{2,1,0:T(8,128)(2,1)S(1)}, u32[]{:S(2)}) copy-start(bf16[2,256,256]{2,1,0:T(8,128)(2,1)S(1)} %collective-permute-done.18.refs_2_) | copy-start | bytes 786436
  166.1 4.4 %collective-permute-start.19 = (bf16[2,256,256]{2,1,0:T(8,128)(2,1)S(1)}, bf16[2,256,256]{2,1,0:T(8,128)(2,1)S(1)}, u32[]{:S(2)}, u32[]{:S(2)}) collective-permute-start(bf16[2,256,256]{2,1,0:T(8,128)(2,1)S(1)} %collective-permute-done.18.refs_2_), channel_id=1, source_target_pairs={{0,1},{1,0},{2,3},{3,2},{4,5},{5,4},{6,7},{7,6},{8,9},{9,8},{10,11... | collective-permute-start | bytes 786440 | tf_op jit(solution)/shard_map/ppermute | solution.py:309
  167.8 11.5 %copy-start.14 = (bf16[2,256,256]{2,1,0:T(8,128)(2,1)}, bf16[2,256,256]{2,1,0:T(8,128)(2,1)S(1)}, u32[]{:S(2)}) copy-start(bf16[2,256,256]{2,1,0:T(8,128)(2,1)S(1)} %collective-permute-done.20.refs_4_) | copy-start | bytes 786436
  167.8 2.7 %collective-permute-start.21 = (bf16[2,256,256]{2,1,0:T(8,128)(2,1)S(1)}, bf16[2,256,256]{2,1,0:T(8,128)(2,1)S(1)}, u32[]{:S(2)}, u32[]{:S(2)}) collective-permute-start(bf16[2,256,256]{2,1,0:T(8,128)(2,1)S(1)} %collective-permute-done.20.refs_4_), channel_id=1, source_target_pairs={{0,1},{1,0},{2,3},{3,2},{4,5},{5,4},{6,7},{7,6},{8,9},{9,8},{10,11... | collective-permute-start | bytes 786440 | tf_op jit(solution)/shard_map/ppermute | solution.py:309
  170.5 8.9 %copy-start.15 = (bf16[2,256,256]{2,1,0:T(8,128)(2,1)}, bf16[2,256,256]{2,1,0:T(8,128)(2,1)S(1)}, u32[]{:S(2)}) copy-start(bf16[2,256,256]{2,1,0:T(8,128)(2,1)S(1)} %collective-permute-done.22.refs_6_) | copy-start | bytes 786436
  170.5 1.7 collective-permute-start.23
  170.5 8.9 %copy-start.16 = (bf16[2,256,256]{2,1,0:T(8,128)(2,1)}, bf16[2,256,256]{2,1,0:T(8,128)(2,1)S(1)}, u32[]{:S(2)}) copy-start(bf16[2,256,256]{2,1,0:T(8,128)(2,1)S(1)} %collective-permute-done.17.refs_1_) | copy-start | bytes 786436
  170.5 0.8 copy-start.17
  171.3 0.7 copy-start.18
  172.3 1.2 copy-start.1
  173.5 1.2 copy-start.2
Sparse Core Ops, SparseCore 0:
  92.8 40.3 all-gather.4
  135.0 37.2 all-gather.6

commit v4 on v3

--- a/solution.py
+++ b/solution.py
@@ -71,7 +71,7 @@
         grid=(count,),
         in_specs=[pl.BlockSpec(memory_space=pltpu.SMEM)],
         out_specs=pl.BlockSpec((depth, 8 * width), lambda k: (k, 0)),
-        compiler_params=pltpu.CompilerParams(vmem_limit_bytes=60 << 20),
+        compiler_params=pltpu.CompilerParams(vmem_limit_bytes=12 << 20),
         cost_estimate=pl.CostEstimate(
             flops=1200 * count * depth * 8 * width,
             bytes_accessed=2 * count * depth * 8 * width,
@@ -153,7 +153,7 @@
         write_run(out, total, width)
 
 
-def project(kernel, leading, specs, steps, width, blocks):
+def project(kernel, leading, specs, steps, width, blocks, vmem):
     rows, params = 4 * blocks[0].shape[0], 2 * blocks[0].shape[1]
     return pl.pallas_call(
         kernel,
@@ -166,7 +166,7 @@
             pltpu.VMEM((rows, 8 * width), F32),
             pltpu.SemaphoreType.DMA((len(blocks),)),
         ],
-        compiler_params=pltpu.CompilerParams(vmem_limit_bytes=60 << 20),
+        compiler_params=pltpu.CompilerParams(vmem_limit_bytes=vmem << 20),
         cost_estimate=pl.CostEstimate(
             flops=2 * rows * params * 8 * width, bytes_accessed=16 << 20, transcendentals=0
         ),
@@ -201,92 +201,90 @@
     )(part, *earlier)
 
 
-def condition_kernel(low, high, mine, other, out):
+RING = (0, -1, -2, -3, -4, 1, 2, 3)
+
+
+def condition_kernel(*refs):
+    runs, (mine, other), (out, pieces, tiles, arrived) = (refs[:8], refs[8:16]), refs[16:18], refs[18:]
     core = lax.axis_index("c")
     yl = lax.axis_index("yl")
-
-    def run(near, far):
+    z = lax.axis_index("zh") * 2 + lax.axis_index("zl")
+    first = [
+        pltpu.make_async_copy(mine, tiles.at[core], arrived.at[16]),
+        pltpu.make_async_copy(other, tiles.at[1 - core], arrived.at[17]),
+    ]
+    copies = []
+    for index in range(8):
+        for run in range(2):
+            target = pieces.at[index, :, :, run * 128 : (run + 1) * 128]
+            copies.append(pltpu.make_async_copy(runs[run][index], target, arrived.at[index * 2 + run]))
+    for copy in first + copies:
+        copy.start()
+    out[...] = jnp.zeros_like(out)
+    for copy in first:
+        copy.wait()
+    for index, away in enumerate(RING):
+        copies[index * 2].wait()
+        copies[index * 2 + 1].wait()
+        source = (z + (away + 8)) & 7
         total = None
-        for zl in range(2):
-            for flips in range(4):
-                tile = (near, far)[flips // 2]
-                start = pl.multiple_of((zl * 2 + (core ^ (flips % 2))) * 256, 256)
-                piece = jnp.concatenate([low[zl, flips], high[zl, flips]], axis=1)
-                term = jnp.dot(piece, tile[pl.ds(start, 256), :], preferred_element_type=F32)
-                total = term if total is None else total + term
-        out[...] = total
-
-    @pl.when(yl == core)
-    def _():
-        run(mine, other)
-
-    @pl.when(yl != core)
-    def _():
-        run(other, mine)
+        for flip in range(4):
+            start = pl.multiple_of(((source & 1) * 2 + (core ^ (flip % 2))) * 256, 256)
+            tile = tiles[yl ^ (flip // 2), pl.ds(start, 256), :]
+            term = jnp.dot(pieces[index, flip], tile, preferred_element_type=F32)
+            total = term if total is None else total + term
+        out[pl.ds(pl.multiple_of((source >> 1) * 128, 128), 128), :] += total
 
 
 def condition(low, high, mine, other):
-    rows = low.shape[2]
+    flips, rows, width = low[0].shape
     return pl.pallas_call(
         condition_kernel,
         out_shape=jax.ShapeDtypeStruct((4 * rows, mine.shape[1]), F32),
-        grid=(4,),
-        in_specs=[
-            pl.BlockSpec((2,) + low.shape[1:], lambda g: (g, 0, 0, 0)),
-            pl.BlockSpec((2,) + high.shape[1:], lambda g: (g, 0, 0, 0)),
-            pl.BlockSpec(mine.shape, lambda g: (0, 0)),
-            pl.BlockSpec(other.shape, lambda g: (0, 0)),
+        in_specs=[pl.BlockSpec(memory_space=pltpu.HBM)] * 18,
+        out_specs=pl.BlockSpec(memory_space=pltpu.VMEM),
+        scratch_shapes=[
+            pltpu.VMEM((8, flips, rows, 2 * width), BF16),
+            pltpu.VMEM((2,) + mine.shape, BF16),
+            pltpu.SemaphoreType.DMA((18,)),
         ],
-        out_specs=pl.BlockSpec((rows, mine.shape[1]), lambda g: (g, 0)),
         compiler_params=pltpu.CompilerParams(vmem_limit_bytes=24 << 20),
         cost_estimate=pl.CostEstimate(flops=2 * 512 * 2048 * 1024, bytes_accessed=7 << 20, transcendentals=0),
-    )(low, high, mine, other)
-
-
-def pair_kernel(parts, *refs):
-    away, (out, rows, pairs, features, arrived) = refs[:8], refs[8:]
-    copies = [pltpu.make_async_copy(a, features.at[i], arrived.at[i]) for i, a in enumerate(away)]
-    for copy in copies:
-        copy.start()
-    yh, x, core = (lax.axis_index(name) for name in PAR)
+    )(*low, *high, mine, other)
+
+
+def pair_kernel(parts, near, far, out, rows, pairs):
+    core = lax.axis_index("c")
     total = parts[0]
     for index in range(1, parts.shape[0]):
         total += parts[index]
     rows[...] = total.astype(BF16)
-    pairs[...] = jnp.zeros_like(pairs)
-    for copy in copies:
-        copy.wait()
-    for shift in range(4):
-        for flip_core in range(2):
-            for flip_yh in range(2):
-                z = (yh ^ flip_yh) * 4 + ((x + 4 - shift) & 3)
-                start = pl.multiple_of(((z & 1) * 2 + (core ^ flip_core)) * 256, 256)
-                at = pl.ds(pl.multiple_of((z >> 1) * 256, 256), 256)
-                pairs[:, at] += lax.dot_general(
+    for zh in range(4):
+        value = None
+        for zl in range(2):
+            for flip in range(2):
+                start = pl.multiple_of((zl * 2 + (core ^ flip)) * 256, 256)
+                term = lax.dot_general(
                     rows[:, pl.ds(start, 256)],
-                    features[shift * 2 + flip_core, flip_yh],
+                    (near, far)[flip][zh * 2 + zl],
                     (((1,), (1,)), ((), ())),
                     preferred_element_type=F32,
                 )
+                value = term if value is None else value + term
+        pairs[:, zh * 256 : (zh + 1) * 256] = value
     for block in range(16):
         piece = pairs[:, block * 64 : (block + 1) * 64]
         out[block, :, :64] = piece[:32]
         out[block, :, 64:] = piece[32:]
 
 
-def pair(parts, features):
+def pair(parts, near, far):
     return pl.pallas_call(
         pair_kernel,
         out_shape=jax.ShapeDtypeStruct((16, 32, 128), F32),
-        in_specs=[pl.BlockSpec(memory_space=pltpu.VMEM)] + [pl.BlockSpec(memory_space=pltpu.HBM)] * 8,
-        scratch_shapes=[
-            pltpu.VMEM((64, 1024), BF16),
-            pltpu.VMEM((64, 1024), F32),
-            pltpu.VMEM((8, 2, 256, 256), BF16),
-            pltpu.SemaphoreType.DMA((8,)),
-        ],
-        compiler_params=pltpu.CompilerParams(vmem_limit_bytes=60 << 20),
-    )(parts, *features)
+        scratch_shapes=[pltpu.VMEM((64, 1024), BF16), pltpu.VMEM((64, 1024), F32)],
+        compiler_params=pltpu.CompilerParams(vmem_limit_bytes=12 << 20),
+    )(parts, near, far)
 
 
 def finish_kernel(parts, out):
@@ -309,48 +307,56 @@
     return lax.ppermute(value, axis, [(0, 1), (1, 0)])
 
 
-def shift_x(value, by):
-    return lax.ppermute(value, "x", [(i, (i + by) % 4) for i in range(4)])
+def ring(value):
+    up, down = [], []
+    ahead = behind = value
+    for step in range(4):
+        ahead = lax.ppermute(ahead, ("zh", "zl"), [(i, (i + 1) % 8) for i in range(8)])
+        up.append(ahead)
+        if step < 3:
+            behind = lax.ppermute(behind, ("zh", "zl"), [(i, (i + 7) % 8) for i in range(8)])
+            down.append(behind)
+    return [value] + up + down
+
+
+def flips(keep, send):
+    received = swap(send, "c")
+    return jnp.stack([keep, received, swap(keep, "yl"), swap(received, "yl")])
 
 
 def per_device(gradients, inverse_gram, hash_words):
     half = gradients.shape[0] // 2
-    next_y = swap(gradients, "yl")
-    next_z = swap(gradients, "zl")
-    own = [gradients, next_y, next_z, swap(next_y[:half], "zl"), swap(next_z[half:], "yl")]
-    other = [swap(a, "c") for a in own]
-    other_tile = swap(inverse_gram, "c")
-
-    blocks = own + other
     width, depth, params = 128, 1024, 2 * gradients.shape[1]
     split = 5
     words_spec = pl.BlockSpec(memory_space=pltpu.SMEM)
-
     first = table(0, width, 0, split, depth, params, hash_words)
     second = table(0, width, split, params // depth - split, depth, params, hash_words)
+
+    next_y = swap(gradients, "yl")
+    next_z = swap(gradients, "zl")
+    first, next_y, next_z = lax.optimization_barrier((first, next_y, next_z))
+    own = [gradients, next_y, next_z, swap(next_y[:half], "zl"), swap(next_z[half:], "yl")]
+    blocks = own + [swap(a, "c") for a in own]
+    other_tile = swap(inverse_gram, "c")
+
     table_specs = [
         pl.BlockSpec((depth, 8 * width), lambda k: (jnp.minimum(k, split - 1), 0)),
         pl.BlockSpec((depth, 8 * width), lambda k: (jnp.maximum(k - split, 0), 0)),
     ]
     partial = project(
-        functools.partial(ready_kernel, split, width), [first, second], table_specs, params // depth, width, blocks
+        functools.partial(ready_kernel, split, width), [first, second], table_specs, params // depth, width, blocks, 24
     )
     part = lax.all_to_all(partial, CHIPS, 0, 0, tiled=True)
-    partial = project(functools.partial(hash_kernel, 1, width), [hash_words], [words_spec], 16, width, blocks)
+    partial = project(functools.partial(hash_kernel, 1, width), [hash_words], [words_spec], 16, width, blocks, 60)
     partial, part = lax.optimization_barrier((partial, part))
     next_part = lax.all_to_all(partial, CHIPS, 0, 0, tiled=True)
 
-    def flips(keep, send):
-        received = swap(send, "c")
-        return jnp.stack([keep, received, swap(keep, "yl"), swap(received, "yl")])
-
     whole, keep, send = sum_parts(part)
-    mine = flips(keep, send)
-    low = lax.all_gather(mine, ("zh", "zl"), axis=0)
-    next_part, mine = lax.optimization_barrier((next_part, mine))
+    low = ring(flips(keep, send))
+    next_part, low = lax.optimization_barrier((next_part, low))
     whole, keep, send = sum_parts(next_part, whole)
-    mine, low = lax.optimization_barrier((flips(keep, send), low))
-    high = lax.all_gather(mine, ("zh", "zl"), axis=0)
+    whole, mine = lax.optimization_barrier((whole, flips(keep, send)))
+    high = ring(mine)
 
     route = []
     for z in range(8):
@@ -359,16 +365,12 @@
                 for c in range(2):
                     route.append((((z * 2 + yl) * 8 + chip) * 2 + c, ((chip * 2 + yl) * 8 + z) * 2 + c))
     turned = lax.ppermute(whole, EX + PAR, route)
-    turned = jnp.stack([turned, swap(turned, "yh")])
-    features = []
-    for by in range(4):
-        shifted_x = shift_x(turned, by) if by else turned
-        features += [shifted_x, swap(shifted_x, "c")]
-
-    high, features = lax.optimization_barrier((high, features))
+    near = lax.all_gather(turned, CHIPS, axis=0)
+    far = swap(near, "c")
+
     conditioned = condition(low, high, inverse_gram, other_tile)
     parts = lax.all_to_all(conditioned.reshape(8, 64, 1024), CHIPS, 0, 0, tiled=True)
-    return finish(lax.all_to_all(pair(parts, features), EX, 0, 0, tiled=True))
+    return finish(lax.all_to_all(pair(parts, near, far), EX, 0, 0, tiled=True))
 
 
 def solution(mesh):

time: 244 us -> 250 us (1.025)
  starting transfers between devices: 31.5 us -> 55.4 us
  blocking collectives: 47.1 us -> 25.4 us
  waiting for transfers between devices: 76.5 us -> 94.9 us
  Pallas kernels: 63.7 us -> 51 us
    all_to_all x2 -> x1, blocking collectives: 47.1 us -> 25.4 us  [per_device(): return finish(lax.all_to_all(pair(parts, near, far), EX, 0, 0, tiled=True))]
    ppermute x3 -> x14, waiting for transfers between devices: 9.52 us -> 31.1 us  [the longest x8 31.1 us: ring(): lax.ppermute(ahead, ('zh', 'zl'), [(i, (i + 1) % 8) for i in range(8)])]
    ppermute x3 -> x14, starting transfers between devices: 2.09 us -> 21.4 us  [the longest x6 20.6 us: ring(): lax.ppermute(behind, ('zh', 'zl'), [(i, (i + 7) % 8) for i in range(8)])]
    all_to_all x1, waiting for transfers between devices: 12.1 us -> 0.01 us  [per_device(): next_part = lax.all_to_all(partial, CHIPS, 0, 0, tiled=True)]
    all_gather x2 -> x1, waiting for transfers between devices: 15.3 us -> 22.8 us  [per_device(): near = lax.all_gather(turned, CHIPS, axis=0)]
    all_to_all x0 -> x1, starting transfers between devices: none -> 6.91 us  [per_device(): lax.all_to_all(conditioned.reshape(8, 64, 1024), CHIPS, 0, 0, tiled=True)]
    pallas_call x2, Pallas kernels: 33.8 us -> 26.9 us  [project(): pl.pallas_call(kernel, out_shape=jax.ShapeDtypeStruct((8, rows, width), F...]
    pallas_call x1, Pallas kernels: 4.79 us -> 0.94 us  [pair(): pl.pallas_call(pair_kernel, out_shape=jax.ShapeDtypeStruct((16, 32, 128),...]
  transfers between devices with their start and end apart: 29 -> 36, of which waited for: 16 -> 20; matrix products, arithmetic and copies ran while one was open for 0% -> 0% of each run, Pallas kernels for 16% -> 16%
where the time goes in v4:
time: 250 us; the launch traced here: 247 us
  waiting for transfers between devices  94.9 us (38%)
  starting transfers between devices  55.4 us (22%)
  Pallas kernels  51 us (20%)
  blocking collectives  25.4 us (10%)
  between operations  13.7 us (5%)
  local copies, waits for them, and re-layouts  7.02 us (3%)
    ppermute x8, waiting for transfers between devices, ring(): lax.ppermute(ahead, ('zh', 'zl'), [(i, (i + 1) % 8) for i in range(8)])  31.1 us
    pallas_call x2, Pallas kernels, project(): pl.pallas_call(kernel, out_shape=jax.ShapeDtypeStruct((8, rows, width), F...  26.9 us
    all_to_all x1, blocking collectives, per_device(): return finish(lax.all_to_all(pair(parts, near, far), EX, 0, 0, tiled=True))  25.4 us
    ppermute x17, waiting for transfers between devices, swap(): return lax.ppermute(value, axis, [(0, 1), (1, 0)])  24.9 us
    all_gather x1, waiting for transfers between devices, per_device(): near = lax.all_gather(turned, CHIPS, axis=0)  22.8 us
    ppermute x6, starting transfers between devices, ring(): lax.ppermute(behind, ('zh', 'zl'), [(i, (i + 7) % 8) for i in range(8)])  20.6 us
    ppermute x1, waiting for transfers between devices, per_device(): turned = lax.ppermute(whole, EX + PAR, route)  16 us
    pallas_call x2, Pallas kernels, table(): pl.pallas_call(functools.partial(table_kernel, part, width, first, params...  15.8 us
  transfers between devices with their start and end apart: 36, of which 20 were waited for; matrix products, arithmetic and copies ran while one was open for 0% of the time, Pallas kernels for 16%

profile of v4, /device:TPU:22, one launch (start us, length us, event | category | flops | bytes accessed | tf_op | source)
XLA Modules:
  0.0 247.4 jit_solution(12289762601154332054)
XLA Ops:
  6.5 1.3 collective-permute-start
  7.8 1.9 collective-permute-start.1
  9.7 0.7 copy-done.13
  10.4 9.7 %shard_map.37.first = bf16[5120,1024]{1,0:T(8,128)(2,1)S(1)} custom-call(s32[4]{0:T(128)S(1)} %copy-done.13), custom_call_target="tpu_custom_call" | custom-call | flops 6291456000 | bytes 10485760 | tf_op jit(solution)/shard_map/pallas_call | solution.py:68
  20.1 0.3 collective-permute-done.refs_1_
  20.4 1.2 collective-permute-done.1.refs_2_
  21.6 1.8 collective-permute-start.2
  23.5 0.8 collective-permute-start.3
  24.3 0.5 collective-permute-start.5
  24.8 0.0 collective-permute-start.6
  24.8 4.0 %collective-permute-done.2.refs_3_ = bf16[32,4096]{1,0:T(8,128)(2,1)S(1)} collective-permute-done((bf16[32,4096]{1,0:T(8,128)(2,1)S(1)}, bf16[32,4096]{1,0:T(8,128)(2,1)S(1)}, u32[]{:S(2)}, u32[]{:S(2)}) %collective-permute-start.2) | collective-permute-done | bytes 262176 | tf_op jit(solution)/shard_map/ppermute | solution.py:307
  28.8 1.3 collective-permute-done.3.refs_4_
  30.1 6.1 %shard_map.39.second = bf16[3072,1024]{1,0:T(8,128)(2,1)S(1)} custom-call(s32[4]{0:T(128)S(1)} %copy-done.14), custom_call_target="tpu_custom_call" | custom-call | flops 3774873600 | bytes 6291456 | tf_op jit(solution)/shard_map/pallas_call | solution.py:68
  36.3 7.7 %shard_map.40 = f32[8,256,128]{2,1,0:T(8,128)} custom-call(bf16[5120,1024]{1,0:T(8,128)(2,1)S(1)} %shard_map.37.first, bf16[3072,1024]{1,0:T(8,128)(2,1)S(1)} %shard_map.39.second, bf16[64,4096]{1,0:T(8,128)(2,1)S(1)} %copy-done.5, bf16[64,4096]{1,0:T(8,128)(2,1)S(1)} %collective-permute-done.refs_1_, bf16[64,4096]{1,0:T(8,128)(2,1)S(1)} %collective-permute-done.1.refs_2_, ...), custom_call_target="tpu_custom_call" | custom-call | flops 4294967296 | bytes 16777216 | tf_op jit(solution)/shard_map/pallas_call | solution.py:158
  44.1 0.7 copy-done.11
  44.9 0.7 copy-done.12
  45.6 7.2 %all-to-all-start = ((f32[8,256,128]{2,1,0:T(8,128)}), f32[8,256,128]{2,1,0:T(8,128)S(1)}, u32[]{:S(2)}, u32[]{:S(2)}) async-start(f32[8,256,128]{2,1,0:T(8,128)} %shard_map.40), calls=%async_computation | async-start | bytes 2097152 | tf_op jit(solution)/shard_map/all_to_all | solution.py:349
  52.8 19.2 %shard_map.38 = f32[8,256,128]{2,1,0:T(8,128)} custom-call(s32[4]{0:T(128)} %words.5, bf16[64,4096]{1,0:T(8,128)(2,1)} %refs_0_.3, bf16[64,4096]{1,0:T(8,128)(2,1)} %copy-done.2, bf16[64,4096]{1,0:T(8,128)(2,1)} %copy-done.3, bf16[32,4096]{1,0:T(8,128)(2,1)} %copy-done.9, bf16[32,4096]{1,0:T(8,128)(2,1)} %copy-done.10, bf16[64,4096]{1,0:T(8,128)(2,1)} %copy-done.6, ...), custom_call_target="tpu_custom_call" | custom-call | flops 4294967296 | bytes 16777216 | tf_op jit(solution)/shard_map/pallas_call | solution.py:158
  72.0 7.2 %all-to-all-start.1 = ((f32[8,256,128]{2,1,0:T(8,128)}), f32[8,256,128]{2,1,0:T(8,128)S(1)}, u32[]{:S(2)}, u32[]{:S(2)}) async-start(f32[8,256,128]{2,1,0:T(8,128)} %shard_map.38), calls=%async_computation.1 | async-start | bytes 2097152 | tf_op jit(solution)/shard_map/all_to_all | solution.py:352
  79.2 0.1 shard_map.41
  79.3 0.1 collective-permute-start.9
  79.4 0.8 collective-permute-start.10
  80.2 0.4 collective-permute-done.9
  80.6 0.9 collective-permute-start.11
  81.5 11.5 %collective-permute-done.10 = bf16[128,128]{1,0:T(8,128)(2,1)S(1)} collective-permute-done((bf16[128,128]{1,0:T(8,128)(2,1)S(1)}, bf16[128,128]{1,0:T(8,128)(2,1)S(1)}, u32[]{:S(2)}, u32[]{:S(2)}) %collective-permute-start.10) | collective-permute-done | bytes 32800 | tf_op jit(solution)/shard_map/ppermute | solution.py:307
  93.0 0.6 collective-permute-done.11
  93.6 0.6 collective-permute-start.12
  94.3 4.5 %collective-permute-start.16 = (bf16[4,128,128]{2,1,0:T(8,128)(2,1)S(1)}, bf16[4,128,128]{2,1,0:T(8,128)(2,1)S(1)}, u32[]{:S(2)}, u32[]{:S(2)}) collective-permute-start(bf16[4,128,128]{2,1,0:T(8,128)(2,1)S(1)} %pad_maximum_fusion.refs_0_), channel_id=1, source_target_pairs={{0,224},{32,0},{64,32},{96,64},{128,96},{160,128},{192,160},{224,1... | collective-permute-start | bytes 393224 | tf_op jit(solution)/shard_map/ppermute | solution.py:317
  98.7 3.6 %collective-permute-done.12.refs_1_ = bf16[4,128,128]{2,1,0:T(8,128)(2,1)S(1)} collective-permute-done((bf16[4,128,128]{2,1,0:T(8,128)(2,1)S(1)}, bf16[4,128,128]{2,1,0:T(8,128)(2,1)S(1)}, u32[]{:S(2)}, u32[]{:S(2)}) %collective-permute-start.12) | collective-permute-done | bytes 131104 | tf_op jit(solution)/shard_map/ppermute | solution.py:314
  102.4 0.0 collective-permute-start.13
  102.4 3.2 %collective-permute-start.17 = (bf16[4,128,128]{2,1,0:T(8,128)(2,1)S(1)}, bf16[4,128,128]{2,1,0:T(8,128)(2,1)S(1)}, u32[]{:S(2)}, u32[]{:S(2)}) collective-permute-start(bf16[4,128,128]{2,1,0:T(8,128)(2,1)S(1)} %collective-permute-done.16.refs_5_), channel_id=1, source_target_pairs={{0,224},{32,0},{64,32},{96,64},{128,96},{160,128},{192,160},{224,1... | collective-permute-start | bytes 393224 | tf_op jit(solution)/shard_map/ppermute | solution.py:317
  105.6 2.9 %collective-permute-done.13.refs_2_ = bf16[4,128,128]{2,1,0:T(8,128)(2,1)S(1)} collective-permute-done((bf16[4,128,128]{2,1,0:T(8,128)(2,1)S(1)}, bf16[4,128,128]{2,1,0:T(8,128)(2,1)S(1)}, u32[]{:S(2)}, u32[]{:S(2)}) %collective-permute-start.13) | collective-permute-done | bytes 131104 | tf_op jit(solution)/shard_map/ppermute | solution.py:314
  108.5 3.2 %collective-permute-start.18 = (bf16[4,128,128]{2,1,0:T(8,128)(2,1)S(1)}, bf16[4,128,128]{2,1,0:T(8,128)(2,1)S(1)}, u32[]{:S(2)}, u32[]{:S(2)}) collective-permute-start(bf16[4,128,128]{2,1,0:T(8,128)(2,1)S(1)} %collective-permute-done.17.refs_6_), channel_id=1, source_target_pairs={{0,224},{32,0},{64,32},{96,64},{128,96},{160,128},{192,160},{224,1... | collective-permute-start | bytes 393224 | tf_op jit(solution)/shard_map/ppermute | solution.py:317
  111.8 2.9 %collective-permute-done.14.refs_3_ = bf16[4,128,128]{2,1,0:T(8,128)(2,1)S(1)} collective-permute-done((bf16[4,128,128]{2,1,0:T(8,128)(2,1)S(1)}, bf16[4,128,128]{2,1,0:T(8,128)(2,1)S(1)}, u32[]{:S(2)}, u32[]{:S(2)}) %collective-permute-start.14) | collective-permute-done | bytes 131104 | tf_op jit(solution)/shard_map/ppermute | solution.py:314
  114.7 6.2 %collective-permute-done.15.refs_4_ = bf16[4,128,128]{2,1,0:T(8,128)(2,1)S(1)} collective-permute-done((bf16[4,128,128]{2,1,0:T(8,128)(2,1)S(1)}, bf16[4,128,128]{2,1,0:T(8,128)(2,1)S(1)}, u32[]{:S(2)}, u32[]{:S(2)}) %collective-permute-start.15) | collective-permute-done | bytes 131104 | tf_op jit(solution)/shard_map/ppermute | solution.py:314
  120.9 0.1 shard_map.42
  121.0 0.1 collective-permute-start.19
  121.1 1.4 collective-permute-start.20
  122.5 1.1 collective-permute-start.21
  123.6 1.5 collective-permute-done.20
  125.1 1.3 collective-permute-done.21
  126.4 1.9 collective-permute-start.30
  128.3 16.0 %collective-permute-done.30 = bf16[256,256]{1,0:T(8,128)(2,1)S(1)} collective-permute-done((bf16[256,256]{1,0:T(8,128)(2,1)S(1)}, bf16[256,256]{1,0:T(8,128)(2,1)S(1)}, u32[]{:S(2)}, u32[]{:S(2)}) %collective-permute-start.30) | collective-permute-done | bytes 131104 | tf_op jit(solution)/shard_map/ppermute | solution.py:367
  144.3 0.7 copy-done.15
  145.0 0.0 all-gather.3.cloned.1.call-update
  145.0 0.1 collective-permute-start.22
  145.1 3.2 %collective-permute-start.26 = (bf16[4,128,128]{2,1,0:T(8,128)(2,1)S(1)}, bf16[4,128,128]{2,1,0:T(8,128)(2,1)S(1)}, u32[]{:S(2)}, u32[]{:S(2)}) collective-permute-start(bf16[4,128,128]{2,1,0:T(8,128)(2,1)S(1)} %pad_maximum_fusion.1.refs_8_), channel_id=1, source_target_pairs={{0,224},{32,0},{64,32},{96,64},{128,96},{160,128},{192,160},{224,1... | collective-permute-start | bytes 393224 | tf_op jit(solution)/shard_map/ppermute | solution.py:317
  148.3 3.4 %collective-permute-done.22.refs_9_ = bf16[4,128,128]{2,1,0:T(8,128)(2,1)S(1)} collective-permute-done((bf16[4,128,128]{2,1,0:T(8,128)(2,1)S(1)}, bf16[4,128,128]{2,1,0:T(8,128)(2,1)S(1)}, u32[]{:S(2)}, u32[]{:S(2)}) %collective-permute-start.22) | collective-permute-done | bytes 131104 | tf_op jit(solution)/shard_map/ppermute | solution.py:314
  151.7 3.2 %collective-permute-start.27 = (bf16[4,128,128]{2,1,0:T(8,128)(2,1)S(1)}, bf16[4,128,128]{2,1,0:T(8,128)(2,1)S(1)}, u32[]{:S(2)}, u32[]{:S(2)}) collective-permute-start(bf16[4,128,128]{2,1,0:T(8,128)(2,1)S(1)} %collective-permute-done.26.refs_13_), channel_id=1, source_target_pairs={{0,224},{32,0},{64,32},{96,64},{128,96},{160,128},{192,160},{224,1... | collective-permute-start | bytes 393224 | tf_op jit(solution)/shard_map/ppermute | solution.py:317
  155.0 2.9 %collective-permute-done.23.refs_10_ = bf16[4,128,128]{2,1,0:T(8,128)(2,1)S(1)} collective-permute-done((bf16[4,128,128]{2,1,0:T(8,128)(2,1)S(1)}, bf16[4,128,128]{2,1,0:T(8,128)(2,1)S(1)}, u32[]{:S(2)}, u32[]{:S(2)}) %collective-permute-start.23) | collective-permute-done | bytes 131104 | tf_op jit(solution)/shard_map/ppermute | solution.py:314
  157.9 3.2 %collective-permute-start.28 = (bf16[4,128,128]{2,1,0:T(8,128)(2,1)S(1)}, bf16[4,128,128]{2,1,0:T(8,128)(2,1)S(1)}, u32[]{:S(2)}, u32[]{:S(2)}) collective-permute-start(bf16[4,128,128]{2,1,0:T(8,128)(2,1)S(1)} %collective-permute-done.27.refs_14_), channel_id=1, source_target_pairs={{0,224},{32,0},{64,32},{96,64},{128,96},{160,128},{192,160},{224,1... | collective-permute-start | bytes 393224 | tf_op jit(solution)/shard_map/ppermute | solution.py:317
  161.1 2.9 %collective-permute-done.24.refs_11_ = bf16[4,128,128]{2,1,0:T(8,128)(2,1)S(1)} collective-permute-done((bf16[4,128,128]{2,1,0:T(8,128)(2,1)S(1)}, bf16[4,128,128]{2,1,0:T(8,128)(2,1)S(1)}, u32[]{:S(2)}, u32[]{:S(2)}) %collective-permute-start.24) | collective-permute-done | bytes 131104 | tf_op jit(solution)/shard_map/ppermute | solution.py:314
  164.1 6.2 %collective-permute-done.25.refs_12_ = bf16[4,128,128]{2,1,0:T(8,128)(2,1)S(1)} collective-permute-done((bf16[4,128,128]{2,1,0:T(8,128)(2,1)S(1)}, bf16[4,128,128]{2,1,0:T(8,128)(2,1)S(1)}, u32[]{:S(2)}, u32[]{:S(2)}) %collective-permute-start.25) | collective-permute-done | bytes 131104 | tf_op jit(solution)/shard_map/ppermute | solution.py:314
  170.3 1.6 copy-done.1
  171.8 5.5 %shard_map.43 = f32[512,1024]{1,0:T(8,128)S(1)} custom-call(bf16[4,128,128]{2,1,0:T(8,128)(2,1)S(1)} %pad_maximum_fusion.refs_0_, bf16[4,128,128]{2,1,0:T(8,128)(2,1)S(1)} %collective-permute-done.12.refs_1_, bf16[4,128,128]{2,1,0:T(8,128)(2,1)S(1)} %collective-permute-done.13.refs_2_, bf16[4,128,128]{2,1,0:T(8,128)(2,1)S(1)} %collective-permute-done.14.refs_3_, ...), custom_call_target="tpu_custom_call" | custom-call | flops 2147483648 | bytes 7340032 | tf_op jit(solution)/shard_map/pallas_call | solution.py:241
  177.4 1.3 copy-done
  178.7 6.9 %all-to-all-start.2 = ((f32[8,64,1024]{2,1,0:T(8,128)}), f32[8,64,1024]{2,1,0:T(8,128)S(1)}, u32[]{:S(2)}, u32[]{:S(2)}) async-start(f32[8,64,1024]{2,1,0:T(8,128)} %bitcast.10), calls=%async_computation.2 | async-start | bytes 4194304 | tf_op jit(solution)/shard_map/all_to_all | solution.py:372
  185.6 22.8 %all-gather.3.cloned.1.call-done = bf16[2048,256]{1,0:T(8,128)(2,1)} async-done(((bf16[256,256]{1,0:T(8,128)(2,1)}), bf16[2048,256]{1,0:T(8,128)(2,1)}) %all-gather.3.cloned.1.call-update) | async-done | bytes 1048592 | tf_op jit(solution)/shard_map/all_gather | solution.py:368
  208.4 0.0 all-to-all-done.2.parts
  208.5 2.8 %collective-permute-done.31.far = bf16[8,256,256]{2,1,0:T(8,128)(2,1)S(1)} collective-permute-done((bf16[8,256,256]{2,1,0:T(8,128)(2,1)}, bf16[8,256,256]{2,1,0:T(8,128)(2,1)S(1)}, u32[]{:S(2)}, u32[]{:S(2)}) %collective-permute-start.31) | collective-permute-done | bytes 1048608 | tf_op jit(solution)/shard_map/ppermute | solution.py:307
  211.3 1.2 copy-done.4
  212.5 0.9 shard_map.44
  213.5 25.4 %all_to_all.20.parts = f32[16,32,128]{2,1,0:T(8,128)} all-to-all(f32[16,32,128]{2,1,0:T(8,128)S(1)} %shard_map.44), channel_id=1, replica_groups=mesh['zh'=4,'zl'=2,'yl'=2,'yh'=2,'x'=4,'c'=2] {'zh','zl','yl'}, dimensions={0} | all-to-all | bytes 524288 | tf_op jit(solution)/shard_map/all_to_all | solution.py:373
  238.9 1.7 shard_map.45
  (55 shorter events, 0.2 us)
Async XLA Ops:
  6.5 17.8 %copy-start.5 = (bf16[64,4096]{1,0:T(8,128)(2,1)S(1)}, bf16[64,4096]{1,0:T(8,128)(2,1)}, u32[]{:S(2)}) copy-start(bf16[64,4096]{1,0:T(8,128)(2,1)} %refs_0_.3) | copy-start | bytes 1572868
  6.5 13.9 %collective-permute-start = (bf16[64,4096]{1,0:T(8,128)(2,1)}, bf16[64,4096]{1,0:T(8,128)(2,1)S(1)}, u32[]{:S(2)}, u32[]{:S(2)}) collective-permute-start(bf16[64,4096]{1,0:T(8,128)(2,1)} %refs_0_.3), channel_id=1, source_target_pairs={{0,16},{16,0},{1,17},{17,1},{2,18},{18,2},{3,19},{19,3},{4,20},{20... | collective-permute-start | bytes 1572872 | tf_op jit(solution)/shard_map/ppermute | solution.py:307
  7.8 13.8 %collective-permute-start.1 = (bf16[64,4096]{1,0:T(8,128)(2,1)}, bf16[64,4096]{1,0:T(8,128)(2,1)S(1)}, u32[]{:S(2)}, u32[]{:S(2)}) collective-permute-start(bf16[64,4096]{1,0:T(8,128)(2,1)} %refs_0_.3), channel_id=1, source_target_pairs={{0,32},{32,0},{1,33},{33,1},{2,34},{34,2},{3,35},{35,3},{4,36},{36... | collective-permute-start | bytes 1572872 | tf_op jit(solution)/shard_map/ppermute | solution.py:307
  9.7 0.7 copy-start.13
  10.4 19.7 %copy-start.14 = (s32[4]{0:T(128)S(1)}, s32[4]{0:T(128)}, u32[]{:S(2)}) copy-start(s32[4]{0:T(128)} %words.5) | copy-start | bytes 52
  20.4 15.9 %copy-start.2 = (bf16[64,4096]{1,0:T(8,128)(2,1)}, bf16[64,4096]{1,0:T(8,128)(2,1)S(1)}, u32[]{:S(2)}) copy-start(bf16[64,4096]{1,0:T(8,128)(2,1)S(1)} %collective-permute-done.refs_1_) | copy-start | bytes 1572868
  21.6 14.7 %copy-start.3 = (bf16[64,4096]{1,0:T(8,128)(2,1)}, bf16[64,4096]{1,0:T(8,128)(2,1)S(1)}, u32[]{:S(2)}) copy-start(bf16[64,4096]{1,0:T(8,128)(2,1)S(1)} %collective-permute-done.1.refs_2_) | copy-start | bytes 1572868
  21.6 7.2 %collective-permute-start.2 = (bf16[32,4096]{1,0:T(8,128)(2,1)S(1)}, bf16[32,4096]{1,0:T(8,128)(2,1)S(1)}, u32[]{:S(2)}, u32[]{:S(2)}) collective-permute-start(bf16[32,4096]{1,0:T(8,128)(2,1)S(1)} %slice.6), channel_id=1, source_target_pairs={{0,32},{32,0},{1,33},{33,1},{2,34},{34,2},{3,35},{35,3},{4,36},{36... | collective-permute-start | bytes 786440 | tf_op jit(solution)/shard_map/ppermute | solution.py:307
  23.5 6.7 %collective-permute-start.3 = (bf16[32,4096]{1,0:T(8,128)(2,1)S(1)}, bf16[32,4096]{1,0:T(8,128)(2,1)S(1)}, u32[]{:S(2)}, u32[]{:S(2)}) collective-permute-start(bf16[32,4096]{1,0:T(8,128)(2,1)S(1)} %slice.7), channel_id=1, source_target_pairs={{0,16},{16,0},{1,17},{17,1},{2,18},{18,2},{3,19},{19,3},{4,20},{20... | collective-permute-start | bytes 786440 | tf_op jit(solution)/shard_map/ppermute | solution.py:307
  24.3 11.9 %collective-permute-start.4 = (bf16[64,4096]{1,0:T(8,128)(2,1)S(1)}, bf16[64,4096]{1,0:T(8,128)(2,1)S(1)}, u32[]{:S(2)}, u32[]{:S(2)}) collective-permute-start(bf16[64,4096]{1,0:T(8,128)(2,1)S(1)} %copy-done.5), channel_id=1, source_target_pairs={{0,1},{1,0},{2,3},{3,2},{4,5},{5,4},{6,7},{7,6},{8,9},{9,8},{10,11... | collective-permute-start | bytes 1572872 | tf_op jit(solution)/shard_map/ppermute | solution.py:307
  24.3 12.0 %collective-permute-start.5 = (bf16[64,4096]{1,0:T(8,128)(2,1)S(1)}, bf16[64,4096]{1,0:T(8,128)(2,1)S(1)}, u32[]{:S(2)}, u32[]{:S(2)}) collective-permute-start(bf16[64,4096]{1,0:T(8,128)(2,1)S(1)} %collective-permute-done.refs_1_), channel_id=1, source_target_pairs={{0,1},{1,0},{2,3},{3,2},{4,5},{5,4},{6,7},{7,6},{8,9},{9,8},{10,11... | collective-permute-start | bytes 1572872 | tf_op jit(solution)/shard_map/ppermute | solution.py:307
  24.8 11.5 %collective-permute-start.6 = (bf16[64,4096]{1,0:T(8,128)(2,1)S(1)}, bf16[64,4096]{1,0:T(8,128)(2,1)S(1)}, u32[]{:S(2)}, u32[]{:S(2)}) collective-permute-start(bf16[64,4096]{1,0:T(8,128)(2,1)S(1)} %collective-permute-done.1.refs_2_), channel_id=1, source_target_pairs={{0,1},{1,0},{2,3},{3,2},{4,5},{5,4},{6,7},{7,6},{8,9},{9,8},{10,11... | collective-permute-start | bytes 1572872 | tf_op jit(solution)/shard_map/ppermute | solution.py:307
  28.8 7.5 %copy-start.9 = (bf16[32,4096]{1,0:T(8,128)(2,1)}, bf16[32,4096]{1,0:T(8,128)(2,1)S(1)}, u32[]{:S(2)}) copy-start(bf16[32,4096]{1,0:T(8,128)(2,1)S(1)} %collective-permute-done.2.refs_3_) | copy-start | bytes 786436
  28.8 7.4 %collective-permute-start.7 = (bf16[32,4096]{1,0:T(8,128)(2,1)S(1)}, bf16[32,4096]{1,0:T(8,128)(2,1)S(1)}, u32[]{:S(2)}, u32[]{:S(2)}) collective-permute-start(bf16[32,4096]{1,0:T(8,128)(2,1)S(1)} %collective-permute-done.2.refs_3_), channel_id=1, source_target_pairs={{0,1},{1,0},{2,3},{3,2},{4,5},{5,4},{6,7},{7,6},{8,9},{9,8},{10,11... | collective-permute-start | bytes 786440 | tf_op jit(solution)/shard_map/ppermute | solution.py:307
  30.1 6.2 %copy-start.10 = (bf16[32,4096]{1,0:T(8,128)(2,1)}, bf16[32,4096]{1,0:T(8,128)(2,1)S(1)}, u32[]{:S(2)}) copy-start(bf16[32,4096]{1,0:T(8,128)(2,1)S(1)} %collective-permute-done.3.refs_4_) | copy-start | bytes 786436
  30.1 6.1 %collective-permute-start.8 = (bf16[32,4096]{1,0:T(8,128)(2,1)S(1)}, bf16[32,4096]{1,0:T(8,128)(2,1)S(1)}, u32[]{:S(2)}, u32[]{:S(2)}) collective-permute-start(bf16[32,4096]{1,0:T(8,128)(2,1)S(1)} %collective-permute-done.3.refs_4_), channel_id=1, source_target_pairs={{0,1},{1,0},{2,3},{3,2},{4,5},{5,4},{6,7},{7,6},{8,9},{9,8},{10,11... | collective-permute-start | bytes 786440 | tf_op jit(solution)/shard_map/ppermute | solution.py:307
  36.2 7.9 %copy-start.6 = (bf16[64,4096]{1,0:T(8,128)(2,1)}, bf16[64,4096]{1,0:T(8,128)(2,1)S(1)}, u32[]{:S(2)}) copy-start(bf16[64,4096]{1,0:T(8,128)(2,1)S(1)} %collective-permute-done.4.refs_5_) | copy-start | bytes 1572868
  36.3 7.8 %copy-start.7 = (bf16[64,4096]{1,0:T(8,128)(2,1)}, bf16[64,4096]{1,0:T(8,128)(2,1)S(1)}, u32[]{:S(2)}) copy-start(bf16[64,4096]{1,0:T(8,128)(2,1)S(1)} %collective-permute-done.5.refs_6_) | copy-start | bytes 1572868
  36.3 7.8 %copy-start.8 = (bf16[64,4096]{1,0:T(8,128)(2,1)}, bf16[64,4096]{1,0:T(8,128)(2,1)S(1)}, u32[]{:S(2)}) copy-start(bf16[64,4096]{1,0:T(8,128)(2,1)S(1)} %collective-permute-done.6.refs_7_) | copy-start | bytes 1572868
  44.1 0.7 copy-start.11
  44.9 0.8 copy-start.12
  45.6 26.4 %all-to-all-start = ((f32[8,256,128]{2,1,0:T(8,128)}), f32[8,256,128]{2,1,0:T(8,128)S(1)}, u32[]{:S(2)}, u32[]{:S(2)}) async-start(f32[8,256,128]{2,1,0:T(8,128)} %shard_map.40), calls=%async_computation | async-start | bytes 2097152 | tf_op jit(solution)/shard_map/all_to_all | solution.py:349
  52.8 111.3 %collective-permute-start.29 = (bf16[1024,1024]{1,0:T(8,128)(2,1)}, bf16[1024,1024]{1,0:T(8,128)(2,1)}, u32[]{:S(2)}, u32[]{:S(2)}) collective-permute-start(bf16[1024,1024]{1,0:T(8,128)(2,1)} %refs_16_.1), channel_id=1, source_target_pairs={{0,1},{1,0},{2,3},{3,2},{4,5},{5,4},{6,7},{7,6},{8,9},{9,8},{10,11... | collective-permute-start | bytes 6291464 | tf_op jit(solution)/shard_map/ppermute | solution.py:307
  72.0 48.9 %all-to-all-start.1 = ((f32[8,256,128]{2,1,0:T(8,128)}), f32[8,256,128]{2,1,0:T(8,128)S(1)}, u32[]{:S(2)}, u32[]{:S(2)}) async-start(f32[8,256,128]{2,1,0:T(8,128)} %shard_map.38), calls=%async_computation.1 | async-start | bytes 2097152 | tf_op jit(solution)/shard_map/all_to_all | solution.py:352
  79.2 129.2 %all-gather.3.cloned.1.call-start = ((), (), s32[]{:S(2)}) async-start(), calls=%async_computation.4 | async-start | bytes 1179648 | tf_op jit(solution)/shard_map/all_gather | solution.py:368
  79.3 1.3 collective-permute-start.9
  79.4 13.6 %collective-permute-start.10 = (bf16[128,128]{1,0:T(8,128)(2,1)S(1)}, bf16[128,128]{1,0:T(8,128)(2,1)S(1)}, u32[]{:S(2)}, u32[]{:S(2)}) collective-permute-start(bf16[128,128]{1,0:T(8,128)(2,1)S(1)} %get-tuple-element.32), channel_id=1, source_target_pairs={{0,16},{16,0},{1,17},{17,1},{2,18},{18,2},{3,19},{19,3},{4,20},{20... | collective-permute-start | bytes 98312 | tf_op jit(solution)/shard_map/ppermute | solution.py:307
  80.6 13.0 %collective-permute-start.11 = (bf16[128,128]{1,0:T(8,128)(2,1)S(1)}, bf16[128,128]{1,0:T(8,128)(2,1)S(1)}, u32[]{:S(2)}, u32[]{:S(2)}) collective-permute-start(bf16[128,128]{1,0:T(8,128)(2,1)S(1)} %collective-permute-done.9), channel_id=1, source_target_pairs={{0,16},{16,0},{1,17},{17,1},{2,18},{18,2},{3,19},{19,3},{4,20},{20... | collective-permute-start | bytes 98312 | tf_op jit(solution)/shard_map/ppermute | solution.py:307
  93.6 8.7 %collective-permute-start.12 = (bf16[4,128,128]{2,1,0:T(8,128)(2,1)S(1)}, bf16[4,128,128]{2,1,0:T(8,128)(2,1)S(1)}, u32[]{:S(2)}, u32[]{:S(2)}) collective-permute-start(bf16[4,128,128]{2,1,0:T(8,128)(2,1)S(1)} %pad_maximum_fusion.refs_0_), channel_id=1, source_target_pairs={{0,32},{32,64},{64,96},{96,128},{128,160},{160,192},{192,224},{224... | collective-permute-start | bytes 393224 | tf_op jit(solution)/shard_map/ppermute | solution.py:314
  94.3 8.1 %collective-permute-start.16 = (bf16[4,128,128]{2,1,0:T(8,128)(2,1)S(1)}, bf16[4,128,128]{2,1,0:T(8,128)(2,1)S(1)}, u32[]{:S(2)}, u32[]{:S(2)}) collective-permute-start(bf16[4,128,128]{2,1,0:T(8,128)(2,1)S(1)} %pad_maximum_fusion.refs_0_), channel_id=1, source_target_pairs={{0,224},{32,0},{64,32},{96,64},{128,96},{160,128},{192,160},{224,1... | collective-permute-start | bytes 393224 | tf_op jit(solution)/shard_map/ppermute | solution.py:317
  102.4 6.2 %collective-permute-start.13 = (bf16[4,128,128]{2,1,0:T(8,128)(2,1)S(1)}, bf16[4,128,128]{2,1,0:T(8,128)(2,1)S(1)}, u32[]{:S(2)}, u32[]{:S(2)}) collective-permute-start(bf16[4,128,128]{2,1,0:T(8,128)(2,1)S(1)} %collective-permute-done.12.refs_1_), channel_id=1, source_target_pairs={{0,32},{32,64},{64,96},{96,128},{128,160},{160,192},{192,224},{224... | collective-permute-start | bytes 393224 | tf_op jit(solution)/shard_map/ppermute | solution.py:314
  102.4 6.2 %collective-permute-start.17 = (bf16[4,128,128]{2,1,0:T(8,128)(2,1)S(1)}, bf16[4,128,128]{2,1,0:T(8,128)(2,1)S(1)}, u32[]{:S(2)}, u32[]{:S(2)}) collective-permute-start(bf16[4,128,128]{2,1,0:T(8,128)(2,1)S(1)} %collective-permute-done.16.refs_5_), channel_id=1, source_target_pairs={{0,224},{32,0},{64,32},{96,64},{128,96},{160,128},{192,160},{224,1... | collective-permute-start | bytes 393224 | tf_op jit(solution)/shard_map/ppermute | solution.py:317
  108.5 6.2 %collective-permute-start.14 = (bf16[4,128,128]{2,1,0:T(8,128)(2,1)S(1)}, bf16[4,128,128]{2,1,0:T(8,128)(2,1)S(1)}, u32[]{:S(2)}, u32[]{:S(2)}) collective-permute-start(bf16[4,128,128]{2,1,0:T(8,128)(2,1)S(1)} %collective-permute-done.13.refs_2_), channel_id=1, source_target_pairs={{0,32},{32,64},{64,96},{96,128},{128,160},{160,192},{192,224},{224... | collective-permute-start | bytes 393224 | tf_op jit(solution)/shard_map/ppermute | solution.py:314
  108.5 6.2 %collective-permute-start.18 = (bf16[4,128,128]{2,1,0:T(8,128)(2,1)S(1)}, bf16[4,128,128]{2,1,0:T(8,128)(2,1)S(1)}, u32[]{:S(2)}, u32[]{:S(2)}) collective-permute-start(bf16[4,128,128]{2,1,0:T(8,128)(2,1)S(1)} %collective-permute-done.17.refs_6_), channel_id=1, source_target_pairs={{0,224},{32,0},{64,32},{96,64},{128,96},{160,128},{192,160},{224,1... | collective-permute-start | bytes 393224 | tf_op jit(solution)/shard_map/ppermute | solution.py:317
  114.7 6.2 %collective-permute-start.15 = (bf16[4,128,128]{2,1,0:T(8,128)(2,1)S(1)}, bf16[4,128,128]{2,1,0:T(8,128)(2,1)S(1)}, u32[]{:S(2)}, u32[]{:S(2)}) collective-permute-start(bf16[4,128,128]{2,1,0:T(8,128)(2,1)S(1)} %collective-permute-done.14.refs_3_), channel_id=1, source_target_pairs={{0,32},{32,64},{64,96},{96,128},{128,160},{160,192},{192,224},{224... | collective-permute-start | bytes 393224 | tf_op jit(solution)/shard_map/ppermute | solution.py:314
  121.0 1.5 collective-permute-start.19
  121.1 4.0 %collective-permute-start.20 = (bf16[128,128]{1,0:T(8,128)(2,1)S(1)}, bf16[128,128]{1,0:T(8,128)(2,1)S(1)}, u32[]{:S(2)}, u32[]{:S(2)}) collective-permute-start(bf16[128,128]{1,0:T(8,128)(2,1)S(1)} %get-tuple-element.45), channel_id=1, source_target_pairs={{0,16},{16,0},{1,17},{17,1},{2,18},{18,2},{3,19},{19,3},{4,20},{20... | collective-permute-start | bytes 98312 | tf_op jit(solution)/shard_map/ppermute | solution.py:307
  122.5 3.9 %collective-permute-start.21 = (bf16[128,128]{1,0:T(8,128)(2,1)S(1)}, bf16[128,128]{1,0:T(8,128)(2,1)S(1)}, u32[]{:S(2)}, u32[]{:S(2)}) collective-permute-start(bf16[128,128]{1,0:T(8,128)(2,1)S(1)} %collective-permute-done.19), channel_id=1, source_target_pairs={{0,16},{16,0},{1,17},{17,1},{2,18},{18,2},{3,19},{19,3},{4,20},{20... | collective-permute-start | bytes 98312 | tf_op jit(solution)/shard_map/ppermute | solution.py:307
  126.4 17.9 %collective-permute-start.30 = (bf16[256,256]{1,0:T(8,128)(2,1)S(1)}, bf16[256,256]{1,0:T(8,128)(2,1)S(1)}, u32[]{:S(2)}, u32[]{:S(2)}) collective-permute-start(bf16[256,256]{1,0:T(8,128)(2,1)S(1)} %get-tuple-element.48), channel_id=1, source_target_pairs={{0,0},{1,1},{2,32},{3,33},{4,64},{5,65},{6,96},{7,97},{8,128},{9,1... | collective-permute-start | bytes 393224 | tf_op jit(solution)/shard_map/ppermute | solution.py:367
  144.3 0.7 copy-start.15
  145.0 6.7 %collective-permute-start.22 = (bf16[4,128,128]{2,1,0:T(8,128)(2,1)S(1)}, bf16[4,128,128]{2,1,0:T(8,128)(2,1)S(1)}, u32[]{:S(2)}, u32[]{:S(2)}) collective-permute-start(bf16[4,128,128]{2,1,0:T(8,128)(2,1)S(1)} %pad_maximum_fusion.1.refs_8_), channel_id=1, source_target_pairs={{0,32},{32,64},{64,96},{96,128},{128,160},{160,192},{192,224},{224... | collective-permute-start | bytes 393224 | tf_op jit(solution)/shard_map/ppermute | solution.py:314
  145.1 6.6 %collective-permute-start.26 = (bf16[4,128,128]{2,1,0:T(8,128)(2,1)S(1)}, bf16[4,128,128]{2,1,0:T(8,128)(2,1)S(1)}, u32[]{:S(2)}, u32[]{:S(2)}) collective-permute-start(bf16[4,128,128]{2,1,0:T(8,128)(2,1)S(1)} %pad_maximum_fusion.1.refs_8_), channel_id=1, source_target_pairs={{0,224},{32,0},{64,32},{96,64},{128,96},{160,128},{192,160},{224,1... | collective-permute-start | bytes 393224 | tf_op jit(solution)/shard_map/ppermute | solution.py:317
  151.7 6.2 %collective-permute-start.23 = (bf16[4,128,128]{2,1,0:T(8,128)(2,1)S(1)}, bf16[4,128,128]{2,1,0:T(8,128)(2,1)S(1)}, u32[]{:S(2)}, u32[]{:S(2)}) collective-permute-start(bf16[4,128,128]{2,1,0:T(8,128)(2,1)S(1)} %collective-permute-done.22.refs_9_), channel_id=1, source_target_pairs={{0,32},{32,64},{64,96},{96,128},{128,160},{160,192},{192,224},{224... | collective-permute-start | bytes 393224 | tf_op jit(solution)/shard_map/ppermute | solution.py:314
  151.7 6.2 %collective-permute-start.27 = (bf16[4,128,128]{2,1,0:T(8,128)(2,1)S(1)}, bf16[4,128,128]{2,1,0:T(8,128)(2,1)S(1)}, u32[]{:S(2)}, u32[]{:S(2)}) collective-permute-start(bf16[4,128,128]{2,1,0:T(8,128)(2,1)S(1)} %collective-permute-done.26.refs_13_), channel_id=1, source_target_pairs={{0,224},{32,0},{64,32},{96,64},{128,96},{160,128},{192,160},{224,1... | collective-permute-start | bytes 393224 | tf_op jit(solution)/shard_map/ppermute | solution.py:317
  157.9 6.2 %collective-permute-start.24 = (bf16[4,128,128]{2,1,0:T(8,128)(2,1)S(1)}, bf16[4,128,128]{2,1,0:T(8,128)(2,1)S(1)}, u32[]{:S(2)}, u32[]{:S(2)}) collective-permute-start(bf16[4,128,128]{2,1,0:T(8,128)(2,1)S(1)} %collective-permute-done.23.refs_10_), channel_id=1, source_target_pairs={{0,32},{32,64},{64,96},{96,128},{128,160},{160,192},{192,224},{224... | collective-permute-start | bytes 393224 | tf_op jit(solution)/shard_map/ppermute | solution.py:314
  157.9 6.2 %collective-permute-start.28 = (bf16[4,128,128]{2,1,0:T(8,128)(2,1)S(1)}, bf16[4,128,128]{2,1,0:T(8,128)(2,1)S(1)}, u32[]{:S(2)}, u32[]{:S(2)}) collective-permute-start(bf16[4,128,128]{2,1,0:T(8,128)(2,1)S(1)} %collective-permute-done.27.refs_14_), channel_id=1, source_target_pairs={{0,224},{32,0},{64,32},{96,64},{128,96},{160,128},{192,160},{224,1... | collective-permute-start | bytes 393224 | tf_op jit(solution)/shard_map/ppermute | solution.py:317
  164.1 6.2 %collective-permute-start.25 = (bf16[4,128,128]{2,1,0:T(8,128)(2,1)S(1)}, bf16[4,128,128]{2,1,0:T(8,128)(2,1)S(1)}, u32[]{:S(2)}, u32[]{:S(2)}) collective-permute-start(bf16[4,128,128]{2,1,0:T(8,128)(2,1)S(1)} %collective-permute-done.24.refs_11_), channel_id=1, source_target_pairs={{0,32},{32,64},{64,96},{96,128},{128,160},{160,192},{192,224},{224... | collective-permute-start | bytes 393224 | tf_op jit(solution)/shard_map/ppermute | solution.py:314
  170.2 1.6 copy-start.1
  177.4 1.3 copy-start
  178.7 29.8 %all-to-all-start.2 = ((f32[8,64,1024]{2,1,0:T(8,128)}), f32[8,64,1024]{2,1,0:T(8,128)S(1)}, u32[]{:S(2)}, u32[]{:S(2)}) async-start(f32[8,64,1024]{2,1,0:T(8,128)} %bitcast.10), calls=%async_computation.2 | async-start | bytes 4194304 | tf_op jit(solution)/shard_map/all_to_all | solution.py:372
  208.4 2.9 %collective-permute-start.31 = (bf16[8,256,256]{2,1,0:T(8,128)(2,1)}, bf16[8,256,256]{2,1,0:T(8,128)(2,1)S(1)}, u32[]{:S(2)}, u32[]{:S(2)}) collective-permute-start(bf16[8,256,256]{2,1,0:T(8,128)(2,1)} %bitcast.11), channel_id=1, source_target_pairs={{0,1},{1,0},{2,3},{3,2},{4,5},{5,4},{6,7},{7,6},{8,9},{9,8},{10,11... | collective-permute-start | bytes 3145736 | tf_op jit(solution)/shard_map/ppermute | solution.py:307
  211.3 1.2 copy-start.4
Sparse Core Ops, SparseCore 0:
  145.1 63.2 all-gather.2

commit v5 on v4

--- a/solution.py
+++ b/solution.py
@@ -205,7 +205,7 @@
 
 
 def condition_kernel(*refs):
-    runs, (mine, other), (out, pieces, tiles, arrived) = (refs[:8], refs[8:16]), refs[16:18], refs[18:]
+    low, high, (mine, other), (out, pieces, tiles, arrived) = refs[0], refs[1:9], refs[9:11], refs[11:]
     core = lax.axis_index("c")
     yl = lax.axis_index("yl")
     z = lax.axis_index("zh") * 2 + lax.axis_index("zl")
@@ -214,10 +214,10 @@
         pltpu.make_async_copy(other, tiles.at[1 - core], arrived.at[17]),
     ]
     copies = []
-    for index in range(8):
-        for run in range(2):
+    for index, away in enumerate(RING):
+        for run, source in enumerate((low.at[(z + (away + 8)) & 7], high[index])):
             target = pieces.at[index, :, :, run * 128 : (run + 1) * 128]
-            copies.append(pltpu.make_async_copy(runs[run][index], target, arrived.at[index * 2 + run]))
+            copies.append(pltpu.make_async_copy(source, target, arrived.at[index * 2 + run]))
     for copy in first + copies:
         copy.start()
     out[...] = jnp.zeros_like(out)
@@ -237,20 +237,20 @@
 
 
 def condition(low, high, mine, other):
-    flips, rows, width = low[0].shape
+    _, flips, rows, width = low.shape
     return pl.pallas_call(
         condition_kernel,
         out_shape=jax.ShapeDtypeStruct((4 * rows, mine.shape[1]), F32),
-        in_specs=[pl.BlockSpec(memory_space=pltpu.HBM)] * 18,
+        in_specs=[pl.BlockSpec(memory_space=pltpu.HBM)] * 11,
         out_specs=pl.BlockSpec(memory_space=pltpu.VMEM),
         scratch_shapes=[
             pltpu.VMEM((8, flips, rows, 2 * width), BF16),
             pltpu.VMEM((2,) + mine.shape, BF16),
             pltpu.SemaphoreType.DMA((18,)),
         ],
-        compiler_params=pltpu.CompilerParams(vmem_limit_bytes=24 << 20),
+        compiler_params=pltpu.CompilerParams(vmem_limit_bytes=60 << 20),
         cost_estimate=pl.CostEstimate(flops=2 * 512 * 2048 * 1024, bytes_accessed=7 << 20, transcendentals=0),
-    )(*low, *high, mine, other)
+    )(low, *high, mine, other)
 
 
 def pair_kernel(parts, near, far, out, rows, pairs):
@@ -259,19 +259,22 @@
     for index in range(1, parts.shape[0]):
         total += parts[index]
     rows[...] = total.astype(BF16)
-    for zh in range(4):
-        value = None
-        for zl in range(2):
-            for flip in range(2):
-                start = pl.multiple_of((zl * 2 + (core ^ flip)) * 256, 256)
-                term = lax.dot_general(
-                    rows[:, pl.ds(start, 256)],
-                    (near, far)[flip][zh * 2 + zl],
-                    (((1,), (1,)), ((), ())),
-                    preferred_element_type=F32,
-                )
-                value = term if value is None else value + term
-        pairs[:, zh * 256 : (zh + 1) * 256] = value
+    yh = lax.axis_index("yh")
+    for flip_yh in range(2):
+        for pair_x in range(2):
+            value = None
+            for zl in range(2):
+                for flip in range(2):
+                    start = pl.multiple_of((zl * 2 + (core ^ flip)) * 256, 256)
+                    term = lax.dot_general(
+                        rows[:, pl.ds(start, 256)],
+                        (near, far)[flip][pair_x * 2 + zl, flip_yh],
+                        (((1,), (1,)), ((), ())),
+                        preferred_element_type=F32,
+                    )
+                    value = term if value is None else value + term
+            zh = (yh ^ flip_yh) * 2 + pair_x
+            pairs[:, pl.ds(pl.multiple_of(zh * 256, 256), 256)] = value
     for block in range(16):
         piece = pairs[:, block * 64 : (block + 1) * 64]
         out[block, :, :64] = piece[:32]
@@ -307,16 +310,23 @@
     return lax.ppermute(value, axis, [(0, 1), (1, 0)])
 
 
-def ring(value):
-    up, down = [], []
-    ahead = behind = value
-    for step in range(4):
-        ahead = lax.ppermute(ahead, ("zh", "zl"), [(i, (i + 1) % 8) for i in range(8)])
-        up.append(ahead)
-        if step < 3:
-            behind = lax.ppermute(behind, ("zh", "zl"), [(i, (i + 7) % 8) for i in range(8)])
-            down.append(behind)
-    return [value] + up + down
+def step_z(value, by):
+    return lax.ppermute(value, ("zh", "zl"), [(i, (i + by) % 8) for i in range(8)])
+
+
+def ring_and_turn(value, piece, route):
+    turned = lax.ppermute(piece, EX + PAR, route)
+    up = [step_z(value, 1)]
+    down = [step_z(value, 7)]
+    up.append(step_z(up[0], 1))
+    down.append(step_z(down[0], 7))
+    turned, up[1], down[1] = lax.optimization_barrier((turned, up[1], down[1]))
+    flipped = swap(turned, "yh")
+    up.append(step_z(up[1], 1))
+    down.append(step_z(down[1], 7))
+    flipped, up[2], down[2] = lax.optimization_barrier((flipped, up[2], down[2]))
+    up.append(step_z(up[2], 1))
+    return [value] + up + down, jnp.stack([turned, flipped])
 
 
 def flips(keep, send):
@@ -351,21 +361,21 @@
     partial, part = lax.optimization_barrier((partial, part))
     next_part = lax.all_to_all(partial, CHIPS, 0, 0, tiled=True)
 
-    whole, keep, send = sum_parts(part)
-    low = ring(flips(keep, send))
-    next_part, low = lax.optimization_barrier((next_part, low))
-    whole, keep, send = sum_parts(next_part, whole)
-    whole, mine = lax.optimization_barrier((whole, flips(keep, send)))
-    high = ring(mine)
-
     route = []
     for z in range(8):
         for yl in range(2):
             for chip in range(8):
                 for c in range(2):
                     route.append((((z * 2 + yl) * 8 + chip) * 2 + c, ((chip * 2 + yl) * 8 + z) * 2 + c))
-    turned = lax.ppermute(whole, EX + PAR, route)
-    near = lax.all_gather(turned, CHIPS, axis=0)
+    whole, keep, send = sum_parts(part)
+    mine = flips(keep, send)
+    low = lax.all_gather(mine, ("zh", "zl"), axis=0)
+    next_part, mine = lax.optimization_barrier((next_part, mine))
+    whole, keep, send = sum_parts(next_part, whole)
+    whole, mine = lax.optimization_barrier((whole, flips(keep, send)))
+    high, turned = ring_and_turn(mine, whole, route)
+    turned, low = lax.optimization_barrier((turned, low))
+    near = lax.all_gather(turned, "x", axis=0)
     far = swap(near, "c")
 
     conditioned = condition(low, high, inverse_gram, other_tile)

time: 250 us -> 223 us (0.89)
  waiting for transfers between devices: 94.9 us -> 72.5 us
  blocking collectives: 25.4 us -> 20.8 us
    ppermute x15 -> x8, waiting for transfers between devices: 47.1 us -> 13.5 us  [the longest x1 9.51 us: ring_and_turn(): turned = lax.ppermute(piece, EX + PAR, route)]
    all_to_all x1, waiting for transfers between devices: 0.01 us -> 12.1 us  [per_device(): next_part = lax.all_to_all(partial, CHIPS, 0, 0, tiled=True)]
    all_to_all x1, waiting for transfers between devices: 0.04 us -> 11.7 us  [per_device(): lax.all_to_all(conditioned.reshape(8, 64, 1024), CHIPS, 0, 0, tiled=True)]
    ppermute x17 -> x18, waiting for transfers between devices: 24.9 us -> 16.6 us  [swap(): return lax.ppermute(value, axis, [(0, 1), (1, 0)])]
    all_to_all x1, blocking collectives: 25.4 us -> 20.8 us  [per_device(): return finish(lax.all_to_all(pair(parts, near, far), EX, 0, 0, tiled=True))]
    all_gather x1 -> x2, waiting for transfers between devices: 22.8 us -> 18.5 us  [the longest x1 18.5 us: per_device(): near = lax.all_gather(turned, 'x', axis=0)]
    unnamed x32 -> x42, local copies, waits for them, and re-layouts: 6.98 us -> 5.58 us
    ppermute x15 -> x8, starting transfers between devices: 23.3 us -> 22 us  [the longest x7 14.5 us: step_z(): lax.ppermute(value, ('zh', 'zl'), [(i, (i + by) % 8) for i in range(8)])]
  transfers between devices with their start and end apart: 36 -> 31, of which waited for: 20 -> 16; matrix products, arithmetic and copies ran while one was open for 0% -> 0% of each run, Pallas kernels for 16% -> 19%
where the time goes in v5:
time: 223 us; the launch traced here: 221 us
  waiting for transfers between devices  72.5 us (33%)
  starting transfers between devices  54.3 us (24%)
  Pallas kernels  52.9 us (24%)
  blocking collectives  20.8 us (9%)
  between operations  13.7 us (6%)
  local copies, waits for them, and re-layouts  5.62 us (3%)
    pallas_call x2, Pallas kernels, project(): pl.pallas_call(kernel, out_shape=jax.ShapeDtypeStruct((8, rows, width), F...  27 us
    all_to_all x1, blocking collectives, per_device(): return finish(lax.all_to_all(pair(parts, near, far), EX, 0, 0, tiled=True))  20.8 us
    all_gather x1, waiting for transfers between devices, per_device(): near = lax.all_gather(turned, 'x', axis=0)  18.5 us
    ppermute x18, waiting for transfers between devices, swap(): return lax.ppermute(value, axis, [(0, 1), (1, 0)])  16.6 us
    pallas_call x2, Pallas kernels, table(): pl.pallas_call(functools.partial(table_kernel, part, width, first, params...  15.8 us
    ppermute x7, starting transfers between devices, step_z(): lax.ppermute(value, ('zh', 'zl'), [(i, (i + by) % 8) for i in range(8)])  14.5 us
    all_to_all x1, waiting for transfers between devices, per_device(): next_part = lax.all_to_all(partial, CHIPS, 0, 0, tiled=True)  12.1 us
    all_to_all x1, waiting for transfers between devices, per_device(): lax.all_to_all(conditioned.reshape(8, 64, 1024), CHIPS, 0, 0, tiled=True)  11.7 us
  transfers between devices with their start and end apart: 31, of which 16 were waited for; matrix products, arithmetic and copies ran while one was open for 0% of the time, Pallas kernels for 19%

profile of v5, /device:TPU:22, one launch (start us, length us, event | category | flops | bytes accessed | tf_op | source)
XLA Modules:
  0.0 221.4 jit_solution(9281670948015882629)
XLA Ops:
  6.5 1.3 collective-permute-start
  7.8 1.9 collective-permute-start.1
  9.7 0.7 copy-done.11
  10.4 9.7 %shard_map.37.first = bf16[5120,1024]{1,0:T(8,128)(2,1)S(1)} custom-call(s32[4]{0:T(128)S(1)} %copy-done.11), custom_call_target="tpu_custom_call" | custom-call | flops 6291456000 | bytes 10485760 | tf_op jit(solution)/shard_map/pallas_call | solution.py:68
  20.1 0.3 collective-permute-done.refs_1_
  20.4 1.2 collective-permute-done.1.refs_2_
  21.6 1.8 collective-permute-start.2
  23.5 0.8 collective-permute-start.3
  24.3 0.5 collective-permute-start.5
  24.8 0.0 collective-permute-start.6
  24.8 4.0 %collective-permute-done.2.refs_3_ = bf16[32,4096]{1,0:T(8,128)(2,1)S(1)} collective-permute-done((bf16[32,4096]{1,0:T(8,128)(2,1)S(1)}, bf16[32,4096]{1,0:T(8,128)(2,1)S(1)}, u32[]{:S(2)}, u32[]{:S(2)}) %collective-permute-start.2) | collective-permute-done | bytes 262176 | tf_op jit(solution)/shard_map/ppermute | solution.py:310
  28.8 0.0 collective-permute-start.7
  28.8 1.3 collective-permute-done.3.refs_4_
  30.1 6.1 %shard_map.39.second = bf16[3072,1024]{1,0:T(8,128)(2,1)S(1)} custom-call(s32[4]{0:T(128)S(1)} %copy-done.11), custom_call_target="tpu_custom_call" | custom-call | flops 3774873600 | bytes 6291456 | tf_op jit(solution)/shard_map/pallas_call | solution.py:68
  36.3 7.8 %shard_map.40 = f32[8,256,128]{2,1,0:T(8,128)} custom-call(bf16[5120,1024]{1,0:T(8,128)(2,1)S(1)} %shard_map.37.first, bf16[3072,1024]{1,0:T(8,128)(2,1)S(1)} %shard_map.39.second, bf16[64,4096]{1,0:T(8,128)(2,1)S(1)} %copy-done.3, bf16[64,4096]{1,0:T(8,128)(2,1)S(1)} %collective-permute-done.refs_1_, bf16[64,4096]{1,0:T(8,128)(2,1)S(1)} %collective-permute-done.1.refs_2_, ...), custom_call_target="tpu_custom_call" | custom-call | flops 4294967296 | bytes 16777216 | tf_op jit(solution)/shard_map/pallas_call | solution.py:158
  44.1 0.8 copy-done.5
  44.9 0.8 copy-done.6
  45.7 0.7 copy-done.9
  46.4 0.7 copy-done.10
  47.1 7.2 %all-to-all-start = ((f32[8,256,128]{2,1,0:T(8,128)}), f32[8,256,128]{2,1,0:T(8,128)S(1)}, u32[]{:S(2)}, u32[]{:S(2)}) async-start(f32[8,256,128]{2,1,0:T(8,128)} %shard_map.40), calls=%async_computation | async-start | bytes 2097152 | tf_op jit(solution)/shard_map/all_to_all | solution.py:359
  54.3 19.2 %shard_map.38 = f32[8,256,128]{2,1,0:T(8,128)} custom-call(s32[4]{0:T(128)} %words.5, bf16[64,4096]{1,0:T(8,128)(2,1)} %refs_0_.3, bf16[64,4096]{1,0:T(8,128)(2,1)} %copy-done, bf16[64,4096]{1,0:T(8,128)(2,1)} %copy-done.1, bf16[32,4096]{1,0:T(8,128)(2,1)} %copy-done.7, bf16[32,4096]{1,0:T(8,128)(2,1)} %copy-done.8, bf16[64,4096]{1,0:T(8,128)(2,1)} %copy-done.4, ...), custom_call_target="tpu_custom_call" | custom-call | flops 4294967296 | bytes 16777216 | tf_op jit(solution)/shard_map/pallas_call | solution.py:158
  73.5 0.0 copy-start.12
  73.5 0.1 shard_map.41
  73.6 0.1 collective-permute-start.9
  73.7 0.8 collective-permute-start.10
  74.5 0.4 collective-permute-done.9
  74.9 0.9 collective-permute-start.11
  75.8 1.9 collective-permute-done.10
  77.7 1.1 collective-permute-done.11
  78.8 0.7 pad_maximum_fusion.1
  79.4 0.0 all-gather.5.cloned.1.call-update
  79.5 7.2 %all-to-all-start.1 = ((f32[8,256,128]{2,1,0:T(8,128)}), f32[8,256,128]{2,1,0:T(8,128)S(1)}, u32[]{:S(2)}, u32[]{:S(2)}) async-start(f32[8,256,128]{2,1,0:T(8,128)} %shard_map.38), calls=%async_computation.1 | async-start | bytes 2097152 | tf_op jit(solution)/shard_map/all_to_all | solution.py:362
  86.7 0.1 collective-permute-start.24
  86.8 12.1 %all-to-all-done.1.part = f32[8,256,128]{2,1,0:T(8,128)S(1)} async-done(((f32[8,256,128]{2,1,0:T(8,128)}), f32[8,256,128]{2,1,0:T(8,128)S(1)}, u32[]{:S(2)}, u32[]{:S(2)}) %all-to-all-start.1) | async-done | bytes 1048608 | tf_op jit(solution)/shard_map/all_to_all | solution.py:362
  98.9 0.1 shard_map.42
  99.0 0.1 collective-permute-start.12
  99.1 0.9 collective-permute-start.13
  100.1 0.2 collective-permute-done.12
  100.3 0.9 collective-permute-start.14
  101.2 1.9 collective-permute-done.13
  103.2 1.1 collective-permute-done.14
  104.3 0.8 collective-permute-start.16
  105.0 4.2 %collective-permute-start.18 = (bf16[4,128,128]{2,1,0:T(8,128)(2,1)S(1)}, bf16[4,128,128]{2,1,0:T(8,128)(2,1)S(1)}, u32[]{:S(2)}, u32[]{:S(2)}) collective-permute-start(bf16[4,128,128]{2,1,0:T(8,128)(2,1)S(1)} %pad_maximum_fusion.2.refs_1_), channel_id=1, source_target_pairs={{0,224},{32,0},{64,32},{96,64},{128,96},{160,128},{192,160},{224,1... | collective-permute-start | bytes 393224 | tf_op jit(solution)/shard_map/ppermute | solution.py:314
  109.2 7.5 %collective-permute-start.15 = (bf16[256,256]{1,0:T(8,128)(2,1)S(1)}, bf16[256,256]{1,0:T(8,128)(2,1)S(1)}, u32[]{:S(2)}, u32[]{:S(2)}) collective-permute-start(bf16[256,256]{1,0:T(8,128)(2,1)S(1)} %get-tuple-element.39), channel_id=1, source_target_pairs={{0,0},{1,1},{2,32},{3,33},{4,64},{5,65},{6,96},{7,97},{8,128},{9,1... | collective-permute-start | bytes 393224 | tf_op jit(solution)/shard_map/ppermute | solution.py:318
  116.7 1.8 collective-permute-start.17
  118.6 2.1 collective-permute-start.19
  120.7 9.5 %collective-permute-done.15 = bf16[256,256]{1,0:T(8,128)(2,1)S(1)} collective-permute-done((bf16[256,256]{1,0:T(8,128)(2,1)S(1)}, bf16[256,256]{1,0:T(8,128)(2,1)S(1)}, u32[]{:S(2)}, u32[]{:S(2)}) %collective-permute-start.15) | collective-permute-done | bytes 131104 | tf_op jit(solution)/shard_map/ppermute | solution.py:318
  130.2 0.1 collective-permute-start.20
  130.3 0.4 collective-permute-start.21
  130.7 2.9 %collective-permute-start.22 = (bf16[4,128,128]{2,1,0:T(8,128)(2,1)S(1)}, bf16[4,128,128]{2,1,0:T(8,128)(2,1)S(1)}, u32[]{:S(2)}, u32[]{:S(2)}) collective-permute-start(bf16[4,128,128]{2,1,0:T(8,128)(2,1)S(1)} %collective-permute-done.19.refs_7_), channel_id=1, source_target_pairs={{0,224},{32,0},{64,32},{96,64},{128,96},{160,128},{192,160},{224,1... | collective-permute-start | bytes 393224 | tf_op jit(solution)/shard_map/ppermute | solution.py:314
  133.7 3.2 %collective-permute-done.20 = bf16[256,256]{1,0:T(8,128)(2,1)S(1)} collective-permute-done((bf16[256,256]{1,0:T(8,128)(2,1)S(1)}, bf16[256,256]{1,0:T(8,128)(2,1)S(1)}, u32[]{:S(2)}, u32[]{:S(2)}) %collective-permute-start.20) | collective-permute-done | bytes 131104 | tf_op jit(solution)/shard_map/ppermute | solution.py:310
  136.9 0.8 pad_maximum_fusion
  137.7 0.0 all-gather.7.cloned.1.call-update
  137.7 2.3 %collective-permute-start.23 = (bf16[4,128,128]{2,1,0:T(8,128)(2,1)S(1)}, bf16[4,128,128]{2,1,0:T(8,128)(2,1)S(1)}, u32[]{:S(2)}, u32[]{:S(2)}) collective-permute-start(bf16[4,128,128]{2,1,0:T(8,128)(2,1)S(1)} %collective-permute-done.21.refs_4_), channel_id=1, source_target_pairs={{0,32},{32,64},{64,96},{96,128},{128,160},{160,192},{192,224},{224... | collective-permute-start | bytes 393224 | tf_op jit(solution)/shard_map/ppermute | solution.py:314
  140.0 4.0 %collective-permute-done.23.refs_5_ = bf16[4,128,128]{2,1,0:T(8,128)(2,1)S(1)} collective-permute-done((bf16[4,128,128]{2,1,0:T(8,128)(2,1)S(1)}, bf16[4,128,128]{2,1,0:T(8,128)(2,1)S(1)}, u32[]{:S(2)}, u32[]{:S(2)}) %collective-permute-start.23) | collective-permute-done | bytes 131104 | tf_op jit(solution)/shard_map/ppermute | solution.py:314
  144.0 0.6 copy-done.20
  144.6 7.4 %shard_map.43 = f32[512,1024]{1,0:T(8,128)} custom-call(bf16[8,4,128,128]{3,2,1,0:T(8,128)(2,1)} %bitcast.18, bf16[4,128,128]{2,1,0:T(8,128)(2,1)} %copy-done.13, bf16[4,128,128]{2,1,0:T(8,128)(2,1)} %copy-done.14, bf16[4,128,128]{2,1,0:T(8,128)(2,1)} %copy-done.16, bf16[4,128,128]{2,1,0:T(8,128)(2,1)} %copy-done.18, bf16[4,128,128]{2,1,0:T(8,128)(2,1)} %copy-done.20, ...), custom_call_target="tpu_custom_call" | custom-call | flops 2147483648 | bytes 7340032 | tf_op jit(solution)/shard_map/pallas_call | solution.py:241
  152.0 7.6 %all-to-all-start.2 = ((f32[8,64,1024]{2,1,0:T(8,128)}), f32[8,64,1024]{2,1,0:T(8,128)S(1)}, u32[]{:S(2)}, u32[]{:S(2)}) async-start(f32[8,64,1024]{2,1,0:T(8,128)} %bitcast.17), calls=%async_computation.2 | async-start | bytes 4194304 | tf_op jit(solution)/shard_map/all_to_all | solution.py:382
  159.6 18.5 %all-gather.7.cloned.1.call-done = bf16[8,256,256]{2,1,0:T(8,128)(2,1)} async-done(((bf16[2,256,256]{2,1,0:T(8,128)(2,1)}), bf16[8,256,256]{2,1,0:T(8,128)(2,1)}) %all-gather.7.cloned.1.call-update) | async-done | bytes 1048592 | tf_op jit(solution)/shard_map/all_gather | solution.py:378
  178.2 11.7 %all-to-all-done.2.parts = f32[8,64,1024]{2,1,0:T(8,128)S(1)} async-done(((f32[8,64,1024]{2,1,0:T(8,128)}), f32[8,64,1024]{2,1,0:T(8,128)S(1)}, u32[]{:S(2)}, u32[]{:S(2)}) %all-to-all-start.2) | async-done | bytes 2097184 | tf_op jit(solution)/shard_map/all_to_all | solution.py:382
  189.9 1.2 copy-done.2
  191.1 1.0 shard_map.44
  192.1 20.8 %all_to_all.20.parts = f32[16,32,128]{2,1,0:T(8,128)} all-to-all(f32[16,32,128]{2,1,0:T(8,128)S(1)} %shard_map.44), channel_id=1, replica_groups=mesh['zh'=4,'zl'=2,'yl'=2,'yh'=2,'x'=4,'c'=2] {'zh','zl','yl'}, dimensions={0} | all-to-all | bytes 524288 | tf_op jit(solution)/shard_map/all_to_all | solution.py:383
  212.9 1.7 shard_map.45
  (57 shorter events, 0.2 us)
Async XLA Ops:
  6.5 17.8 %copy-start.3 = (bf16[64,4096]{1,0:T(8,128)(2,1)S(1)}, bf16[64,4096]{1,0:T(8,128)(2,1)}, u32[]{:S(2)}) copy-start(bf16[64,4096]{1,0:T(8,128)(2,1)} %refs_0_.3) | copy-start | bytes 1572868
  6.5 13.9 %collective-permute-start = (bf16[64,4096]{1,0:T(8,128)(2,1)}, bf16[64,4096]{1,0:T(8,128)(2,1)S(1)}, u32[]{:S(2)}, u32[]{:S(2)}) collective-permute-start(bf16[64,4096]{1,0:T(8,128)(2,1)} %refs_0_.3), channel_id=1, source_target_pairs={{0,16},{16,0},{1,17},{17,1},{2,18},{18,2},{3,19},{19,3},{4,20},{20... | collective-permute-start | bytes 1572872 | tf_op jit(solution)/shard_map/ppermute | solution.py:310
  7.8 13.8 %collective-permute-start.1 = (bf16[64,4096]{1,0:T(8,128)(2,1)}, bf16[64,4096]{1,0:T(8,128)(2,1)S(1)}, u32[]{:S(2)}, u32[]{:S(2)}) collective-permute-start(bf16[64,4096]{1,0:T(8,128)(2,1)} %refs_0_.3), channel_id=1, source_target_pairs={{0,32},{32,0},{1,33},{33,1},{2,34},{34,2},{3,35},{35,3},{4,36},{36... | collective-permute-start | bytes 1572872 | tf_op jit(solution)/shard_map/ppermute | solution.py:310
  9.7 0.7 copy-start.11
  20.4 15.8 %copy-start = (bf16[64,4096]{1,0:T(8,128)(2,1)}, bf16[64,4096]{1,0:T(8,128)(2,1)S(1)}, u32[]{:S(2)}) copy-start(bf16[64,4096]{1,0:T(8,128)(2,1)S(1)} %collective-permute-done.refs_1_) | copy-start | bytes 1572868
  21.6 14.6 %copy-start.1 = (bf16[64,4096]{1,0:T(8,128)(2,1)}, bf16[64,4096]{1,0:T(8,128)(2,1)S(1)}, u32[]{:S(2)}) copy-start(bf16[64,4096]{1,0:T(8,128)(2,1)S(1)} %collective-permute-done.1.refs_2_) | copy-start | bytes 1572868
  21.6 7.2 %collective-permute-start.2 = (bf16[32,4096]{1,0:T(8,128)(2,1)S(1)}, bf16[32,4096]{1,0:T(8,128)(2,1)S(1)}, u32[]{:S(2)}, u32[]{:S(2)}) collective-permute-start(bf16[32,4096]{1,0:T(8,128)(2,1)S(1)} %slice.6), channel_id=1, source_target_pairs={{0,32},{32,0},{1,33},{33,1},{2,34},{34,2},{3,35},{35,3},{4,36},{36... | collective-permute-start | bytes 786440 | tf_op jit(solution)/shard_map/ppermute | solution.py:310
  23.5 6.7 %collective-permute-start.3 = (bf16[32,4096]{1,0:T(8,128)(2,1)S(1)}, bf16[32,4096]{1,0:T(8,128)(2,1)S(1)}, u32[]{:S(2)}, u32[]{:S(2)}) collective-permute-start(bf16[32,4096]{1,0:T(8,128)(2,1)S(1)} %slice.7), channel_id=1, source_target_pairs={{0,16},{16,0},{1,17},{17,1},{2,18},{18,2},{3,19},{19,3},{4,20},{20... | collective-permute-start | bytes 786440 | tf_op jit(solution)/shard_map/ppermute | solution.py:310
  24.3 11.9 %collective-permute-start.4 = (bf16[64,4096]{1,0:T(8,128)(2,1)S(1)}, bf16[64,4096]{1,0:T(8,128)(2,1)S(1)}, u32[]{:S(2)}, u32[]{:S(2)}) collective-permute-start(bf16[64,4096]{1,0:T(8,128)(2,1)S(1)} %copy-done.3), channel_id=1, source_target_pairs={{0,1},{1,0},{2,3},{3,2},{4,5},{5,4},{6,7},{7,6},{8,9},{9,8},{10,11... | collective-permute-start | bytes 1572872 | tf_op jit(solution)/shard_map/ppermute | solution.py:310
  24.3 11.9 %collective-permute-start.5 = (bf16[64,4096]{1,0:T(8,128)(2,1)S(1)}, bf16[64,4096]{1,0:T(8,128)(2,1)S(1)}, u32[]{:S(2)}, u32[]{:S(2)}) collective-permute-start(bf16[64,4096]{1,0:T(8,128)(2,1)S(1)} %collective-permute-done.refs_1_), channel_id=1, source_target_pairs={{0,1},{1,0},{2,3},{3,2},{4,5},{5,4},{6,7},{7,6},{8,9},{9,8},{10,11... | collective-permute-start | bytes 1572872 | tf_op jit(solution)/shard_map/ppermute | solution.py:310
  24.8 11.4 %collective-permute-start.6 = (bf16[64,4096]{1,0:T(8,128)(2,1)S(1)}, bf16[64,4096]{1,0:T(8,128)(2,1)S(1)}, u32[]{:S(2)}, u32[]{:S(2)}) collective-permute-start(bf16[64,4096]{1,0:T(8,128)(2,1)S(1)} %collective-permute-done.1.refs_2_), channel_id=1, source_target_pairs={{0,1},{1,0},{2,3},{3,2},{4,5},{5,4},{6,7},{7,6},{8,9},{9,8},{10,11... | collective-permute-start | bytes 1572872 | tf_op jit(solution)/shard_map/ppermute | solution.py:310
  28.8 7.5 %copy-start.7 = (bf16[32,4096]{1,0:T(8,128)(2,1)}, bf16[32,4096]{1,0:T(8,128)(2,1)S(1)}, u32[]{:S(2)}) copy-start(bf16[32,4096]{1,0:T(8,128)(2,1)S(1)} %collective-permute-done.2.refs_3_) | copy-start | bytes 786436
  28.8 7.4 %collective-permute-start.7 = (bf16[32,4096]{1,0:T(8,128)(2,1)S(1)}, bf16[32,4096]{1,0:T(8,128)(2,1)S(1)}, u32[]{:S(2)}, u32[]{:S(2)}) collective-permute-start(bf16[32,4096]{1,0:T(8,128)(2,1)S(1)} %collective-permute-done.2.refs_3_), channel_id=1, source_target_pairs={{0,1},{1,0},{2,3},{3,2},{4,5},{5,4},{6,7},{7,6},{8,9},{9,8},{10,11... | collective-permute-start | bytes 786440 | tf_op jit(solution)/shard_map/ppermute | solution.py:310
  30.1 6.2 %copy-start.8 = (bf16[32,4096]{1,0:T(8,128)(2,1)}, bf16[32,4096]{1,0:T(8,128)(2,1)S(1)}, u32[]{:S(2)}) copy-start(bf16[32,4096]{1,0:T(8,128)(2,1)S(1)} %collective-permute-done.3.refs_4_) | copy-start | bytes 786436
  30.1 6.1 %collective-permute-start.8 = (bf16[32,4096]{1,0:T(8,128)(2,1)S(1)}, bf16[32,4096]{1,0:T(8,128)(2,1)S(1)}, u32[]{:S(2)}, u32[]{:S(2)}) collective-permute-start(bf16[32,4096]{1,0:T(8,128)(2,1)S(1)} %collective-permute-done.3.refs_4_), channel_id=1, source_target_pairs={{0,1},{1,0},{2,3},{3,2},{4,5},{5,4},{6,7},{7,6},{8,9},{9,8},{10,11... | collective-permute-start | bytes 786440 | tf_op jit(solution)/shard_map/ppermute | solution.py:310
  36.2 7.9 %copy-start.4 = (bf16[64,4096]{1,0:T(8,128)(2,1)}, bf16[64,4096]{1,0:T(8,128)(2,1)S(1)}, u32[]{:S(2)}) copy-start(bf16[64,4096]{1,0:T(8,128)(2,1)S(1)} %collective-permute-done.4.refs_5_) | copy-start | bytes 1572868
  44.1 0.8 copy-start.5
  44.9 0.8 copy-start.6
  45.7 0.7 copy-start.9
  46.4 0.7 copy-start.10
  47.1 26.4 %all-to-all-start = ((f32[8,256,128]{2,1,0:T(8,128)}), f32[8,256,128]{2,1,0:T(8,128)S(1)}, u32[]{:S(2)}, u32[]{:S(2)}) async-start(f32[8,256,128]{2,1,0:T(8,128)} %shard_map.40), calls=%async_computation | async-start | bytes 2097152 | tf_op jit(solution)/shard_map/all_to_all | solution.py:359
  54.3 83.4 %all-gather.5.cloned.1.call-start = ((), (), s32[]{:S(2)}) async-start(), calls=%async_computation.4 | async-start | bytes 1179648 | tf_op jit(solution)/shard_map/all_gather | solution.py:372
  73.5 13.2 %copy-start.12 = (bf16[1024,1024]{1,0:T(8,128)(2,1)S(1)}, bf16[1024,1024]{1,0:T(8,128)(2,1)}, u32[]{:S(2)}) copy-start(bf16[1024,1024]{1,0:T(8,128)(2,1)} %refs_9_.1) | copy-start | bytes 6291460
  73.6 1.3 collective-permute-start.9
  73.7 4.1 %collective-permute-start.10 = (bf16[128,128]{1,0:T(8,128)(2,1)S(1)}, bf16[128,128]{1,0:T(8,128)(2,1)S(1)}, u32[]{:S(2)}, u32[]{:S(2)}) collective-permute-start(bf16[128,128]{1,0:T(8,128)(2,1)S(1)} %get-tuple-element.32), channel_id=1, source_target_pairs={{0,16},{16,0},{1,17},{17,1},{2,18},{18,2},{3,19},{19,3},{4,20},{20... | collective-permute-start | bytes 98312 | tf_op jit(solution)/shard_map/ppermute | solution.py:310
  74.9 3.9 %collective-permute-start.11 = (bf16[128,128]{1,0:T(8,128)(2,1)S(1)}, bf16[128,128]{1,0:T(8,128)(2,1)S(1)}, u32[]{:S(2)}, u32[]{:S(2)}) collective-permute-start(bf16[128,128]{1,0:T(8,128)(2,1)S(1)} %collective-permute-done.9), channel_id=1, source_target_pairs={{0,16},{16,0},{1,17},{17,1},{2,18},{18,2},{3,19},{19,3},{4,20},{20... | collective-permute-start | bytes 98312 | tf_op jit(solution)/shard_map/ppermute | solution.py:310
  79.5 19.5 %all-to-all-start.1 = ((f32[8,256,128]{2,1,0:T(8,128)}), f32[8,256,128]{2,1,0:T(8,128)S(1)}, u32[]{:S(2)}, u32[]{:S(2)}) async-start(f32[8,256,128]{2,1,0:T(8,128)} %shard_map.38), calls=%async_computation.1 | async-start | bytes 2097152 | tf_op jit(solution)/shard_map/all_to_all | solution.py:362
  86.7 91.5 %all-gather.7.cloned.1.call-start = ((), (), s32[]{:S(2)}) async-start(), calls=%async_computation.5 | async-start | bytes 1310720 | tf_op jit(solution)/shard_map/all_gather | solution.py:378
  86.7 53.3 %collective-permute-start.24 = (bf16[1024,1024]{1,0:T(8,128)(2,1)S(1)}, bf16[1024,1024]{1,0:T(8,128)(2,1)}, u32[]{:S(2)}, u32[]{:S(2)}) collective-permute-start(bf16[1024,1024]{1,0:T(8,128)(2,1)S(1)} %copy-done.12), channel_id=1, source_target_pairs={{0,1},{1,0},{2,3},{3,2},{4,5},{5,4},{6,7},{7,6},{8,9},{9,8},{10,11... | collective-permute-start | bytes 6291464 | tf_op jit(solution)/shard_map/ppermute | solution.py:310
  99.0 1.3 collective-permute-start.12
  99.1 4.1 %collective-permute-start.13 = (bf16[128,128]{1,0:T(8,128)(2,1)S(1)}, bf16[128,128]{1,0:T(8,128)(2,1)S(1)}, u32[]{:S(2)}, u32[]{:S(2)}) collective-permute-start(bf16[128,128]{1,0:T(8,128)(2,1)S(1)} %get-tuple-element.37), channel_id=1, source_target_pairs={{0,16},{16,0},{1,17},{17,1},{2,18},{18,2},{3,19},{19,3},{4,20},{20... | collective-permute-start | bytes 98312 | tf_op jit(solution)/shard_map/ppermute | solution.py:310
  100.3 3.9 %collective-permute-start.14 = (bf16[128,128]{1,0:T(8,128)(2,1)S(1)}, bf16[128,128]{1,0:T(8,128)(2,1)S(1)}, u32[]{:S(2)}, u32[]{:S(2)}) collective-permute-start(bf16[128,128]{1,0:T(8,128)(2,1)S(1)} %collective-permute-done.12), channel_id=1, source_target_pairs={{0,16},{16,0},{1,17},{17,1},{2,18},{18,2},{3,19},{19,3},{4,20},{20... | collective-permute-start | bytes 98312 | tf_op jit(solution)/shard_map/ppermute | solution.py:310
  104.3 39.7 %copy-start.13 = (bf16[4,128,128]{2,1,0:T(8,128)(2,1)}, bf16[4,128,128]{2,1,0:T(8,128)(2,1)S(1)}, u32[]{:S(2)}) copy-start(bf16[4,128,128]{2,1,0:T(8,128)(2,1)S(1)} %pad_maximum_fusion.2.refs_1_) | copy-start | bytes 393220
  104.3 12.4 %collective-permute-start.16 = (bf16[4,128,128]{2,1,0:T(8,128)(2,1)S(1)}, bf16[4,128,128]{2,1,0:T(8,128)(2,1)S(1)}, u32[]{:S(2)}, u32[]{:S(2)}) collective-permute-start(bf16[4,128,128]{2,1,0:T(8,128)(2,1)S(1)} %pad_maximum_fusion.2.refs_1_), channel_id=1, source_target_pairs={{0,32},{32,64},{64,96},{96,128},{128,160},{160,192},{192,224},{224... | collective-permute-start | bytes 393224 | tf_op jit(solution)/shard_map/ppermute | solution.py:314
  105.0 13.5 %collective-permute-start.18 = (bf16[4,128,128]{2,1,0:T(8,128)(2,1)S(1)}, bf16[4,128,128]{2,1,0:T(8,128)(2,1)S(1)}, u32[]{:S(2)}, u32[]{:S(2)}) collective-permute-start(bf16[4,128,128]{2,1,0:T(8,128)(2,1)S(1)} %pad_maximum_fusion.2.refs_1_), channel_id=1, source_target_pairs={{0,224},{32,0},{64,32},{96,64},{128,96},{160,128},{192,160},{224,1... | collective-permute-start | bytes 393224 | tf_op jit(solution)/shard_map/ppermute | solution.py:314
  109.2 20.9 %collective-permute-start.15 = (bf16[256,256]{1,0:T(8,128)(2,1)S(1)}, bf16[256,256]{1,0:T(8,128)(2,1)S(1)}, u32[]{:S(2)}, u32[]{:S(2)}) collective-permute-start(bf16[256,256]{1,0:T(8,128)(2,1)S(1)} %get-tuple-element.39), channel_id=1, source_target_pairs={{0,0},{1,1},{2,32},{3,33},{4,64},{5,65},{6,96},{7,97},{8,128},{9,1... | collective-permute-start | bytes 393224 | tf_op jit(solution)/shard_map/ppermute | solution.py:318
  116.7 27.2 %copy-start.14 = (bf16[4,128,128]{2,1,0:T(8,128)(2,1)}, bf16[4,128,128]{2,1,0:T(8,128)(2,1)S(1)}, u32[]{:S(2)}) copy-start(bf16[4,128,128]{2,1,0:T(8,128)(2,1)S(1)} %collective-permute-done.16.refs_2_) | copy-start | bytes 393220
  116.7 13.4 %collective-permute-start.17 = (bf16[4,128,128]{2,1,0:T(8,128)(2,1)S(1)}, bf16[4,128,128]{2,1,0:T(8,128)(2,1)S(1)}, u32[]{:S(2)}, u32[]{:S(2)}) collective-permute-start(bf16[4,128,128]{2,1,0:T(8,128)(2,1)S(1)} %collective-permute-done.16.refs_2_), channel_id=1, source_target_pairs={{0,32},{32,64},{64,96},{96,128},{128,160},{160,192},{192,224},{224... | collective-permute-start | bytes 393224 | tf_op jit(solution)/shard_map/ppermute | solution.py:314
  118.6 25.4 %copy-start.15 = (bf16[4,128,128]{2,1,0:T(8,128)(2,1)}, bf16[4,128,128]{2,1,0:T(8,128)(2,1)S(1)}, u32[]{:S(2)}) copy-start(bf16[4,128,128]{2,1,0:T(8,128)(2,1)S(1)} %collective-permute-done.18.refs_6_) | copy-start | bytes 393220
  118.6 11.6 %collective-permute-start.19 = (bf16[4,128,128]{2,1,0:T(8,128)(2,1)S(1)}, bf16[4,128,128]{2,1,0:T(8,128)(2,1)S(1)}, u32[]{:S(2)}, u32[]{:S(2)}) collective-permute-start(bf16[4,128,128]{2,1,0:T(8,128)(2,1)S(1)} %collective-permute-done.18.refs_6_), channel_id=1, source_target_pairs={{0,224},{32,0},{64,32},{96,64},{128,96},{160,128},{192,160},{224,1... | collective-permute-start | bytes 393224 | tf_op jit(solution)/shard_map/ppermute | solution.py:314
  130.2 13.8 %copy-start.16 = (bf16[4,128,128]{2,1,0:T(8,128)(2,1)}, bf16[4,128,128]{2,1,0:T(8,128)(2,1)S(1)}, u32[]{:S(2)}) copy-start(bf16[4,128,128]{2,1,0:T(8,128)(2,1)S(1)} %collective-permute-done.17.refs_3_) | copy-start | bytes 393220
  130.2 13.8 %copy-start.17 = (bf16[4,128,128]{2,1,0:T(8,128)(2,1)}, bf16[4,128,128]{2,1,0:T(8,128)(2,1)S(1)}, u32[]{:S(2)}) copy-start(bf16[4,128,128]{2,1,0:T(8,128)(2,1)S(1)} %collective-permute-done.19.refs_7_) | copy-start | bytes 393220
  130.2 6.7 %collective-permute-start.20 = (bf16[256,256]{1,0:T(8,128)(2,1)S(1)}, bf16[256,256]{1,0:T(8,128)(2,1)S(1)}, u32[]{:S(2)}, u32[]{:S(2)}) collective-permute-start(bf16[256,256]{1,0:T(8,128)(2,1)S(1)} %collective-permute-done.15), channel_id=1, source_target_pairs={{0,8},{8,0},{1,9},{9,1},{2,10},{10,2},{3,11},{11,3},{4,12},{12,4},... | collective-permute-start | bytes 393224 | tf_op jit(solution)/shard_map/ppermute | solution.py:310
  130.3 6.6 %collective-permute-start.21 = (bf16[4,128,128]{2,1,0:T(8,128)(2,1)S(1)}, bf16[4,128,128]{2,1,0:T(8,128)(2,1)S(1)}, u32[]{:S(2)}, u32[]{:S(2)}) collective-permute-start(bf16[4,128,128]{2,1,0:T(8,128)(2,1)S(1)} %collective-permute-done.17.refs_3_), channel_id=1, source_target_pairs={{0,32},{32,64},{64,96},{96,128},{128,160},{160,192},{192,224},{224... | collective-permute-start | bytes 393224 | tf_op jit(solution)/shard_map/ppermute | solution.py:314
  130.7 6.1 %collective-permute-start.22 = (bf16[4,128,128]{2,1,0:T(8,128)(2,1)S(1)}, bf16[4,128,128]{2,1,0:T(8,128)(2,1)S(1)}, u32[]{:S(2)}, u32[]{:S(2)}) collective-permute-start(bf16[4,128,128]{2,1,0:T(8,128)(2,1)S(1)} %collective-permute-done.19.refs_7_), channel_id=1, source_target_pairs={{0,224},{32,0},{64,32},{96,64},{128,96},{160,128},{192,160},{224,1... | collective-permute-start | bytes 393224 | tf_op jit(solution)/shard_map/ppermute | solution.py:314
  136.8 7.1 %copy-start.18 = (bf16[4,128,128]{2,1,0:T(8,128)(2,1)}, bf16[4,128,128]{2,1,0:T(8,128)(2,1)S(1)}, u32[]{:S(2)}) copy-start(bf16[4,128,128]{2,1,0:T(8,128)(2,1)S(1)} %collective-permute-done.21.refs_4_) | copy-start | bytes 393220
  136.8 7.1 %copy-start.19 = (bf16[4,128,128]{2,1,0:T(8,128)(2,1)}, bf16[4,128,128]{2,1,0:T(8,128)(2,1)S(1)}, u32[]{:S(2)}) copy-start(bf16[4,128,128]{2,1,0:T(8,128)(2,1)S(1)} %collective-permute-done.22.refs_8_) | copy-start | bytes 393220
  137.7 6.3 %collective-permute-start.23 = (bf16[4,128,128]{2,1,0:T(8,128)(2,1)S(1)}, bf16[4,128,128]{2,1,0:T(8,128)(2,1)S(1)}, u32[]{:S(2)}, u32[]{:S(2)}) collective-permute-start(bf16[4,128,128]{2,1,0:T(8,128)(2,1)S(1)} %collective-permute-done.21.refs_4_), channel_id=1, source_target_pairs={{0,32},{32,64},{64,96},{96,128},{128,160},{160,192},{192,224},{224... | collective-permute-start | bytes 393224 | tf_op jit(solution)/shard_map/ppermute | solution.py:314
  144.0 0.7 copy-start.20
  152.0 37.9 %all-to-all-start.2 = ((f32[8,64,1024]{2,1,0:T(8,128)}), f32[8,64,1024]{2,1,0:T(8,128)S(1)}, u32[]{:S(2)}, u32[]{:S(2)}) async-start(f32[8,64,1024]{2,1,0:T(8,128)} %bitcast.17), calls=%async_computation.2 | async-start | bytes 4194304 | tf_op jit(solution)/shard_map/all_to_all | solution.py:382
  178.2 11.7 %collective-permute-start.25 = (bf16[4,2,256,256]{3,2,1,0:T(8,128)(2,1)}, bf16[4,2,256,256]{3,2,1,0:T(8,128)(2,1)S(1)}, u32[]{:S(2)}, u32[]{:S(2)}) collective-permute-start(bf16[4,2,256,256]{3,2,1,0:T(8,128)(2,1)} %bitcast.13), channel_id=1, source_target_pairs={{0,1},{1,0},{2,3},{3,2},{4,5},{5,4},{6,7},{7,6},{8,9},{9,8},{10,11... | collective-permute-start | bytes 3145736 | tf_op jit(solution)/shard_map/ppermute | solution.py:310
  189.9 1.2 copy-start.2
Sparse Core Ops, SparseCore 0:
  79.6 46.0 all-gather.4
  137.8 40.3 all-gather.6

commit v6 on v5

v6 whole, which is shorter than its diff:
```python
import functools

import jax
import jax.numpy as jnp
from jax import lax
from jax.experimental import pallas as pl
from jax.experimental.pallas import tpu as pltpu
from jax.sharding import Mesh
from jax.sharding import PartitionSpec as P

FEATURES = 16384
SCALE = FEATURES ** (-0.5)
BF16 = jnp.bfloat16
F32 = jnp.float32

EX = ("zh", "zl", "yl")
CHIPS = ("yh", "x")
PAR = ("yh", "x", "c")
FEATURES_PER_CHIP = FEATURES // 8


def shifted(values, amount):
    return lax.shift_right_logical(values, jnp.full(values.shape, amount, jnp.int32))


def signs(hash_words, row_start, rows, cols):
    m0 = hash_words[0] | 1
    row_ids = lax.broadcasted_iota(jnp.int32, (rows, cols.shape[1]), 0)
    mixed = row_ids * (FEATURES * m0) + (cols * m0 + (row_start * (FEATURES * m0) + hash_words[1]))
    mixed = mixed ^ shifted(mixed, 15)
    mixed = mixed * (hash_words[2] | 1)
    mixed = mixed ^ shifted(mixed, 13)
    mixed = mixed * (hash_words[3] | 1)
    return jnp.where(mixed < 0, BF16(-1), BF16(1))


def columns(first, count, part, width):
    slice_id = lax.axis_index("yl") * 4 + lax.axis_index("zl") * 2 + lax.axis_index("c")
    column = lax.broadcasted_iota(jnp.int32, (1, count), 1)
    group, within = column // width, column % width
    return (group + first // width) * FEATURES_PER_CHIP + within + (slice_id * 256 + part * width)


def first_parameter(block, depth, params):
    per_core = params // 2 // depth
    core = lax.axis_index("c")
    chip = lax.axis_index("yh") * 4 + lax.axis_index("x")
    which = jnp.where(block < per_core, core, 1 - core)
    inner = jnp.where(block < per_core, block, block - per_core)
    return (chip * 2 + which) * (params // 2) + inner * depth


def table_kernel(part, width, first, params, words, out):
    depth, wide = out.shape
    row_start = first_parameter(pl.program_id(0) + first, depth, params)
    rows = 32

    def chunk(index, carry):
        start = pl.multiple_of(index * rows, rows)
        cols = columns(0, wide, part, width)
        out[pl.ds(start, rows), :] = signs(words, row_start + start, rows, cols)
        return carry

    lax.fori_loop(0, depth // rows, chunk, 0)


def table(part, width, first, count, depth, params, words):
    return pl.pallas_call(
        functools.partial(table_kernel, part, width, first, params),
        out_shape=jax.ShapeDtypeStruct((count * depth, 8 * width), BF16),
        grid=(count,),
        in_specs=[pl.BlockSpec(memory_space=pltpu.SMEM)],
        out_specs=pl.BlockSpec((depth, 8 * width), lambda k: (k, 0)),
        compiler_params=pltpu.CompilerParams(vmem_limit_bytes=12 << 20),
        cost_estimate=pl.CostEstimate(
            flops=1200 * count * depth * 8 * width,
            bytes_accessed=2 * count * depth * 8 * width,
            transcendentals=0,
        ),
    )(words)


def load_examples(blocks, examples, arrived):
    me = lax.axis_index("zl") * 2 + lax.axis_index("yl")
    half = len(blocks) // 2
    params = blocks[0].shape[1]
    rows = blocks[0].shape[0]
    copies = []
    for index, block in enumerate(blocks):
        kind = index % half
        start = (me ^ min(kind, 3)) * rows + (rows // 2 if kind == 4 else 0)
        target = examples.at[
            pl.ds(pl.multiple_of(start, 32), block.shape[0]),
            (index // half) * params : (index // half + 1) * params,
        ]
        copies.append(pltpu.make_async_copy(block, target, arrived.at[index]))
    for copy in copies:
        copy.start()
    for copy in copies:
        copy.wait()


def write_run(out, total, width):
    for block in range(8):
        out[block] = total[:, block * width : (block + 1) * width] * SCALE


def ready_kernel(split, width, first, second, *refs):
    blocks, (out, gathered, examples, total, arrived) = refs[:-5], refs[-5:]
    step = pl.program_id(0)
    depth = first.shape[0]
    hand_on = pltpu.make_async_copy(examples, gathered, arrived.at[len(blocks)])

    @pl.when(step == 0)
    def _():
        load_examples(blocks, examples, arrived)
        hand_on.start()
        total[...] = jnp.zeros_like(total)

    held = examples[:, pl.ds(pl.multiple_of(step * depth, depth), depth)]

    @pl.when(step < split)
    def _():
        total[...] += jnp.dot(held, first[...], preferred_element_type=F32)

    @pl.when(step >= split)
    def _():
        total[...] += jnp.dot(held, second[...], preferred_element_type=F32)

    @pl.when(step == pl.num_programs(0) - 1)
    def _():
        hand_on.wait()
        write_run(out, total, width)


def project_ready(first, second, width, blocks):
    rows, params = 4 * blocks[0].shape[0], 2 * blocks[0].shape[1]
    depth = 1024
    split = first.shape[0] // depth
    return pl.pallas_call(
        functools.partial(ready_kernel, split, width),
        out_shape=[
            jax.ShapeDtypeStruct((8, rows, width), F32),
            jax.ShapeDtypeStruct((rows, params), BF16),
        ],
        grid=(params // depth,),
        in_specs=[
            pl.BlockSpec((depth, 8 * width), lambda k: (jnp.minimum(k, split - 1), 0)),
            pl.BlockSpec((depth, 8 * width), lambda k: (jnp.maximum(k - split, 0), 0)),
        ]
        + [pl.BlockSpec(memory_space=pltpu.HBM)] * len(blocks),
        out_specs=[
            pl.BlockSpec((8, rows, width), lambda k: (0, 0, 0)),
            pl.BlockSpec(memory_space=pltpu.HBM),
        ],
        scratch_shapes=[
            pltpu.VMEM((rows, params), BF16),
            pltpu.VMEM((rows, 8 * width), F32),
            pltpu.SemaphoreType.DMA((len(blocks) + 1,)),
        ],
        compiler_params=pltpu.CompilerParams(vmem_limit_bytes=24 << 20),
        cost_estimate=pl.CostEstimate(
            flops=2 * rows * params * 8 * width, bytes_accessed=16 << 20, transcendentals=0
        ),
    )(first, second, *blocks)


def hash_kernel(part, width, words, gathered, out, examples, total, arrived):
    step = pl.program_id(0)
    steps = arrived.shape[0]
    params = examples.shape[1]
    depth = params // steps
    wide = 512

    def bring(index):
        at = pl.ds(pl.multiple_of(index * depth, depth), depth)
        return pltpu.make_async_copy(gathered.at[:, at], examples.at[:, at], arrived.at[index])

    @pl.when(step == 0)
    def _():
        for index in range(steps):
            bring(index).start()
        total[...] = jnp.zeros_like(total)

    bring(step).wait()
    held = examples[:, pl.ds(pl.multiple_of(step * depth, depth), depth)]
    row_start = first_parameter(step, depth, params)
    for first in range(0, 8 * width, wide):
        made = signs(words, row_start, depth, columns(first, wide, part, width))
        total[:, first : first + wide] += jnp.dot(held, made, preferred_element_type=F32)

    @pl.when(step == steps - 1)
    def _():
        write_run(out, total, width)


def project_hash(part, width, words, gathered, steps=16):
    rows, params = gathered.shape
    return pl.pallas_call(
        functools.partial(hash_kernel, part, width),
        out_shape=jax.ShapeDtypeStruct((8, rows, width), F32),
        grid=(steps,),
        in_specs=[pl.BlockSpec(memory_space=pltpu.SMEM), pl.BlockSpec(memory_space=pltpu.HBM)],
        out_specs=pl.BlockSpec((8, rows, width), lambda k: (0, 0, 0)),
        scratch_shapes=[
            pltpu.VMEM((rows, params), BF16),
            pltpu.VMEM((rows, 8 * width), F32),
            pltpu.SemaphoreType.DMA((steps,)),
        ],
        compiler_params=pltpu.CompilerParams(vmem_limit_bytes=60 << 20),
        cost_estimate=pl.CostEstimate(
            flops=2 * rows * params * 8 * width, bytes_accessed=16 << 20, transcendentals=0
        ),
    )(words, gathered)


def sum_kernel(part, whole, keep, send):
    core = lax.axis_index("c")
    total = part[0]
    for index in range(1, part.shape[0]):
        total += part[index]
    whole[...] = total.astype(BF16)
    for block in range(2):
        for target, which in ((keep, core), (send, 1 - core)):
            start = pl.multiple_of(block * 128 + which * 64, 64)
            target[block * 64 : (block + 1) * 64, :] = whole[pl.ds(start, 64), :]


def sum_parts(part):
    _, rows, width = part.shape
    shapes = [(rows, width), (rows // 2, width), (rows // 2, width)]
    return pl.pallas_call(
        sum_kernel,
        out_shape=[jax.ShapeDtypeStruct(shape, BF16) for shape in shapes],
        compiler_params=pltpu.CompilerParams(vmem_limit_bytes=8 << 20),
    )(part)


RING = (0, -1, -2, -3, -4, 1, 2, 3)


def condition_kernel(*refs):
    low, high, (mine, other), (out, pieces, tiles, arrived) = refs[0], refs[1:9], refs[9:11], refs[11:]
    core = lax.axis_index("c")
    yl = lax.axis_index("yl")
    z = lax.axis_index("zh") * 2 + lax.axis_index("zl")
    zl = lax.axis_index("zl")
    tile_copies = []
    for group in range(2):
        rows = pl.ds(pl.multiple_of((zl ^ group) * 512, 512), 512)
        for which, (source, place) in enumerate(((mine, core), (other, 1 - core))):
            tile_copies.append(
                pltpu.make_async_copy(
                    source.at[rows, :], tiles.at[place, rows, :], arrived.at[16 + group * 2 + which]
                )
            )
    copies = []
    for index, away in enumerate(RING):
        for run, source in enumerate((low.at[(z + (away + 8)) & 7], high[index])):
            target = pieces.at[index, :, :, run * 128 : (run + 1) * 128]
            copies.append(pltpu.make_async_copy(source, target, arrived.at[index * 2 + run]))
    for group in range(2):
        for copy in tile_copies[group * 2 : group * 2 + 2]:
            copy.start()
        for index, away in enumerate(RING):
            if away % 2 == group:
                copies[index * 2].start()
                copies[index * 2 + 1].start()
    for group in range(2):
        for copy in tile_copies[group * 2 : group * 2 + 2]:
            copy.wait()
        for index, away in enumerate(RING):
            if away % 2 != group:
                continue
            copies[index * 2].wait()
            copies[index * 2 + 1].wait()
            source = (z + (away + 8)) & 7
            total = None
            for flip in range(4):
                start = pl.multiple_of(((zl ^ group) * 2 + (core ^ (flip % 2))) * 256, 256)
                tile = tiles[yl ^ (flip // 2), pl.ds(start, 256), :]
                term = jnp.dot(pieces[index, flip], tile, preferred_element_type=F32)
                total = term if total is None else total + term
            at = pl.ds(pl.multiple_of((source >> 1) * 128, 128), 128)
            if group == 0:
                out[at, :] = total
            else:
                out[at, :] += total


def condition(low, high, mine, other):
    _, flips, rows, width = low.shape
    return pl.pallas_call(
        condition_kernel,
        out_shape=jax.ShapeDtypeStruct((4 * rows, mine.shape[1]), F32),
        in_specs=[pl.BlockSpec(memory_space=pltpu.HBM)] * 11,
        out_specs=pl.BlockSpec(memory_space=pltpu.VMEM),
        scratch_shapes=[
            pltpu.VMEM((8, flips, rows, 2 * width), BF16),
            pltpu.VMEM((2,) + mine.shape, BF16),
            pltpu.SemaphoreType.DMA((20,)),
        ],
        compiler_params=pltpu.CompilerParams(vmem_limit_bytes=60 << 20),
        cost_estimate=pl.CostEstimate(flops=2 * 512 * 2048 * 1024, bytes_accessed=7 << 20, transcendentals=0),
    )(low, *high, mine, other)


def pair_kernel(parts, *refs):
    features, (out, rows, pairs) = refs[:8], refs[8:]
    yh, x, core = (lax.axis_index(name) for name in PAR)
    total = parts[0]
    for index in range(1, parts.shape[0]):
        total += parts[index]
    rows[...] = total.astype(BF16)
    pairs[...] = jnp.zeros_like(pairs)
    for flip_yh in range(2):
        for shift in range(4):
            place = (x + 4 - shift) & 3
            zh = (yh ^ flip_yh) * 2 + (place >> 1)
            value = None
            for flip_core in range(2):
                start = pl.multiple_of(((place & 1) * 2 + (core ^ flip_core)) * 256, 256)
                held = features[flip_core * 4 + shift]
                term = lax.dot_general(
                    rows[:, pl.ds(start, 256)],
                    jnp.concatenate([held[flip_yh * 2], held[flip_yh * 2 + 1]], axis=1),
                    (((1,), (1,)), ((), ())),
                    preferred_element_type=F32,
                )
                value = term if value is None else value + term
            pairs[:, pl.ds(pl.multiple_of(zh * 256, 256), 256)] += value
    for block in range(16):
        piece = pairs[:, block * 64 : (block + 1) * 64]
        out[block % 4, block // 4, :, :64] = piece[:32]
        out[block % 4, block // 4, :, 64:] = piece[32:]


def pair(parts, features):
    return pl.pallas_call(
        pair_kernel,
        out_shape=jax.ShapeDtypeStruct((4, 4, 32, 128), F32),
        scratch_shapes=[pltpu.VMEM((64, 1024), BF16), pltpu.VMEM((64, 1024), F32)],
        compiler_params=pltpu.CompilerParams(vmem_limit_bytes=12 << 20),
    )(parts, *features)


def add_kernel(parts, out):
    out[...] = (parts[0] + parts[1]) + (parts[2] + parts[3])


def add(parts):
    return pl.pallas_call(add_kernel, out_shape=jax.ShapeDtypeStruct(parts.shape[1:], F32))(parts)


def finish_kernel(parts, out):
    total = ((parts[0] + parts[1]) + (parts[2] + parts[3])) * SCALE
    out[:32] = total[:, :64]
    out[32:] = total[:, 64:]


def finish(parts):
    return pl.pallas_call(finish_kernel, out_shape=jax.ShapeDtypeStruct((64, 64), F32))(parts)


def swap(value, axis):
    return lax.ppermute(value, axis, [(0, 1), (1, 0)])


def step_z(value, by):
    return lax.ppermute(value, ("zh", "zl"), [(i, (i + by) % 8) for i in range(8)])


def ring_and_turn(value, earlier, piece, route):
    turned = lax.ppermute(piece, EX + PAR, route)
    up = [step_z(value, 1)]
    down = [step_z(value, 7)]
    up.append(step_z(up[0], 1))
    down.append(step_z(down[0], 7))
    turned, up[1], down[1] = lax.optimization_barrier((turned, up[1], down[1]))
    both = jnp.stack([earlier, turned])
    flipped = swap(both, "yh")
    up.append(step_z(up[1], 1))
    down.append(step_z(down[1], 7))
    flipped, up[2], down[2] = lax.optimization_barrier((flipped, up[2], down[2]))
    up.append(step_z(up[2], 1))
    four = jnp.concatenate([both, flipped])
    along_x = [four]
    for by in range(1, 4):
        along_x.append(lax.ppermute(four, "x", [(i, (i + by) % 4) for i in range(4)]))
    return [value] + up + down, along_x


def flips(keep, send):
    received = swap(send, "c")
    return jnp.stack([keep, received, swap(keep, "yl"), swap(received, "yl")])


def per_device(gradients, inverse_gram, hash_words):
    half = gradients.shape[0] // 2
    width, depth, params = 128, 1024, 2 * gradients.shape[1]
    split = 5
    first = table(0, width, 0, split, depth, params, hash_words)
    second = table(0, width, split, params // depth - split, depth, params, hash_words)

    next_y = swap(gradients, "yl")
    next_z = swap(gradients, "zl")
    first, next_y, next_z = lax.optimization_barrier((first, next_y, next_z))
    diag_a, diag_b = swap(next_y[:half], "zl"), swap(next_z[half:], "yl")
    diag_a, diag_b, second = lax.optimization_barrier((diag_a, diag_b, second))
    own = [gradients, next_y, next_z, diag_a, diag_b]
    blocks = own + [swap(a, "c") for a in own]
    other_tile = swap(inverse_gram, "c")

    partial, gathered = project_ready(first, second, width, blocks)
    part = lax.all_to_all(partial, CHIPS, 0, 0, tiled=True)
    partial = project_hash(1, width, hash_words, gathered)
    partial, part = lax.optimization_barrier((partial, part))
    next_part = lax.all_to_all(partial, CHIPS, 0, 0, tiled=True)

    route = []
    for z in range(8):
        for yl in range(2):
            for chip in range(8):
                for c in range(2):
                    route.append((((z * 2 + yl) * 8 + chip) * 2 + c, ((chip * 2 + yl) * 8 + z) * 2 + c))
    whole, keep, send = sum_parts(part)
    mine = flips(keep, send)
    low = lax.all_gather(mine, ("zh", "zl"), axis=0)
    turned = lax.ppermute(whole, EX + PAR, route)
    next_part, mine, turned = lax.optimization_barrier((next_part, mine, turned))
    whole, keep, send = sum_parts(next_part)
    whole, mine = lax.optimization_barrier((whole, flips(keep, send)))
    high, near = ring_and_turn(mine, turned, whole, route)

    conditioned = condition(low, high, inverse_gram, other_tile)
    conditioned, near = lax.optimization_barrier((conditioned, near))
    far = [swap(v, "c") for v in near]
    parts = lax.all_to_all(conditioned.reshape(8, 64, 1024), CHIPS, 0, 0, tiled=True)
    scores = add(lax.all_to_all(pair(parts, near + far), ("zl", "yl"), 0, 0, tiled=True))
    return finish(lax.all_to_all(scores, "zh", 0, 0, tiled=True))


def solution(mesh):
    fine = Mesh(mesh.devices.reshape(4, 2, 2, 2, 4, 2), EX + PAR)
    return jax.shard_map(
        per_device,
        mesh=fine,
        in_specs=(P(EX, PAR), P(PAR, EX), P()),
        out_specs=P(PAR, EX),
        check_vma=False,
    )
```

time: 223 us -> 224 us (level)
  waiting for transfers between devices: 72.5 us -> 56.1 us
  starting transfers between devices: 54.3 us -> 62.9 us
  blocking collectives: 20.8 us -> 29.1 us
  local copies, waits for them, and re-layouts: 5.62 us -> 7.99 us
    all_gather x1 -> x0, waiting for transfers between devices: 18.5 us -> none  [per_device(): near = lax.all_gather(turned, 'x', axis=0)]
    all_to_all x1, waiting for transfers between devices: 12.1 us -> 0.01 us  [per_device(): next_part = lax.all_to_all(partial, CHIPS, 0, 0, tiled=True)]
    ppermute x0 -> x4, starting transfers between devices: none -> 11 us  [the longest x1 6.28 us: per_device(): turned = lax.ppermute(whole, EX + PAR, route)]
    ppermute x0 -> x4, waiting for transfers between devices: none -> 10.8 us  [the longest x1 9.73 us: per_device(): turned = lax.ppermute(whole, EX + PAR, route)]
    all_to_all x1 -> x2, blocking collectives: 20.8 us -> 29.1 us  [the longest x1 14.8 us: per_device(): lax.all_to_all(pair(parts, near + far), ('zl', 'yl'), 0, 0, tiled=True)]
    all_to_all x1, waiting for transfers between devices: 11.7 us -> 18 us  [per_device(): lax.all_to_all(conditioned.reshape(8, 64, 1024), CHIPS, 0, 0, tiled=True)]
    ppermute x1, starting transfers between devices: 7.45 us -> 4.94 us  [ring_and_turn(): turned = lax.ppermute(piece, EX + PAR, route)]
    unnamed x42 -> x36, local copies, waits for them, and re-layouts: 5.58 us -> 7.95 us
  transfers between devices with their start and end apart: 31 -> 37, of which waited for: 16 -> 20; matrix products, arithmetic and copies ran while one was open for 0% -> 0% of each run, Pallas kernels for 19% -> 18%
where the time goes in v6:
time: 224 us; the launch traced here: 223 us
  starting transfers between devices  62.9 us (28%)
  waiting for transfers between devices  56.1 us (25%)
  Pallas kernels  52.8 us (24%)
  blocking collectives  29.1 us (13%)
  between operations  13.7 us (6%)
  local copies, waits for them, and re-layouts  7.99 us (4%)
    all_to_all x1, waiting for transfers between devices, per_device(): lax.all_to_all(conditioned.reshape(8, 64, 1024), CHIPS, 0, 0, tiled=True)  18 us
    pallas_call x1, Pallas kernels, project_hash(): pl.pallas_call(functools.partial(hash_kernel, part, width), out_shape=jax...  18 us
    pallas_call x2, Pallas kernels, table(): pl.pallas_call(functools.partial(table_kernel, part, width, first, params...  15.8 us
    all_to_all x1, blocking collectives, per_device(): lax.all_to_all(pair(parts, near + far), ('zl', 'yl'), 0, 0, tiled=True)  14.8 us
    ppermute x21, waiting for transfers between devices, swap(): return lax.ppermute(value, axis, [(0, 1), (1, 0)])  14.4 us
    all_to_all x1, blocking collectives, per_device(): return finish(lax.all_to_all(scores, 'zh', 0, 0, tiled=True))  14.3 us
    ppermute x7, starting transfers between devices, step_z(): lax.ppermute(value, ('zh', 'zl'), [(i, (i + by) % 8) for i in range(8)])  12.4 us
    ppermute x21, starting transfers between devices, swap(): return lax.ppermute(value, axis, [(0, 1), (1, 0)])  12.4 us
  transfers between devices with their start and end apart: 37, of which 20 were waited for; matrix products, arithmetic and copies ran while one was open for 0% of the time, Pallas kernels for 18%

profile of v6, /device:TPU:22, one launch (start us, length us, event | category | flops | bytes accessed | tf_op | source)
XLA Modules:
  0.0 223.3 jit_solution(10903770413294305904)
XLA Ops:
  6.5 1.3 collective-permute-start
  7.8 1.9 collective-permute-start.1
  9.7 0.7 copy-done.8
  10.4 9.7 %shard_map.37.first = bf16[5120,1024]{1,0:T(8,128)(2,1)S(1)} custom-call(s32[4]{0:T(128)S(1)} %copy-done.8), custom_call_target="tpu_custom_call" | custom-call | flops 6291456000 | bytes 10485760 | tf_op jit(solution)/shard_map/pallas_call | solution.py:68
  20.4 1.2 collective-permute-done.1.refs_2_
  21.8 0.6 collective-permute-start.6
  22.4 1.7 collective-permute-start.2
  24.1 0.7 collective-permute-start.3
  24.8 6.0 %shard_map.38.second = bf16[3072,1024]{1,0:T(8,128)(2,1)S(1)} custom-call(s32[4]{0:T(128)S(1)} %copy-done.9), custom_call_target="tpu_custom_call" | custom-call | flops 3774873600 | bytes 6291456 | tf_op jit(solution)/shard_map/pallas_call | solution.py:68
  30.9 1.2 collective-permute-done.3.refs_4_
  32.1 0.5 collective-permute-start.8
  32.6 1.0 collective-permute-done.7.refs_8_
  33.6 0.4 collective-permute-done.8.refs_9_
  34.0 8.0 %shard_map.39 = (f32[8,256,128]{2,1,0:T(8,128)}, bf16[256,8192]{1,0:T(8,128)(2,1)S(1)}) custom-call(bf16[5120,1024]{1,0:T(8,128)(2,1)S(1)} %shard_map.37.first, bf16[3072,1024]{1,0:T(8,128)(2,1)S(1)} %shard_map.38.second, bf16[64,4096]{1,0:T(8,128)(2,1)S(1)} %copy-done, bf16[64,4096]{1,0:T(8,128)(2,1)S(1)} %collective-permute-done.refs_1_, ...), custom_call_target="tpu_custom_call" | custom-call | flops 4294967296 | bytes 16777216 | tf_op jit(solution)/shard_map/pallas_call | solution.py:140
  42.1 2.0 copy-done.7
  44.1 7.3 %all-to-all-start = ((f32[8,256,128]{2,1,0:T(8,128)}), f32[8,256,128]{2,1,0:T(8,128)S(1)}, u32[]{:S(2)}, u32[]{:S(2)}) async-start(f32[8,256,128]{2,1,0:T(8,128)} %get-tuple-element.43), calls=%async_computation | async-start | bytes 2097152 | tf_op jit(solution)/shard_map/all_to_all | solution.py:415
  51.5 18.0 %shard_map.40 = f32[8,256,128]{2,1,0:T(8,128)} custom-call(s32[4]{0:T(128)} %words.5, bf16[256,8192]{1,0:T(8,128)(2,1)} %copy-done.7), custom_call_target="tpu_custom_call" | custom-call | flops 4294967296 | bytes 16777216 | tf_op jit(solution)/shard_map/pallas_call | solution.py:199
  69.5 0.6 collective-permute-start.9
  70.1 0.7 collective-permute-start.10
  71.0 1.2 collective-permute-start.11
  72.1 2.0 collective-permute-done.10
  74.1 0.8 collective-permute-done.11
  74.9 0.7 pad_maximum_fusion.1
  75.6 7.2 %all-to-all-start.1 = ((f32[8,256,128]{2,1,0:T(8,128)}), f32[8,256,128]{2,1,0:T(8,128)S(1)}, u32[]{:S(2)}, u32[]{:S(2)}) async-start(f32[8,256,128]{2,1,0:T(8,128)} %shard_map.40), calls=%async_computation.1 | async-start | bytes 2097152 | tf_op jit(solution)/shard_map/all_to_all | solution.py:418
  82.8 6.3 %collective-permute-start.12 = (bf16[256,128]{1,0:T(8,128)(2,1)S(1)}, bf16[256,128]{1,0:T(8,128)(2,1)S(1)}, u32[]{:S(2)}, u32[]{:S(2)}) collective-permute-start(bf16[256,128]{1,0:T(8,128)(2,1)S(1)} %get-tuple-element.48), channel_id=1, source_target_pairs={{0,0},{1,1},{2,32},{3,33},{4,64},{5,65},{6,96},{7,97},{8,128},{9,1... | collective-permute-start | bytes 196616 | tf_op jit(solution)/shard_map/ppermute | solution.py:429
  89.1 9.7 %collective-permute-done.12 = bf16[256,128]{1,0:T(8,128)(2,1)S(1)} collective-permute-done((bf16[256,128]{1,0:T(8,128)(2,1)S(1)}, bf16[256,128]{1,0:T(8,128)(2,1)S(1)}, u32[]{:S(2)}, u32[]{:S(2)}) %collective-permute-start.12) | collective-permute-done | bytes 65568 | tf_op jit(solution)/shard_map/ppermute | solution.py:429
  99.0 0.8 collective-permute-start.14
  99.8 0.4 collective-permute-done.13
  100.2 0.9 collective-permute-start.15
  101.1 1.9 collective-permute-done.14
  103.0 1.1 collective-permute-done.15
  104.1 1.2 collective-permute-start.16
  105.3 4.2 %collective-permute-start.19 = (bf16[4,128,128]{2,1,0:T(8,128)(2,1)S(1)}, bf16[4,128,128]{2,1,0:T(8,128)(2,1)S(1)}, u32[]{:S(2)}, u32[]{:S(2)}) collective-permute-start(bf16[4,128,128]{2,1,0:T(8,128)(2,1)S(1)} %pad_maximum_fusion.2.refs_1_), channel_id=1, source_target_pairs={{0,224},{32,0},{64,32},{96,64},{128,96},{160,128},{192,160},{224,1... | collective-permute-start | bytes 393224 | tf_op jit(solution)/shard_map/ppermute | solution.py:370
  109.6 4.3 %collective-permute-done.16.refs_2_ = bf16[4,128,128]{2,1,0:T(8,128)(2,1)S(1)} collective-permute-done((bf16[4,128,128]{2,1,0:T(8,128)(2,1)S(1)}, bf16[4,128,128]{2,1,0:T(8,128)(2,1)S(1)}, u32[]{:S(2)}, u32[]{:S(2)}) %collective-permute-start.16) | collective-permute-done | bytes 131104 | tf_op jit(solution)/shard_map/ppermute | solution.py:370
  113.9 3.2 %collective-permute-start.20 = (bf16[4,128,128]{2,1,0:T(8,128)(2,1)S(1)}, bf16[4,128,128]{2,1,0:T(8,128)(2,1)S(1)}, u32[]{:S(2)}, u32[]{:S(2)}) collective-permute-start(bf16[4,128,128]{2,1,0:T(8,128)(2,1)S(1)} %collective-permute-done.19.refs_6_), channel_id=1, source_target_pairs={{0,224},{32,0},{64,32},{96,64},{128,96},{160,128},{192,160},{224,1... | collective-permute-start | bytes 393224 | tf_op jit(solution)/shard_map/ppermute | solution.py:370
  117.1 4.9 %collective-permute-start.17 = (bf16[256,128]{1,0:T(8,128)(2,1)S(1)}, bf16[256,128]{1,0:T(8,128)(2,1)S(1)}, u32[]{:S(2)}, u32[]{:S(2)}) collective-permute-start(bf16[256,128]{1,0:T(8,128)(2,1)S(1)} %get-tuple-element.54), channel_id=1, source_target_pairs={{0,0},{1,1},{2,32},{3,33},{4,64},{5,65},{6,96},{7,97},{8,128},{9,1... | collective-permute-start | bytes 196616 | tf_op jit(solution)/shard_map/ppermute | solution.py:374
  122.0 7.7 %collective-permute-done.17 = bf16[256,128]{1,0:T(8,128)(2,1)S(1)} collective-permute-done((bf16[256,128]{1,0:T(8,128)(2,1)S(1)}, bf16[256,128]{1,0:T(8,128)(2,1)S(1)}, u32[]{:S(2)}, u32[]{:S(2)}) %collective-permute-start.17) | collective-permute-done | bytes 65568 | tf_op jit(solution)/shard_map/ppermute | solution.py:374
  129.9 0.4 collective-permute-start.22
  130.3 2.9 %collective-permute-start.23 = (bf16[4,128,128]{2,1,0:T(8,128)(2,1)S(1)}, bf16[4,128,128]{2,1,0:T(8,128)(2,1)S(1)}, u32[]{:S(2)}, u32[]{:S(2)}) collective-permute-start(bf16[4,128,128]{2,1,0:T(8,128)(2,1)S(1)} %collective-permute-done.20.refs_7_), channel_id=1, source_target_pairs={{0,224},{32,0},{64,32},{96,64},{128,96},{160,128},{192,160},{224,1... | collective-permute-start | bytes 393224 | tf_op jit(solution)/shard_map/ppermute | solution.py:370
  133.2 3.1 %collective-permute-done.21 = bf16[2,256,128]{2,1,0:T(8,128)(2,1)S(1)} collective-permute-done((bf16[2,256,128]{2,1,0:T(8,128)(2,1)S(1)}, bf16[2,256,128]{2,1,0:T(8,128)(2,1)S(1)}, u32[]{:S(2)}, u32[]{:S(2)}) %collective-permute-start.21) | collective-permute-done | bytes 131104 | tf_op jit(solution)/shard_map/ppermute | solution.py:366
  136.4 0.4 collective-permute-start.24
  137.1 2.0 collective-permute-start.26
  139.1 1.6 collective-permute-start.27
  140.7 1.1 collective-permute-start.28
  141.8 0.9 collective-permute-done.24.refs_5_
  142.8 6.7 %shard_map.43 = f32[512,1024]{1,0:T(8,128)} custom-call(bf16[8,4,128,128]{3,2,1,0:T(8,128)(2,1)} %bitcast.15, bf16[4,128,128]{2,1,0:T(8,128)(2,1)} %copy-done.11, bf16[4,128,128]{2,1,0:T(8,128)(2,1)} %copy-done.12, bf16[4,128,128]{2,1,0:T(8,128)(2,1)} %copy-done.14, bf16[4,128,128]{2,1,0:T(8,128)(2,1)} %copy-done.16, ...), custom_call_target="tpu_custom_call" | custom-call | flops 2147483648 | bytes 7340032 | tf_op jit(solution)/shard_map/pallas_call | solution.py:293
  149.5 1.1 collective-permute-done.28.refs_3_
  150.6 7.7 %all-to-all-start.2 = ((f32[8,64,1024]{2,1,0:T(8,128)}), f32[8,64,1024]{2,1,0:T(8,128)S(1)}, u32[]{:S(2)}, u32[]{:S(2)}) async-start(f32[8,64,1024]{2,1,0:T(8,128)} %bitcast.14), calls=%async_computation.2 | async-start | bytes 4194304 | tf_op jit(solution)/shard_map/all_to_all | solution.py:438
  158.3 0.5 collective-permute-start.30
  158.8 0.5 collective-permute-start.32
  159.3 0.5 collective-permute-done.29.refs_4_
  159.8 0.4 collective-permute-done.30.refs_5_
  160.2 0.7 copy-done.1
  160.9 0.7 copy-done.3
  161.6 0.7 copy-done.5
  162.3 18.0 %all-to-all-done.2.parts = f32[8,64,1024]{2,1,0:T(8,128)S(1)} async-done(((f32[8,64,1024]{2,1,0:T(8,128)}), f32[8,64,1024]{2,1,0:T(8,128)S(1)}, u32[]{:S(2)}, u32[]{:S(2)}) %all-to-all-start.2) | async-done | bytes 2097184 | tf_op jit(solution)/shard_map/all_to_all | solution.py:438
  180.4 0.9 copy-done.2
  181.3 0.9 copy-done.4
  182.3 0.9 copy-done.6
  183.2 1.0 shard_map.44
  184.3 14.8 %all_to_all.25.parts = f32[4,4,32,128]{3,2,1,0:T(8,128)} all-to-all(f32[4,4,32,128]{3,2,1,0:T(8,128)S(1)} %shard_map.44), channel_id=1, replica_groups=mesh['zh'=4,'zl'=2,'yl'=2,'yh'=2,'x'=4,'c'=2] {'zl','yl'}, dimensions={0} | all-to-all | bytes 524288 | tf_op jit(solution)/shard_map/all_to_all | solution.py:439
  199.1 1.6 shard_map.45
  200.7 14.3 %all_to_all.26.parts = f32[4,32,128]{2,1,0:T(8,128)} all-to-all(f32[4,32,128]{2,1,0:T(8,128)} %shard_map.45), channel_id=1, replica_groups=mesh['zh'=4,'zl'=2,'yl'=2,'yh'=2,'x'=4,'c'=2] {'zh'}, dimensions={0} | all-to-all | bytes 131072 | tf_op jit(solution)/shard_map/all_to_all | solution.py:440
  214.9 1.5 shard_map.46
  (65 shorter events, 1.4 us)
Async XLA Ops:
  6.5 13.9 %collective-permute-start = (bf16[64,4096]{1,0:T(8,128)(2,1)}, bf16[64,4096]{1,0:T(8,128)(2,1)S(1)}, u32[]{:S(2)}, u32[]{:S(2)}) collective-permute-start(bf16[64,4096]{1,0:T(8,128)(2,1)} %refs_0_.1), channel_id=1, source_target_pairs={{0,16},{16,0},{1,17},{17,1},{2,18},{18,2},{3,19},{19,3},{4,20},{20... | collective-permute-start | bytes 1572872 | tf_op jit(solution)/shard_map/ppermute | solution.py:366
  7.8 13.8 %collective-permute-start.1 = (bf16[64,4096]{1,0:T(8,128)(2,1)}, bf16[64,4096]{1,0:T(8,128)(2,1)S(1)}, u32[]{:S(2)}, u32[]{:S(2)}) collective-permute-start(bf16[64,4096]{1,0:T(8,128)(2,1)} %refs_0_.1), channel_id=1, source_target_pairs={{0,32},{32,0},{1,33},{33,1},{2,34},{34,2},{3,35},{35,3},{4,36},{36... | collective-permute-start | bytes 1572872 | tf_op jit(solution)/shard_map/ppermute | solution.py:366
  9.7 22.9 %collective-permute-start.4 = (bf16[64,4096]{1,0:T(8,128)(2,1)}, bf16[64,4096]{1,0:T(8,128)(2,1)S(1)}, u32[]{:S(2)}, u32[]{:S(2)}) collective-permute-start(bf16[64,4096]{1,0:T(8,128)(2,1)} %refs_0_.1), channel_id=1, source_target_pairs={{0,1},{1,0},{2,3},{3,2},{4,5},{5,4},{6,7},{7,6},{8,9},{9,8},{10,11... | collective-permute-start | bytes 1572872 | tf_op jit(solution)/shard_map/ppermute | solution.py:366
  9.7 0.7 copy-start.8
  10.4 14.4 %copy-start.9 = (s32[4]{0:T(128)S(1)}, s32[4]{0:T(128)}, u32[]{:S(2)}) copy-start(s32[4]{0:T(128)} %words.5) | copy-start | bytes 52
  21.6 12.4 %collective-permute-start.5 = (bf16[64,4096]{1,0:T(8,128)(2,1)S(1)}, bf16[64,4096]{1,0:T(8,128)(2,1)S(1)}, u32[]{:S(2)}, u32[]{:S(2)}) collective-permute-start(bf16[64,4096]{1,0:T(8,128)(2,1)S(1)} %collective-permute-done.refs_1_), channel_id=1, source_target_pairs={{0,1},{1,0},{2,3},{3,2},{4,5},{5,4},{6,7},{7,6},{8,9},{9,8},{10,11... | collective-permute-start | bytes 1572872 | tf_op jit(solution)/shard_map/ppermute | solution.py:366
  21.8 12.3 %copy-start = (bf16[64,4096]{1,0:T(8,128)(2,1)S(1)}, bf16[64,4096]{1,0:T(8,128)(2,1)}, u32[]{:S(2)}) copy-start(bf16[64,4096]{1,0:T(8,128)(2,1)} %refs_0_.1) | copy-start | bytes 1572868
  21.8 12.2 %collective-permute-start.6 = (bf16[64,4096]{1,0:T(8,128)(2,1)S(1)}, bf16[64,4096]{1,0:T(8,128)(2,1)S(1)}, u32[]{:S(2)}, u32[]{:S(2)}) collective-permute-start(bf16[64,4096]{1,0:T(8,128)(2,1)S(1)} %collective-permute-done.1.refs_2_), channel_id=1, source_target_pairs={{0,1},{1,0},{2,3},{3,2},{4,5},{5,4},{6,7},{7,6},{8,9},{9,8},{10,11... | collective-permute-start | bytes 1572872 | tf_op jit(solution)/shard_map/ppermute | solution.py:366
  22.4 8.5 %collective-permute-start.2 = (bf16[32,4096]{1,0:T(8,128)(2,1)S(1)}, bf16[32,4096]{1,0:T(8,128)(2,1)S(1)}, u32[]{:S(2)}, u32[]{:S(2)}) collective-permute-start(bf16[32,4096]{1,0:T(8,128)(2,1)S(1)} %slice.6), channel_id=1, source_target_pairs={{0,32},{32,0},{1,33},{33,1},{2,34},{34,2},{3,35},{35,3},{4,36},{36... | collective-permute-start | bytes 786440 | tf_op jit(solution)/shard_map/ppermute | solution.py:366
  24.1 8.0 %collective-permute-start.3 = (bf16[32,4096]{1,0:T(8,128)(2,1)S(1)}, bf16[32,4096]{1,0:T(8,128)(2,1)S(1)}, u32[]{:S(2)}, u32[]{:S(2)}) collective-permute-start(bf16[32,4096]{1,0:T(8,128)(2,1)S(1)} %slice.7), channel_id=1, source_target_pairs={{0,16},{16,0},{1,17},{17,1},{2,18},{18,2},{3,19},{19,3},{4,20},{20... | collective-permute-start | bytes 786440 | tf_op jit(solution)/shard_map/ppermute | solution.py:366
  32.1 1.5 collective-permute-start.7
  32.1 1.9 collective-permute-start.8
  42.1 2.0 copy-start.7
  44.1 7.3 %copy-start.10 = (bf16[1024,1024]{1,0:T(8,128)(2,1)S(1)}, bf16[1024,1024]{1,0:T(8,128)(2,1)}, u32[]{:S(2)}) copy-start(bf16[1024,1024]{1,0:T(8,128)(2,1)} %refs_9_.1) | copy-start | bytes 6291460
  44.1 25.4 %all-to-all-start = ((f32[8,256,128]{2,1,0:T(8,128)}), f32[8,256,128]{2,1,0:T(8,128)S(1)}, u32[]{:S(2)}, u32[]{:S(2)}) async-start(f32[8,256,128]{2,1,0:T(8,128)} %get-tuple-element.43), calls=%async_computation | async-start | bytes 2097152 | tf_op jit(solution)/shard_map/all_to_all | solution.py:415
  51.4 91.4 %all-gather.3.cloned.1.call-start = ((), (), s32[]{:S(2)}) async-start(), calls=%async_computation.5 | async-start | bytes 1179648 | tf_op jit(solution)/shard_map/all_gather | solution.py:428
  51.4 90.5 %collective-permute-start.25 = (bf16[1024,1024]{1,0:T(8,128)(2,1)S(1)}, bf16[1024,1024]{1,0:T(8,128)(2,1)}, u32[]{:S(2)}, u32[]{:S(2)}) collective-permute-start(bf16[1024,1024]{1,0:T(8,128)(2,1)S(1)} %copy-done.10), channel_id=1, source_target_pairs={{0,1},{1,0},{2,3},{3,2},{4,5},{5,4},{6,7},{7,6},{8,9},{9,8},{10,11... | collective-permute-start | bytes 6291464 | tf_op jit(solution)/shard_map/ppermute | solution.py:366
  69.5 1.4 collective-permute-start.9
  70.1 4.0 %collective-permute-start.10 = (bf16[128,128]{1,0:T(8,128)(2,1)S(1)}, bf16[128,128]{1,0:T(8,128)(2,1)S(1)}, u32[]{:S(2)}, u32[]{:S(2)}) collective-permute-start(bf16[128,128]{1,0:T(8,128)(2,1)S(1)} %get-tuple-element.45), channel_id=1, source_target_pairs={{0,16},{16,0},{1,17},{17,1},{2,18},{18,2},{3,19},{19,3},{4,20},{20... | collective-permute-start | bytes 98312 | tf_op jit(solution)/shard_map/ppermute | solution.py:366
  71.0 3.9 %collective-permute-start.11 = (bf16[128,128]{1,0:T(8,128)(2,1)S(1)}, bf16[128,128]{1,0:T(8,128)(2,1)S(1)}, u32[]{:S(2)}, u32[]{:S(2)}) collective-permute-start(bf16[128,128]{1,0:T(8,128)(2,1)S(1)} %collective-permute-done.9), channel_id=1, source_target_pairs={{0,16},{16,0},{1,17},{17,1},{2,18},{18,2},{3,19},{19,3},{4,20},{20... | collective-permute-start | bytes 98312 | tf_op jit(solution)/shard_map/ppermute | solution.py:366
  75.6 23.2 %all-to-all-start.1 = ((f32[8,256,128]{2,1,0:T(8,128)}), f32[8,256,128]{2,1,0:T(8,128)S(1)}, u32[]{:S(2)}, u32[]{:S(2)}) async-start(f32[8,256,128]{2,1,0:T(8,128)} %shard_map.40), calls=%async_computation.1 | async-start | bytes 2097152 | tf_op jit(solution)/shard_map/all_to_all | solution.py:418
  82.8 16.0 %collective-permute-start.12 = (bf16[256,128]{1,0:T(8,128)(2,1)S(1)}, bf16[256,128]{1,0:T(8,128)(2,1)S(1)}, u32[]{:S(2)}, u32[]{:S(2)}) collective-permute-start(bf16[256,128]{1,0:T(8,128)(2,1)S(1)} %get-tuple-element.48), channel_id=1, source_target_pairs={{0,0},{1,1},{2,32},{3,33},{4,64},{5,65},{6,96},{7,97},{8,128},{9,1... | collective-permute-start | bytes 196616 | tf_op jit(solution)/shard_map/ppermute | solution.py:429
  98.9 1.3 collective-permute-start.13
  99.0 4.1 %collective-permute-start.14 = (bf16[128,128]{1,0:T(8,128)(2,1)S(1)}, bf16[128,128]{1,0:T(8,128)(2,1)S(1)}, u32[]{:S(2)}, u32[]{:S(2)}) collective-permute-start(bf16[128,128]{1,0:T(8,128)(2,1)S(1)} %get-tuple-element.51), channel_id=1, source_target_pairs={{0,16},{16,0},{1,17},{17,1},{2,18},{18,2},{3,19},{19,3},{4,20},{20... | collective-permute-start | bytes 98312 | tf_op jit(solution)/shard_map/ppermute | solution.py:366
  100.2 3.9 %collective-permute-start.15 = (bf16[128,128]{1,0:T(8,128)(2,1)S(1)}, bf16[128,128]{1,0:T(8,128)(2,1)S(1)}, u32[]{:S(2)}, u32[]{:S(2)}) collective-permute-start(bf16[128,128]{1,0:T(8,128)(2,1)S(1)} %collective-permute-done.13), channel_id=1, source_target_pairs={{0,16},{16,0},{1,17},{17,1},{2,18},{18,2},{3,19},{19,3},{4,20},{20... | collective-permute-start | bytes 98312 | tf_op jit(solution)/shard_map/ppermute | solution.py:366
  104.1 38.6 %copy-start.11 = (bf16[4,128,128]{2,1,0:T(8,128)(2,1)}, bf16[4,128,128]{2,1,0:T(8,128)(2,1)S(1)}, u32[]{:S(2)}) copy-start(bf16[4,128,128]{2,1,0:T(8,128)(2,1)S(1)} %pad_maximum_fusion.2.refs_1_) | copy-start | bytes 393220
  104.1 9.7 %collective-permute-start.16 = (bf16[4,128,128]{2,1,0:T(8,128)(2,1)S(1)}, bf16[4,128,128]{2,1,0:T(8,128)(2,1)S(1)}, u32[]{:S(2)}, u32[]{:S(2)}) collective-permute-start(bf16[4,128,128]{2,1,0:T(8,128)(2,1)S(1)} %pad_maximum_fusion.2.refs_1_), channel_id=1, source_target_pairs={{0,32},{32,64},{64,96},{96,128},{128,160},{160,192},{192,224},{224... | collective-permute-start | bytes 393224 | tf_op jit(solution)/shard_map/ppermute | solution.py:370
  105.3 8.5 %collective-permute-start.19 = (bf16[4,128,128]{2,1,0:T(8,128)(2,1)S(1)}, bf16[4,128,128]{2,1,0:T(8,128)(2,1)S(1)}, u32[]{:S(2)}, u32[]{:S(2)}) collective-permute-start(bf16[4,128,128]{2,1,0:T(8,128)(2,1)S(1)} %pad_maximum_fusion.2.refs_1_), channel_id=1, source_target_pairs={{0,224},{32,0},{64,32},{96,64},{128,96},{160,128},{192,160},{224,1... | collective-permute-start | bytes 393224 | tf_op jit(solution)/shard_map/ppermute | solution.py:370
  113.8 28.9 %copy-start.12 = (bf16[4,128,128]{2,1,0:T(8,128)(2,1)}, bf16[4,128,128]{2,1,0:T(8,128)(2,1)S(1)}, u32[]{:S(2)}) copy-start(bf16[4,128,128]{2,1,0:T(8,128)(2,1)S(1)} %collective-permute-done.16.refs_2_) | copy-start | bytes 393220
  113.8 15.9 %collective-permute-start.18 = (bf16[4,128,128]{2,1,0:T(8,128)(2,1)S(1)}, bf16[4,128,128]{2,1,0:T(8,128)(2,1)S(1)}, u32[]{:S(2)}, u32[]{:S(2)}) collective-permute-start(bf16[4,128,128]{2,1,0:T(8,128)(2,1)S(1)} %collective-permute-done.16.refs_2_), channel_id=1, source_target_pairs={{0,32},{32,64},{64,96},{96,128},{128,160},{160,192},{192,224},{224... | collective-permute-start | bytes 393224 | tf_op jit(solution)/shard_map/ppermute | solution.py:370
  113.8 28.9 %copy-start.13 = (bf16[4,128,128]{2,1,0:T(8,128)(2,1)}, bf16[4,128,128]{2,1,0:T(8,128)(2,1)S(1)}, u32[]{:S(2)}) copy-start(bf16[4,128,128]{2,1,0:T(8,128)(2,1)S(1)} %collective-permute-done.19.refs_6_) | copy-start | bytes 393220
  113.9 15.9 %collective-permute-start.20 = (bf16[4,128,128]{2,1,0:T(8,128)(2,1)S(1)}, bf16[4,128,128]{2,1,0:T(8,128)(2,1)S(1)}, u32[]{:S(2)}, u32[]{:S(2)}) collective-permute-start(bf16[4,128,128]{2,1,0:T(8,128)(2,1)S(1)} %collective-permute-done.19.refs_6_), channel_id=1, source_target_pairs={{0,224},{32,0},{64,32},{96,64},{128,96},{160,128},{192,160},{224,1... | collective-permute-start | bytes 393224 | tf_op jit(solution)/shard_map/ppermute | solution.py:370
  117.1 12.7 %collective-permute-start.17 = (bf16[256,128]{1,0:T(8,128)(2,1)S(1)}, bf16[256,128]{1,0:T(8,128)(2,1)S(1)}, u32[]{:S(2)}, u32[]{:S(2)}) collective-permute-start(bf16[256,128]{1,0:T(8,128)(2,1)S(1)} %get-tuple-element.54), channel_id=1, source_target_pairs={{0,0},{1,1},{2,32},{3,33},{4,64},{5,65},{6,96},{7,97},{8,128},{9,1... | collective-permute-start | bytes 196616 | tf_op jit(solution)/shard_map/ppermute | solution.py:374
  129.7 6.6 %copy-start.14 = (bf16[4,128,128]{2,1,0:T(8,128)(2,1)}, bf16[4,128,128]{2,1,0:T(8,128)(2,1)S(1)}, u32[]{:S(2)}) copy-start(bf16[4,128,128]{2,1,0:T(8,128)(2,1)S(1)} %collective-permute-done.18.refs_3_) | copy-start | bytes 393220
  129.7 6.6 %copy-start.15 = (bf16[4,128,128]{2,1,0:T(8,128)(2,1)}, bf16[4,128,128]{2,1,0:T(8,128)(2,1)S(1)}, u32[]{:S(2)}) copy-start(bf16[4,128,128]{2,1,0:T(8,128)(2,1)S(1)} %collective-permute-done.20.refs_7_) | copy-start | bytes 393220
  129.8 6.6 %collective-permute-start.21 = (bf16[2,256,128]{2,1,0:T(8,128)(2,1)S(1)}, bf16[2,256,128]{2,1,0:T(8,128)(2,1)S(1)}, u32[]{:S(2)}, u32[]{:S(2)}) collective-permute-start(bf16[2,256,128]{2,1,0:T(8,128)(2,1)S(1)} %pad_maximum_fusion.3), channel_id=1, source_target_pairs={{0,8},{8,0},{1,9},{9,1},{2,10},{10,2},{3,11},{11,3},{4,12},{12,4},... | collective-permute-start | bytes 393224 | tf_op jit(solution)/shard_map/ppermute | solution.py:366
  129.9 6.5 %collective-permute-start.22 = (bf16[4,128,128]{2,1,0:T(8,128)(2,1)S(1)}, bf16[4,128,128]{2,1,0:T(8,128)(2,1)S(1)}, u32[]{:S(2)}, u32[]{:S(2)}) collective-permute-start(bf16[4,128,128]{2,1,0:T(8,128)(2,1)S(1)} %collective-permute-done.18.refs_3_), channel_id=1, source_target_pairs={{0,32},{32,64},{64,96},{96,128},{128,160},{160,192},{192,224},{224... | collective-permute-start | bytes 393224 | tf_op jit(solution)/shard_map/ppermute | solution.py:370
  130.3 6.1 %collective-permute-start.23 = (bf16[4,128,128]{2,1,0:T(8,128)(2,1)S(1)}, bf16[4,128,128]{2,1,0:T(8,128)(2,1)S(1)}, u32[]{:S(2)}, u32[]{:S(2)}) collective-permute-start(bf16[4,128,128]{2,1,0:T(8,128)(2,1)S(1)} %collective-permute-done.20.refs_7_), channel_id=1, source_target_pairs={{0,224},{32,0},{64,32},{96,64},{128,96},{160,128},{192,160},{224,1... | collective-permute-start | bytes 393224 | tf_op jit(solution)/shard_map/ppermute | solution.py:370
  136.3 5.5 %copy-start.16 = (bf16[4,128,128]{2,1,0:T(8,128)(2,1)}, bf16[4,128,128]{2,1,0:T(8,128)(2,1)S(1)}, u32[]{:S(2)}) copy-start(bf16[4,128,128]{2,1,0:T(8,128)(2,1)S(1)} %collective-permute-done.22.refs_4_) | copy-start | bytes 393220
  136.4 0.7 copy-start.17
  136.4 6.4 %collective-permute-start.24 = (bf16[4,128,128]{2,1,0:T(8,128)(2,1)S(1)}, bf16[4,128,128]{2,1,0:T(8,128)(2,1)}, u32[]{:S(2)}, u32[]{:S(2)}) collective-permute-start(bf16[4,128,128]{2,1,0:T(8,128)(2,1)S(1)} %collective-permute-done.22.refs_4_), channel_id=1, source_target_pairs={{0,32},{32,64},{64,96},{96,128},{128,160},{160,192},{192,224},{224... | collective-permute-start | bytes 393224 | tf_op jit(solution)/shard_map/ppermute | solution.py:370
  137.1 12.4 %collective-permute-start.26 = (bf16[4,256,128]{2,1,0:T(8,128)(2,1)S(1)}, bf16[4,256,128]{2,1,0:T(8,128)(2,1)S(1)}, u32[]{:S(2)}, u32[]{:S(2)}) collective-permute-start(bf16[4,256,128]{2,1,0:T(8,128)(2,1)S(1)} %pad_maximum_fusion.refs_0_), channel_id=1, source_target_pairs={{0,2},{2,4},{4,6},{6,0},{1,3},{3,5},{5,7},{7,1},{8,10},{10,12},{12... | collective-permute-start | bytes 786440 | tf_op jit(solution)/shard_map/ppermute | solution.py:389
  139.1 10.4 %collective-permute-start.27 = (bf16[4,256,128]{2,1,0:T(8,128)(2,1)S(1)}, bf16[4,256,128]{2,1,0:T(8,128)(2,1)S(1)}, u32[]{:S(2)}, u32[]{:S(2)}) collective-permute-start(bf16[4,256,128]{2,1,0:T(8,128)(2,1)S(1)} %pad_maximum_fusion.refs_0_), channel_id=1, source_target_pairs={{0,4},{2,6},{4,0},{6,2},{1,5},{3,7},{5,1},{7,3},{8,12},{10,14},{12... | collective-permute-start | bytes 786440 | tf_op jit(solution)/shard_map/ppermute | solution.py:389
  140.7 9.9 %collective-permute-start.28 = (bf16[4,256,128]{2,1,0:T(8,128)(2,1)S(1)}, bf16[4,256,128]{2,1,0:T(8,128)(2,1)S(1)}, u32[]{:S(2)}, u32[]{:S(2)}) collective-permute-start(bf16[4,256,128]{2,1,0:T(8,128)(2,1)S(1)} %pad_maximum_fusion.refs_0_), channel_id=1, source_target_pairs={{0,6},{2,0},{4,2},{6,4},{1,7},{3,1},{5,3},{7,5},{8,14},{10,8},{12,... | collective-permute-start | bytes 786440 | tf_op jit(solution)/shard_map/ppermute | solution.py:389
  150.6 29.8 %all-to-all-start.2 = ((f32[8,64,1024]{2,1,0:T(8,128)}), f32[8,64,1024]{2,1,0:T(8,128)S(1)}, u32[]{:S(2)}, u32[]{:S(2)}) async-start(f32[8,64,1024]{2,1,0:T(8,128)} %bitcast.14), calls=%async_computation.2 | async-start | bytes 4194304 | tf_op jit(solution)/shard_map/all_to_all | solution.py:438
  158.3 1.5 collective-permute-start.29
  158.3 1.9 collective-permute-start.30
  158.8 2.1 collective-permute-start.31
  158.8 2.8 %collective-permute-start.32 = (bf16[4,256,128]{2,1,0:T(8,128)(2,1)S(1)}, bf16[4,256,128]{2,1,0:T(8,128)(2,1)S(1)}, u32[]{:S(2)}, u32[]{:S(2)}) collective-permute-start(bf16[4,256,128]{2,1,0:T(8,128)(2,1)S(1)} %collective-permute-done.28.refs_3_), channel_id=1, source_target_pairs={{0,1},{1,0},{2,3},{3,2},{4,5},{5,4},{6,7},{7,6},{8,9},{9,8},{10,11... | collective-permute-start | bytes 786440 | tf_op jit(solution)/shard_map/ppermute | solution.py:366
  160.2 0.7 copy-start.1
  160.9 0.7 copy-start.3
  161.6 0.7 copy-start.5
  180.4 1.0 copy-start.2
  181.3 0.9 copy-start.4
  182.3 0.9 copy-start.6
Sparse Core Ops, SparseCore 0:
  75.7 42.0 all-gather.2

commit v7 on v6

--- a/solution.py
+++ b/solution.py
@@ -305,8 +305,21 @@
     )(low, *high, mine, other)
 
 
+def join_kernel(*refs):
+    for index, ref in enumerate(refs[:-1]):
+        refs[-1][index] = ref[...]
+
+
+def join(values):
+    return pl.pallas_call(
+        join_kernel,
+        out_shape=jax.ShapeDtypeStruct((len(values),) + values[0].shape, values[0].dtype),
+        compiler_params=pltpu.CompilerParams(vmem_limit_bytes=6 << 20),
+    )(*values)
+
+
 def pair_kernel(parts, *refs):
-    features, (out, rows, pairs) = refs[:8], refs[8:]
+    features, (out, rows, pairs) = refs[:2], refs[2:]
     yh, x, core = (lax.axis_index(name) for name in PAR)
     total = parts[0]
     for index in range(1, parts.shape[0]):
@@ -320,10 +333,10 @@
             value = None
             for flip_core in range(2):
                 start = pl.multiple_of(((place & 1) * 2 + (core ^ flip_core)) * 256, 256)
-                held = features[flip_core * 4 + shift]
+                held = features[flip_core].at[shift, flip_yh]
                 term = lax.dot_general(
                     rows[:, pl.ds(start, 256)],
-                    jnp.concatenate([held[flip_yh * 2], held[flip_yh * 2 + 1]], axis=1),
+                    jnp.concatenate([held[0], held[1]], axis=1),
                     (((1,), (1,)), ((), ())),
                     preferred_element_type=F32,
                 )
@@ -331,29 +344,24 @@
             pairs[:, pl.ds(pl.multiple_of(zh * 256, 256), 256)] += value
     for block in range(16):
         piece = pairs[:, block * 64 : (block + 1) * 64]
-        out[block % 4, block // 4, :, :64] = piece[:32]
-        out[block % 4, block // 4, :, 64:] = piece[32:]
-
-
-def pair(parts, features):
+        out[block, :, :64] = piece[:32]
+        out[block, :, 64:] = piece[32:]
+
+
+def pair(parts, near, far):
     return pl.pallas_call(
         pair_kernel,
-        out_shape=jax.ShapeDtypeStruct((4, 4, 32, 128), F32),
+        out_shape=jax.ShapeDtypeStruct((16, 32, 128), F32),
         scratch_shapes=[pltpu.VMEM((64, 1024), BF16), pltpu.VMEM((64, 1024), F32)],
         compiler_params=pltpu.CompilerParams(vmem_limit_bytes=12 << 20),
-    )(parts, *features)
-
-
-def add_kernel(parts, out):
-    out[...] = (parts[0] + parts[1]) + (parts[2] + parts[3])
-
-
-def add(parts):
-    return pl.pallas_call(add_kernel, out_shape=jax.ShapeDtypeStruct(parts.shape[1:], F32))(parts)
+    )(parts, near, far)
 
 
 def finish_kernel(parts, out):
-    total = ((parts[0] + parts[1]) + (parts[2] + parts[3])) * SCALE
+    total = parts[0]
+    for index in range(1, parts.shape[0]):
+        total += parts[index]
+    total = total * SCALE
     out[:32] = total[:, :64]
     out[32:] = total[:, 64:]
 
@@ -370,29 +378,19 @@
     return lax.ppermute(value, ("zh", "zl"), [(i, (i + by) % 8) for i in range(8)])
 
 
-def ring_and_turn(value, earlier, piece, route):
-    turned = lax.ppermute(piece, EX + PAR, route)
+def ring(value):
     up = [step_z(value, 1)]
     down = [step_z(value, 7)]
-    up.append(step_z(up[0], 1))
-    down.append(step_z(down[0], 7))
-    turned, up[1], down[1] = lax.optimization_barrier((turned, up[1], down[1]))
-    both = jnp.stack([earlier, turned])
-    flipped = swap(both, "yh")
-    up.append(step_z(up[1], 1))
-    down.append(step_z(down[1], 7))
-    flipped, up[2], down[2] = lax.optimization_barrier((flipped, up[2], down[2]))
-    up.append(step_z(up[2], 1))
-    four = jnp.concatenate([both, flipped])
-    along_x = [four]
-    for by in range(1, 4):
-        along_x.append(lax.ppermute(four, "x", [(i, (i + by) % 4) for i in range(4)]))
-    return [value] + up + down, along_x
+    for _ in range(2):
+        up.append(step_z(up[-1], 1))
+        down.append(step_z(down[-1], 7))
+    up.append(step_z(up[-1], 1))
+    return [value] + up + down
 
 
 def flips(keep, send):
     received = swap(send, "c")
-    return jnp.stack([keep, received, swap(keep, "yl"), swap(received, "yl")])
+    return join([keep, received, swap(keep, "yl"), swap(received, "yl")])
 
 
 def per_device(gradients, inverse_gram, hash_words):
@@ -430,14 +428,19 @@
     next_part, mine, turned = lax.optimization_barrier((next_part, mine, turned))
     whole, keep, send = sum_parts(next_part)
     whole, mine = lax.optimization_barrier((whole, flips(keep, send)))
-    high, near = ring_and_turn(mine, turned, whole, route)
-
+    whole, high = lax.optimization_barrier((whole, ring(mine)))
+    next_turned = lax.ppermute(whole, EX + PAR, route)
     conditioned = condition(low, high, inverse_gram, other_tile)
-    conditioned, near = lax.optimization_barrier((conditioned, near))
-    far = [swap(v, "c") for v in near]
+    conditioned, next_turned = lax.optimization_barrier((conditioned, next_turned))
     parts = lax.all_to_all(conditioned.reshape(8, 64, 1024), CHIPS, 0, 0, tiled=True)
-    scores = add(lax.all_to_all(pair(parts, near + far), ("zl", "yl"), 0, 0, tiled=True))
-    return finish(lax.all_to_all(scores, "zh", 0, 0, tiled=True))
+
+    both = join([turned, next_turned])
+    four = join([both, swap(both, "yh")])
+    near = [four]
+    for by in range(1, 4):
+        near.append(lax.ppermute(four, "x", [(i, (i + by) % 4) for i in range(4)]))
+    near = join(near)
+    return finish(lax.all_to_all(pair(parts, near, swap(near, "c")), EX, 0, 0, tiled=True))
 
 
 def solution(mesh):

time: 224 us -> 223 us (level); the launches traced: 223 us -> 219 us
  waiting for transfers between devices: 56.1 us -> 71.5 us
  blocking collectives: 29.1 us -> 17.7 us
  starting transfers between devices: 62.9 us -> 59.2 us
  local copies, waits for them, and re-layouts: 7.99 us -> 4.91 us
    ppermute x21 -> x18, waiting for transfers between devices: 14.4 us -> 33.6 us  [swap(): return lax.ppermute(value, axis, [(0, 1), (1, 0)])]
    all_to_all x1, waiting for transfers between devices: 18 us -> 0.01 us  [per_device(): lax.all_to_all(conditioned.reshape(8, 64, 1024), CHIPS, 0, 0, tiled=True)]
    all_to_all x2 -> x1, blocking collectives: 29.1 us -> 17.7 us  [per_device(): lax.all_to_all(pair(parts, near, swap(near, 'c')), EX, 0, 0, tiled=True)]
    ppermute x7, waiting for transfers between devices: 5.18 us -> 16.3 us  [step_z(): lax.ppermute(value, ('zh', 'zl'), [(i, (i + by) % 8) for i in range(8)])]
    unnamed x36 -> x28, local copies, waits for them, and re-layouts: 7.95 us -> 4.87 us
    ppermute x4, waiting for transfers between devices: 8.76 us -> 11.8 us  [the longest x3 10.8 us: per_device(): near.append(lax.ppermute(four, 'x', [(i, (i + by) % 4) for i in range(4)]))]
    ppermute x21 -> x18, starting transfers between devices: 12.4 us -> 11.9 us  [swap(): return lax.ppermute(value, axis, [(0, 1), (1, 0)])]
  transfers between devices with their start and end apart: 37 -> 34, of which waited for: 20 -> 22; matrix products, arithmetic and copies ran while one was open for 0% -> 0% of each run, Pallas kernels for 18% -> 19%
where the time goes in v7:
time: 223 us; the launch traced here: 219 us
  waiting for transfers between devices  71.5 us (32%)
  starting transfers between devices  59.2 us (27%)
  Pallas kernels  52 us (23%)
  blocking collectives  17.7 us (8%)
  between operations  13.7 us (6%)
  local copies, waits for them, and re-layouts  4.91 us (2%)
    ppermute x18, waiting for transfers between devices, swap(): return lax.ppermute(value, axis, [(0, 1), (1, 0)])  33.6 us
    pallas_call x1, Pallas kernels, project_hash(): pl.pallas_call(functools.partial(hash_kernel, part, width), out_shape=jax...  17.9 us
    all_to_all x1, blocking collectives, per_device(): lax.all_to_all(pair(parts, near, swap(near, 'c')), EX, 0, 0, tiled=True)  17.7 us
    ppermute x7, waiting for transfers between devices, step_z(): lax.ppermute(value, ('zh', 'zl'), [(i, (i + by) % 8) for i in range(8)])  16.3 us
    pallas_call x2, Pallas kernels, table(): pl.pallas_call(functools.partial(table_kernel, part, width, first, params...  15.8 us
    ppermute x18, starting transfers between devices, swap(): return lax.ppermute(value, axis, [(0, 1), (1, 0)])  11.9 us
    ppermute x7, starting transfers between devices, step_z(): lax.ppermute(value, ('zh', 'zl'), [(i, (i + by) % 8) for i in range(8)])  11.9 us
    ppermute x3, waiting for transfers between devices, per_device(): near.append(lax.ppermute(four, 'x', [(i, (i + by) % 4) for i in range(4)]))  10.8 us
  transfers between devices with their start and end apart: 34, of which 22 were waited for; matrix products, arithmetic and copies ran while one was open for 0% of the time, Pallas kernels for 19%

profile of v7, /device:TPU:22, one launch (start us, length us, event | category | flops | bytes accessed | tf_op | source)
XLA Modules:
  0.0 219.0 jit_solution(14843116339452554078)
XLA Ops:
  6.5 1.3 collective-permute-start
  7.8 1.9 collective-permute-start.1
  9.7 0.7 copy-done.5
  10.4 9.7 %shard_map.37.first = bf16[5120,1024]{1,0:T(8,128)(2,1)S(1)} custom-call(s32[4]{0:T(128)S(1)} %copy-done.5), custom_call_target="tpu_custom_call" | custom-call | flops 6291456000 | bytes 10485760 | tf_op jit(solution)/shard_map/pallas_call | solution.py:68
  20.1 0.3 collective-permute-done.refs_1_
  20.4 1.2 collective-permute-done.1.refs_2_
  21.6 0.1 collective-permute-start.5
  21.8 0.6 collective-permute-start.6
  22.4 1.7 collective-permute-start.2
  24.1 0.7 collective-permute-start.3
  24.8 6.0 %shard_map.38.second = bf16[3072,1024]{1,0:T(8,128)(2,1)S(1)} custom-call(s32[4]{0:T(128)S(1)} %copy-done.6), custom_call_target="tpu_custom_call" | custom-call | flops 3774873600 | bytes 6291456 | tf_op jit(solution)/shard_map/pallas_call | solution.py:68
  30.9 1.2 collective-permute-done.3.refs_4_
  32.1 0.5 collective-permute-start.8
  32.6 1.0 collective-permute-done.7.refs_8_
  33.6 0.4 collective-permute-done.8.refs_9_
  34.0 8.0 %shard_map.39 = (f32[8,256,128]{2,1,0:T(8,128)}, bf16[256,8192]{1,0:T(8,128)(2,1)S(1)}) custom-call(bf16[5120,1024]{1,0:T(8,128)(2,1)S(1)} %shard_map.37.first, bf16[3072,1024]{1,0:T(8,128)(2,1)S(1)} %shard_map.38.second, bf16[64,4096]{1,0:T(8,128)(2,1)S(1)} %copy-done.3, bf16[64,4096]{1,0:T(8,128)(2,1)S(1)} %collective-permute-done.refs_1_, ...), custom_call_target="tpu_custom_call" | custom-call | flops 4294967296 | bytes 16777216 | tf_op jit(solution)/shard_map/pallas_call | solution.py:140
  42.1 2.0 copy-done.4
  44.0 7.2 %all-to-all-start = ((f32[8,256,128]{2,1,0:T(8,128)}), f32[8,256,128]{2,1,0:T(8,128)S(1)}, u32[]{:S(2)}, u32[]{:S(2)}) async-start(f32[8,256,128]{2,1,0:T(8,128)} %get-tuple-element.43), calls=%async_computation | async-start | bytes 2097152 | tf_op jit(solution)/shard_map/all_to_all | solution.py:413
  51.2 17.9 %shard_map.40 = f32[8,256,128]{2,1,0:T(8,128)} custom-call(s32[4]{0:T(128)} %words.5, bf16[256,8192]{1,0:T(8,128)(2,1)} %copy-done.4), custom_call_target="tpu_custom_call" | custom-call | flops 4294967296 | bytes 16777216 | tf_op jit(solution)/shard_map/pallas_call | solution.py:199
  69.2 0.1 shard_map.41
  69.3 0.6 collective-permute-start.9
  69.8 0.7 collective-permute-start.10
  70.6 0.1 collective-permute-done.9.refs_1_
  70.7 1.2 collective-permute-start.11
  71.9 2.0 collective-permute-done.10.refs_2_
  73.8 0.8 collective-permute-done.11.refs_3_
  74.6 0.7 shard_map.42
  75.3 7.2 %all-to-all-start.1 = ((f32[8,256,128]{2,1,0:T(8,128)}), f32[8,256,128]{2,1,0:T(8,128)S(1)}, u32[]{:S(2)}, u32[]{:S(2)}) async-start(f32[8,256,128]{2,1,0:T(8,128)} %shard_map.40), calls=%async_computation.1 | async-start | bytes 2097152 | tf_op jit(solution)/shard_map/all_to_all | solution.py:416
  82.5 6.3 %collective-permute-start.12 = (bf16[256,128]{1,0:T(8,128)(2,1)S(1)}, bf16[256,128]{1,0:T(8,128)(2,1)S(1)}, u32[]{:S(2)}, u32[]{:S(2)}) collective-permute-start(bf16[256,128]{1,0:T(8,128)(2,1)S(1)} %get-tuple-element.48), channel_id=1, source_target_pairs={{0,0},{1,1},{2,32},{3,33},{4,64},{5,65},{6,96},{7,97},{8,128},{9,1... | collective-permute-start | bytes 196616 | tf_op jit(solution)/shard_map/ppermute | solution.py:427
  88.8 9.7 %collective-permute-done.12.refs_0_ = bf16[256,128]{1,0:T(8,128)(2,1)S(1)} collective-permute-done((bf16[256,128]{1,0:T(8,128)(2,1)S(1)}, bf16[256,128]{1,0:T(8,128)(2,1)S(1)}, u32[]{:S(2)}, u32[]{:S(2)}) %collective-permute-start.12) | collective-permute-done | bytes 65568 | tf_op jit(solution)/shard_map/ppermute | solution.py:427
  98.6 0.1 collective-permute-start.13
  98.7 0.8 collective-permute-start.14
  99.5 0.4 collective-permute-done.13.refs_1_
  99.9 0.9 collective-permute-start.15
  100.8 1.9 collective-permute-done.14.refs_2_
  102.7 1.1 collective-permute-done.15.refs_3_
  103.8 1.2 collective-permute-start.16
  105.0 4.2 %collective-permute-start.20 = (bf16[4,128,128]{2,1,0:T(8,128)(2,1)S(1)}, bf16[4,128,128]{2,1,0:T(8,128)(2,1)S(1)}, u32[]{:S(2)}, u32[]{:S(2)}) collective-permute-start(bf16[4,128,128]{2,1,0:T(8,128)(2,1)S(1)} %shard_map.44.refs_1_), channel_id=1, source_target_pairs={{0,224},{32,0},{64,32},{96,64},{128,96},{160,128},{192,160},{224,1... | collective-permute-start | bytes 393224 | tf_op jit(solution)/shard_map/ppermute | solution.py:378
  109.3 4.3 %collective-permute-done.16.refs_2_ = bf16[4,128,128]{2,1,0:T(8,128)(2,1)S(1)} collective-permute-done((bf16[4,128,128]{2,1,0:T(8,128)(2,1)S(1)}, bf16[4,128,128]{2,1,0:T(8,128)(2,1)S(1)}, u32[]{:S(2)}, u32[]{:S(2)}) %collective-permute-start.16) | collective-permute-done | bytes 131104 | tf_op jit(solution)/shard_map/ppermute | solution.py:378
  113.6 3.2 %collective-permute-start.21 = (bf16[4,128,128]{2,1,0:T(8,128)(2,1)S(1)}, bf16[4,128,128]{2,1,0:T(8,128)(2,1)S(1)}, u32[]{:S(2)}, u32[]{:S(2)}) collective-permute-start(bf16[4,128,128]{2,1,0:T(8,128)(2,1)S(1)} %collective-permute-done.20.refs_6_), channel_id=1, source_target_pairs={{0,224},{32,0},{64,32},{96,64},{128,96},{160,128},{192,160},{224,1... | collective-permute-start | bytes 393224 | tf_op jit(solution)/shard_map/ppermute | solution.py:378
  116.8 2.9 %collective-permute-done.17.refs_3_ = bf16[4,128,128]{2,1,0:T(8,128)(2,1)S(1)} collective-permute-done((bf16[4,128,128]{2,1,0:T(8,128)(2,1)S(1)}, bf16[4,128,128]{2,1,0:T(8,128)(2,1)S(1)}, u32[]{:S(2)}, u32[]{:S(2)}) %collective-permute-start.17) | collective-permute-done | bytes 131104 | tf_op jit(solution)/shard_map/ppermute | solution.py:378
  119.7 3.2 %collective-permute-start.22 = (bf16[4,128,128]{2,1,0:T(8,128)(2,1)S(1)}, bf16[4,128,128]{2,1,0:T(8,128)(2,1)S(1)}, u32[]{:S(2)}, u32[]{:S(2)}) collective-permute-start(bf16[4,128,128]{2,1,0:T(8,128)(2,1)S(1)} %collective-permute-done.21.refs_7_), channel_id=1, source_target_pairs={{0,224},{32,0},{64,32},{96,64},{128,96},{160,128},{192,160},{224,1... | collective-permute-start | bytes 393224 | tf_op jit(solution)/shard_map/ppermute | solution.py:378
  123.0 2.9 %collective-permute-done.18.refs_4_ = bf16[4,128,128]{2,1,0:T(8,128)(2,1)S(1)} collective-permute-done((bf16[4,128,128]{2,1,0:T(8,128)(2,1)S(1)}, bf16[4,128,128]{2,1,0:T(8,128)(2,1)S(1)}, u32[]{:S(2)}, u32[]{:S(2)}) %collective-permute-start.18) | collective-permute-done | bytes 131104 | tf_op jit(solution)/shard_map/ppermute | solution.py:378
  125.9 6.2 %collective-permute-done.19.refs_5_ = bf16[4,128,128]{2,1,0:T(8,128)(2,1)S(1)} collective-permute-done((bf16[4,128,128]{2,1,0:T(8,128)(2,1)S(1)}, bf16[4,128,128]{2,1,0:T(8,128)(2,1)S(1)}, u32[]{:S(2)}, u32[]{:S(2)}) %collective-permute-start.19) | collective-permute-done | bytes 131104 | tf_op jit(solution)/shard_map/ppermute | solution.py:378
  132.1 4.4 %collective-permute-start.24 = (bf16[256,128]{1,0:T(8,128)(2,1)S(1)}, bf16[256,128]{1,0:T(8,128)(2,1)S(1)}, u32[]{:S(2)}, u32[]{:S(2)}) collective-permute-start(bf16[256,128]{1,0:T(8,128)(2,1)S(1)} %get-tuple-element.63), channel_id=1, source_target_pairs={{0,0},{1,1},{2,32},{3,33},{4,64},{5,65},{6,96},{7,97},{8,128},{9,1... | collective-permute-start | bytes 196616 | tf_op jit(solution)/shard_map/ppermute | solution.py:432
  136.7 6.7 %shard_map.45 = f32[512,1024]{1,0:T(8,128)} custom-call(bf16[8,4,128,128]{3,2,1,0:T(8,128)(2,1)} %bitcast.3, bf16[4,128,128]{2,1,0:T(8,128)(2,1)} %copy-done.2, bf16[4,128,128]{2,1,0:T(8,128)(2,1)} %copy-done.7, bf16[4,128,128]{2,1,0:T(8,128)(2,1)} %copy-done.9, bf16[4,128,128]{2,1,0:T(8,128)(2,1)} %copy-done.11, bf16[4,128,128]{2,1,0:T(8,128)(2,1)} %copy-done.13, ...), custom_call_target="tpu_custom_call" | custom-call | flops 2147483648 | bytes 7340032 | tf_op jit(solution)/shard_map/pallas_call | solution.py:293
  143.4 1.1 collective-permute-done.24.refs_1_
  144.5 7.0 %all-to-all-start.2 = ((f32[8,64,1024]{2,1,0:T(8,128)}), f32[8,64,1024]{2,1,0:T(8,128)S(1)}, u32[]{:S(2)}, u32[]{:S(2)}) async-start(f32[8,64,1024]{2,1,0:T(8,128)} %bitcast.2), calls=%async_computation.2 | async-start | bytes 4194304 | tf_op jit(solution)/shard_map/all_to_all | solution.py:435
  151.5 0.6 collective-permute-start.25
  152.2 20.6 %collective-permute-done.25.refs_1_ = bf16[2,256,128]{2,1,0:T(8,128)(2,1)S(1)} collective-permute-done((bf16[2,256,128]{2,1,0:T(8,128)(2,1)S(1)}, bf16[2,256,128]{2,1,0:T(8,128)(2,1)S(1)}, u32[]{:S(2)}, u32[]{:S(2)}) %collective-permute-start.25) | collective-permute-done | bytes 131104 | tf_op jit(solution)/shard_map/ppermute | solution.py:374
  172.8 0.1 collective-permute-start.26
  172.9 2.9 %collective-permute-start.27 = (bf16[2,2,256,128]{3,2,1,0:T(8,128)(2,1)S(1)}, bf16[2,2,256,128]{3,2,1,0:T(8,128)(2,1)S(1)}, u32[]{:S(2)}, u32[]{:S(2)}) collective-permute-start(bf16[2,2,256,128]{3,2,1,0:T(8,128)(2,1)S(1)} %shard_map.47.refs_0_), channel_id=1, source_target_pairs={{0,4},{2,6},{4,0},{6,2},{1,5},{3,7},{5,1},{7,3},{8,12},{10,14},{12... | collective-permute-start | bytes 786440 | tf_op jit(solution)/shard_map/ppermute | solution.py:441
  175.8 0.2 collective-permute-start.28
  176.0 6.1 %collective-permute-done.26.refs_1_ = bf16[2,2,256,128]{3,2,1,0:T(8,128)(2,1)S(1)} collective-permute-done((bf16[2,2,256,128]{3,2,1,0:T(8,128)(2,1)S(1)}, bf16[2,2,256,128]{3,2,1,0:T(8,128)(2,1)S(1)}, u32[]{:S(2)}, u32[]{:S(2)}) %collective-permute-start.26) | collective-permute-done | bytes 262176 | tf_op jit(solution)/shard_map/ppermute | solution.py:441
  182.1 1.6 collective-permute-done.27.refs_2_
  183.7 3.1 %collective-permute-done.28.refs_3_ = bf16[2,2,256,128]{3,2,1,0:T(8,128)(2,1)S(1)} collective-permute-done((bf16[2,2,256,128]{3,2,1,0:T(8,128)(2,1)S(1)}, bf16[2,2,256,128]{3,2,1,0:T(8,128)(2,1)S(1)}, u32[]{:S(2)}, u32[]{:S(2)}) %collective-permute-start.28) | collective-permute-done | bytes 262176 | tf_op jit(solution)/shard_map/ppermute | solution.py:441
  186.8 0.1 shard_map.48.refs_0_
  186.9 0.1 collective-permute-start.29
  187.0 2.6 %collective-permute-done.29.refs_1_ = bf16[4,2,2,256,128]{4,3,2,1,0:T(8,128)(2,1)S(1)} collective-permute-done((bf16[4,2,2,256,128]{4,3,2,1,0:T(8,128)(2,1)S(1)}, bf16[4,2,2,256,128]{4,3,2,1,0:T(8,128)(2,1)S(1)}, u32[]{:S(2)}, u32[]{:S(2)}) %collective-permute-start.29) | collective-permute-done | bytes 1048608 | tf_op jit(solution)/shard_map/ppermute | solution.py:374
  189.6 1.0 copy-done
  190.6 1.2 copy-done.1
  191.8 1.0 shard_map.49
  192.9 17.7 %all_to_all.20.parts = f32[16,32,128]{2,1,0:T(8,128)} all-to-all(f32[16,32,128]{2,1,0:T(8,128)S(1)} %shard_map.49), channel_id=1, replica_groups=mesh['zh'=4,'zl'=2,'yl'=2,'yh'=2,'x'=4,'c'=2] {'zh','zl','yl'}, dimensions={0} | all-to-all | bytes 524288 | tf_op jit(solution)/shard_map/all_to_all | solution.py:443
  210.5 1.7 shard_map.50
  (50 shorter events, 0.3 us)
Async XLA Ops:
  6.5 13.9 %collective-permute-start = (bf16[64,4096]{1,0:T(8,128)(2,1)}, bf16[64,4096]{1,0:T(8,128)(2,1)S(1)}, u32[]{:S(2)}, u32[]{:S(2)}) collective-permute-start(bf16[64,4096]{1,0:T(8,128)(2,1)} %refs_0_.1), channel_id=1, source_target_pairs={{0,16},{16,0},{1,17},{17,1},{2,18},{18,2},{3,19},{19,3},{4,20},{20... | collective-permute-start | bytes 1572872 | tf_op jit(solution)/shard_map/ppermute | solution.py:374
  7.8 13.8 %collective-permute-start.1 = (bf16[64,4096]{1,0:T(8,128)(2,1)}, bf16[64,4096]{1,0:T(8,128)(2,1)S(1)}, u32[]{:S(2)}, u32[]{:S(2)}) collective-permute-start(bf16[64,4096]{1,0:T(8,128)(2,1)} %refs_0_.1), channel_id=1, source_target_pairs={{0,32},{32,0},{1,33},{33,1},{2,34},{34,2},{3,35},{35,3},{4,36},{36... | collective-permute-start | bytes 1572872 | tf_op jit(solution)/shard_map/ppermute | solution.py:374
  9.7 22.9 %collective-permute-start.4 = (bf16[64,4096]{1,0:T(8,128)(2,1)}, bf16[64,4096]{1,0:T(8,128)(2,1)S(1)}, u32[]{:S(2)}, u32[]{:S(2)}) collective-permute-start(bf16[64,4096]{1,0:T(8,128)(2,1)} %refs_0_.1), channel_id=1, source_target_pairs={{0,1},{1,0},{2,3},{3,2},{4,5},{5,4},{6,7},{7,6},{8,9},{9,8},{10,11... | collective-permute-start | bytes 1572872 | tf_op jit(solution)/shard_map/ppermute | solution.py:374
  9.7 0.7 copy-start.5
  10.4 14.4 %copy-start.6 = (s32[4]{0:T(128)S(1)}, s32[4]{0:T(128)}, u32[]{:S(2)}) copy-start(s32[4]{0:T(128)} %words.5) | copy-start | bytes 52
  21.6 12.4 %collective-permute-start.5 = (bf16[64,4096]{1,0:T(8,128)(2,1)S(1)}, bf16[64,4096]{1,0:T(8,128)(2,1)S(1)}, u32[]{:S(2)}, u32[]{:S(2)}) collective-permute-start(bf16[64,4096]{1,0:T(8,128)(2,1)S(1)} %collective-permute-done.refs_1_), channel_id=1, source_target_pairs={{0,1},{1,0},{2,3},{3,2},{4,5},{5,4},{6,7},{7,6},{8,9},{9,8},{10,11... | collective-permute-start | bytes 1572872 | tf_op jit(solution)/shard_map/ppermute | solution.py:374
  21.8 12.3 %copy-start.3 = (bf16[64,4096]{1,0:T(8,128)(2,1)S(1)}, bf16[64,4096]{1,0:T(8,128)(2,1)}, u32[]{:S(2)}) copy-start(bf16[64,4096]{1,0:T(8,128)(2,1)} %refs_0_.1) | copy-start | bytes 1572868
  21.8 12.2 %collective-permute-start.6 = (bf16[64,4096]{1,0:T(8,128)(2,1)S(1)}, bf16[64,4096]{1,0:T(8,128)(2,1)S(1)}, u32[]{:S(2)}, u32[]{:S(2)}) collective-permute-start(bf16[64,4096]{1,0:T(8,128)(2,1)S(1)} %collective-permute-done.1.refs_2_), channel_id=1, source_target_pairs={{0,1},{1,0},{2,3},{3,2},{4,5},{5,4},{6,7},{7,6},{8,9},{9,8},{10,11... | collective-permute-start | bytes 1572872 | tf_op jit(solution)/shard_map/ppermute | solution.py:374
  22.4 8.5 %collective-permute-start.2 = (bf16[32,4096]{1,0:T(8,128)(2,1)S(1)}, bf16[32,4096]{1,0:T(8,128)(2,1)S(1)}, u32[]{:S(2)}, u32[]{:S(2)}) collective-permute-start(bf16[32,4096]{1,0:T(8,128)(2,1)S(1)} %slice.6), channel_id=1, source_target_pairs={{0,32},{32,0},{1,33},{33,1},{2,34},{34,2},{3,35},{35,3},{4,36},{36... | collective-permute-start | bytes 786440 | tf_op jit(solution)/shard_map/ppermute | solution.py:374
  24.1 8.0 %collective-permute-start.3 = (bf16[32,4096]{1,0:T(8,128)(2,1)S(1)}, bf16[32,4096]{1,0:T(8,128)(2,1)S(1)}, u32[]{:S(2)}, u32[]{:S(2)}) collective-permute-start(bf16[32,4096]{1,0:T(8,128)(2,1)S(1)} %slice.7), channel_id=1, source_target_pairs={{0,16},{16,0},{1,17},{17,1},{2,18},{18,2},{3,19},{19,3},{4,20},{20... | collective-permute-start | bytes 786440 | tf_op jit(solution)/shard_map/ppermute | solution.py:374
  32.1 1.5 collective-permute-start.7
  32.1 1.9 collective-permute-start.8
  42.0 2.0 copy-start.4
  44.0 25.2 %all-to-all-start = ((f32[8,256,128]{2,1,0:T(8,128)}), f32[8,256,128]{2,1,0:T(8,128)S(1)}, u32[]{:S(2)}, u32[]{:S(2)}) async-start(f32[8,256,128]{2,1,0:T(8,128)} %get-tuple-element.43), calls=%async_computation | async-start | bytes 2097152 | tf_op jit(solution)/shard_map/all_to_all | solution.py:413
  51.2 85.4 %all-gather.3.cloned.1.call-start = ((), (), s32[]{:S(2)}) async-start(), calls=%async_computation.4 | async-start | bytes 1179648 | tf_op jit(solution)/shard_map/all_gather | solution.py:426
  51.2 85.3 %collective-permute-start.23 = (bf16[1024,1024]{1,0:T(8,128)(2,1)}, bf16[1024,1024]{1,0:T(8,128)(2,1)}, u32[]{:S(2)}, u32[]{:S(2)}) collective-permute-start(bf16[1024,1024]{1,0:T(8,128)(2,1)} %refs_9_.1), channel_id=1, source_target_pairs={{0,1},{1,0},{2,3},{3,2},{4,5},{5,4},{6,7},{7,6},{8,9},{9,8},{10,11... | collective-permute-start | bytes 6291464 | tf_op jit(solution)/shard_map/ppermute | solution.py:374
  69.3 1.4 collective-permute-start.9
  69.8 4.0 %collective-permute-start.10 = (bf16[128,128]{1,0:T(8,128)(2,1)S(1)}, bf16[128,128]{1,0:T(8,128)(2,1)S(1)}, u32[]{:S(2)}, u32[]{:S(2)}) collective-permute-start(bf16[128,128]{1,0:T(8,128)(2,1)S(1)} %get-tuple-element.45.refs_0_), channel_id=1, source_target_pairs={{0,16},{16,0},{1,17},{17,1},{2,18},{18,2},{3,19},{19,3},{4,20},{20... | collective-permute-start | bytes 98312 | tf_op jit(solution)/shard_map/ppermute | solution.py:374
  70.7 3.9 %collective-permute-start.11 = (bf16[128,128]{1,0:T(8,128)(2,1)S(1)}, bf16[128,128]{1,0:T(8,128)(2,1)S(1)}, u32[]{:S(2)}, u32[]{:S(2)}) collective-permute-start(bf16[128,128]{1,0:T(8,128)(2,1)S(1)} %collective-permute-done.9.refs_1_), channel_id=1, source_target_pairs={{0,16},{16,0},{1,17},{17,1},{2,18},{18,2},{3,19},{19,3},{4,20},{20... | collective-permute-start | bytes 98312 | tf_op jit(solution)/shard_map/ppermute | solution.py:374
  75.3 23.3 %all-to-all-start.1 = ((f32[8,256,128]{2,1,0:T(8,128)}), f32[8,256,128]{2,1,0:T(8,128)S(1)}, u32[]{:S(2)}, u32[]{:S(2)}) async-start(f32[8,256,128]{2,1,0:T(8,128)} %shard_map.40), calls=%async_computation.1 | async-start | bytes 2097152 | tf_op jit(solution)/shard_map/all_to_all | solution.py:416
  82.5 16.0 %collective-permute-start.12 = (bf16[256,128]{1,0:T(8,128)(2,1)S(1)}, bf16[256,128]{1,0:T(8,128)(2,1)S(1)}, u32[]{:S(2)}, u32[]{:S(2)}) collective-permute-start(bf16[256,128]{1,0:T(8,128)(2,1)S(1)} %get-tuple-element.48), channel_id=1, source_target_pairs={{0,0},{1,1},{2,32},{3,33},{4,64},{5,65},{6,96},{7,97},{8,128},{9,1... | collective-permute-start | bytes 196616 | tf_op jit(solution)/shard_map/ppermute | solution.py:427
  98.6 1.3 collective-permute-start.13
  98.7 4.1 %collective-permute-start.14 = (bf16[128,128]{1,0:T(8,128)(2,1)S(1)}, bf16[128,128]{1,0:T(8,128)(2,1)S(1)}, u32[]{:S(2)}, u32[]{:S(2)}) collective-permute-start(bf16[128,128]{1,0:T(8,128)(2,1)S(1)} %get-tuple-element.51.refs_0_), channel_id=1, source_target_pairs={{0,16},{16,0},{1,17},{17,1},{2,18},{18,2},{3,19},{19,3},{4,20},{20... | collective-permute-start | bytes 98312 | tf_op jit(solution)/shard_map/ppermute | solution.py:374
  99.9 3.9 %collective-permute-start.15 = (bf16[128,128]{1,0:T(8,128)(2,1)S(1)}, bf16[128,128]{1,0:T(8,128)(2,1)S(1)}, u32[]{:S(2)}, u32[]{:S(2)}) collective-permute-start(bf16[128,128]{1,0:T(8,128)(2,1)S(1)} %collective-permute-done.13.refs_1_), channel_id=1, source_target_pairs={{0,16},{16,0},{1,17},{17,1},{2,18},{18,2},{3,19},{19,3},{4,20},{20... | collective-permute-start | bytes 98312 | tf_op jit(solution)/shard_map/ppermute | solution.py:374
  103.8 32.8 %copy-start.2 = (bf16[4,128,128]{2,1,0:T(8,128)(2,1)}, bf16[4,128,128]{2,1,0:T(8,128)(2,1)S(1)}, u32[]{:S(2)}) copy-start(bf16[4,128,128]{2,1,0:T(8,128)(2,1)S(1)} %shard_map.44.refs_1_) | copy-start | bytes 393220
  103.8 9.7 %collective-permute-start.16 = (bf16[4,128,128]{2,1,0:T(8,128)(2,1)S(1)}, bf16[4,128,128]{2,1,0:T(8,128)(2,1)S(1)}, u32[]{:S(2)}, u32[]{:S(2)}) collective-permute-start(bf16[4,128,128]{2,1,0:T(8,128)(2,1)S(1)} %shard_map.44.refs_1_), channel_id=1, source_target_pairs={{0,32},{32,64},{64,96},{96,128},{128,160},{160,192},{192,224},{224... | collective-permute-start | bytes 393224 | tf_op jit(solution)/shard_map/ppermute | solution.py:378
  105.0 8.5 %collective-permute-start.20 = (bf16[4,128,128]{2,1,0:T(8,128)(2,1)S(1)}, bf16[4,128,128]{2,1,0:T(8,128)(2,1)S(1)}, u32[]{:S(2)}, u32[]{:S(2)}) collective-permute-start(bf16[4,128,128]{2,1,0:T(8,128)(2,1)S(1)} %shard_map.44.refs_1_), channel_id=1, source_target_pairs={{0,224},{32,0},{64,32},{96,64},{128,96},{160,128},{192,160},{224,1... | collective-permute-start | bytes 393224 | tf_op jit(solution)/shard_map/ppermute | solution.py:378
  113.5 23.1 %copy-start.7 = (bf16[4,128,128]{2,1,0:T(8,128)(2,1)}, bf16[4,128,128]{2,1,0:T(8,128)(2,1)S(1)}, u32[]{:S(2)}) copy-start(bf16[4,128,128]{2,1,0:T(8,128)(2,1)S(1)} %collective-permute-done.16.refs_2_) | copy-start | bytes 393220
  113.5 6.2 %collective-permute-start.17 = (bf16[4,128,128]{2,1,0:T(8,128)(2,1)S(1)}, bf16[4,128,128]{2,1,0:T(8,128)(2,1)S(1)}, u32[]{:S(2)}, u32[]{:S(2)}) collective-permute-start(bf16[4,128,128]{2,1,0:T(8,128)(2,1)S(1)} %collective-permute-done.16.refs_2_), channel_id=1, source_target_pairs={{0,32},{32,64},{64,96},{96,128},{128,160},{160,192},{192,224},{224... | collective-permute-start | bytes 393224 | tf_op jit(solution)/shard_map/ppermute | solution.py:378
  113.5 23.1 %copy-start.8 = (bf16[4,128,128]{2,1,0:T(8,128)(2,1)}, bf16[4,128,128]{2,1,0:T(8,128)(2,1)S(1)}, u32[]{:S(2)}) copy-start(bf16[4,128,128]{2,1,0:T(8,128)(2,1)S(1)} %collective-permute-done.20.refs_6_) | copy-start | bytes 393220
  113.6 6.2 %collective-permute-start.21 = (bf16[4,128,128]{2,1,0:T(8,128)(2,1)S(1)}, bf16[4,128,128]{2,1,0:T(8,128)(2,1)S(1)}, u32[]{:S(2)}, u32[]{:S(2)}) collective-permute-start(bf16[4,128,128]{2,1,0:T(8,128)(2,1)S(1)} %collective-permute-done.20.refs_6_), channel_id=1, source_target_pairs={{0,224},{32,0},{64,32},{96,64},{128,96},{160,128},{192,160},{224,1... | collective-permute-start | bytes 393224 | tf_op jit(solution)/shard_map/ppermute | solution.py:378
  119.7 16.9 %copy-start.9 = (bf16[4,128,128]{2,1,0:T(8,128)(2,1)}, bf16[4,128,128]{2,1,0:T(8,128)(2,1)S(1)}, u32[]{:S(2)}) copy-start(bf16[4,128,128]{2,1,0:T(8,128)(2,1)S(1)} %collective-permute-done.17.refs_3_) | copy-start | bytes 393220
  119.7 6.2 %collective-permute-start.18 = (bf16[4,128,128]{2,1,0:T(8,128)(2,1)S(1)}, bf16[4,128,128]{2,1,0:T(8,128)(2,1)S(1)}, u32[]{:S(2)}, u32[]{:S(2)}) collective-permute-start(bf16[4,128,128]{2,1,0:T(8,128)(2,1)S(1)} %collective-permute-done.17.refs_3_), channel_id=1, source_target_pairs={{0,32},{32,64},{64,96},{96,128},{128,160},{160,192},{192,224},{224... | collective-permute-start | bytes 393224 | tf_op jit(solution)/shard_map/ppermute | solution.py:378
  119.7 16.9 %copy-start.10 = (bf16[4,128,128]{2,1,0:T(8,128)(2,1)}, bf16[4,128,128]{2,1,0:T(8,128)(2,1)S(1)}, u32[]{:S(2)}) copy-start(bf16[4,128,128]{2,1,0:T(8,128)(2,1)S(1)} %collective-permute-done.21.refs_7_) | copy-start | bytes 393220
  119.7 6.2 %collective-permute-start.22 = (bf16[4,128,128]{2,1,0:T(8,128)(2,1)S(1)}, bf16[4,128,128]{2,1,0:T(8,128)(2,1)S(1)}, u32[]{:S(2)}, u32[]{:S(2)}) collective-permute-start(bf16[4,128,128]{2,1,0:T(8,128)(2,1)S(1)} %collective-permute-done.21.refs_7_), channel_id=1, source_target_pairs={{0,224},{32,0},{64,32},{96,64},{128,96},{160,128},{192,160},{224,1... | collective-permute-start | bytes 393224 | tf_op jit(solution)/shard_map/ppermute | solution.py:378
  125.9 10.7 %copy-start.11 = (bf16[4,128,128]{2,1,0:T(8,128)(2,1)}, bf16[4,128,128]{2,1,0:T(8,128)(2,1)S(1)}, u32[]{:S(2)}) copy-start(bf16[4,128,128]{2,1,0:T(8,128)(2,1)S(1)} %collective-permute-done.18.refs_4_) | copy-start | bytes 393220
  125.9 6.2 %collective-permute-start.19 = (bf16[4,128,128]{2,1,0:T(8,128)(2,1)S(1)}, bf16[4,128,128]{2,1,0:T(8,128)(2,1)S(1)}, u32[]{:S(2)}, u32[]{:S(2)}) collective-permute-start(bf16[4,128,128]{2,1,0:T(8,128)(2,1)S(1)} %collective-permute-done.18.refs_4_), channel_id=1, source_target_pairs={{0,32},{32,64},{64,96},{96,128},{128,160},{160,192},{192,224},{224... | collective-permute-start | bytes 393224 | tf_op jit(solution)/shard_map/ppermute | solution.py:378
  125.9 10.7 %copy-start.12 = (bf16[4,128,128]{2,1,0:T(8,128)(2,1)}, bf16[4,128,128]{2,1,0:T(8,128)(2,1)S(1)}, u32[]{:S(2)}) copy-start(bf16[4,128,128]{2,1,0:T(8,128)(2,1)S(1)} %collective-permute-done.22.refs_8_) | copy-start | bytes 393220
  132.1 4.6 %copy-start.13 = (bf16[4,128,128]{2,1,0:T(8,128)(2,1)}, bf16[4,128,128]{2,1,0:T(8,128)(2,1)S(1)}, u32[]{:S(2)}) copy-start(bf16[4,128,128]{2,1,0:T(8,128)(2,1)S(1)} %collective-permute-done.19.refs_5_) | copy-start | bytes 393220
  132.1 12.4 %collective-permute-start.24 = (bf16[256,128]{1,0:T(8,128)(2,1)S(1)}, bf16[256,128]{1,0:T(8,128)(2,1)S(1)}, u32[]{:S(2)}, u32[]{:S(2)}) collective-permute-start(bf16[256,128]{1,0:T(8,128)(2,1)S(1)} %get-tuple-element.63), channel_id=1, source_target_pairs={{0,0},{1,1},{2,32},{3,33},{4,64},{5,65},{6,96},{7,97},{8,128},{9,1... | collective-permute-start | bytes 196616 | tf_op jit(solution)/shard_map/ppermute | solution.py:432
  144.5 46.2 %all-to-all-start.2 = ((f32[8,64,1024]{2,1,0:T(8,128)}), f32[8,64,1024]{2,1,0:T(8,128)S(1)}, u32[]{:S(2)}, u32[]{:S(2)}) async-start(f32[8,64,1024]{2,1,0:T(8,128)} %bitcast.2), calls=%async_computation.2 | async-start | bytes 4194304 | tf_op jit(solution)/shard_map/all_to_all | solution.py:435
  151.5 21.3 %collective-permute-start.25 = (bf16[2,256,128]{2,1,0:T(8,128)(2,1)S(1)}, bf16[2,256,128]{2,1,0:T(8,128)(2,1)S(1)}, u32[]{:S(2)}, u32[]{:S(2)}) collective-permute-start(bf16[2,256,128]{2,1,0:T(8,128)(2,1)S(1)} %shard_map.46.refs_0_), channel_id=1, source_target_pairs={{0,8},{8,0},{1,9},{9,1},{2,10},{10,2},{3,11},{11,3},{4,12},{12,4},... | collective-permute-start | bytes 393224 | tf_op jit(solution)/shard_map/ppermute | solution.py:374
  172.8 9.3 %collective-permute-start.26 = (bf16[2,2,256,128]{3,2,1,0:T(8,128)(2,1)S(1)}, bf16[2,2,256,128]{3,2,1,0:T(8,128)(2,1)S(1)}, u32[]{:S(2)}, u32[]{:S(2)}) collective-permute-start(bf16[2,2,256,128]{3,2,1,0:T(8,128)(2,1)S(1)} %shard_map.47.refs_0_), channel_id=1, source_target_pairs={{0,2},{2,4},{4,6},{6,0},{1,3},{3,5},{5,7},{7,1},{8,10},{10,12},{12... | collective-permute-start | bytes 786440 | tf_op jit(solution)/shard_map/ppermute | solution.py:441
  172.9 10.8 %collective-permute-start.27 = (bf16[2,2,256,128]{3,2,1,0:T(8,128)(2,1)S(1)}, bf16[2,2,256,128]{3,2,1,0:T(8,128)(2,1)S(1)}, u32[]{:S(2)}, u32[]{:S(2)}) collective-permute-start(bf16[2,2,256,128]{3,2,1,0:T(8,128)(2,1)S(1)} %shard_map.47.refs_0_), channel_id=1, source_target_pairs={{0,4},{2,6},{4,0},{6,2},{1,5},{3,7},{5,1},{7,3},{8,12},{10,14},{12... | collective-permute-start | bytes 786440 | tf_op jit(solution)/shard_map/ppermute | solution.py:441
  175.8 11.0 %collective-permute-start.28 = (bf16[2,2,256,128]{3,2,1,0:T(8,128)(2,1)S(1)}, bf16[2,2,256,128]{3,2,1,0:T(8,128)(2,1)S(1)}, u32[]{:S(2)}, u32[]{:S(2)}) collective-permute-start(bf16[2,2,256,128]{3,2,1,0:T(8,128)(2,1)S(1)} %shard_map.47.refs_0_), channel_id=1, source_target_pairs={{0,6},{2,0},{4,2},{6,4},{1,7},{3,1},{5,3},{7,5},{8,14},{10,8},{12,... | collective-permute-start | bytes 786440 | tf_op jit(solution)/shard_map/ppermute | solution.py:441
  186.9 2.7 %collective-permute-start.29 = (bf16[4,2,2,256,128]{4,3,2,1,0:T(8,128)(2,1)S(1)}, bf16[4,2,2,256,128]{4,3,2,1,0:T(8,128)(2,1)S(1)}, u32[]{:S(2)}, u32[]{:S(2)}) collective-permute-start(bf16[4,2,2,256,128]{4,3,2,1,0:T(8,128)(2,1)S(1)} %shard_map.48.refs_0_), channel_id=1, source_target_pairs={{0,1},{1,0},{2,3},{3,2},{4,5},{5,4},{6,7},{7,6},{8,9},{9,8},{10,11... | collective-permute-start | bytes 3145736 | tf_op jit(solution)/shard_map/ppermute | solution.py:374
  189.6 1.0 copy-start
  190.6 1.2 copy-start.1
Sparse Core Ops, SparseCore 0:
  75.4 42.0 all-gather.2

commit v8 on v7

--- a/solution.py
+++ b/solution.py
@@ -320,28 +320,28 @@
 
 def pair_kernel(parts, *refs):
     features, (out, rows, pairs) = refs[:2], refs[2:]
-    yh, x, core = (lax.axis_index(name) for name in PAR)
+    yh, core = lax.axis_index("yh"), lax.axis_index("c")
+    place = lax.axis_index("zh") * 2 + lax.axis_index("zl")
     total = parts[0]
     for index in range(1, parts.shape[0]):
         total += parts[index]
     rows[...] = total.astype(BF16)
     pairs[...] = jnp.zeros_like(pairs)
-    for flip_yh in range(2):
-        for shift in range(4):
-            place = (x + 4 - shift) & 3
-            zh = (yh ^ flip_yh) * 2 + (place >> 1)
+    for x in range(4):
+        for flip_yh in range(2):
+            source = (yh * 4 + x) ^ (flip_yh * 4) ^ place
             value = None
             for flip_core in range(2):
-                start = pl.multiple_of(((place & 1) * 2 + (core ^ flip_core)) * 256, 256)
-                held = features[flip_core].at[shift, flip_yh]
+                start = pl.multiple_of(((source & 1) * 2 + (core ^ flip_core)) * 256, 256)
+                held = features[flip_core].at[x]
                 term = lax.dot_general(
                     rows[:, pl.ds(start, 256)],
-                    jnp.concatenate([held[0], held[1]], axis=1),
+                    jnp.concatenate([held[flip_yh * 2], held[flip_yh * 2 + 1]], axis=1),
                     (((1,), (1,)), ((), ())),
                     preferred_element_type=F32,
                 )
                 value = term if value is None else value + term
-            pairs[:, pl.ds(pl.multiple_of(zh * 256, 256), 256)] += value
+            pairs[:, pl.ds(pl.multiple_of((source >> 1) * 256, 256), 256)] += value
     for block in range(16):
         piece = pairs[:, block * 64 : (block + 1) * 64]
         out[block, :, :64] = piece[:32]
@@ -378,14 +378,16 @@
     return lax.ppermute(value, ("zh", "zl"), [(i, (i + by) % 8) for i in range(8)])
 
 
-def ring(value):
+def ring(value, beside):
     up = [step_z(value, 1)]
     down = [step_z(value, 7)]
-    for _ in range(2):
-        up.append(step_z(up[-1], 1))
-        down.append(step_z(down[-1], 7))
-    up.append(step_z(up[-1], 1))
-    return [value] + up + down
+    up.append(step_z(up[0], 1))
+    down.append(step_z(down[0], 7))
+    beside, up[1], down[1] = lax.optimization_barrier((beside, up[1], down[1]))
+    up.append(step_z(up[1], 1))
+    down.append(step_z(down[1], 7))
+    up.append(step_z(up[2], 1))
+    return beside, [value] + up + down
 
 
 def flips(keep, send):
@@ -415,31 +417,35 @@
     partial, part = lax.optimization_barrier((partial, part))
     next_part = lax.all_to_all(partial, CHIPS, 0, 0, tiled=True)
 
-    route = []
-    for z in range(8):
-        for yl in range(2):
-            for chip in range(8):
-                for c in range(2):
-                    route.append((((z * 2 + yl) * 8 + chip) * 2 + c, ((chip * 2 + yl) * 8 + z) * 2 + c))
+    def turn(value):
+        return [
+            lax.ppermute(
+                value,
+                EX + PAR,
+                [
+                    (((z * 2 + yl) * 8 + chip) * 2 + c, ((chip * 2 + yl) * 8 + (z ^ chip ^ flip)) * 2 + c)
+                    for z in range(8)
+                    for yl in range(2)
+                    for chip in range(8)
+                    for c in range(2)
+                ],
+            )
+            for flip in (0, 4)
+        ]
+
     whole, keep, send = sum_parts(part)
     mine = flips(keep, send)
     low = lax.all_gather(mine, ("zh", "zl"), axis=0)
-    turned = lax.ppermute(whole, EX + PAR, route)
+    turned = turn(whole)
     next_part, mine, turned = lax.optimization_barrier((next_part, mine, turned))
     whole, keep, send = sum_parts(next_part)
     whole, mine = lax.optimization_barrier((whole, flips(keep, send)))
-    whole, high = lax.optimization_barrier((whole, ring(mine)))
-    next_turned = lax.ppermute(whole, EX + PAR, route)
+    next_turned, high = ring(mine, turn(whole))
+    near = join([turned[0], next_turned[0], turned[1], next_turned[1]])
+    near, low = lax.optimization_barrier((near, low))
+    near = lax.all_gather(near, "x", axis=0)
     conditioned = condition(low, high, inverse_gram, other_tile)
-    conditioned, next_turned = lax.optimization_barrier((conditioned, next_turned))
     parts = lax.all_to_all(conditioned.reshape(8, 64, 1024), CHIPS, 0, 0, tiled=True)
-
-    both = join([turned, next_turned])
-    four = join([both, swap(both, "yh")])
-    near = [four]
-    for by in range(1, 4):
-        near.append(lax.ppermute(four, "x", [(i, (i + by) % 4) for i in range(4)]))
-    near = join(near)
     return finish(lax.all_to_all(pair(parts, near, swap(near, "c")), EX, 0, 0, tiled=True))
 
 

time: 223 us -> 221 us (level)
  starting transfers between devices: 59.2 us -> 67.4 us
  waiting for transfers between devices: 71.5 us -> 63.7 us
  blocking collectives: 17.7 us -> 14.5 us
    ppermute x18 -> x17, waiting for transfers between devices: 33.6 us -> 10.8 us  [swap(): return lax.ppermute(value, axis, [(0, 1), (1, 0)])]
    all_to_all x1, waiting for transfers between devices: 0.01 us -> 21.5 us  [per_device(): lax.all_to_all(conditioned.reshape(8, 64, 1024), CHIPS, 0, 0, tiled=True)]
    ppermute x5 -> x4, starting transfers between devices: 14 us -> 22.5 us  [turn(): lax.ppermute(value, EX + PAR, [(((z * 2 + yl) * 8 + chip) * 2 + c, ((chip...]
    ppermute x5 -> x4, waiting for transfers between devices: 21.6 us -> 18.1 us  [turn(): lax.ppermute(value, EX + PAR, [(((z * 2 + yl) * 8 + chip) * 2 + c, ((chip...]
    all_to_all x1, blocking collectives: 17.7 us -> 14.5 us  [per_device(): lax.all_to_all(pair(parts, near, swap(near, 'c')), EX, 0, 0, tiled=True)]
    ppermute x7, waiting for transfers between devices: 16.3 us -> 13.2 us  [step_z(): lax.ppermute(value, ('zh', 'zl'), [(i, (i + by) % 8) for i in range(8)])]
    ppermute x18 -> x17, starting transfers between devices: 11.9 us -> 10.6 us  [swap(): return lax.ppermute(value, axis, [(0, 1), (1, 0)])]
  transfers between devices with their start and end apart: 34 -> 33, of which waited for: 22 -> 17; matrix products, arithmetic and copies ran while one was open for 0% -> 0% of each run, Pallas kernels for 19% -> 19%
where the time goes in v8:
time: 221 us; the launch traced here: 217 us
  starting transfers between devices  67.4 us (30%)
  waiting for transfers between devices  63.7 us (29%)
  Pallas kernels  52.8 us (24%)
  blocking collectives  14.5 us (7%)
  between operations  13.7 us (6%)
  local copies, waits for them, and re-layouts  4.61 us (2%)
    ppermute x4, starting transfers between devices, turn(): lax.ppermute(value, EX + PAR, [(((z * 2 + yl) * 8 + chip) * 2 + c, ((chip...  22.5 us
    all_to_all x1, waiting for transfers between devices, per_device(): lax.all_to_all(conditioned.reshape(8, 64, 1024), CHIPS, 0, 0, tiled=True)  21.5 us
    ppermute x4, waiting for transfers between devices, turn(): lax.ppermute(value, EX + PAR, [(((z * 2 + yl) * 8 + chip) * 2 + c, ((chip...  18.1 us
    pallas_call x1, Pallas kernels, project_hash(): pl.pallas_call(functools.partial(hash_kernel, part, width), out_shape=jax...  18 us
    pallas_call x2, Pallas kernels, table(): pl.pallas_call(functools.partial(table_kernel, part, width, first, params...  15.8 us
    all_to_all x1, blocking collectives, per_device(): lax.all_to_all(pair(parts, near, swap(near, 'c')), EX, 0, 0, tiled=True)  14.5 us
    ppermute x7, waiting for transfers between devices, step_z(): lax.ppermute(value, ('zh', 'zl'), [(i, (i + by) % 8) for i in range(8)])  13.2 us
    ppermute x7, starting transfers between devices, step_z(): lax.ppermute(value, ('zh', 'zl'), [(i, (i + by) % 8) for i in range(8)])  13 us
  transfers between devices with their start and end apart: 33, of which 17 were waited for; matrix products, arithmetic and copies ran while one was open for 0% of the time, Pallas kernels for 19%

profile of v8, /device:TPU:22, one launch (start us, length us, event | category | flops | bytes accessed | tf_op | source)
XLA Modules:
  0.0 216.8 jit_solution(6744667274460819994)
XLA Ops:
  6.5 1.3 collective-permute-start
  7.8 1.9 collective-permute-start.1
  9.7 0.7 copy-done.4
  10.4 9.7 %shard_map.37.first = bf16[5120,1024]{1,0:T(8,128)(2,1)S(1)} custom-call(s32[4]{0:T(128)S(1)} %copy-done.4), custom_call_target="tpu_custom_call" | custom-call | flops 6291456000 | bytes 10485760 | tf_op jit(solution)/shard_map/pallas_call | solution.py:68
  20.1 0.3 collective-permute-done.refs_1_
  20.4 1.2 collective-permute-done.1.refs_2_
  21.6 0.1 collective-permute-start.5
  21.8 0.0 copy-start.2
  21.8 0.6 collective-permute-start.6
  22.4 1.7 collective-permute-start.2
  24.1 0.7 collective-permute-start.3
  24.8 6.0 %shard_map.38.second = bf16[3072,1024]{1,0:T(8,128)(2,1)S(1)} custom-call(s32[4]{0:T(128)S(1)} %copy-done.5), custom_call_target="tpu_custom_call" | custom-call | flops 3774873600 | bytes 6291456 | tf_op jit(solution)/shard_map/pallas_call | solution.py:68
  30.9 0.0 collective-permute-done.2.refs_3_
  30.9 1.2 collective-permute-done.3.refs_4_
  32.1 0.0 collective-permute-start.7
  32.1 0.5 collective-permute-start.8
  32.6 1.0 collective-permute-done.7.refs_8_
  33.6 0.4 collective-permute-done.8.refs_9_
  34.0 8.0 %shard_map.39 = (f32[8,256,128]{2,1,0:T(8,128)}, bf16[256,8192]{1,0:T(8,128)(2,1)S(1)}) custom-call(bf16[5120,1024]{1,0:T(8,128)(2,1)S(1)} %shard_map.37.first, bf16[3072,1024]{1,0:T(8,128)(2,1)S(1)} %shard_map.38.second, bf16[64,4096]{1,0:T(8,128)(2,1)S(1)} %copy-done.2, bf16[64,4096]{1,0:T(8,128)(2,1)S(1)} %collective-permute-done.refs_1_, ...), custom_call_target="tpu_custom_call" | custom-call | flops 4294967296 | bytes 16777216 | tf_op jit(solution)/shard_map/pallas_call | solution.py:140
  42.1 2.0 copy-done.3
  44.0 7.2 %all-to-all-start = ((f32[8,256,128]{2,1,0:T(8,128)}), f32[8,256,128]{2,1,0:T(8,128)S(1)}, u32[]{:S(2)}, u32[]{:S(2)}) async-start(f32[8,256,128]{2,1,0:T(8,128)} %get-tuple-element.39), calls=%async_computation | async-start | bytes 2097152 | tf_op jit(solution)/shard_map/all_to_all | solution.py:415
  51.2 18.0 %shard_map.40 = f32[8,256,128]{2,1,0:T(8,128)} custom-call(s32[4]{0:T(128)} %words.5, bf16[256,8192]{1,0:T(8,128)(2,1)} %copy-done.3), custom_call_target="tpu_custom_call" | custom-call | flops 4294967296 | bytes 16777216 | tf_op jit(solution)/shard_map/pallas_call | solution.py:199
  69.3 0.1 shard_map.41
  69.3 0.1 collective-permute-start.9
  69.4 0.8 collective-permute-start.10
  70.3 0.4 collective-permute-done.9.refs_1_
  70.6 0.9 collective-permute-start.11
  71.6 1.9 collective-permute-done.10.refs_2_
  73.5 1.1 collective-permute-done.11.refs_3_
  74.5 0.7 shard_map.42
  75.2 0.0 all-gather.5.cloned.1.call-update
  75.3 0.1 collective-permute-start.26
  75.4 7.2 %all-to-all-start.1 = ((f32[8,256,128]{2,1,0:T(8,128)}), f32[8,256,128]{2,1,0:T(8,128)S(1)}, u32[]{:S(2)}, u32[]{:S(2)}) async-start(f32[8,256,128]{2,1,0:T(8,128)} %shard_map.40), calls=%async_computation.1 | async-start | bytes 2097152 | tf_op jit(solution)/shard_map/all_to_all | solution.py:418
  82.6 6.8 %collective-permute-start.12 = (bf16[256,128]{1,0:T(8,128)(2,1)S(1)}, bf16[256,128]{1,0:T(8,128)(2,1)S(1)}, u32[]{:S(2)}, u32[]{:S(2)}) collective-permute-start(bf16[256,128]{1,0:T(8,128)(2,1)S(1)} %get-tuple-element.44), channel_id=1, source_target_pairs={{0,0},{1,1},{2,34},{3,35},{4,68},{5,69},{6,102},{7,103},{8,136},{9... | collective-permute-start | bytes 196616 | tf_op jit(solution)/shard_map/ppermute | solution.py:422
  89.4 5.1 %collective-permute-start.13 = (bf16[256,128]{1,0:T(8,128)(2,1)S(1)}, bf16[256,128]{1,0:T(8,128)(2,1)S(1)}, u32[]{:S(2)}, u32[]{:S(2)}) collective-permute-start(bf16[256,128]{1,0:T(8,128)(2,1)S(1)} %get-tuple-element.44), channel_id=1, source_target_pairs={{0,8},{1,9},{2,42},{3,43},{4,76},{5,77},{6,110},{7,111},{8,128},{9... | collective-permute-start | bytes 196616 | tf_op jit(solution)/shard_map/ppermute | solution.py:422
  94.6 9.8 %collective-permute-done.12.refs_0_ = bf16[256,128]{1,0:T(8,128)(2,1)S(1)} collective-permute-done((bf16[256,128]{1,0:T(8,128)(2,1)S(1)}, bf16[256,128]{1,0:T(8,128)(2,1)S(1)}, u32[]{:S(2)}, u32[]{:S(2)}) %collective-permute-start.12) | collective-permute-done | bytes 65568 | tf_op jit(solution)/shard_map/ppermute | solution.py:422
  104.3 0.1 shard_map.43
  104.4 0.1 collective-permute-start.14
  104.5 0.9 collective-permute-start.15
  105.4 0.3 collective-permute-done.14.refs_1_
  105.7 0.9 collective-permute-start.16
  106.6 1.9 collective-permute-done.15.refs_2_
  108.6 1.1 collective-permute-done.16.refs_3_
  109.6 0.8 collective-permute-start.19
  110.5 5.6 %collective-permute-start.21 = (bf16[4,128,128]{2,1,0:T(8,128)(2,1)S(1)}, bf16[4,128,128]{2,1,0:T(8,128)(2,1)S(1)}, u32[]{:S(2)}, u32[]{:S(2)}) collective-permute-start(bf16[4,128,128]{2,1,0:T(8,128)(2,1)S(1)} %shard_map.44.refs_1_), channel_id=1, source_target_pairs={{0,224},{32,0},{64,32},{96,64},{128,96},{160,128},{192,160},{224,1... | collective-permute-start | bytes 393224 | tf_op jit(solution)/shard_map/ppermute | solution.py:378
  116.1 4.1 %collective-permute-done.19.refs_2_ = bf16[4,128,128]{2,1,0:T(8,128)(2,1)S(1)} collective-permute-done((bf16[4,128,128]{2,1,0:T(8,128)(2,1)S(1)}, bf16[4,128,128]{2,1,0:T(8,128)(2,1)S(1)}, u32[]{:S(2)}, u32[]{:S(2)}) %collective-permute-start.19) | collective-permute-done | bytes 131104 | tf_op jit(solution)/shard_map/ppermute | solution.py:378
  120.2 3.2 %collective-permute-start.22 = (bf16[4,128,128]{2,1,0:T(8,128)(2,1)S(1)}, bf16[4,128,128]{2,1,0:T(8,128)(2,1)S(1)}, u32[]{:S(2)}, u32[]{:S(2)}) collective-permute-start(bf16[4,128,128]{2,1,0:T(8,128)(2,1)S(1)} %collective-permute-done.21.refs_6_), channel_id=1, source_target_pairs={{0,224},{32,0},{64,32},{96,64},{128,96},{160,128},{192,160},{224,1... | collective-permute-start | bytes 393224 | tf_op jit(solution)/shard_map/ppermute | solution.py:378
  123.4 2.1 collective-permute-start.17
  125.5 8.4 %collective-permute-start.18 = (bf16[256,128]{1,0:T(8,128)(2,1)S(1)}, bf16[256,128]{1,0:T(8,128)(2,1)S(1)}, u32[]{:S(2)}, u32[]{:S(2)}) collective-permute-start(bf16[256,128]{1,0:T(8,128)(2,1)S(1)} %get-tuple-element.50), channel_id=1, source_target_pairs={{0,8},{1,9},{2,42},{3,43},{4,76},{5,77},{6,110},{7,111},{8,128},{9... | collective-permute-start | bytes 196616 | tf_op jit(solution)/shard_map/ppermute | solution.py:422
  133.9 8.4 %collective-permute-done.17.refs_1_ = bf16[256,128]{1,0:T(8,128)(2,1)S(1)} collective-permute-done((bf16[256,128]{1,0:T(8,128)(2,1)S(1)}, bf16[256,128]{1,0:T(8,128)(2,1)S(1)}, u32[]{:S(2)}, u32[]{:S(2)}) %collective-permute-start.17) | collective-permute-done | bytes 65568 | tf_op jit(solution)/shard_map/ppermute | solution.py:422
  142.3 0.8 shard_map.45
  143.1 0.0 all-gather.7.cloned.1.call-update
  143.2 0.1 collective-permute-start.23
  143.3 3.2 %collective-permute-start.25 = (bf16[4,128,128]{2,1,0:T(8,128)(2,1)S(1)}, bf16[4,128,128]{2,1,0:T(8,128)(2,1)S(1)}, u32[]{:S(2)}, u32[]{:S(2)}) collective-permute-start(bf16[4,128,128]{2,1,0:T(8,128)(2,1)S(1)} %collective-permute-done.22.refs_7_), channel_id=1, source_target_pairs={{0,224},{32,0},{64,32},{96,64},{128,96},{160,128},{192,160},{224,1... | collective-permute-start | bytes 393224 | tf_op jit(solution)/shard_map/ppermute | solution.py:378
  146.5 2.9 %collective-permute-done.23.refs_4_ = bf16[4,128,128]{2,1,0:T(8,128)(2,1)S(1)} collective-permute-done((bf16[4,128,128]{2,1,0:T(8,128)(2,1)S(1)}, bf16[4,128,128]{2,1,0:T(8,128)(2,1)S(1)}, u32[]{:S(2)}, u32[]{:S(2)}) %collective-permute-start.23) | collective-permute-done | bytes 131104 | tf_op jit(solution)/shard_map/ppermute | solution.py:378
  149.5 6.1 %collective-permute-done.24.refs_5_ = bf16[4,128,128]{2,1,0:T(8,128)(2,1)S(1)} collective-permute-done((bf16[4,128,128]{2,1,0:T(8,128)(2,1)S(1)}, bf16[4,128,128]{2,1,0:T(8,128)(2,1)S(1)}, u32[]{:S(2)}, u32[]{:S(2)}) %collective-permute-start.24) | collective-permute-done | bytes 131104 | tf_op jit(solution)/shard_map/ppermute | solution.py:378
  155.7 0.7 copy-done.13
  156.3 6.7 %shard_map.46 = f32[512,1024]{1,0:T(8,128)} custom-call(bf16[8,4,128,128]{3,2,1,0:T(8,128)(2,1)} %bitcast.6, bf16[4,128,128]{2,1,0:T(8,128)(2,1)} %copy-done.1, bf16[4,128,128]{2,1,0:T(8,128)(2,1)} %copy-done.7, bf16[4,128,128]{2,1,0:T(8,128)(2,1)} %copy-done.9, bf16[4,128,128]{2,1,0:T(8,128)(2,1)} %copy-done.11, bf16[4,128,128]{2,1,0:T(8,128)(2,1)} %copy-done.13, ...), custom_call_target="tpu_custom_call" | custom-call | flops 2147483648 | bytes 7340032 | tf_op jit(solution)/shard_map/pallas_call | solution.py:293
  163.1 6.9 %all-to-all-start.2 = ((f32[8,64,1024]{2,1,0:T(8,128)}), f32[8,64,1024]{2,1,0:T(8,128)S(1)}, u32[]{:S(2)}, u32[]{:S(2)}) async-start(f32[8,64,1024]{2,1,0:T(8,128)} %bitcast.5), calls=%async_computation.2 | async-start | bytes 4194304 | tf_op jit(solution)/shard_map/all_to_all | solution.py:448
  170.0 21.5 %all-to-all-done.2.parts = f32[8,64,1024]{2,1,0:T(8,128)S(1)} async-done(((f32[8,64,1024]{2,1,0:T(8,128)}), f32[8,64,1024]{2,1,0:T(8,128)S(1)}, u32[]{:S(2)}, u32[]{:S(2)}) %all-to-all-start.2) | async-done | bytes 2097184 | tf_op jit(solution)/shard_map/all_to_all | solution.py:448
  191.6 1.2 copy-done
  192.8 1.0 shard_map.47
  193.8 14.5 %all_to_all.20.parts = f32[16,32,128]{2,1,0:T(8,128)} all-to-all(f32[16,32,128]{2,1,0:T(8,128)S(1)} %shard_map.47), channel_id=1, replica_groups=mesh['zh'=4,'zl'=2,'yl'=2,'yh'=2,'x'=4,'c'=2] {'zh','zl','yl'}, dimensions={0} | all-to-all | bytes 524288 | tf_op jit(solution)/shard_map/all_to_all | solution.py:449
  208.3 1.7 shard_map.48
  (47 shorter events, 0.1 us)
Async XLA Ops:
  6.5 13.9 %collective-permute-start = (bf16[64,4096]{1,0:T(8,128)(2,1)}, bf16[64,4096]{1,0:T(8,128)(2,1)S(1)}, u32[]{:S(2)}, u32[]{:S(2)}) collective-permute-start(bf16[64,4096]{1,0:T(8,128)(2,1)} %refs_0_.1), channel_id=1, source_target_pairs={{0,16},{16,0},{1,17},{17,1},{2,18},{18,2},{3,19},{19,3},{4,20},{20... | collective-permute-start | bytes 1572872 | tf_op jit(solution)/shard_map/ppermute | solution.py:374
  7.8 13.8 %collective-permute-start.1 = (bf16[64,4096]{1,0:T(8,128)(2,1)}, bf16[64,4096]{1,0:T(8,128)(2,1)S(1)}, u32[]{:S(2)}, u32[]{:S(2)}) collective-permute-start(bf16[64,4096]{1,0:T(8,128)(2,1)} %refs_0_.1), channel_id=1, source_target_pairs={{0,32},{32,0},{1,33},{33,1},{2,34},{34,2},{3,35},{35,3},{4,36},{36... | collective-permute-start | bytes 1572872 | tf_op jit(solution)/shard_map/ppermute | solution.py:374
  9.7 22.9 %collective-permute-start.4 = (bf16[64,4096]{1,0:T(8,128)(2,1)}, bf16[64,4096]{1,0:T(8,128)(2,1)S(1)}, u32[]{:S(2)}, u32[]{:S(2)}) collective-permute-start(bf16[64,4096]{1,0:T(8,128)(2,1)} %refs_0_.1), channel_id=1, source_target_pairs={{0,1},{1,0},{2,3},{3,2},{4,5},{5,4},{6,7},{7,6},{8,9},{9,8},{10,11... | collective-permute-start | bytes 1572872 | tf_op jit(solution)/shard_map/ppermute | solution.py:374
  9.7 0.7 copy-start.4
  10.4 14.4 %copy-start.5 = (s32[4]{0:T(128)S(1)}, s32[4]{0:T(128)}, u32[]{:S(2)}) copy-start(s32[4]{0:T(128)} %words.5) | copy-start | bytes 52
  21.6 12.4 %collective-permute-start.5 = (bf16[64,4096]{1,0:T(8,128)(2,1)S(1)}, bf16[64,4096]{1,0:T(8,128)(2,1)S(1)}, u32[]{:S(2)}, u32[]{:S(2)}) collective-permute-start(bf16[64,4096]{1,0:T(8,128)(2,1)S(1)} %collective-permute-done.refs_1_), channel_id=1, source_target_pairs={{0,1},{1,0},{2,3},{3,2},{4,5},{5,4},{6,7},{7,6},{8,9},{9,8},{10,11... | collective-permute-start | bytes 1572872 | tf_op jit(solution)/shard_map/ppermute | solution.py:374
  21.8 12.3 %copy-start.2 = (bf16[64,4096]{1,0:T(8,128)(2,1)S(1)}, bf16[64,4096]{1,0:T(8,128)(2,1)}, u32[]{:S(2)}) copy-start(bf16[64,4096]{1,0:T(8,128)(2,1)} %refs_0_.1) | copy-start | bytes 1572868
  21.8 12.2 %collective-permute-start.6 = (bf16[64,4096]{1,0:T(8,128)(2,1)S(1)}, bf16[64,4096]{1,0:T(8,128)(2,1)S(1)}, u32[]{:S(2)}, u32[]{:S(2)}) collective-permute-start(bf16[64,4096]{1,0:T(8,128)(2,1)S(1)} %collective-permute-done.1.refs_2_), channel_id=1, source_target_pairs={{0,1},{1,0},{2,3},{3,2},{4,5},{5,4},{6,7},{7,6},{8,9},{9,8},{10,11... | collective-permute-start | bytes 1572872 | tf_op jit(solution)/shard_map/ppermute | solution.py:374
  22.4 8.5 %collective-permute-start.2 = (bf16[32,4096]{1,0:T(8,128)(2,1)S(1)}, bf16[32,4096]{1,0:T(8,128)(2,1)S(1)}, u32[]{:S(2)}, u32[]{:S(2)}) collective-permute-start(bf16[32,4096]{1,0:T(8,128)(2,1)S(1)} %slice.6), channel_id=1, source_target_pairs={{0,32},{32,0},{1,33},{33,1},{2,34},{34,2},{3,35},{35,3},{4,36},{36... | collective-permute-start | bytes 786440 | tf_op jit(solution)/shard_map/ppermute | solution.py:374
  24.1 8.0 %collective-permute-start.3 = (bf16[32,4096]{1,0:T(8,128)(2,1)S(1)}, bf16[32,4096]{1,0:T(8,128)(2,1)S(1)}, u32[]{:S(2)}, u32[]{:S(2)}) collective-permute-start(bf16[32,4096]{1,0:T(8,128)(2,1)S(1)} %slice.7), channel_id=1, source_target_pairs={{0,16},{16,0},{1,17},{17,1},{2,18},{18,2},{3,19},{19,3},{4,20},{20... | collective-permute-start | bytes 786440 | tf_op jit(solution)/shard_map/ppermute | solution.py:374
  32.1 1.5 collective-permute-start.7
  32.1 1.9 collective-permute-start.8
  42.1 2.0 copy-start.3
  44.0 25.2 %all-to-all-start = ((f32[8,256,128]{2,1,0:T(8,128)}), f32[8,256,128]{2,1,0:T(8,128)S(1)}, u32[]{:S(2)}, u32[]{:S(2)}) async-start(f32[8,256,128]{2,1,0:T(8,128)} %get-tuple-element.39), calls=%async_computation | async-start | bytes 2097152 | tf_op jit(solution)/shard_map/all_to_all | solution.py:415
  51.2 91.9 %all-gather.5.cloned.1.call-start = ((), (), s32[]{:S(2)}) async-start(), calls=%async_computation.4 | async-start | bytes 1179648 | tf_op jit(solution)/shard_map/all_gather | solution.py:438
  51.2 24.0 %copy-start.6 = (bf16[1024,1024]{1,0:T(8,128)(2,1)S(1)}, bf16[1024,1024]{1,0:T(8,128)(2,1)}, u32[]{:S(2)}) copy-start(bf16[1024,1024]{1,0:T(8,128)(2,1)} %refs_9_.1) | copy-start | bytes 6291460
  69.3 1.3 collective-permute-start.9
  69.4 4.1 %collective-permute-start.10 = (bf16[128,128]{1,0:T(8,128)(2,1)S(1)}, bf16[128,128]{1,0:T(8,128)(2,1)S(1)}, u32[]{:S(2)}, u32[]{:S(2)}) collective-permute-start(bf16[128,128]{1,0:T(8,128)(2,1)S(1)} %get-tuple-element.42.refs_0_), channel_id=1, source_target_pairs={{0,16},{16,0},{1,17},{17,1},{2,18},{18,2},{3,19},{19,3},{4,20},{20... | collective-permute-start | bytes 98312 | tf_op jit(solution)/shard_map/ppermute | solution.py:374
  70.6 3.9 %collective-permute-start.11 = (bf16[128,128]{1,0:T(8,128)(2,1)S(1)}, bf16[128,128]{1,0:T(8,128)(2,1)S(1)}, u32[]{:S(2)}, u32[]{:S(2)}) collective-permute-start(bf16[128,128]{1,0:T(8,128)(2,1)S(1)} %collective-permute-done.9.refs_1_), channel_id=1, source_target_pairs={{0,16},{16,0},{1,17},{17,1},{2,18},{18,2},{3,19},{19,3},{4,20},{20... | collective-permute-start | bytes 98312 | tf_op jit(solution)/shard_map/ppermute | solution.py:374
  75.3 74.2 %collective-permute-start.26 = (bf16[1024,1024]{1,0:T(8,128)(2,1)S(1)}, bf16[1024,1024]{1,0:T(8,128)(2,1)}, u32[]{:S(2)}, u32[]{:S(2)}) collective-permute-start(bf16[1024,1024]{1,0:T(8,128)(2,1)S(1)} %copy-done.6), channel_id=1, source_target_pairs={{0,1},{1,0},{2,3},{3,2},{4,5},{5,4},{6,7},{7,6},{8,9},{9,8},{10,11... | collective-permute-start | bytes 6291464 | tf_op jit(solution)/shard_map/ppermute | solution.py:374
  75.4 29.0 %all-to-all-start.1 = ((f32[8,256,128]{2,1,0:T(8,128)}), f32[8,256,128]{2,1,0:T(8,128)S(1)}, u32[]{:S(2)}, u32[]{:S(2)}) async-start(f32[8,256,128]{2,1,0:T(8,128)} %shard_map.40), calls=%async_computation.1 | async-start | bytes 2097152 | tf_op jit(solution)/shard_map/all_to_all | solution.py:418
  82.6 87.4 %all-gather.7.cloned.1.call-start = ((), (), s32[]{:S(2)}) async-start(), calls=%async_computation.5 | async-start | bytes 1310720 | tf_op jit(solution)/shard_map/all_gather | solution.py:446
  82.6 21.8 %collective-permute-start.12 = (bf16[256,128]{1,0:T(8,128)(2,1)S(1)}, bf16[256,128]{1,0:T(8,128)(2,1)S(1)}, u32[]{:S(2)}, u32[]{:S(2)}) collective-permute-start(bf16[256,128]{1,0:T(8,128)(2,1)S(1)} %get-tuple-element.44), channel_id=1, source_target_pairs={{0,0},{1,1},{2,34},{3,35},{4,68},{5,69},{6,102},{7,103},{8,136},{9... | collective-permute-start | bytes 196616 | tf_op jit(solution)/shard_map/ppermute | solution.py:422
  89.4 14.9 %collective-permute-start.13 = (bf16[256,128]{1,0:T(8,128)(2,1)S(1)}, bf16[256,128]{1,0:T(8,128)(2,1)S(1)}, u32[]{:S(2)}, u32[]{:S(2)}) collective-permute-start(bf16[256,128]{1,0:T(8,128)(2,1)S(1)} %get-tuple-element.44), channel_id=1, source_target_pairs={{0,8},{1,9},{2,42},{3,43},{4,76},{5,77},{6,110},{7,111},{8,128},{9... | collective-permute-start | bytes 196616 | tf_op jit(solution)/shard_map/ppermute | solution.py:422
  104.4 1.3 collective-permute-start.14
  104.5 4.1 %collective-permute-start.15 = (bf16[128,128]{1,0:T(8,128)(2,1)S(1)}, bf16[128,128]{1,0:T(8,128)(2,1)S(1)}, u32[]{:S(2)}, u32[]{:S(2)}) collective-permute-start(bf16[128,128]{1,0:T(8,128)(2,1)S(1)} %get-tuple-element.48.refs_0_), channel_id=1, source_target_pairs={{0,16},{16,0},{1,17},{17,1},{2,18},{18,2},{3,19},{19,3},{4,20},{20... | collective-permute-start | bytes 98312 | tf_op jit(solution)/shard_map/ppermute | solution.py:374
  105.7 3.9 %collective-permute-start.16 = (bf16[128,128]{1,0:T(8,128)(2,1)S(1)}, bf16[128,128]{1,0:T(8,128)(2,1)S(1)}, u32[]{:S(2)}, u32[]{:S(2)}) collective-permute-start(bf16[128,128]{1,0:T(8,128)(2,1)S(1)} %collective-permute-done.14.refs_1_), channel_id=1, source_target_pairs={{0,16},{16,0},{1,17},{17,1},{2,18},{18,2},{3,19},{19,3},{4,20},{20... | collective-permute-start | bytes 98312 | tf_op jit(solution)/shard_map/ppermute | solution.py:374
  109.6 46.0 %copy-start.1 = (bf16[4,128,128]{2,1,0:T(8,128)(2,1)}, bf16[4,128,128]{2,1,0:T(8,128)(2,1)S(1)}, u32[]{:S(2)}) copy-start(bf16[4,128,128]{2,1,0:T(8,128)(2,1)S(1)} %shard_map.44.refs_1_) | copy-start | bytes 393220
  109.6 10.5 %collective-permute-start.19 = (bf16[4,128,128]{2,1,0:T(8,128)(2,1)S(1)}, bf16[4,128,128]{2,1,0:T(8,128)(2,1)S(1)}, u32[]{:S(2)}, u32[]{:S(2)}) collective-permute-start(bf16[4,128,128]{2,1,0:T(8,128)(2,1)S(1)} %shard_map.44.refs_1_), channel_id=1, source_target_pairs={{0,32},{32,64},{64,96},{96,128},{128,160},{160,192},{192,224},{224... | collective-permute-start | bytes 393224 | tf_op jit(solution)/shard_map/ppermute | solution.py:378
  110.5 9.7 %collective-permute-start.21 = (bf16[4,128,128]{2,1,0:T(8,128)(2,1)S(1)}, bf16[4,128,128]{2,1,0:T(8,128)(2,1)S(1)}, u32[]{:S(2)}, u32[]{:S(2)}) collective-permute-start(bf16[4,128,128]{2,1,0:T(8,128)(2,1)S(1)} %shard_map.44.refs_1_), channel_id=1, source_target_pairs={{0,224},{32,0},{64,32},{96,64},{128,96},{160,128},{192,160},{224,1... | collective-permute-start | bytes 393224 | tf_op jit(solution)/shard_map/ppermute | solution.py:378
  120.2 35.4 %copy-start.7 = (bf16[4,128,128]{2,1,0:T(8,128)(2,1)}, bf16[4,128,128]{2,1,0:T(8,128)(2,1)S(1)}, u32[]{:S(2)}) copy-start(bf16[4,128,128]{2,1,0:T(8,128)(2,1)S(1)} %collective-permute-done.19.refs_2_) | copy-start | bytes 393220
  120.2 22.1 %collective-permute-start.20 = (bf16[4,128,128]{2,1,0:T(8,128)(2,1)S(1)}, bf16[4,128,128]{2,1,0:T(8,128)(2,1)S(1)}, u32[]{:S(2)}, u32[]{:S(2)}) collective-permute-start(bf16[4,128,128]{2,1,0:T(8,128)(2,1)S(1)} %collective-permute-done.19.refs_2_), channel_id=1, source_target_pairs={{0,32},{32,64},{64,96},{96,128},{128,160},{160,192},{192,224},{224... | collective-permute-start | bytes 393224 | tf_op jit(solution)/shard_map/ppermute | solution.py:378
  120.2 35.4 %copy-start.8 = (bf16[4,128,128]{2,1,0:T(8,128)(2,1)}, bf16[4,128,128]{2,1,0:T(8,128)(2,1)S(1)}, u32[]{:S(2)}) copy-start(bf16[4,128,128]{2,1,0:T(8,128)(2,1)S(1)} %collective-permute-done.21.refs_6_) | copy-start | bytes 393220
  120.2 22.1 %collective-permute-start.22 = (bf16[4,128,128]{2,1,0:T(8,128)(2,1)S(1)}, bf16[4,128,128]{2,1,0:T(8,128)(2,1)S(1)}, u32[]{:S(2)}, u32[]{:S(2)}) collective-permute-start(bf16[4,128,128]{2,1,0:T(8,128)(2,1)S(1)} %collective-permute-done.21.refs_6_), channel_id=1, source_target_pairs={{0,224},{32,0},{64,32},{96,64},{128,96},{160,128},{192,160},{224,1... | collective-permute-start | bytes 393224 | tf_op jit(solution)/shard_map/ppermute | solution.py:378
  123.4 18.9 %collective-permute-start.17 = (bf16[256,128]{1,0:T(8,128)(2,1)S(1)}, bf16[256,128]{1,0:T(8,128)(2,1)S(1)}, u32[]{:S(2)}, u32[]{:S(2)}) collective-permute-start(bf16[256,128]{1,0:T(8,128)(2,1)S(1)} %get-tuple-element.50), channel_id=1, source_target_pairs={{0,0},{1,1},{2,34},{3,35},{4,68},{5,69},{6,102},{7,103},{8,136},{9... | collective-permute-start | bytes 196616 | tf_op jit(solution)/shard_map/ppermute | solution.py:422
  125.5 16.8 %collective-permute-start.18 = (bf16[256,128]{1,0:T(8,128)(2,1)S(1)}, bf16[256,128]{1,0:T(8,128)(2,1)S(1)}, u32[]{:S(2)}, u32[]{:S(2)}) collective-permute-start(bf16[256,128]{1,0:T(8,128)(2,1)S(1)} %get-tuple-element.50), channel_id=1, source_target_pairs={{0,8},{1,9},{2,42},{3,43},{4,76},{5,77},{6,110},{7,111},{8,128},{9... | collective-permute-start | bytes 196616 | tf_op jit(solution)/shard_map/ppermute | solution.py:422
  142.3 13.3 %copy-start.9 = (bf16[4,128,128]{2,1,0:T(8,128)(2,1)}, bf16[4,128,128]{2,1,0:T(8,128)(2,1)S(1)}, u32[]{:S(2)}) copy-start(bf16[4,128,128]{2,1,0:T(8,128)(2,1)S(1)} %collective-permute-done.20.refs_3_) | copy-start | bytes 393220
  142.3 13.3 %copy-start.10 = (bf16[4,128,128]{2,1,0:T(8,128)(2,1)}, bf16[4,128,128]{2,1,0:T(8,128)(2,1)S(1)}, u32[]{:S(2)}) copy-start(bf16[4,128,128]{2,1,0:T(8,128)(2,1)S(1)} %collective-permute-done.22.refs_7_) | copy-start | bytes 393220
  143.2 6.3 %collective-permute-start.23 = (bf16[4,128,128]{2,1,0:T(8,128)(2,1)S(1)}, bf16[4,128,128]{2,1,0:T(8,128)(2,1)S(1)}, u32[]{:S(2)}, u32[]{:S(2)}) collective-permute-start(bf16[4,128,128]{2,1,0:T(8,128)(2,1)S(1)} %collective-permute-done.20.refs_3_), channel_id=1, source_target_pairs={{0,32},{32,64},{64,96},{96,128},{128,160},{160,192},{192,224},{224... | collective-permute-start | bytes 393224 | tf_op jit(solution)/shard_map/ppermute | solution.py:378
  143.3 6.2 %collective-permute-start.25 = (bf16[4,128,128]{2,1,0:T(8,128)(2,1)S(1)}, bf16[4,128,128]{2,1,0:T(8,128)(2,1)S(1)}, u32[]{:S(2)}, u32[]{:S(2)}) collective-permute-start(bf16[4,128,128]{2,1,0:T(8,128)(2,1)S(1)} %collective-permute-done.22.refs_7_), channel_id=1, source_target_pairs={{0,224},{32,0},{64,32},{96,64},{128,96},{160,128},{192,160},{224,1... | collective-permute-start | bytes 393224 | tf_op jit(solution)/shard_map/ppermute | solution.py:378
  149.4 6.2 %copy-start.11 = (bf16[4,128,128]{2,1,0:T(8,128)(2,1)}, bf16[4,128,128]{2,1,0:T(8,128)(2,1)S(1)}, u32[]{:S(2)}) copy-start(bf16[4,128,128]{2,1,0:T(8,128)(2,1)S(1)} %collective-permute-done.23.refs_4_) | copy-start | bytes 393220
  149.4 6.2 %collective-permute-start.24 = (bf16[4,128,128]{2,1,0:T(8,128)(2,1)S(1)}, bf16[4,128,128]{2,1,0:T(8,128)(2,1)S(1)}, u32[]{:S(2)}, u32[]{:S(2)}) collective-permute-start(bf16[4,128,128]{2,1,0:T(8,128)(2,1)S(1)} %collective-permute-done.23.refs_4_), channel_id=1, source_target_pairs={{0,32},{32,64},{64,96},{96,128},{128,160},{160,192},{192,224},{224... | collective-permute-start | bytes 393224 | tf_op jit(solution)/shard_map/ppermute | solution.py:378
  149.4 6.2 %copy-start.12 = (bf16[4,128,128]{2,1,0:T(8,128)(2,1)}, bf16[4,128,128]{2,1,0:T(8,128)(2,1)S(1)}, u32[]{:S(2)}) copy-start(bf16[4,128,128]{2,1,0:T(8,128)(2,1)S(1)} %collective-permute-done.25.refs_8_) | copy-start | bytes 393220
  155.7 0.7 copy-start.13
  163.1 28.5 %all-to-all-start.2 = ((f32[8,64,1024]{2,1,0:T(8,128)}), f32[8,64,1024]{2,1,0:T(8,128)S(1)}, u32[]{:S(2)}, u32[]{:S(2)}) async-start(f32[8,64,1024]{2,1,0:T(8,128)} %bitcast.5), calls=%async_computation.2 | async-start | bytes 4194304 | tf_op jit(solution)/shard_map/all_to_all | solution.py:448
  170.0 21.5 %collective-permute-start.27 = (bf16[4,4,256,128]{3,2,1,0:T(8,128)(2,1)}, bf16[4,4,256,128]{3,2,1,0:T(8,128)(2,1)S(1)}, u32[]{:S(2)}, u32[]{:S(2)}) collective-permute-start(bf16[4,4,256,128]{3,2,1,0:T(8,128)(2,1)} %bitcast.3), channel_id=1, source_target_pairs={{0,1},{1,0},{2,3},{3,2},{4,5},{5,4},{6,7},{7,6},{8,9},{9,8},{10,11... | collective-permute-start | bytes 3145736 | tf_op jit(solution)/shard_map/ppermute | solution.py:374
  191.6 1.2 copy-start
Sparse Core Ops, SparseCore 0:
  75.4 45.3 all-gather.4
  143.3 22.1 all-gather.6

commit v9 on v8

--- a/solution.py
+++ b/solution.py
@@ -336,7 +336,7 @@
                 held = features[flip_core].at[x]
                 term = lax.dot_general(
                     rows[:, pl.ds(start, 256)],
-                    jnp.concatenate([held[flip_yh * 2], held[flip_yh * 2 + 1]], axis=1),
+                    jnp.concatenate([held[flip_yh, 0], held[flip_yh, 1]], axis=1),
                     (((1,), (1,)), ((), ())),
                     preferred_element_type=F32,
                 )
@@ -378,16 +378,14 @@
     return lax.ppermute(value, ("zh", "zl"), [(i, (i + by) % 8) for i in range(8)])
 
 
-def ring(value, beside):
+def ring(value):
     up = [step_z(value, 1)]
     down = [step_z(value, 7)]
-    up.append(step_z(up[0], 1))
-    down.append(step_z(down[0], 7))
-    beside, up[1], down[1] = lax.optimization_barrier((beside, up[1], down[1]))
-    up.append(step_z(up[1], 1))
-    down.append(step_z(down[1], 7))
-    up.append(step_z(up[2], 1))
-    return beside, [value] + up + down
+    for _ in range(2):
+        up.append(step_z(up[-1], 1))
+        down.append(step_z(down[-1], 7))
+    up.append(step_z(up[-1], 1))
+    return [value] + up + down
 
 
 def flips(keep, send):
@@ -436,15 +434,13 @@
     whole, keep, send = sum_parts(part)
     mine = flips(keep, send)
     low = lax.all_gather(mine, ("zh", "zl"), axis=0)
-    turned = turn(whole)
-    next_part, mine, turned = lax.optimization_barrier((next_part, mine, turned))
-    whole, keep, send = sum_parts(next_part)
-    whole, mine = lax.optimization_barrier((whole, flips(keep, send)))
-    next_turned, high = ring(mine, turn(whole))
-    near = join([turned[0], next_turned[0], turned[1], next_turned[1]])
-    near, low = lax.optimization_barrier((near, low))
-    near = lax.all_gather(near, "x", axis=0)
+    next_part, mine = lax.optimization_barrier((next_part, mine))
+    next_whole, keep, send = sum_parts(next_part)
+    next_whole, high = lax.optimization_barrier((next_whole, ring(flips(keep, send))))
+    turned = turn(join([whole, next_whole]))
     conditioned = condition(low, high, inverse_gram, other_tile)
+    conditioned, turned = lax.optimization_barrier((conditioned, turned))
+    near = lax.all_gather(join(turned), "x", axis=0)
     parts = lax.all_to_all(conditioned.reshape(8, 64, 1024), CHIPS, 0, 0, tiled=True)
     return finish(lax.all_to_all(pair(parts, near, swap(near, "c")), EX, 0, 0, tiled=True))
 

time: 221 us -> 231 us (1.045); the launches traced: 217 us -> 230 us
  blocking collectives: 14.5 us -> 39.6 us
  starting transfers between devices: 67.4 us -> 49 us
  waiting for transfers between devices: 63.7 us -> 71 us
    all_gather x1, waiting for transfers between devices: 0.01 us -> 32.8 us  [per_device(): near = lax.all_gather(join(turned), 'x', axis=0)]
    all_to_all x1, waiting for transfers between devices: 21.5 us -> 0.01 us  [per_device(): lax.all_to_all(conditioned.reshape(8, 64, 1024), CHIPS, 0, 0, tiled=True)]
    all_to_all x0 -> x1, blocking collectives: none -> 19.8 us  [per_device(): next_part = lax.all_to_all(partial, CHIPS, 0, 0, tiled=True)]
    ppermute x4 -> x2, starting transfers between devices: 22.5 us -> 10.7 us  [turn(): lax.ppermute(value, EX + PAR, [(((z * 2 + yl) * 8 + chip) * 2 + c, ((chip...]
    ppermute x4 -> x2, waiting for transfers between devices: 18.1 us -> 8.42 us  [turn(): lax.ppermute(value, EX + PAR, [(((z * 2 + yl) * 8 + chip) * 2 + c, ((chip...]
    all_to_all x1 -> x0, starting transfers between devices: 7.21 us -> none  [per_device(): next_part = lax.all_to_all(partial, CHIPS, 0, 0, tiled=True)]
    all_to_all x1, blocking collectives: 14.5 us -> 19.8 us  [per_device(): lax.all_to_all(pair(parts, near, swap(near, 'c')), EX, 0, 0, tiled=True)]
    ppermute x7, waiting for transfers between devices: 13.2 us -> 16.6 us  [step_z(): lax.ppermute(value, ('zh', 'zl'), [(i, (i + by) % 8) for i in range(8)])]
  transfers between devices with their start and end apart: 33 -> 30, of which waited for: 17 -> 18; matrix products, arithmetic and copies ran while one was open for 0% -> 0% of each run, Pallas kernels for 19% -> 18%
where the time goes in v9:
time: 231 us; the launch traced here: 230 us
  waiting for transfers between devices  71 us (31%)
  Pallas kernels  52.6 us (23%)
  starting transfers between devices  49 us (21%)
  blocking collectives  39.6 us (17%)
  between operations  13.7 us (6%)
  local copies, waits for them, and re-layouts  4.57 us (2%)
    all_gather x1, waiting for transfers between devices, per_device(): near = lax.all_gather(join(turned), 'x', axis=0)  32.8 us
    all_to_all x1, blocking collectives, per_device(): lax.all_to_all(pair(parts, near, swap(near, 'c')), EX, 0, 0, tiled=True)  19.8 us
    all_to_all x1, blocking collectives, per_device(): next_part = lax.all_to_all(partial, CHIPS, 0, 0, tiled=True)  19.8 us
    pallas_call x1, Pallas kernels, project_hash(): pl.pallas_call(functools.partial(hash_kernel, part, width), out_shape=jax...  17.9 us
    ppermute x7, waiting for transfers between devices, step_z(): lax.ppermute(value, ('zh', 'zl'), [(i, (i + by) % 8) for i in range(8)])  16.6 us
    pallas_call x2, Pallas kernels, table(): pl.pallas_call(functools.partial(table_kernel, part, width, first, params...  15.8 us
    ppermute x17, waiting for transfers between devices, swap(): return lax.ppermute(value, axis, [(0, 1), (1, 0)])  13.2 us
    ppermute x7, starting transfers between devices, step_z(): lax.ppermute(value, ('zh', 'zl'), [(i, (i + by) % 8) for i in range(8)])  11.9 us
  transfers between devices with their start and end apart: 30, of which 18 were waited for; matrix products, arithmetic and copies ran while one was open for 0% of the time, Pallas kernels for 18%

profile of v9, /device:TPU:22, one launch (start us, length us, event | category | flops | bytes accessed | tf_op | source)
XLA Modules:
  0.0 230.5 jit_solution(16360347559624682316)
XLA Ops:
  6.5 1.3 collective-permute-start
  7.8 1.9 collective-permute-start.1
  9.7 0.7 copy-done.4
  10.4 9.7 %shard_map.37.first = bf16[5120,1024]{1,0:T(8,128)(2,1)S(1)} custom-call(s32[4]{0:T(128)S(1)} %copy-done.4), custom_call_target="tpu_custom_call" | custom-call | flops 6291456000 | bytes 10485760 | tf_op jit(solution)/shard_map/pallas_call | solution.py:68
  20.1 0.3 collective-permute-done.refs_1_
  20.4 1.2 collective-permute-done.1.refs_2_
  21.6 0.1 collective-permute-start.5
  21.8 0.0 copy-start.2
  21.8 0.6 collective-permute-start.6
  22.4 1.7 collective-permute-start.2
  24.1 0.7 collective-permute-start.3
  24.8 6.0 %shard_map.38.second = bf16[3072,1024]{1,0:T(8,128)(2,1)S(1)} custom-call(s32[4]{0:T(128)S(1)} %copy-done.5), custom_call_target="tpu_custom_call" | custom-call | flops 3774873600 | bytes 6291456 | tf_op jit(solution)/shard_map/pallas_call | solution.py:68
  30.9 1.2 collective-permute-done.3.refs_4_
  32.1 0.0 collective-permute-start.7
  32.1 0.5 collective-permute-start.8
  32.6 1.0 collective-permute-done.7.refs_8_
  33.6 0.4 collective-permute-done.8.refs_9_
  34.0 8.0 %shard_map.39 = (f32[8,256,128]{2,1,0:T(8,128)}, bf16[256,8192]{1,0:T(8,128)(2,1)S(1)}) custom-call(bf16[5120,1024]{1,0:T(8,128)(2,1)S(1)} %shard_map.37.first, bf16[3072,1024]{1,0:T(8,128)(2,1)S(1)} %shard_map.38.second, bf16[64,4096]{1,0:T(8,128)(2,1)S(1)} %copy-done.2, bf16[64,4096]{1,0:T(8,128)(2,1)S(1)} %collective-permute-done.refs_1_, ...), custom_call_target="tpu_custom_call" | custom-call | flops 4294967296 | bytes 16777216 | tf_op jit(solution)/shard_map/pallas_call | solution.py:140
  42.1 2.0 copy-done.3
  44.0 7.3 %all-to-all-start = ((f32[8,256,128]{2,1,0:T(8,128)}), f32[8,256,128]{2,1,0:T(8,128)S(1)}, u32[]{:S(2)}, u32[]{:S(2)}) async-start(f32[8,256,128]{2,1,0:T(8,128)} %get-tuple-element.41), calls=%async_computation | async-start | bytes 2097152 | tf_op jit(solution)/shard_map/all_to_all | solution.py:413
  51.3 0.1 collective-permute-start.22
  51.4 17.9 %shard_map.40 = f32[8,256,128]{2,1,0:T(8,128)} custom-call(s32[4]{0:T(128)} %words.5, bf16[256,8192]{1,0:T(8,128)(2,1)} %copy-done.3), custom_call_target="tpu_custom_call" | custom-call | flops 4294967296 | bytes 16777216 | tf_op jit(solution)/shard_map/pallas_call | solution.py:199
  69.4 0.1 shard_map.41
  69.5 0.6 collective-permute-start.9
  70.0 0.7 collective-permute-start.10
  70.8 0.1 collective-permute-done.9.refs_1_
  70.9 1.2 collective-permute-start.11
  72.1 2.0 collective-permute-done.10.refs_2_
  74.1 0.8 collective-permute-done.11.refs_3_
  74.8 0.7 shard_map.42
  75.5 0.0 all-gather.5.cloned.1.call-update
  75.5 0.0 all-gather.7.cloned.1.call-start
  75.5 19.8 %all_to_all.20.part = f32[8,256,128]{2,1,0:T(8,128)S(1)} all-to-all(f32[8,256,128]{2,1,0:T(8,128)} %shard_map.40), channel_id=1, replica_groups=mesh['zh'=4,'zl'=2,'yl'=2,'yh'=2,'x'=4,'c'=2] {'yh','x'}, dimensions={0} | all-to-all | bytes 2097152 | tf_op jit(solution)/shard_map/all_to_all | solution.py:416
  95.3 0.1 shard_map.43
  95.4 0.1 collective-permute-start.12
  95.5 0.8 collective-permute-start.13
  96.3 0.4 collective-permute-done.12.refs_1_
  96.7 0.9 collective-permute-start.14
  97.6 1.9 collective-permute-done.13.refs_2_
  99.5 1.1 collective-permute-done.14.refs_3_
  100.6 0.5 collective-permute-start.15
  101.1 4.7 %collective-permute-start.19 = (bf16[4,128,128]{2,1,0:T(8,128)(2,1)S(1)}, bf16[4,128,128]{2,1,0:T(8,128)(2,1)S(1)}, u32[]{:S(2)}, u32[]{:S(2)}) collective-permute-start(bf16[4,128,128]{2,1,0:T(8,128)(2,1)S(1)} %shard_map.44.refs_1_), channel_id=1, source_target_pairs={{0,224},{32,0},{64,32},{96,64},{128,96},{160,128},{192,160},{224,1... | collective-permute-start | bytes 393224 | tf_op jit(solution)/shard_map/ppermute | solution.py:378
  105.7 4.7 %collective-permute-done.15.refs_2_ = bf16[4,128,128]{2,1,0:T(8,128)(2,1)S(1)} collective-permute-done((bf16[4,128,128]{2,1,0:T(8,128)(2,1)S(1)}, bf16[4,128,128]{2,1,0:T(8,128)(2,1)S(1)}, u32[]{:S(2)}, u32[]{:S(2)}) %collective-permute-start.15) | collective-permute-done | bytes 131104 | tf_op jit(solution)/shard_map/ppermute | solution.py:378
  110.4 3.5 %collective-permute-start.20 = (bf16[4,128,128]{2,1,0:T(8,128)(2,1)S(1)}, bf16[4,128,128]{2,1,0:T(8,128)(2,1)S(1)}, u32[]{:S(2)}, u32[]{:S(2)}) collective-permute-start(bf16[4,128,128]{2,1,0:T(8,128)(2,1)S(1)} %collective-permute-done.19.refs_6_), channel_id=1, source_target_pairs={{0,224},{32,0},{64,32},{96,64},{128,96},{160,128},{192,160},{224,1... | collective-permute-start | bytes 393224 | tf_op jit(solution)/shard_map/ppermute | solution.py:378
  113.9 2.9 %collective-permute-done.16.refs_3_ = bf16[4,128,128]{2,1,0:T(8,128)(2,1)S(1)} collective-permute-done((bf16[4,128,128]{2,1,0:T(8,128)(2,1)S(1)}, bf16[4,128,128]{2,1,0:T(8,128)(2,1)S(1)}, u32[]{:S(2)}, u32[]{:S(2)}) %collective-permute-start.16) | collective-permute-done | bytes 131104 | tf_op jit(solution)/shard_map/ppermute | solution.py:378
  116.8 3.3 %collective-permute-start.21 = (bf16[4,128,128]{2,1,0:T(8,128)(2,1)S(1)}, bf16[4,128,128]{2,1,0:T(8,128)(2,1)S(1)}, u32[]{:S(2)}, u32[]{:S(2)}) collective-permute-start(bf16[4,128,128]{2,1,0:T(8,128)(2,1)S(1)} %collective-permute-done.20.refs_7_), channel_id=1, source_target_pairs={{0,224},{32,0},{64,32},{96,64},{128,96},{160,128},{192,160},{224,1... | collective-permute-start | bytes 393224 | tf_op jit(solution)/shard_map/ppermute | solution.py:378
  120.1 2.9 %collective-permute-done.17.refs_4_ = bf16[4,128,128]{2,1,0:T(8,128)(2,1)S(1)} collective-permute-done((bf16[4,128,128]{2,1,0:T(8,128)(2,1)S(1)}, bf16[4,128,128]{2,1,0:T(8,128)(2,1)S(1)}, u32[]{:S(2)}, u32[]{:S(2)}) %collective-permute-start.17) | collective-permute-done | bytes 131104 | tf_op jit(solution)/shard_map/ppermute | solution.py:378
  123.0 6.2 %collective-permute-done.18.refs_5_ = bf16[4,128,128]{2,1,0:T(8,128)(2,1)S(1)} collective-permute-done((bf16[4,128,128]{2,1,0:T(8,128)(2,1)S(1)}, bf16[4,128,128]{2,1,0:T(8,128)(2,1)S(1)}, u32[]{:S(2)}, u32[]{:S(2)}) %collective-permute-start.18) | collective-permute-done | bytes 131104 | tf_op jit(solution)/shard_map/ppermute | solution.py:378
  129.2 0.7 copy-done.13
  129.8 1.9 collective-permute-start.23
  131.7 8.8 %collective-permute-start.24 = (bf16[2,256,128]{2,1,0:T(8,128)(2,1)S(1)}, bf16[2,256,128]{2,1,0:T(8,128)(2,1)S(1)}, u32[]{:S(2)}, u32[]{:S(2)}) collective-permute-start(bf16[2,256,128]{2,1,0:T(8,128)(2,1)S(1)} %shard_map.46), channel_id=1, source_target_pairs={{0,8},{1,9},{2,42},{3,43},{4,76},{5,77},{6,110},{7,111},{8,128},{9... | collective-permute-start | bytes 393224 | tf_op jit(solution)/shard_map/ppermute | solution.py:420
  140.5 0.0 all-gather.5.cloned.1.call-done
  140.6 6.7 %shard_map.45 = f32[512,1024]{1,0:T(8,128)} custom-call(bf16[8,4,128,128]{3,2,1,0:T(8,128)(2,1)} %bitcast.6, bf16[4,128,128]{2,1,0:T(8,128)(2,1)} %copy-done.1, bf16[4,128,128]{2,1,0:T(8,128)(2,1)} %copy-done.7, bf16[4,128,128]{2,1,0:T(8,128)(2,1)} %copy-done.9, bf16[4,128,128]{2,1,0:T(8,128)(2,1)} %copy-done.11, bf16[4,128,128]{2,1,0:T(8,128)(2,1)} %copy-done.13, ...), custom_call_target="tpu_custom_call" | custom-call | flops 2147483648 | bytes 7340032 | tf_op jit(solution)/shard_map/pallas_call | solution.py:293
  147.4 8.4 %collective-permute-done.23.refs_0_ = bf16[2,256,128]{2,1,0:T(8,128)(2,1)S(1)} collective-permute-done((bf16[2,256,128]{2,1,0:T(8,128)(2,1)S(1)}, bf16[2,256,128]{2,1,0:T(8,128)(2,1)S(1)}, u32[]{:S(2)}, u32[]{:S(2)}) %collective-permute-start.23) | collective-permute-done | bytes 131104 | tf_op jit(solution)/shard_map/ppermute | solution.py:420
  155.8 0.7 shard_map.47
  156.5 0.0 all-gather.7.cloned.1.call-update
  156.5 7.8 %all-to-all-start.2 = ((f32[8,64,1024]{2,1,0:T(8,128)}), f32[8,64,1024]{2,1,0:T(8,128)S(1)}, u32[]{:S(2)}, u32[]{:S(2)}) async-start(f32[8,64,1024]{2,1,0:T(8,128)} %bitcast.5), calls=%async_computation.2 | async-start | bytes 4194304 | tf_op jit(solution)/shard_map/all_to_all | solution.py:444
  164.3 32.8 %all-gather.7.cloned.1.call-done = bf16[8,2,256,128]{3,2,1,0:T(8,128)(2,1)} async-done(((bf16[2,2,256,128]{3,2,1,0:T(8,128)(2,1)}), bf16[8,2,256,128]{3,2,1,0:T(8,128)(2,1)}) %all-gather.7.cloned.1.call-update) | async-done | bytes 1048592 | tf_op jit(solution)/shard_map/all_gather | solution.py:443
  197.1 0.0 collective-permute-start.25
  197.1 2.8 %collective-permute-done.25.refs_1_ = bf16[4,2,2,256,128]{4,3,2,1,0:T(8,128)(2,1)S(1)} collective-permute-done((bf16[4,2,2,256,128]{4,3,2,1,0:T(8,128)(2,1)}, bf16[4,2,2,256,128]{4,3,2,1,0:T(8,128)(2,1)S(1)}, u32[]{:S(2)}, u32[]{:S(2)}) %collective-permute-start.25) | collective-permute-done | bytes 1048608 | tf_op jit(solution)/shard_map/ppermute | solution.py:374
  199.9 1.2 copy-done
  201.2 1.0 shard_map.48
  202.2 19.8 %all_to_all.21.parts = f32[16,32,128]{2,1,0:T(8,128)} all-to-all(f32[16,32,128]{2,1,0:T(8,128)S(1)} %shard_map.48), channel_id=1, replica_groups=mesh['zh'=4,'zl'=2,'yl'=2,'yh'=2,'x'=4,'c'=2] {'zh','zl','yl'}, dimensions={0} | all-to-all | bytes 524288 | tf_op jit(solution)/shard_map/all_to_all | solution.py:445
  222.0 1.7 shard_map.49
  (43 shorter events, 0.1 us)
Async XLA Ops:
  6.5 13.9 %collective-permute-start = (bf16[64,4096]{1,0:T(8,128)(2,1)}, bf16[64,4096]{1,0:T(8,128)(2,1)S(1)}, u32[]{:S(2)}, u32[]{:S(2)}) collective-permute-start(bf16[64,4096]{1,0:T(8,128)(2,1)} %refs_0_.1), channel_id=1, source_target_pairs={{0,16},{16,0},{1,17},{17,1},{2,18},{18,2},{3,19},{19,3},{4,20},{20... | collective-permute-start | bytes 1572872 | tf_op jit(solution)/shard_map/ppermute | solution.py:374
  7.8 13.8 %collective-permute-start.1 = (bf16[64,4096]{1,0:T(8,128)(2,1)}, bf16[64,4096]{1,0:T(8,128)(2,1)S(1)}, u32[]{:S(2)}, u32[]{:S(2)}) collective-permute-start(bf16[64,4096]{1,0:T(8,128)(2,1)} %refs_0_.1), channel_id=1, source_target_pairs={{0,32},{32,0},{1,33},{33,1},{2,34},{34,2},{3,35},{35,3},{4,36},{36... | collective-permute-start | bytes 1572872 | tf_op jit(solution)/shard_map/ppermute | solution.py:374
  9.7 22.9 %collective-permute-start.4 = (bf16[64,4096]{1,0:T(8,128)(2,1)}, bf16[64,4096]{1,0:T(8,128)(2,1)S(1)}, u32[]{:S(2)}, u32[]{:S(2)}) collective-permute-start(bf16[64,4096]{1,0:T(8,128)(2,1)} %refs_0_.1), channel_id=1, source_target_pairs={{0,1},{1,0},{2,3},{3,2},{4,5},{5,4},{6,7},{7,6},{8,9},{9,8},{10,11... | collective-permute-start | bytes 1572872 | tf_op jit(solution)/shard_map/ppermute | solution.py:374
  9.7 0.7 copy-start.4
  10.4 14.4 %copy-start.5 = (s32[4]{0:T(128)S(1)}, s32[4]{0:T(128)}, u32[]{:S(2)}) copy-start(s32[4]{0:T(128)} %words.5) | copy-start | bytes 52
  21.6 12.4 %collective-permute-start.5 = (bf16[64,4096]{1,0:T(8,128)(2,1)S(1)}, bf16[64,4096]{1,0:T(8,128)(2,1)S(1)}, u32[]{:S(2)}, u32[]{:S(2)}) collective-permute-start(bf16[64,4096]{1,0:T(8,128)(2,1)S(1)} %collective-permute-done.refs_1_), channel_id=1, source_target_pairs={{0,1},{1,0},{2,3},{3,2},{4,5},{5,4},{6,7},{7,6},{8,9},{9,8},{10,11... | collective-permute-start | bytes 1572872 | tf_op jit(solution)/shard_map/ppermute | solution.py:374
  21.8 12.3 %copy-start.2 = (bf16[64,4096]{1,0:T(8,128)(2,1)S(1)}, bf16[64,4096]{1,0:T(8,128)(2,1)}, u32[]{:S(2)}) copy-start(bf16[64,4096]{1,0:T(8,128)(2,1)} %refs_0_.1) | copy-start | bytes 1572868
  21.8 12.2 %collective-permute-start.6 = (bf16[64,4096]{1,0:T(8,128)(2,1)S(1)}, bf16[64,4096]{1,0:T(8,128)(2,1)S(1)}, u32[]{:S(2)}, u32[]{:S(2)}) collective-permute-start(bf16[64,4096]{1,0:T(8,128)(2,1)S(1)} %collective-permute-done.1.refs_2_), channel_id=1, source_target_pairs={{0,1},{1,0},{2,3},{3,2},{4,5},{5,4},{6,7},{7,6},{8,9},{9,8},{10,11... | collective-permute-start | bytes 1572872 | tf_op jit(solution)/shard_map/ppermute | solution.py:374
  22.4 8.5 %collective-permute-start.2 = (bf16[32,4096]{1,0:T(8,128)(2,1)S(1)}, bf16[32,4096]{1,0:T(8,128)(2,1)S(1)}, u32[]{:S(2)}, u32[]{:S(2)}) collective-permute-start(bf16[32,4096]{1,0:T(8,128)(2,1)S(1)} %slice.6), channel_id=1, source_target_pairs={{0,32},{32,0},{1,33},{33,1},{2,34},{34,2},{3,35},{35,3},{4,36},{36... | collective-permute-start | bytes 786440 | tf_op jit(solution)/shard_map/ppermute | solution.py:374
  24.1 8.0 %collective-permute-start.3 = (bf16[32,4096]{1,0:T(8,128)(2,1)S(1)}, bf16[32,4096]{1,0:T(8,128)(2,1)S(1)}, u32[]{:S(2)}, u32[]{:S(2)}) collective-permute-start(bf16[32,4096]{1,0:T(8,128)(2,1)S(1)} %slice.7), channel_id=1, source_target_pairs={{0,16},{16,0},{1,17},{17,1},{2,18},{18,2},{3,19},{19,3},{4,20},{20... | collective-permute-start | bytes 786440 | tf_op jit(solution)/shard_map/ppermute | solution.py:374
  32.1 1.5 collective-permute-start.7
  32.1 1.9 collective-permute-start.8
  42.1 2.0 copy-start.3
  44.0 7.3 %copy-start.6 = (bf16[1024,1024]{1,0:T(8,128)(2,1)S(1)}, bf16[1024,1024]{1,0:T(8,128)(2,1)}, u32[]{:S(2)}) copy-start(bf16[1024,1024]{1,0:T(8,128)(2,1)} %refs_9_.1) | copy-start | bytes 6291460
  44.0 25.4 %all-to-all-start = ((f32[8,256,128]{2,1,0:T(8,128)}), f32[8,256,128]{2,1,0:T(8,128)S(1)}, u32[]{:S(2)}, u32[]{:S(2)}) async-start(f32[8,256,128]{2,1,0:T(8,128)} %get-tuple-element.41), calls=%async_computation | async-start | bytes 2097152 | tf_op jit(solution)/shard_map/all_to_all | solution.py:413
  51.3 89.2 %all-gather.5.cloned.1.call-start = ((), (), s32[]{:S(2)}) async-start(), calls=%async_computation.4 | async-start | bytes 1179648 | tf_op jit(solution)/shard_map/all_gather | solution.py:436
  51.3 89.2 %collective-permute-start.22 = (bf16[1024,1024]{1,0:T(8,128)(2,1)S(1)}, bf16[1024,1024]{1,0:T(8,128)(2,1)}, u32[]{:S(2)}, u32[]{:S(2)}) collective-permute-start(bf16[1024,1024]{1,0:T(8,128)(2,1)S(1)} %copy-done.6), channel_id=1, source_target_pairs={{0,1},{1,0},{2,3},{3,2},{4,5},{5,4},{6,7},{7,6},{8,9},{9,8},{10,11... | collective-permute-start | bytes 6291464 | tf_op jit(solution)/shard_map/ppermute | solution.py:374
  69.5 1.4 collective-permute-start.9
  70.0 4.0 %collective-permute-start.10 = (bf16[128,128]{1,0:T(8,128)(2,1)S(1)}, bf16[128,128]{1,0:T(8,128)(2,1)S(1)}, u32[]{:S(2)}, u32[]{:S(2)}) collective-permute-start(bf16[128,128]{1,0:T(8,128)(2,1)S(1)} %get-tuple-element.43.refs_0_), channel_id=1, source_target_pairs={{0,16},{16,0},{1,17},{17,1},{2,18},{18,2},{3,19},{19,3},{4,20},{20... | collective-permute-start | bytes 98312 | tf_op jit(solution)/shard_map/ppermute | solution.py:374
  70.9 3.9 %collective-permute-start.11 = (bf16[128,128]{1,0:T(8,128)(2,1)S(1)}, bf16[128,128]{1,0:T(8,128)(2,1)S(1)}, u32[]{:S(2)}, u32[]{:S(2)}) collective-permute-start(bf16[128,128]{1,0:T(8,128)(2,1)S(1)} %collective-permute-done.9.refs_1_), channel_id=1, source_target_pairs={{0,16},{16,0},{1,17},{17,1},{2,18},{18,2},{3,19},{19,3},{4,20},{20... | collective-permute-start | bytes 98312 | tf_op jit(solution)/shard_map/ppermute | solution.py:374
  75.5 121.6 %all-gather.7.cloned.1.call-start = ((), (), s32[]{:S(2)}) async-start(), calls=%async_computation.5 | async-start | bytes 1310720 | tf_op jit(solution)/shard_map/all_gather | solution.py:443
  95.4 1.3 collective-permute-start.12
  95.5 4.1 %collective-permute-start.13 = (bf16[128,128]{1,0:T(8,128)(2,1)S(1)}, bf16[128,128]{1,0:T(8,128)(2,1)S(1)}, u32[]{:S(2)}, u32[]{:S(2)}) collective-permute-start(bf16[128,128]{1,0:T(8,128)(2,1)S(1)} %get-tuple-element.48.refs_0_), channel_id=1, source_target_pairs={{0,16},{16,0},{1,17},{17,1},{2,18},{18,2},{3,19},{19,3},{4,20},{20... | collective-permute-start | bytes 98312 | tf_op jit(solution)/shard_map/ppermute | solution.py:374
  96.7 3.9 %collective-permute-start.14 = (bf16[128,128]{1,0:T(8,128)(2,1)S(1)}, bf16[128,128]{1,0:T(8,128)(2,1)S(1)}, u32[]{:S(2)}, u32[]{:S(2)}) collective-permute-start(bf16[128,128]{1,0:T(8,128)(2,1)S(1)} %collective-permute-done.12.refs_1_), channel_id=1, source_target_pairs={{0,16},{16,0},{1,17},{17,1},{2,18},{18,2},{3,19},{19,3},{4,20},{20... | collective-permute-start | bytes 98312 | tf_op jit(solution)/shard_map/ppermute | solution.py:374
  100.6 40.0 %copy-start.1 = (bf16[4,128,128]{2,1,0:T(8,128)(2,1)}, bf16[4,128,128]{2,1,0:T(8,128)(2,1)S(1)}, u32[]{:S(2)}) copy-start(bf16[4,128,128]{2,1,0:T(8,128)(2,1)S(1)} %shard_map.44.refs_1_) | copy-start | bytes 393220
  100.6 9.8 %collective-permute-start.15 = (bf16[4,128,128]{2,1,0:T(8,128)(2,1)S(1)}, bf16[4,128,128]{2,1,0:T(8,128)(2,1)S(1)}, u32[]{:S(2)}, u32[]{:S(2)}) collective-permute-start(bf16[4,128,128]{2,1,0:T(8,128)(2,1)S(1)} %shard_map.44.refs_1_), channel_id=1, source_target_pairs={{0,32},{32,64},{64,96},{96,128},{128,160},{160,192},{192,224},{224... | collective-permute-start | bytes 393224 | tf_op jit(solution)/shard_map/ppermute | solution.py:378
  101.1 9.3 %collective-permute-start.19 = (bf16[4,128,128]{2,1,0:T(8,128)(2,1)S(1)}, bf16[4,128,128]{2,1,0:T(8,128)(2,1)S(1)}, u32[]{:S(2)}, u32[]{:S(2)}) collective-permute-start(bf16[4,128,128]{2,1,0:T(8,128)(2,1)S(1)} %shard_map.44.refs_1_), channel_id=1, source_target_pairs={{0,224},{32,0},{64,32},{96,64},{128,96},{160,128},{192,160},{224,1... | collective-permute-start | bytes 393224 | tf_op jit(solution)/shard_map/ppermute | solution.py:378
  110.4 30.2 %copy-start.7 = (bf16[4,128,128]{2,1,0:T(8,128)(2,1)}, bf16[4,128,128]{2,1,0:T(8,128)(2,1)S(1)}, u32[]{:S(2)}) copy-start(bf16[4,128,128]{2,1,0:T(8,128)(2,1)S(1)} %collective-permute-done.15.refs_2_) | copy-start | bytes 393220
  110.4 6.4 %collective-permute-start.16 = (bf16[4,128,128]{2,1,0:T(8,128)(2,1)S(1)}, bf16[4,128,128]{2,1,0:T(8,128)(2,1)S(1)}, u32[]{:S(2)}, u32[]{:S(2)}) collective-permute-start(bf16[4,128,128]{2,1,0:T(8,128)(2,1)S(1)} %collective-permute-done.15.refs_2_), channel_id=1, source_target_pairs={{0,32},{32,64},{64,96},{96,128},{128,160},{160,192},{192,224},{224... | collective-permute-start | bytes 393224 | tf_op jit(solution)/shard_map/ppermute | solution.py:378
  110.4 30.2 %copy-start.8 = (bf16[4,128,128]{2,1,0:T(8,128)(2,1)}, bf16[4,128,128]{2,1,0:T(8,128)(2,1)S(1)}, u32[]{:S(2)}) copy-start(bf16[4,128,128]{2,1,0:T(8,128)(2,1)S(1)} %collective-permute-done.19.refs_6_) | copy-start | bytes 393220
  110.4 6.4 %collective-permute-start.20 = (bf16[4,128,128]{2,1,0:T(8,128)(2,1)S(1)}, bf16[4,128,128]{2,1,0:T(8,128)(2,1)S(1)}, u32[]{:S(2)}, u32[]{:S(2)}) collective-permute-start(bf16[4,128,128]{2,1,0:T(8,128)(2,1)S(1)} %collective-permute-done.19.refs_6_), channel_id=1, source_target_pairs={{0,224},{32,0},{64,32},{96,64},{128,96},{160,128},{192,160},{224,1... | collective-permute-start | bytes 393224 | tf_op jit(solution)/shard_map/ppermute | solution.py:378
  116.8 23.8 %copy-start.9 = (bf16[4,128,128]{2,1,0:T(8,128)(2,1)}, bf16[4,128,128]{2,1,0:T(8,128)(2,1)S(1)}, u32[]{:S(2)}) copy-start(bf16[4,128,128]{2,1,0:T(8,128)(2,1)S(1)} %collective-permute-done.16.refs_3_) | copy-start | bytes 393220
  116.8 6.2 %collective-permute-start.17 = (bf16[4,128,128]{2,1,0:T(8,128)(2,1)S(1)}, bf16[4,128,128]{2,1,0:T(8,128)(2,1)S(1)}, u32[]{:S(2)}, u32[]{:S(2)}) collective-permute-start(bf16[4,128,128]{2,1,0:T(8,128)(2,1)S(1)} %collective-permute-done.16.refs_3_), channel_id=1, source_target_pairs={{0,32},{32,64},{64,96},{96,128},{128,160},{160,192},{192,224},{224... | collective-permute-start | bytes 393224 | tf_op jit(solution)/shard_map/ppermute | solution.py:378
  116.8 23.8 %copy-start.10 = (bf16[4,128,128]{2,1,0:T(8,128)(2,1)}, bf16[4,128,128]{2,1,0:T(8,128)(2,1)S(1)}, u32[]{:S(2)}) copy-start(bf16[4,128,128]{2,1,0:T(8,128)(2,1)S(1)} %collective-permute-done.20.refs_7_) | copy-start | bytes 393220
  116.8 6.2 %collective-permute-start.21 = (bf16[4,128,128]{2,1,0:T(8,128)(2,1)S(1)}, bf16[4,128,128]{2,1,0:T(8,128)(2,1)S(1)}, u32[]{:S(2)}, u32[]{:S(2)}) collective-permute-start(bf16[4,128,128]{2,1,0:T(8,128)(2,1)S(1)} %collective-permute-done.20.refs_7_), channel_id=1, source_target_pairs={{0,224},{32,0},{64,32},{96,64},{128,96},{160,128},{192,160},{224,1... | collective-permute-start | bytes 393224 | tf_op jit(solution)/shard_map/ppermute | solution.py:378
  123.0 17.6 %copy-start.11 = (bf16[4,128,128]{2,1,0:T(8,128)(2,1)}, bf16[4,128,128]{2,1,0:T(8,128)(2,1)S(1)}, u32[]{:S(2)}) copy-start(bf16[4,128,128]{2,1,0:T(8,128)(2,1)S(1)} %collective-permute-done.17.refs_4_) | copy-start | bytes 393220
  123.0 6.2 %collective-permute-start.18 = (bf16[4,128,128]{2,1,0:T(8,128)(2,1)S(1)}, bf16[4,128,128]{2,1,0:T(8,128)(2,1)S(1)}, u32[]{:S(2)}, u32[]{:S(2)}) collective-permute-start(bf16[4,128,128]{2,1,0:T(8,128)(2,1)S(1)} %collective-permute-done.17.refs_4_), channel_id=1, source_target_pairs={{0,32},{32,64},{64,96},{96,128},{128,160},{160,192},{192,224},{224... | collective-permute-start | bytes 393224 | tf_op jit(solution)/shard_map/ppermute | solution.py:378
  123.0 17.6 %copy-start.12 = (bf16[4,128,128]{2,1,0:T(8,128)(2,1)}, bf16[4,128,128]{2,1,0:T(8,128)(2,1)S(1)}, u32[]{:S(2)}) copy-start(bf16[4,128,128]{2,1,0:T(8,128)(2,1)S(1)} %collective-permute-done.21.refs_8_) | copy-start | bytes 393220
  129.2 0.7 copy-start.13
  129.8 26.0 %collective-permute-start.23 = (bf16[2,256,128]{2,1,0:T(8,128)(2,1)S(1)}, bf16[2,256,128]{2,1,0:T(8,128)(2,1)S(1)}, u32[]{:S(2)}, u32[]{:S(2)}) collective-permute-start(bf16[2,256,128]{2,1,0:T(8,128)(2,1)S(1)} %shard_map.46), channel_id=1, source_target_pairs={{0,0},{1,1},{2,34},{3,35},{4,68},{5,69},{6,102},{7,103},{8,136},{9... | collective-permute-start | bytes 393224 | tf_op jit(solution)/shard_map/ppermute | solution.py:420
  131.7 24.0 %collective-permute-start.24 = (bf16[2,256,128]{2,1,0:T(8,128)(2,1)S(1)}, bf16[2,256,128]{2,1,0:T(8,128)(2,1)S(1)}, u32[]{:S(2)}, u32[]{:S(2)}) collective-permute-start(bf16[2,256,128]{2,1,0:T(8,128)(2,1)S(1)} %shard_map.46), channel_id=1, source_target_pairs={{0,8},{1,9},{2,42},{3,43},{4,76},{5,77},{6,110},{7,111},{8,128},{9... | collective-permute-start | bytes 393224 | tf_op jit(solution)/shard_map/ppermute | solution.py:420
  156.5 40.6 %all-to-all-start.2 = ((f32[8,64,1024]{2,1,0:T(8,128)}), f32[8,64,1024]{2,1,0:T(8,128)S(1)}, u32[]{:S(2)}, u32[]{:S(2)}) async-start(f32[8,64,1024]{2,1,0:T(8,128)} %bitcast.5), calls=%async_computation.2 | async-start | bytes 4194304 | tf_op jit(solution)/shard_map/all_to_all | solution.py:444
  197.1 2.9 %collective-permute-start.25 = (bf16[4,2,2,256,128]{4,3,2,1,0:T(8,128)(2,1)}, bf16[4,2,2,256,128]{4,3,2,1,0:T(8,128)(2,1)S(1)}, u32[]{:S(2)}, u32[]{:S(2)}) collective-permute-start(bf16[4,2,2,256,128]{4,3,2,1,0:T(8,128)(2,1)} %bitcast.3), channel_id=1, source_target_pairs={{0,1},{1,0},{2,3},{3,2},{4,5},{5,4},{6,7},{7,6},{8,9},{9,8},{10,11... | collective-permute-start | bytes 3145736 | tf_op jit(solution)/shard_map/ppermute | solution.py:374
  199.9 1.2 copy-start
Sparse Core Ops, SparseCore 0:
  75.6 41.0 all-gather.4
  156.7 40.3 all-gather.6

commit v10 on v9

--- a/solution.py
+++ b/solution.py
@@ -214,7 +214,7 @@
     )(words, gathered)
 
 
-def sum_kernel(part, whole, keep, send):
+def sum_kernel(part, keep, send, whole):
     core = lax.axis_index("c")
     total = part[0]
     for index in range(1, part.shape[0]):
@@ -228,10 +228,11 @@
 
 def sum_parts(part):
     _, rows, width = part.shape
-    shapes = [(rows, width), (rows // 2, width), (rows // 2, width)]
+    shapes = [(rows // 2, width), (rows // 2, width)]
     return pl.pallas_call(
         sum_kernel,
         out_shape=[jax.ShapeDtypeStruct(shape, BF16) for shape in shapes],
+        scratch_shapes=[pltpu.VMEM((rows, width), BF16)],
         compiler_params=pltpu.CompilerParams(vmem_limit_bytes=8 << 20),
     )(part)
 
@@ -318,41 +319,68 @@
     )(*values)
 
 
-def pair_kernel(parts, *refs):
-    features, (out, rows, pairs) = refs[:2], refs[2:]
-    yh, core = lax.axis_index("yh"), lax.axis_index("c")
+def pack_kernel(low, *refs):
+    high, (out, arrived) = refs[:8], refs[8:]
+    z = lax.axis_index("zh") * 2 + lax.axis_index("zl")
+    copies = []
+    for index, away in enumerate(RING):
+        for run, source in enumerate((low.at[(z + (away + 8)) & 7, 0:2], high[index].at[0:2])):
+            copies.append(pltpu.make_async_copy(source, out.at[run, index], arrived.at[index * 2 + run]))
+    for copy in copies:
+        copy.start()
+    for copy in copies:
+        copy.wait()
+
+
+def pack(low, high):
+    _, _, rows, width = low.shape
+    return pl.pallas_call(
+        pack_kernel,
+        out_shape=jax.ShapeDtypeStruct((2, 8, 2, rows, width), BF16),
+        in_specs=[pl.BlockSpec(memory_space=pltpu.HBM)] * 9,
+        out_specs=pl.BlockSpec(memory_space=pltpu.HBM),
+        scratch_shapes=[pltpu.SemaphoreType.DMA((16,))],
+        compiler_params=pltpu.CompilerParams(vmem_limit_bytes=4 << 20),
+    )(low, *high)
+
+
+def pair_kernel(parts, near, far, out, rows, pairs):
+    core = lax.axis_index("c")
     place = lax.axis_index("zh") * 2 + lax.axis_index("zl")
+    origin = (lax.axis_index("yh") * 4 + lax.axis_index("x")) ^ place
     total = parts[0]
     for index in range(1, parts.shape[0]):
         total += parts[index]
     rows[...] = total.astype(BF16)
-    pairs[...] = jnp.zeros_like(pairs)
-    for x in range(4):
-        for flip_yh in range(2):
-            source = (yh * 4 + x) ^ (flip_yh * 4) ^ place
+    for half, held in enumerate((near, far)):
+        for index, away in enumerate(RING):
+            source = (origin + (away + 8)) & 7
             value = None
-            for flip_core in range(2):
-                start = pl.multiple_of(((source & 1) * 2 + (core ^ flip_core)) * 256, 256)
-                held = features[flip_core].at[x]
+            for flip in range(2):
+                start = ((source & 1) * 2 + (core ^ half ^ flip)) * 256
                 term = lax.dot_general(
-                    rows[:, pl.ds(start, 256)],
-                    jnp.concatenate([held[flip_yh, 0], held[flip_yh, 1]], axis=1),
+                    rows[:, pl.ds(pl.multiple_of(start, 256), 256)],
+                    jnp.concatenate([held[0, index, flip], held[1, index, flip]], axis=1),
                     (((1,), (1,)), ((), ())),
                     preferred_element_type=F32,
                 )
                 value = term if value is None else value + term
-            pairs[:, pl.ds(pl.multiple_of((source >> 1) * 256, 256), 256)] += value
-    for block in range(16):
-        piece = pairs[:, block * 64 : (block + 1) * 64]
-        out[block, :, :64] = piece[:32]
-        out[block, :, 64:] = piece[32:]
+            pairs[half, source] = value
+    for half in range(2):
+        for zh in range(4):
+            value = pairs[half, zh * 2] + pairs[half, zh * 2 + 1]
+            for block in range(2):
+                piece = value[:, block * 64 : (block + 1) * 64]
+                target = zh * 4 + block * 2 + (core ^ half)
+                out[target, :, :64] = piece[:32]
+                out[target, :, 64:] = piece[32:]
 
 
 def pair(parts, near, far):
     return pl.pallas_call(
         pair_kernel,
         out_shape=jax.ShapeDtypeStruct((16, 32, 128), F32),
-        scratch_shapes=[pltpu.VMEM((64, 1024), BF16), pltpu.VMEM((64, 1024), F32)],
+        scratch_shapes=[pltpu.VMEM((64, 1024), BF16), pltpu.VMEM((2, 8, 64, 128), F32)],
         compiler_params=pltpu.CompilerParams(vmem_limit_bytes=12 << 20),
     )(parts, near, far)
 
@@ -415,32 +443,23 @@
     partial, part = lax.optimization_barrier((partial, part))
     next_part = lax.all_to_all(partial, CHIPS, 0, 0, tiled=True)
 
-    def turn(value):
-        return [
-            lax.ppermute(
-                value,
-                EX + PAR,
-                [
-                    (((z * 2 + yl) * 8 + chip) * 2 + c, ((chip * 2 + yl) * 8 + (z ^ chip ^ flip)) * 2 + c)
-                    for z in range(8)
-                    for yl in range(2)
-                    for chip in range(8)
-                    for c in range(2)
-                ],
-            )
-            for flip in (0, 4)
-        ]
-
-    whole, keep, send = sum_parts(part)
+    keep, send = sum_parts(part)
     mine = flips(keep, send)
     low = lax.all_gather(mine, ("zh", "zl"), axis=0)
     next_part, mine = lax.optimization_barrier((next_part, mine))
-    next_whole, keep, send = sum_parts(next_part)
-    next_whole, high = lax.optimization_barrier((next_whole, ring(flips(keep, send))))
-    turned = turn(join([whole, next_whole]))
+    high = ring(flips(*sum_parts(next_part)))
+
+    route = [
+        (((z * 2 + yl) * 8 + chip) * 2 + c, ((chip * 2 + yl) * 8 + (z ^ chip)) * 2 + c)
+        for z in range(8)
+        for yl in range(2)
+        for chip in range(8)
+        for c in range(2)
+    ]
+    packed = pack(low, high)
+    packed, high = lax.optimization_barrier((packed, high))
+    near = lax.ppermute(packed, EX + PAR, route)
     conditioned = condition(low, high, inverse_gram, other_tile)
-    conditioned, turned = lax.optimization_barrier((conditioned, turned))
-    near = lax.all_gather(join(turned), "x", axis=0)
     parts = lax.all_to_all(conditioned.reshape(8, 64, 1024), CHIPS, 0, 0, tiled=True)
     return finish(lax.all_to_all(pair(parts, near, swap(near, "c")), EX, 0, 0, tiled=True))
 

time: 231 us -> 283 us (1.23); the launches traced: 230 us -> 279 us
  blocking collectives: 39.6 us -> 78.5 us
  waiting for transfers between devices: 71 us -> 86.8 us
  starting transfers between devices: 49 us -> 41.3 us
    ppermute x2 -> x1, waiting for transfers between devices: 8.42 us -> 56.2 us  [per_device(): near = lax.ppermute(packed, EX + PAR, route)]
    all_to_all x1, blocking collectives: 19.8 us -> 58.9 us  [per_device(): lax.all_to_all(pair(parts, near, swap(near, 'c')), EX, 0, 0, tiled=True)]
    all_gather x1 -> x0, waiting for transfers between devices: 32.8 us -> none  [per_device(): near = lax.all_gather(join(turned), 'x', axis=0)]
    ppermute x2 -> x1, starting transfers between devices: 10.7 us -> 1.92 us  [per_device(): near = lax.ppermute(packed, EX + PAR, route)]
  transfers between devices with their start and end apart: 30 -> 28, of which waited for: 18 -> 17; matrix products, arithmetic and copies ran while one was open for 0% -> 0% of each run, Pallas kernels for 18% -> 15%
where the time goes in v10:
time: 283 us; the launch traced here: 279 us
  waiting for transfers between devices  86.8 us (31%)
  blocking collectives  78.5 us (28%)
  Pallas kernels  54.3 us (19%)
  starting transfers between devices  41.3 us (15%)
  between operations  13.7 us (5%)
  local copies, waits for them, and re-layouts  3.97 us (1%)
    all_to_all x1, blocking collectives, per_device(): lax.all_to_all(pair(parts, near, swap(near, 'c')), EX, 0, 0, tiled=True)  58.9 us
    ppermute x1, waiting for transfers between devices, per_device(): near = lax.ppermute(packed, EX + PAR, route)  56.2 us
    all_to_all x1, blocking collectives, per_device(): next_part = lax.all_to_all(partial, CHIPS, 0, 0, tiled=True)  19.6 us
    pallas_call x1, Pallas kernels, project_hash(): pl.pallas_call(functools.partial(hash_kernel, part, width), out_shape=jax...  17.9 us
    ppermute x7, waiting for transfers between devices, step_z(): lax.ppermute(value, ('zh', 'zl'), [(i, (i + by) % 8) for i in range(8)])  17.4 us
    pallas_call x2, Pallas kernels, table(): pl.pallas_call(functools.partial(table_kernel, part, width, first, params...  15.8 us
    ppermute x17, waiting for transfers between devices, swap(): return lax.ppermute(value, axis, [(0, 1), (1, 0)])  13.1 us
    ppermute x7, starting transfers between devices, step_z(): lax.ppermute(value, ('zh', 'zl'), [(i, (i + by) % 8) for i in range(8)])  11.6 us
  transfers between devices with their start and end apart: 28, of which 17 were waited for; matrix products, arithmetic and copies ran while one was open for 0% of the time, Pallas kernels for 15%

profile of v10, /device:TPU:22, one launch (start us, length us, event | category | flops | bytes accessed | tf_op | source)
XLA Modules:
  0.0 278.5 jit_solution(11309843671806383888)
XLA Ops:
  6.5 1.3 collective-permute-start
  7.8 1.9 collective-permute-start.1
  9.7 0.0 collective-permute-start.4
  9.7 0.7 copy-done.11
  10.4 9.7 %shard_map.37.first = bf16[5120,1024]{1,0:T(8,128)(2,1)S(1)} custom-call(s32[4]{0:T(128)S(1)} %copy-done.11), custom_call_target="tpu_custom_call" | custom-call | flops 6291456000 | bytes 10485760 | tf_op jit(solution)/shard_map/pallas_call | solution.py:68
  20.1 0.3 collective-permute-done.refs_1_
  20.4 1.2 collective-permute-done.1.refs_2_
  21.6 0.1 collective-permute-start.5
  21.8 0.0 copy-start.9
  21.8 0.6 collective-permute-start.6
  22.4 1.7 collective-permute-start.2
  24.1 0.7 collective-permute-start.3
  24.8 6.0 %shard_map.38.second = bf16[3072,1024]{1,0:T(8,128)(2,1)S(1)} custom-call(s32[4]{0:T(128)S(1)} %copy-done.12), custom_call_target="tpu_custom_call" | custom-call | flops 3774873600 | bytes 6291456 | tf_op jit(solution)/shard_map/pallas_call | solution.py:68
  30.9 0.0 collective-permute-done.2.refs_3_
  30.9 1.2 collective-permute-done.3.refs_4_
  32.1 0.0 collective-permute-start.7
  32.1 0.5 collective-permute-start.8
  32.6 1.0 collective-permute-done.7.refs_8_
  33.6 0.4 collective-permute-done.8.refs_9_
  34.0 0.0 collective-permute-done.6.refs_7_
  34.0 8.0 %shard_map.39 = (f32[8,256,128]{2,1,0:T(8,128)}, bf16[256,8192]{1,0:T(8,128)(2,1)S(1)}) custom-call(bf16[5120,1024]{1,0:T(8,128)(2,1)S(1)} %shard_map.37.first, bf16[3072,1024]{1,0:T(8,128)(2,1)S(1)} %shard_map.38.second, bf16[64,4096]{1,0:T(8,128)(2,1)S(1)} %copy-done.9, bf16[64,4096]{1,0:T(8,128)(2,1)S(1)} %collective-permute-done.refs_1_, ...), custom_call_target="tpu_custom_call" | custom-call | flops 4294967296 | bytes 16777216 | tf_op jit(solution)/shard_map/pallas_call | solution.py:140
  42.1 2.0 copy-done.10
  44.0 7.2 %all-to-all-start = ((f32[8,256,128]{2,1,0:T(8,128)}), f32[8,256,128]{2,1,0:T(8,128)S(1)}, u32[]{:S(2)}, u32[]{:S(2)}) async-start(f32[8,256,128]{2,1,0:T(8,128)} %get-tuple-element.36), calls=%async_computation | async-start | bytes 2097152 | tf_op jit(solution)/shard_map/all_to_all | solution.py:441
  51.2 0.0 collective-permute-start.22
  51.2 17.9 %shard_map.40 = f32[8,256,128]{2,1,0:T(8,128)} custom-call(s32[4]{0:T(128)} %words.5, bf16[256,8192]{1,0:T(8,128)(2,1)} %copy-done.10), custom_call_target="tpu_custom_call" | custom-call | flops 4294967296 | bytes 16777216 | tf_op jit(solution)/shard_map/pallas_call | solution.py:199
  69.2 0.1 shard_map.41
  69.2 0.6 collective-permute-start.9
  69.8 0.7 collective-permute-start.10
  70.6 0.1 collective-permute-done.9.refs_1_
  70.7 1.2 collective-permute-start.11
  71.9 2.0 collective-permute-done.10.refs_2_
  73.9 0.8 collective-permute-done.11.refs_3_
  74.6 0.7 shard_map.42
  75.3 0.0 all-gather.3.cloned.1.call-update
  75.3 19.6 %all_to_all.20.part = f32[8,256,128]{2,1,0:T(8,128)S(1)} all-to-all(f32[8,256,128]{2,1,0:T(8,128)S(1)} %copy-done.13), channel_id=1, replica_groups=mesh['zh'=4,'zl'=2,'yl'=2,'yh'=2,'x'=4,'c'=2] {'yh','x'}, dimensions={0} | all-to-all | bytes 2097152 | tf_op jit(solution)/shard_map/all_to_all | solution.py:444
  94.9 0.1 shard_map.43
  94.9 0.1 collective-permute-start.12
  95.0 0.8 collective-permute-start.13
  95.8 0.4 collective-permute-done.12.refs_1_
  96.2 0.9 collective-permute-start.14
  97.1 1.9 collective-permute-done.13.refs_2_
  99.1 1.1 collective-permute-done.14.refs_3_
  100.2 0.5 collective-permute-start.15
  100.6 4.7 %collective-permute-start.19 = (bf16[4,128,128]{2,1,0:T(8,128)(2,1)S(1)}, bf16[4,128,128]{2,1,0:T(8,128)(2,1)S(1)}, u32[]{:S(2)}, u32[]{:S(2)}) collective-permute-start(bf16[4,128,128]{2,1,0:T(8,128)(2,1)S(1)} %shard_map.44.refs_0_.refs_1_), channel_id=1, source_target_pairs={{0,224},{32,0},{64,32},{96,64},{128,96},{160,128},{192,160},{224,1... | collective-permute-start | bytes 393224 | tf_op jit(solution)/shard_map/ppermute | solution.py:406
  105.3 4.8 %collective-permute-done.15.refs_1_.refs_2_ = bf16[4,128,128]{2,1,0:T(8,128)(2,1)S(1)} collective-permute-done((bf16[4,128,128]{2,1,0:T(8,128)(2,1)S(1)}, bf16[4,128,128]{2,1,0:T(8,128)(2,1)S(1)}, u32[]{:S(2)}, u32[]{:S(2)}) %collective-permute-start.15) | collective-permute-done | bytes 131104 | tf_op jit(solution)/shard_map/ppermute | solution.py:406
  110.1 3.2 %collective-permute-start.20 = (bf16[4,128,128]{2,1,0:T(8,128)(2,1)S(1)}, bf16[4,128,128]{2,1,0:T(8,128)(2,1)S(1)}, u32[]{:S(2)}, u32[]{:S(2)}) collective-permute-start(bf16[4,128,128]{2,1,0:T(8,128)(2,1)S(1)} %collective-permute-done.19.refs_5_.refs_6_), channel_id=1, source_target_pairs={{0,224},{32,0},{64,32},{96,64},{128,96},{160,128},{192,160},{224,1... | collective-permute-start | bytes 393224 | tf_op jit(solution)/shard_map/ppermute | solution.py:406
  113.3 3.3 %collective-permute-done.16.refs_2_.refs_3_ = bf16[4,128,128]{2,1,0:T(8,128)(2,1)S(1)} collective-permute-done((bf16[4,128,128]{2,1,0:T(8,128)(2,1)S(1)}, bf16[4,128,128]{2,1,0:T(8,128)(2,1)S(1)}, u32[]{:S(2)}, u32[]{:S(2)}) %collective-permute-start.16) | collective-permute-done | bytes 131104 | tf_op jit(solution)/shard_map/ppermute | solution.py:406
  116.6 0.0 collective-permute-start.17
  116.6 0.0 collective-permute-done.20.refs_6_.refs_7_
  116.6 3.2 %collective-permute-start.21 = (bf16[4,128,128]{2,1,0:T(8,128)(2,1)S(1)}, bf16[4,128,128]{2,1,0:T(8,128)(2,1)S(1)}, u32[]{:S(2)}, u32[]{:S(2)}) collective-permute-start(bf16[4,128,128]{2,1,0:T(8,128)(2,1)S(1)} %collective-permute-done.20.refs_6_.refs_7_), channel_id=1, source_target_pairs={{0,224},{32,0},{64,32},{96,64},{128,96},{160,128},{192,160},{224,1... | collective-permute-start | bytes 393224 | tf_op jit(solution)/shard_map/ppermute | solution.py:406
  119.8 3.2 %collective-permute-done.17.refs_3_.refs_4_ = bf16[4,128,128]{2,1,0:T(8,128)(2,1)S(1)} collective-permute-done((bf16[4,128,128]{2,1,0:T(8,128)(2,1)S(1)}, bf16[4,128,128]{2,1,0:T(8,128)(2,1)S(1)}, u32[]{:S(2)}, u32[]{:S(2)}) %collective-permute-start.17) | collective-permute-done | bytes 131104 | tf_op jit(solution)/shard_map/ppermute | solution.py:406
  123.0 0.0 collective-permute-start.18
  123.0 0.0 collective-permute-done.21.refs_7_.refs_8_
  123.1 6.2 %collective-permute-done.18.refs_4_.refs_5_ = bf16[4,128,128]{2,1,0:T(8,128)(2,1)S(1)} collective-permute-done((bf16[4,128,128]{2,1,0:T(8,128)(2,1)S(1)}, bf16[4,128,128]{2,1,0:T(8,128)(2,1)S(1)}, u32[]{:S(2)}, u32[]{:S(2)}) %collective-permute-start.18) | collective-permute-done | bytes 131104 | tf_op jit(solution)/shard_map/ppermute | solution.py:406
  129.2 1.3 copy-done
  130.5 1.1 shard_map.45
  131.6 1.9 collective-permute-start.23
  133.6 6.7 %shard_map.46 = f32[512,1024]{1,0:T(8,128)} custom-call(bf16[8,4,128,128]{3,2,1,0:T(8,128)(2,1)} %bitcast.2, bf16[4,128,128]{2,1,0:T(8,128)(2,1)} %copy-done.1, bf16[4,128,128]{2,1,0:T(8,128)(2,1)} %copy-done.2, bf16[4,128,128]{2,1,0:T(8,128)(2,1)} %copy-done.4, bf16[4,128,128]{2,1,0:T(8,128)(2,1)} %copy-done.6, bf16[4,128,128]{2,1,0:T(8,128)(2,1)} %copy-done.8, ...), custom_call_target="tpu_custom_call" | custom-call | flops 2147483648 | bytes 7340032 | tf_op jit(solution)/shard_map/pallas_call | solution.py:294
  140.4 9.4 %all-to-all-start.2 = ((f32[8,64,1024]{2,1,0:T(8,128)}), f32[8,64,1024]{2,1,0:T(8,128)S(1)}, u32[]{:S(2)}, u32[]{:S(2)}) async-start(f32[8,64,1024]{2,1,0:T(8,128)} %bitcast.4), calls=%async_computation.2 | async-start | bytes 4194304 | tf_op jit(solution)/shard_map/all_to_all | solution.py:463
  149.8 56.2 %collective-permute-done.23.near = bf16[2,8,2,128,128]{4,3,2,1,0:T(8,128)(2,1)S(1)} collective-permute-done((bf16[2,8,2,128,128]{4,3,2,1,0:T(8,128)(2,1)}, bf16[2,8,2,128,128]{4,3,2,1,0:T(8,128)(2,1)S(1)}, u32[]{:S(2)}, u32[]{:S(2)}) %collective-permute-start.23) | collective-permute-done | bytes 1048608 | tf_op jit(solution)/shard_map/ppermute | solution.py:461
  206.0 2.8 %collective-permute-done.24.far = bf16[2,8,2,128,128]{4,3,2,1,0:T(8,128)(2,1)} collective-permute-done((bf16[2,8,2,128,128]{4,3,2,1,0:T(8,128)(2,1)S(1)}, bf16[2,8,2,128,128]{4,3,2,1,0:T(8,128)(2,1)}, u32[]{:S(2)}, u32[]{:S(2)}) %collective-permute-start.24) | collective-permute-done | bytes 1048608 | tf_op jit(solution)/shard_map/ppermute | solution.py:402
  208.8 2.3 shard_map.47
  211.1 58.9 %all_to_all.21.parts = f32[16,32,128]{2,1,0:T(8,128)} all-to-all(f32[16,32,128]{2,1,0:T(8,128)S(1)} %shard_map.47), channel_id=1, replica_groups=mesh['zh'=4,'zl'=2,'yl'=2,'yh'=2,'x'=4,'c'=2] {'zh','zl','yl'}, dimensions={0} | all-to-all | bytes 524288 | tf_op jit(solution)/shard_map/all_to_all | solution.py:464
  270.0 1.7 shard_map.48
  (37 shorter events, 0.1 us)
Async XLA Ops:
  6.5 13.9 %collective-permute-start = (bf16[64,4096]{1,0:T(8,128)(2,1)}, bf16[64,4096]{1,0:T(8,128)(2,1)S(1)}, u32[]{:S(2)}, u32[]{:S(2)}) collective-permute-start(bf16[64,4096]{1,0:T(8,128)(2,1)} %refs_0_.1), channel_id=1, source_target_pairs={{0,16},{16,0},{1,17},{17,1},{2,18},{18,2},{3,19},{19,3},{4,20},{20... | collective-permute-start | bytes 1572872 | tf_op jit(solution)/shard_map/ppermute | solution.py:402
  7.8 13.8 %collective-permute-start.1 = (bf16[64,4096]{1,0:T(8,128)(2,1)}, bf16[64,4096]{1,0:T(8,128)(2,1)S(1)}, u32[]{:S(2)}, u32[]{:S(2)}) collective-permute-start(bf16[64,4096]{1,0:T(8,128)(2,1)} %refs_0_.1), channel_id=1, source_target_pairs={{0,32},{32,0},{1,33},{33,1},{2,34},{34,2},{3,35},{35,3},{4,36},{36... | collective-permute-start | bytes 1572872 | tf_op jit(solution)/shard_map/ppermute | solution.py:402
  9.7 22.9 %collective-permute-start.4 = (bf16[64,4096]{1,0:T(8,128)(2,1)}, bf16[64,4096]{1,0:T(8,128)(2,1)S(1)}, u32[]{:S(2)}, u32[]{:S(2)}) collective-permute-start(bf16[64,4096]{1,0:T(8,128)(2,1)} %refs_0_.1), channel_id=1, source_target_pairs={{0,1},{1,0},{2,3},{3,2},{4,5},{5,4},{6,7},{7,6},{8,9},{9,8},{10,11... | collective-permute-start | bytes 1572872 | tf_op jit(solution)/shard_map/ppermute | solution.py:402
  9.7 0.7 copy-start.11
  10.4 14.4 %copy-start.12 = (s32[4]{0:T(128)S(1)}, s32[4]{0:T(128)}, u32[]{:S(2)}) copy-start(s32[4]{0:T(128)} %words.5) | copy-start | bytes 52
  21.6 12.4 %collective-permute-start.5 = (bf16[64,4096]{1,0:T(8,128)(2,1)S(1)}, bf16[64,4096]{1,0:T(8,128)(2,1)S(1)}, u32[]{:S(2)}, u32[]{:S(2)}) collective-permute-start(bf16[64,4096]{1,0:T(8,128)(2,1)S(1)} %collective-permute-done.refs_1_), channel_id=1, source_target_pairs={{0,1},{1,0},{2,3},{3,2},{4,5},{5,4},{6,7},{7,6},{8,9},{9,8},{10,11... | collective-permute-start | bytes 1572872 | tf_op jit(solution)/shard_map/ppermute | solution.py:402
  21.8 12.3 %copy-start.9 = (bf16[64,4096]{1,0:T(8,128)(2,1)S(1)}, bf16[64,4096]{1,0:T(8,128)(2,1)}, u32[]{:S(2)}) copy-start(bf16[64,4096]{1,0:T(8,128)(2,1)} %refs_0_.1) | copy-start | bytes 1572868
  21.8 12.2 %collective-permute-start.6 = (bf16[64,4096]{1,0:T(8,128)(2,1)S(1)}, bf16[64,4096]{1,0:T(8,128)(2,1)S(1)}, u32[]{:S(2)}, u32[]{:S(2)}) collective-permute-start(bf16[64,4096]{1,0:T(8,128)(2,1)S(1)} %collective-permute-done.1.refs_2_), channel_id=1, source_target_pairs={{0,1},{1,0},{2,3},{3,2},{4,5},{5,4},{6,7},{7,6},{8,9},{9,8},{10,11... | collective-permute-start | bytes 1572872 | tf_op jit(solution)/shard_map/ppermute | solution.py:402
  22.4 8.5 %collective-permute-start.2 = (bf16[32,4096]{1,0:T(8,128)(2,1)S(1)}, bf16[32,4096]{1,0:T(8,128)(2,1)S(1)}, u32[]{:S(2)}, u32[]{:S(2)}) collective-permute-start(bf16[32,4096]{1,0:T(8,128)(2,1)S(1)} %slice.6), channel_id=1, source_target_pairs={{0,32},{32,0},{1,33},{33,1},{2,34},{34,2},{3,35},{35,3},{4,36},{36... | collective-permute-start | bytes 786440 | tf_op jit(solution)/shard_map/ppermute | solution.py:402
  24.1 8.0 %collective-permute-start.3 = (bf16[32,4096]{1,0:T(8,128)(2,1)S(1)}, bf16[32,4096]{1,0:T(8,128)(2,1)S(1)}, u32[]{:S(2)}, u32[]{:S(2)}) collective-permute-start(bf16[32,4096]{1,0:T(8,128)(2,1)S(1)} %slice.7), channel_id=1, source_target_pairs={{0,16},{16,0},{1,17},{17,1},{2,18},{18,2},{3,19},{19,3},{4,20},{20... | collective-permute-start | bytes 786440 | tf_op jit(solution)/shard_map/ppermute | solution.py:402
  32.1 1.5 collective-permute-start.7
  32.1 1.9 collective-permute-start.8
  42.1 2.0 copy-start.10
  44.0 25.2 %all-to-all-start = ((f32[8,256,128]{2,1,0:T(8,128)}), f32[8,256,128]{2,1,0:T(8,128)S(1)}, u32[]{:S(2)}, u32[]{:S(2)}) async-start(f32[8,256,128]{2,1,0:T(8,128)} %get-tuple-element.36), calls=%async_computation | async-start | bytes 2097152 | tf_op jit(solution)/shard_map/all_to_all | solution.py:441
  51.2 78.0 %all-gather.3.cloned.1.call-start = ((), (), s32[]{:S(2)}) async-start(), calls=%async_computation.4 | async-start | bytes 1179648 | tf_op jit(solution)/shard_map/all_gather | solution.py:448
  51.2 82.3 %collective-permute-start.22 = (bf16[1024,1024]{1,0:T(8,128)(2,1)}, bf16[1024,1024]{1,0:T(8,128)(2,1)}, u32[]{:S(2)}, u32[]{:S(2)}) collective-permute-start(bf16[1024,1024]{1,0:T(8,128)(2,1)} %refs_9_.1), channel_id=1, source_target_pairs={{0,1},{1,0},{2,3},{3,2},{4,5},{5,4},{6,7},{7,6},{8,9},{9,8},{10,11... | collective-permute-start | bytes 6291464 | tf_op jit(solution)/shard_map/ppermute | solution.py:402
  69.2 6.1 %copy-start.13 = (f32[8,256,128]{2,1,0:T(8,128)S(1)}, f32[8,256,128]{2,1,0:T(8,128)}, u32[]{:S(2)}) copy-start(f32[8,256,128]{2,1,0:T(8,128)} %shard_map.40) | copy-start | bytes 3145732
  69.2 1.4 collective-permute-start.9
  69.8 4.0 %collective-permute-start.10 = (bf16[128,128]{1,0:T(8,128)(2,1)S(1)}, bf16[128,128]{1,0:T(8,128)(2,1)S(1)}, u32[]{:S(2)}, u32[]{:S(2)}) collective-permute-start(bf16[128,128]{1,0:T(8,128)(2,1)S(1)} %get-tuple-element.38.refs_0_), channel_id=1, source_target_pairs={{0,16},{16,0},{1,17},{17,1},{2,18},{18,2},{3,19},{19,3},{4,20},{20... | collective-permute-start | bytes 98312 | tf_op jit(solution)/shard_map/ppermute | solution.py:402
  70.7 3.9 %collective-permute-start.11 = (bf16[128,128]{1,0:T(8,128)(2,1)S(1)}, bf16[128,128]{1,0:T(8,128)(2,1)S(1)}, u32[]{:S(2)}, u32[]{:S(2)}) collective-permute-start(bf16[128,128]{1,0:T(8,128)(2,1)S(1)} %collective-permute-done.9.refs_1_), channel_id=1, source_target_pairs={{0,16},{16,0},{1,17},{17,1},{2,18},{18,2},{3,19},{19,3},{4,20},{20... | collective-permute-start | bytes 98312 | tf_op jit(solution)/shard_map/ppermute | solution.py:402
  94.9 1.3 collective-permute-start.12
  95.0 4.1 %collective-permute-start.13 = (bf16[128,128]{1,0:T(8,128)(2,1)S(1)}, bf16[128,128]{1,0:T(8,128)(2,1)S(1)}, u32[]{:S(2)}, u32[]{:S(2)}) collective-permute-start(bf16[128,128]{1,0:T(8,128)(2,1)S(1)} %get-tuple-element.42.refs_0_), channel_id=1, source_target_pairs={{0,16},{16,0},{1,17},{17,1},{2,18},{18,2},{3,19},{19,3},{4,20},{20... | collective-permute-start | bytes 98312 | tf_op jit(solution)/shard_map/ppermute | solution.py:402
  96.2 3.9 %collective-permute-start.14 = (bf16[128,128]{1,0:T(8,128)(2,1)S(1)}, bf16[128,128]{1,0:T(8,128)(2,1)S(1)}, u32[]{:S(2)}, u32[]{:S(2)}) collective-permute-start(bf16[128,128]{1,0:T(8,128)(2,1)S(1)} %collective-permute-done.12.refs_1_), channel_id=1, source_target_pairs={{0,16},{16,0},{1,17},{17,1},{2,18},{18,2},{3,19},{19,3},{4,20},{20... | collective-permute-start | bytes 98312 | tf_op jit(solution)/shard_map/ppermute | solution.py:402
  100.1 33.4 %copy-start.1 = (bf16[4,128,128]{2,1,0:T(8,128)(2,1)}, bf16[4,128,128]{2,1,0:T(8,128)(2,1)S(1)}, u32[]{:S(2)}) copy-start(bf16[4,128,128]{2,1,0:T(8,128)(2,1)S(1)} %shard_map.44.refs_0_.refs_1_) | copy-start | bytes 393220
  100.2 9.9 %collective-permute-start.15 = (bf16[4,128,128]{2,1,0:T(8,128)(2,1)S(1)}, bf16[4,128,128]{2,1,0:T(8,128)(2,1)S(1)}, u32[]{:S(2)}, u32[]{:S(2)}) collective-permute-start(bf16[4,128,128]{2,1,0:T(8,128)(2,1)S(1)} %shard_map.44.refs_0_.refs_1_), channel_id=1, source_target_pairs={{0,32},{32,64},{64,96},{96,128},{128,160},{160,192},{192,224},{224... | collective-permute-start | bytes 393224 | tf_op jit(solution)/shard_map/ppermute | solution.py:406
  100.6 9.5 %collective-permute-start.19 = (bf16[4,128,128]{2,1,0:T(8,128)(2,1)S(1)}, bf16[4,128,128]{2,1,0:T(8,128)(2,1)S(1)}, u32[]{:S(2)}, u32[]{:S(2)}) collective-permute-start(bf16[4,128,128]{2,1,0:T(8,128)(2,1)S(1)} %shard_map.44.refs_0_.refs_1_), channel_id=1, source_target_pairs={{0,224},{32,0},{64,32},{96,64},{128,96},{160,128},{192,160},{224,1... | collective-permute-start | bytes 393224 | tf_op jit(solution)/shard_map/ppermute | solution.py:406
  110.1 23.5 %copy-start.2 = (bf16[4,128,128]{2,1,0:T(8,128)(2,1)}, bf16[4,128,128]{2,1,0:T(8,128)(2,1)S(1)}, u32[]{:S(2)}) copy-start(bf16[4,128,128]{2,1,0:T(8,128)(2,1)S(1)} %collective-permute-done.15.refs_1_.refs_2_) | copy-start | bytes 393220
  110.1 6.5 %collective-permute-start.16 = (bf16[4,128,128]{2,1,0:T(8,128)(2,1)S(1)}, bf16[4,128,128]{2,1,0:T(8,128)(2,1)S(1)}, u32[]{:S(2)}, u32[]{:S(2)}) collective-permute-start(bf16[4,128,128]{2,1,0:T(8,128)(2,1)S(1)} %collective-permute-done.15.refs_1_.refs_2_), channel_id=1, source_target_pairs={{0,32},{32,64},{64,96},{96,128},{128,160},{160,192},{192,224},{224... | collective-permute-start | bytes 393224 | tf_op jit(solution)/shard_map/ppermute | solution.py:406
  110.1 23.5 %copy-start.3 = (bf16[4,128,128]{2,1,0:T(8,128)(2,1)}, bf16[4,128,128]{2,1,0:T(8,128)(2,1)S(1)}, u32[]{:S(2)}) copy-start(bf16[4,128,128]{2,1,0:T(8,128)(2,1)S(1)} %collective-permute-done.19.refs_5_.refs_6_) | copy-start | bytes 393220
  110.1 6.5 %collective-permute-start.20 = (bf16[4,128,128]{2,1,0:T(8,128)(2,1)S(1)}, bf16[4,128,128]{2,1,0:T(8,128)(2,1)S(1)}, u32[]{:S(2)}, u32[]{:S(2)}) collective-permute-start(bf16[4,128,128]{2,1,0:T(8,128)(2,1)S(1)} %collective-permute-done.19.refs_5_.refs_6_), channel_id=1, source_target_pairs={{0,224},{32,0},{64,32},{96,64},{128,96},{160,128},{192,160},{224,1... | collective-permute-start | bytes 393224 | tf_op jit(solution)/shard_map/ppermute | solution.py:406
  116.6 17.0 %copy-start.4 = (bf16[4,128,128]{2,1,0:T(8,128)(2,1)}, bf16[4,128,128]{2,1,0:T(8,128)(2,1)S(1)}, u32[]{:S(2)}) copy-start(bf16[4,128,128]{2,1,0:T(8,128)(2,1)S(1)} %collective-permute-done.16.refs_2_.refs_3_) | copy-start | bytes 393220
  116.6 6.4 %collective-permute-start.17 = (bf16[4,128,128]{2,1,0:T(8,128)(2,1)S(1)}, bf16[4,128,128]{2,1,0:T(8,128)(2,1)S(1)}, u32[]{:S(2)}, u32[]{:S(2)}) collective-permute-start(bf16[4,128,128]{2,1,0:T(8,128)(2,1)S(1)} %collective-permute-done.16.refs_2_.refs_3_), channel_id=1, source_target_pairs={{0,32},{32,64},{64,96},{96,128},{128,160},{160,192},{192,224},{224... | collective-permute-start | bytes 393224 | tf_op jit(solution)/shard_map/ppermute | solution.py:406
  116.6 17.0 %copy-start.5 = (bf16[4,128,128]{2,1,0:T(8,128)(2,1)}, bf16[4,128,128]{2,1,0:T(8,128)(2,1)S(1)}, u32[]{:S(2)}) copy-start(bf16[4,128,128]{2,1,0:T(8,128)(2,1)S(1)} %collective-permute-done.20.refs_6_.refs_7_) | copy-start | bytes 393220
  116.6 6.4 %collective-permute-start.21 = (bf16[4,128,128]{2,1,0:T(8,128)(2,1)S(1)}, bf16[4,128,128]{2,1,0:T(8,128)(2,1)S(1)}, u32[]{:S(2)}, u32[]{:S(2)}) collective-permute-start(bf16[4,128,128]{2,1,0:T(8,128)(2,1)S(1)} %collective-permute-done.20.refs_6_.refs_7_), channel_id=1, source_target_pairs={{0,224},{32,0},{64,32},{96,64},{128,96},{160,128},{192,160},{224,1... | collective-permute-start | bytes 393224 | tf_op jit(solution)/shard_map/ppermute | solution.py:406
  123.0 10.6 %copy-start.6 = (bf16[4,128,128]{2,1,0:T(8,128)(2,1)}, bf16[4,128,128]{2,1,0:T(8,128)(2,1)S(1)}, u32[]{:S(2)}) copy-start(bf16[4,128,128]{2,1,0:T(8,128)(2,1)S(1)} %collective-permute-done.17.refs_3_.refs_4_) | copy-start | bytes 393220
  123.0 6.2 %collective-permute-start.18 = (bf16[4,128,128]{2,1,0:T(8,128)(2,1)S(1)}, bf16[4,128,128]{2,1,0:T(8,128)(2,1)S(1)}, u32[]{:S(2)}, u32[]{:S(2)}) collective-permute-start(bf16[4,128,128]{2,1,0:T(8,128)(2,1)S(1)} %collective-permute-done.17.refs_3_.refs_4_), channel_id=1, source_target_pairs={{0,32},{32,64},{64,96},{96,128},{128,160},{160,192},{192,224},{224... | collective-permute-start | bytes 393224 | tf_op jit(solution)/shard_map/ppermute | solution.py:406
  123.0 10.6 %copy-start.7 = (bf16[4,128,128]{2,1,0:T(8,128)(2,1)}, bf16[4,128,128]{2,1,0:T(8,128)(2,1)S(1)}, u32[]{:S(2)}) copy-start(bf16[4,128,128]{2,1,0:T(8,128)(2,1)S(1)} %collective-permute-done.21.refs_7_.refs_8_) | copy-start | bytes 393220
  129.2 4.4 %copy-start.8 = (bf16[4,128,128]{2,1,0:T(8,128)(2,1)}, bf16[4,128,128]{2,1,0:T(8,128)(2,1)S(1)}, u32[]{:S(2)}) copy-start(bf16[4,128,128]{2,1,0:T(8,128)(2,1)S(1)} %collective-permute-done.18.refs_4_.refs_5_) | copy-start | bytes 393220
  129.2 1.3 copy-start
  131.6 74.4 %collective-permute-start.23 = (bf16[2,8,2,128,128]{4,3,2,1,0:T(8,128)(2,1)}, bf16[2,8,2,128,128]{4,3,2,1,0:T(8,128)(2,1)S(1)}, u32[]{:S(2)}, u32[]{:S(2)}) collective-permute-start(bf16[2,8,2,128,128]{4,3,2,1,0:T(8,128)(2,1)} %shard_map.45), channel_id=1, source_target_pairs={{0,0},{1,1},{2,34},{3,35},{4,68},{5,69},{6,102},{7,103},{8,136},{9... | collective-permute-start | bytes 3145736 | tf_op jit(solution)/shard_map/ppermute | solution.py:461
  140.4 65.7 %all-to-all-start.2 = ((f32[8,64,1024]{2,1,0:T(8,128)}), f32[8,64,1024]{2,1,0:T(8,128)S(1)}, u32[]{:S(2)}, u32[]{:S(2)}) async-start(f32[8,64,1024]{2,1,0:T(8,128)} %bitcast.4), calls=%async_computation.2 | async-start | bytes 4194304 | tf_op jit(solution)/shard_map/all_to_all | solution.py:463
  206.0 2.8 %collective-permute-start.24 = (bf16[2,8,2,128,128]{4,3,2,1,0:T(8,128)(2,1)S(1)}, bf16[2,8,2,128,128]{4,3,2,1,0:T(8,128)(2,1)}, u32[]{:S(2)}, u32[]{:S(2)}) collective-permute-start(bf16[2,8,2,128,128]{4,3,2,1,0:T(8,128)(2,1)S(1)} %collective-permute-done.23.near), channel_id=1, source_target_pairs={{0,1},{1,0},{2,3},{3,2},{4,5},{5,4},{6,7},{7,6},{8,9},{9,8},{10,11... | collective-permute-start | bytes 3145736 | tf_op jit(solution)/shard_map/ppermute | solution.py:402
Sparse Core Ops, SparseCore 0:
  75.4 41.0 all-gather.2

commit v11 on v10

--- a/solution.py
+++ b/solution.py
@@ -449,17 +449,19 @@
     next_part, mine = lax.optimization_barrier((next_part, mine))
     high = ring(flips(*sum_parts(next_part)))
 
-    route = [
-        (((z * 2 + yl) * 8 + chip) * 2 + c, ((chip * 2 + yl) * 8 + (z ^ chip)) * 2 + c)
-        for z in range(8)
-        for yl in range(2)
-        for chip in range(8)
-        for c in range(2)
-    ]
+    places = [(z, yl, chip, c) for z in range(8) for yl in range(2) for chip in range(8) for c in range(2)]
+
+    def flat(z, yl, chip, c):
+        return ((z * 2 + yl) * 8 + chip) * 2 + c
+
+    across = [(flat(z, yl, chip, c), flat(z, yl, z ^ chip, c)) for z, yl, chip, c in places]
+    along = [(flat(z, yl, chip, c), flat(z ^ chip, yl, chip, c)) for z, yl, chip, c in places]
     packed = pack(low, high)
     packed, high = lax.optimization_barrier((packed, high))
-    near = lax.ppermute(packed, EX + PAR, route)
+    packed = lax.ppermute(packed, EX + PAR, across)
     conditioned = condition(low, high, inverse_gram, other_tile)
+    conditioned, packed = lax.optimization_barrier((conditioned, packed))
+    near = lax.ppermute(packed, EX + PAR, along)
     parts = lax.all_to_all(conditioned.reshape(8, 64, 1024), CHIPS, 0, 0, tiled=True)
     return finish(lax.all_to_all(pair(parts, near, swap(near, "c")), EX, 0, 0, tiled=True))
 

time: 283 us -> 237 us (0.84)
  blocking collectives: 78.5 us -> 20.4 us
  starting transfers between devices: 41.3 us -> 65.8 us
  waiting for transfers between devices: 86.8 us -> 74 us
    all_to_all x1, blocking collectives: 58.9 us -> 20.4 us  [per_device(): lax.all_to_all(pair(parts, near, swap(near, 'c')), EX, 0, 0, tiled=True)]
    ppermute x1 -> x2, waiting for transfers between devices: 56.2 us -> 30.8 us  [the longest x1 30.8 us: per_device(): near = lax.ppermute(packed, EX + PAR, along)]
    all_to_all x1 -> x0, blocking collectives: 19.6 us -> none  [per_device(): next_part = lax.all_to_all(partial, CHIPS, 0, 0, tiled=True)]
    ppermute x1 -> x2, starting transfers between devices: 1.92 us -> 20.1 us  [the longest x1 18.5 us: per_device(): near = lax.ppermute(packed, EX + PAR, along)]
    all_to_all x0 -> x1, waiting for transfers between devices: none -> 12.3 us  [per_device(): next_part = lax.all_to_all(partial, CHIPS, 0, 0, tiled=True)]
    all_to_all x0 -> x1, starting transfers between devices: none -> 7.22 us  [per_device(): next_part = lax.all_to_all(partial, CHIPS, 0, 0, tiled=True)]
  transfers between devices with their start and end apart: 28 -> 30, of which waited for: 17 -> 18; matrix products, arithmetic and copies ran while one was open for 0% -> 0% of each run, Pallas kernels for 15% -> 18%
where the time goes in v11:
time: 237 us; the launch traced here: 232 us
  waiting for transfers between devices  74 us (31%)
  starting transfers between devices  65.8 us (28%)
  Pallas kernels  54.7 us (23%)
  blocking collectives  20.4 us (9%)
  between operations  13.7 us (6%)
  local copies, waits for them, and re-layouts  3.95 us (2%)
    ppermute x1, waiting for transfers between devices, per_device(): near = lax.ppermute(packed, EX + PAR, along)  30.8 us
    all_to_all x1, blocking collectives, per_device(): lax.all_to_all(pair(parts, near, swap(near, 'c')), EX, 0, 0, tiled=True)  20.4 us
    ppermute x1, starting transfers between devices, per_device(): near = lax.ppermute(packed, EX + PAR, along)  18.5 us
    pallas_call x1, Pallas kernels, project_hash(): pl.pallas_call(functools.partial(hash_kernel, part, width), out_shape=jax...  17.9 us
    ppermute x7, waiting for transfers between devices, step_z(): lax.ppermute(value, ('zh', 'zl'), [(i, (i + by) % 8) for i in range(8)])  17.3 us
    pallas_call x2, Pallas kernels, table(): pl.pallas_call(functools.partial(table_kernel, part, width, first, params...  15.8 us
    ppermute x17, waiting for transfers between devices, swap(): return lax.ppermute(value, axis, [(0, 1), (1, 0)])  13.5 us
    all_to_all x1, waiting for transfers between devices, per_device(): next_part = lax.all_to_all(partial, CHIPS, 0, 0, tiled=True)  12.3 us
  transfers between devices with their start and end apart: 30, of which 18 were waited for; matrix products, arithmetic and copies ran while one was open for 0% of the time, Pallas kernels for 18%

profile of v11, /device:TPU:22, one launch (start us, length us, event | category | flops | bytes accessed | tf_op | source)
XLA Modules:
  0.0 232.4 jit_solution(12129817287905602329)
XLA Ops:
  6.5 1.3 collective-permute-start
  7.8 1.9 collective-permute-start.1
  9.7 0.7 copy-done.11
  10.4 9.7 %shard_map.37.first = bf16[5120,1024]{1,0:T(8,128)(2,1)S(1)} custom-call(s32[4]{0:T(128)S(1)} %copy-done.11), custom_call_target="tpu_custom_call" | custom-call | flops 6291456000 | bytes 10485760 | tf_op jit(solution)/shard_map/pallas_call | solution.py:68
  20.1 0.3 collective-permute-done.refs_1_
  20.4 1.2 collective-permute-done.1.refs_2_
  21.6 0.1 collective-permute-start.5
  21.8 0.0 copy-start.9
  21.8 0.6 collective-permute-start.6
  22.4 1.7 collective-permute-start.2
  24.1 0.7 collective-permute-start.3
  24.8 6.0 %shard_map.38.second = bf16[3072,1024]{1,0:T(8,128)(2,1)S(1)} custom-call(s32[4]{0:T(128)S(1)} %copy-done.12), custom_call_target="tpu_custom_call" | custom-call | flops 3774873600 | bytes 6291456 | tf_op jit(solution)/shard_map/pallas_call | solution.py:68
  30.9 0.0 collective-permute-done.2.refs_3_
  30.9 1.2 collective-permute-done.3.refs_4_
  32.1 0.0 collective-permute-start.7
  32.1 0.5 collective-permute-start.8
  32.6 0.0 collective-permute-done.4.refs_5_
  32.6 1.0 collective-permute-done.7.refs_8_
  33.6 0.4 collective-permute-done.8.refs_9_
  34.0 0.0 collective-permute-done.5.refs_6_
  34.0 8.0 %shard_map.39 = (f32[8,256,128]{2,1,0:T(8,128)}, bf16[256,8192]{1,0:T(8,128)(2,1)S(1)}) custom-call(bf16[5120,1024]{1,0:T(8,128)(2,1)S(1)} %shard_map.37.first, bf16[3072,1024]{1,0:T(8,128)(2,1)S(1)} %shard_map.38.second, bf16[64,4096]{1,0:T(8,128)(2,1)S(1)} %copy-done.9, bf16[64,4096]{1,0:T(8,128)(2,1)S(1)} %collective-permute-done.refs_1_, ...), custom_call_target="tpu_custom_call" | custom-call | flops 4294967296 | bytes 16777216 | tf_op jit(solution)/shard_map/pallas_call | solution.py:140
  42.1 1.9 copy-done.10
  44.0 7.2 %all-to-all-start = ((f32[8,256,128]{2,1,0:T(8,128)}), f32[8,256,128]{2,1,0:T(8,128)S(1)}, u32[]{:S(2)}, u32[]{:S(2)}) async-start(f32[8,256,128]{2,1,0:T(8,128)} %get-tuple-element.38), calls=%async_computation | async-start | bytes 2097152 | tf_op jit(solution)/shard_map/all_to_all | solution.py:441
  51.2 17.9 %shard_map.40 = f32[8,256,128]{2,1,0:T(8,128)} custom-call(s32[4]{0:T(128)} %words.5, bf16[256,8192]{1,0:T(8,128)(2,1)} %copy-done.10), custom_call_target="tpu_custom_call" | custom-call | flops 4294967296 | bytes 16777216 | tf_op jit(solution)/shard_map/pallas_call | solution.py:199
  69.1 0.0 all-to-all-done.part
  69.1 0.1 shard_map.41
  69.2 0.1 collective-permute-start.9
  69.3 0.8 collective-permute-start.10
  70.1 0.4 collective-permute-done.9.refs_1_
  70.5 0.9 collective-permute-start.11
  71.4 1.9 collective-permute-done.10.refs_2_
  73.3 1.1 collective-permute-done.11.refs_3_
  74.4 0.7 shard_map.42
  75.0 0.0 all-gather.3.cloned.1.call-update
  75.1 7.2 %all-to-all-start.1 = ((f32[8,256,128]{2,1,0:T(8,128)}), f32[8,256,128]{2,1,0:T(8,128)S(1)}, u32[]{:S(2)}, u32[]{:S(2)}) async-start(f32[8,256,128]{2,1,0:T(8,128)} %shard_map.40), calls=%async_computation.1 | async-start | bytes 2097152 | tf_op jit(solution)/shard_map/all_to_all | solution.py:444
  82.3 0.0 collective-permute-start.22
  82.3 12.3 %all-to-all-done.1.part = f32[8,256,128]{2,1,0:T(8,128)S(1)} async-done(((f32[8,256,128]{2,1,0:T(8,128)}), f32[8,256,128]{2,1,0:T(8,128)S(1)}, u32[]{:S(2)}, u32[]{:S(2)}) %all-to-all-start.1) | async-done | bytes 1048608 | tf_op jit(solution)/shard_map/all_to_all | solution.py:444
  94.5 0.1 shard_map.43
  94.6 0.1 collective-permute-start.12
  94.7 0.9 collective-permute-start.13
  95.7 0.2 collective-permute-done.12.refs_1_
  95.9 0.9 collective-permute-start.14
  96.8 1.9 collective-permute-done.13.refs_2_
  98.8 1.1 collective-permute-done.14.refs_3_
  99.8 0.5 collective-permute-start.15
  100.3 4.7 %collective-permute-start.19 = (bf16[4,128,128]{2,1,0:T(8,128)(2,1)S(1)}, bf16[4,128,128]{2,1,0:T(8,128)(2,1)S(1)}, u32[]{:S(2)}, u32[]{:S(2)}) collective-permute-start(bf16[4,128,128]{2,1,0:T(8,128)(2,1)S(1)} %shard_map.44.refs_0_.refs_1_), channel_id=1, source_target_pairs={{0,224},{32,0},{64,32},{96,64},{128,96},{160,128},{192,160},{224,1... | collective-permute-start | bytes 393224 | tf_op jit(solution)/shard_map/ppermute | solution.py:406
  104.9 4.4 %collective-permute-done.15.refs_1_.refs_2_ = bf16[4,128,128]{2,1,0:T(8,128)(2,1)S(1)} collective-permute-done((bf16[4,128,128]{2,1,0:T(8,128)(2,1)S(1)}, bf16[4,128,128]{2,1,0:T(8,128)(2,1)S(1)}, u32[]{:S(2)}, u32[]{:S(2)}) %collective-permute-start.15) | collective-permute-done | bytes 131104 | tf_op jit(solution)/shard_map/ppermute | solution.py:406
  109.4 0.0 collective-permute-start.16
  109.4 3.2 %collective-permute-start.20 = (bf16[4,128,128]{2,1,0:T(8,128)(2,1)S(1)}, bf16[4,128,128]{2,1,0:T(8,128)(2,1)S(1)}, u32[]{:S(2)}, u32[]{:S(2)}) collective-permute-start(bf16[4,128,128]{2,1,0:T(8,128)(2,1)S(1)} %collective-permute-done.19.refs_5_.refs_6_), channel_id=1, source_target_pairs={{0,224},{32,0},{64,32},{96,64},{128,96},{160,128},{192,160},{224,1... | collective-permute-start | bytes 393224 | tf_op jit(solution)/shard_map/ppermute | solution.py:406
  112.6 3.3 %collective-permute-done.16.refs_2_.refs_3_ = bf16[4,128,128]{2,1,0:T(8,128)(2,1)S(1)} collective-permute-done((bf16[4,128,128]{2,1,0:T(8,128)(2,1)S(1)}, bf16[4,128,128]{2,1,0:T(8,128)(2,1)S(1)}, u32[]{:S(2)}, u32[]{:S(2)}) %collective-permute-start.16) | collective-permute-done | bytes 131104 | tf_op jit(solution)/shard_map/ppermute | solution.py:406
  115.9 3.2 %collective-permute-start.21 = (bf16[4,128,128]{2,1,0:T(8,128)(2,1)S(1)}, bf16[4,128,128]{2,1,0:T(8,128)(2,1)S(1)}, u32[]{:S(2)}, u32[]{:S(2)}) collective-permute-start(bf16[4,128,128]{2,1,0:T(8,128)(2,1)S(1)} %collective-permute-done.20.refs_6_.refs_7_), channel_id=1, source_target_pairs={{0,224},{32,0},{64,32},{96,64},{128,96},{160,128},{192,160},{224,1... | collective-permute-start | bytes 393224 | tf_op jit(solution)/shard_map/ppermute | solution.py:406
  119.2 3.5 %collective-permute-done.17.refs_3_.refs_4_ = bf16[4,128,128]{2,1,0:T(8,128)(2,1)S(1)} collective-permute-done((bf16[4,128,128]{2,1,0:T(8,128)(2,1)S(1)}, bf16[4,128,128]{2,1,0:T(8,128)(2,1)S(1)}, u32[]{:S(2)}, u32[]{:S(2)}) %collective-permute-start.17) | collective-permute-done | bytes 131104 | tf_op jit(solution)/shard_map/ppermute | solution.py:406
  122.6 6.2 %collective-permute-done.18.refs_4_.refs_5_ = bf16[4,128,128]{2,1,0:T(8,128)(2,1)S(1)} collective-permute-done((bf16[4,128,128]{2,1,0:T(8,128)(2,1)S(1)}, bf16[4,128,128]{2,1,0:T(8,128)(2,1)S(1)}, u32[]{:S(2)}, u32[]{:S(2)}) %collective-permute-start.18) | collective-permute-done | bytes 131104 | tf_op jit(solution)/shard_map/ppermute | solution.py:406
  128.8 1.3 copy-done
  130.1 1.5 shard_map.45
  131.6 1.6 collective-permute-start.23
  133.3 6.7 %shard_map.46 = f32[512,1024]{1,0:T(8,128)} custom-call(bf16[8,4,128,128]{3,2,1,0:T(8,128)(2,1)} %bitcast.2, bf16[4,128,128]{2,1,0:T(8,128)(2,1)} %copy-done.1, bf16[4,128,128]{2,1,0:T(8,128)(2,1)} %copy-done.2, bf16[4,128,128]{2,1,0:T(8,128)(2,1)} %copy-done.4, bf16[4,128,128]{2,1,0:T(8,128)(2,1)} %copy-done.6, bf16[4,128,128]{2,1,0:T(8,128)(2,1)} %copy-done.8, ...), custom_call_target="tpu_custom_call" | custom-call | flops 2147483648 | bytes 7340032 | tf_op jit(solution)/shard_map/pallas_call | solution.py:294
  140.0 18.5 %collective-permute-start.24 = (bf16[2,8,2,128,128]{4,3,2,1,0:T(8,128)(2,1)}, bf16[2,8,2,128,128]{4,3,2,1,0:T(8,128)(2,1)S(1)}, u32[]{:S(2)}, u32[]{:S(2)}) collective-permute-start(bf16[2,8,2,128,128]{4,3,2,1,0:T(8,128)(2,1)} %collective-permute-done.23), channel_id=1, source_target_pairs={{0,0},{1,1},{2,34},{3,35},{4,68},{5,69},{6,102},{7,103},{8,136},{9... | collective-permute-start | bytes 3145736 | tf_op jit(solution)/shard_map/ppermute | solution.py:464
  158.5 9.0 %all-to-all-start.2 = ((f32[8,64,1024]{2,1,0:T(8,128)}), f32[8,64,1024]{2,1,0:T(8,128)S(1)}, u32[]{:S(2)}, u32[]{:S(2)}) async-start(f32[8,64,1024]{2,1,0:T(8,128)} %bitcast.4), calls=%async_computation.2 | async-start | bytes 4194304 | tf_op jit(solution)/shard_map/all_to_all | solution.py:465
  167.6 30.8 %collective-permute-done.24.near = bf16[2,8,2,128,128]{4,3,2,1,0:T(8,128)(2,1)S(1)} collective-permute-done((bf16[2,8,2,128,128]{4,3,2,1,0:T(8,128)(2,1)}, bf16[2,8,2,128,128]{4,3,2,1,0:T(8,128)(2,1)S(1)}, u32[]{:S(2)}, u32[]{:S(2)}) %collective-permute-start.24) | collective-permute-done | bytes 1048608 | tf_op jit(solution)/shard_map/ppermute | solution.py:464
  198.4 2.8 %collective-permute-done.25.far = bf16[2,8,2,128,128]{4,3,2,1,0:T(8,128)(2,1)} collective-permute-done((bf16[2,8,2,128,128]{4,3,2,1,0:T(8,128)(2,1)S(1)}, bf16[2,8,2,128,128]{4,3,2,1,0:T(8,128)(2,1)}, u32[]{:S(2)}, u32[]{:S(2)}) %collective-permute-start.25) | collective-permute-done | bytes 1048608 | tf_op jit(solution)/shard_map/ppermute | solution.py:402
  201.2 2.3 shard_map.47
  203.5 20.4 %all_to_all.20.parts = f32[16,32,128]{2,1,0:T(8,128)} all-to-all(f32[16,32,128]{2,1,0:T(8,128)S(1)} %shard_map.47), channel_id=1, replica_groups=mesh['zh'=4,'zl'=2,'yl'=2,'yh'=2,'x'=4,'c'=2] {'zh','zl','yl'}, dimensions={0} | all-to-all | bytes 524288 | tf_op jit(solution)/shard_map/all_to_all | solution.py:466
  223.9 1.7 shard_map.48
  (38 shorter events, 0.1 us)
Async XLA Ops:
  6.5 13.9 %collective-permute-start = (bf16[64,4096]{1,0:T(8,128)(2,1)}, bf16[64,4096]{1,0:T(8,128)(2,1)S(1)}, u32[]{:S(2)}, u32[]{:S(2)}) collective-permute-start(bf16[64,4096]{1,0:T(8,128)(2,1)} %refs_0_.1), channel_id=1, source_target_pairs={{0,16},{16,0},{1,17},{17,1},{2,18},{18,2},{3,19},{19,3},{4,20},{20... | collective-permute-start | bytes 1572872 | tf_op jit(solution)/shard_map/ppermute | solution.py:402
  7.8 13.8 %collective-permute-start.1 = (bf16[64,4096]{1,0:T(8,128)(2,1)}, bf16[64,4096]{1,0:T(8,128)(2,1)S(1)}, u32[]{:S(2)}, u32[]{:S(2)}) collective-permute-start(bf16[64,4096]{1,0:T(8,128)(2,1)} %refs_0_.1), channel_id=1, source_target_pairs={{0,32},{32,0},{1,33},{33,1},{2,34},{34,2},{3,35},{35,3},{4,36},{36... | collective-permute-start | bytes 1572872 | tf_op jit(solution)/shard_map/ppermute | solution.py:402
  9.7 22.9 %collective-permute-start.4 = (bf16[64,4096]{1,0:T(8,128)(2,1)}, bf16[64,4096]{1,0:T(8,128)(2,1)S(1)}, u32[]{:S(2)}, u32[]{:S(2)}) collective-permute-start(bf16[64,4096]{1,0:T(8,128)(2,1)} %refs_0_.1), channel_id=1, source_target_pairs={{0,1},{1,0},{2,3},{3,2},{4,5},{5,4},{6,7},{7,6},{8,9},{9,8},{10,11... | collective-permute-start | bytes 1572872 | tf_op jit(solution)/shard_map/ppermute | solution.py:402
  9.7 0.7 copy-start.11
  10.4 14.4 %copy-start.12 = (s32[4]{0:T(128)S(1)}, s32[4]{0:T(128)}, u32[]{:S(2)}) copy-start(s32[4]{0:T(128)} %words.5) | copy-start | bytes 52
  21.6 12.4 %collective-permute-start.5 = (bf16[64,4096]{1,0:T(8,128)(2,1)S(1)}, bf16[64,4096]{1,0:T(8,128)(2,1)S(1)}, u32[]{:S(2)}, u32[]{:S(2)}) collective-permute-start(bf16[64,4096]{1,0:T(8,128)(2,1)S(1)} %collective-permute-done.refs_1_), channel_id=1, source_target_pairs={{0,1},{1,0},{2,3},{3,2},{4,5},{5,4},{6,7},{7,6},{8,9},{9,8},{10,11... | collective-permute-start | bytes 1572872 | tf_op jit(solution)/shard_map/ppermute | solution.py:402
  21.8 12.3 %copy-start.9 = (bf16[64,4096]{1,0:T(8,128)(2,1)S(1)}, bf16[64,4096]{1,0:T(8,128)(2,1)}, u32[]{:S(2)}) copy-start(bf16[64,4096]{1,0:T(8,128)(2,1)} %refs_0_.1) | copy-start | bytes 1572868
  21.8 12.2 %collective-permute-start.6 = (bf16[64,4096]{1,0:T(8,128)(2,1)S(1)}, bf16[64,4096]{1,0:T(8,128)(2,1)S(1)}, u32[]{:S(2)}, u32[]{:S(2)}) collective-permute-start(bf16[64,4096]{1,0:T(8,128)(2,1)S(1)} %collective-permute-done.1.refs_2_), channel_id=1, source_target_pairs={{0,1},{1,0},{2,3},{3,2},{4,5},{5,4},{6,7},{7,6},{8,9},{9,8},{10,11... | collective-permute-start | bytes 1572872 | tf_op jit(solution)/shard_map/ppermute | solution.py:402
  22.4 8.5 %collective-permute-start.2 = (bf16[32,4096]{1,0:T(8,128)(2,1)S(1)}, bf16[32,4096]{1,0:T(8,128)(2,1)S(1)}, u32[]{:S(2)}, u32[]{:S(2)}) collective-permute-start(bf16[32,4096]{1,0:T(8,128)(2,1)S(1)} %slice.6), channel_id=1, source_target_pairs={{0,32},{32,0},{1,33},{33,1},{2,34},{34,2},{3,35},{35,3},{4,36},{36... | collective-permute-start | bytes 786440 | tf_op jit(solution)/shard_map/ppermute | solution.py:402
  24.1 8.0 %collective-permute-start.3 = (bf16[32,4096]{1,0:T(8,128)(2,1)S(1)}, bf16[32,4096]{1,0:T(8,128)(2,1)S(1)}, u32[]{:S(2)}, u32[]{:S(2)}) collective-permute-start(bf16[32,4096]{1,0:T(8,128)(2,1)S(1)} %slice.7), channel_id=1, source_target_pairs={{0,16},{16,0},{1,17},{17,1},{2,18},{18,2},{3,19},{19,3},{4,20},{20... | collective-permute-start | bytes 786440 | tf_op jit(solution)/shard_map/ppermute | solution.py:402
  32.1 1.5 collective-permute-start.7
  32.1 1.9 collective-permute-start.8
  42.1 2.0 copy-start.10
  44.0 25.1 %all-to-all-start = ((f32[8,256,128]{2,1,0:T(8,128)}), f32[8,256,128]{2,1,0:T(8,128)S(1)}, u32[]{:S(2)}, u32[]{:S(2)}) async-start(f32[8,256,128]{2,1,0:T(8,128)} %get-tuple-element.38), calls=%async_computation | async-start | bytes 2097152 | tf_op jit(solution)/shard_map/all_to_all | solution.py:441
  51.2 77.6 %all-gather.3.cloned.1.call-start = ((), (), s32[]{:S(2)}) async-start(), calls=%async_computation.4 | async-start | bytes 1179648 | tf_op jit(solution)/shard_map/all_gather | solution.py:448
  69.2 1.3 collective-permute-start.9
  69.3 4.1 %collective-permute-start.10 = (bf16[128,128]{1,0:T(8,128)(2,1)S(1)}, bf16[128,128]{1,0:T(8,128)(2,1)S(1)}, u32[]{:S(2)}, u32[]{:S(2)}) collective-permute-start(bf16[128,128]{1,0:T(8,128)(2,1)S(1)} %get-tuple-element.40.refs_0_), channel_id=1, source_target_pairs={{0,16},{16,0},{1,17},{17,1},{2,18},{18,2},{3,19},{19,3},{4,20},{20... | collective-permute-start | bytes 98312 | tf_op jit(solution)/shard_map/ppermute | solution.py:402
  70.5 3.9 %collective-permute-start.11 = (bf16[128,128]{1,0:T(8,128)(2,1)S(1)}, bf16[128,128]{1,0:T(8,128)(2,1)S(1)}, u32[]{:S(2)}, u32[]{:S(2)}) collective-permute-start(bf16[128,128]{1,0:T(8,128)(2,1)S(1)} %collective-permute-done.9.refs_1_), channel_id=1, source_target_pairs={{0,16},{16,0},{1,17},{17,1},{2,18},{18,2},{3,19},{19,3},{4,20},{20... | collective-permute-start | bytes 98312 | tf_op jit(solution)/shard_map/ppermute | solution.py:402
  75.1 19.5 %all-to-all-start.1 = ((f32[8,256,128]{2,1,0:T(8,128)}), f32[8,256,128]{2,1,0:T(8,128)S(1)}, u32[]{:S(2)}, u32[]{:S(2)}) async-start(f32[8,256,128]{2,1,0:T(8,128)} %shard_map.40), calls=%async_computation.1 | async-start | bytes 2097152 | tf_op jit(solution)/shard_map/all_to_all | solution.py:444
  82.3 51.0 %collective-permute-start.22 = (bf16[1024,1024]{1,0:T(8,128)(2,1)}, bf16[1024,1024]{1,0:T(8,128)(2,1)}, u32[]{:S(2)}, u32[]{:S(2)}) collective-permute-start(bf16[1024,1024]{1,0:T(8,128)(2,1)} %refs_9_.1), channel_id=1, source_target_pairs={{0,1},{1,0},{2,3},{3,2},{4,5},{5,4},{6,7},{7,6},{8,9},{9,8},{10,11... | collective-permute-start | bytes 6291464 | tf_op jit(solution)/shard_map/ppermute | solution.py:402
  94.6 1.3 collective-permute-start.12
  94.7 4.1 %collective-permute-start.13 = (bf16[128,128]{1,0:T(8,128)(2,1)S(1)}, bf16[128,128]{1,0:T(8,128)(2,1)S(1)}, u32[]{:S(2)}, u32[]{:S(2)}) collective-permute-start(bf16[128,128]{1,0:T(8,128)(2,1)S(1)} %get-tuple-element.44.refs_0_), channel_id=1, source_target_pairs={{0,16},{16,0},{1,17},{17,1},{2,18},{18,2},{3,19},{19,3},{4,20},{20... | collective-permute-start | bytes 98312 | tf_op jit(solution)/shard_map/ppermute | solution.py:402
  95.9 3.9 %collective-permute-start.14 = (bf16[128,128]{1,0:T(8,128)(2,1)S(1)}, bf16[128,128]{1,0:T(8,128)(2,1)S(1)}, u32[]{:S(2)}, u32[]{:S(2)}) collective-permute-start(bf16[128,128]{1,0:T(8,128)(2,1)S(1)} %collective-permute-done.12.refs_1_), channel_id=1, source_target_pairs={{0,16},{16,0},{1,17},{17,1},{2,18},{18,2},{3,19},{19,3},{4,20},{20... | collective-permute-start | bytes 98312 | tf_op jit(solution)/shard_map/ppermute | solution.py:402
  99.8 33.4 %copy-start.1 = (bf16[4,128,128]{2,1,0:T(8,128)(2,1)}, bf16[4,128,128]{2,1,0:T(8,128)(2,1)S(1)}, u32[]{:S(2)}) copy-start(bf16[4,128,128]{2,1,0:T(8,128)(2,1)S(1)} %shard_map.44.refs_0_.refs_1_) | copy-start | bytes 393220
  99.8 9.5 %collective-permute-start.15 = (bf16[4,128,128]{2,1,0:T(8,128)(2,1)S(1)}, bf16[4,128,128]{2,1,0:T(8,128)(2,1)S(1)}, u32[]{:S(2)}, u32[]{:S(2)}) collective-permute-start(bf16[4,128,128]{2,1,0:T(8,128)(2,1)S(1)} %shard_map.44.refs_0_.refs_1_), channel_id=1, source_target_pairs={{0,32},{32,64},{64,96},{96,128},{128,160},{160,192},{192,224},{224... | collective-permute-start | bytes 393224 | tf_op jit(solution)/shard_map/ppermute | solution.py:406
  100.3 9.1 %collective-permute-start.19 = (bf16[4,128,128]{2,1,0:T(8,128)(2,1)S(1)}, bf16[4,128,128]{2,1,0:T(8,128)(2,1)S(1)}, u32[]{:S(2)}, u32[]{:S(2)}) collective-permute-start(bf16[4,128,128]{2,1,0:T(8,128)(2,1)S(1)} %shard_map.44.refs_0_.refs_1_), channel_id=1, source_target_pairs={{0,224},{32,0},{64,32},{96,64},{128,96},{160,128},{192,160},{224,1... | collective-permute-start | bytes 393224 | tf_op jit(solution)/shard_map/ppermute | solution.py:406
  109.4 23.9 %copy-start.2 = (bf16[4,128,128]{2,1,0:T(8,128)(2,1)}, bf16[4,128,128]{2,1,0:T(8,128)(2,1)S(1)}, u32[]{:S(2)}) copy-start(bf16[4,128,128]{2,1,0:T(8,128)(2,1)S(1)} %collective-permute-done.15.refs_1_.refs_2_) | copy-start | bytes 393220
  109.4 6.5 %collective-permute-start.16 = (bf16[4,128,128]{2,1,0:T(8,128)(2,1)S(1)}, bf16[4,128,128]{2,1,0:T(8,128)(2,1)S(1)}, u32[]{:S(2)}, u32[]{:S(2)}) collective-permute-start(bf16[4,128,128]{2,1,0:T(8,128)(2,1)S(1)} %collective-permute-done.15.refs_1_.refs_2_), channel_id=1, source_target_pairs={{0,32},{32,64},{64,96},{96,128},{128,160},{160,192},{192,224},{224... | collective-permute-start | bytes 393224 | tf_op jit(solution)/shard_map/ppermute | solution.py:406
  109.4 23.9 %copy-start.3 = (bf16[4,128,128]{2,1,0:T(8,128)(2,1)}, bf16[4,128,128]{2,1,0:T(8,128)(2,1)S(1)}, u32[]{:S(2)}) copy-start(bf16[4,128,128]{2,1,0:T(8,128)(2,1)S(1)} %collective-permute-done.19.refs_5_.refs_6_) | copy-start | bytes 393220
  109.4 6.5 %collective-permute-start.20 = (bf16[4,128,128]{2,1,0:T(8,128)(2,1)S(1)}, bf16[4,128,128]{2,1,0:T(8,128)(2,1)S(1)}, u32[]{:S(2)}, u32[]{:S(2)}) collective-permute-start(bf16[4,128,128]{2,1,0:T(8,128)(2,1)S(1)} %collective-permute-done.19.refs_5_.refs_6_), channel_id=1, source_target_pairs={{0,224},{32,0},{64,32},{96,64},{128,96},{160,128},{192,160},{224,1... | collective-permute-start | bytes 393224 | tf_op jit(solution)/shard_map/ppermute | solution.py:406
  115.9 17.4 %copy-start.4 = (bf16[4,128,128]{2,1,0:T(8,128)(2,1)}, bf16[4,128,128]{2,1,0:T(8,128)(2,1)S(1)}, u32[]{:S(2)}) copy-start(bf16[4,128,128]{2,1,0:T(8,128)(2,1)S(1)} %collective-permute-done.16.refs_2_.refs_3_) | copy-start | bytes 393220
  115.9 6.7 %collective-permute-start.17 = (bf16[4,128,128]{2,1,0:T(8,128)(2,1)S(1)}, bf16[4,128,128]{2,1,0:T(8,128)(2,1)S(1)}, u32[]{:S(2)}, u32[]{:S(2)}) collective-permute-start(bf16[4,128,128]{2,1,0:T(8,128)(2,1)S(1)} %collective-permute-done.16.refs_2_.refs_3_), channel_id=1, source_target_pairs={{0,32},{32,64},{64,96},{96,128},{128,160},{160,192},{192,224},{224... | collective-permute-start | bytes 393224 | tf_op jit(solution)/shard_map/ppermute | solution.py:406
  115.9 17.4 %copy-start.5 = (bf16[4,128,128]{2,1,0:T(8,128)(2,1)}, bf16[4,128,128]{2,1,0:T(8,128)(2,1)S(1)}, u32[]{:S(2)}) copy-start(bf16[4,128,128]{2,1,0:T(8,128)(2,1)S(1)} %collective-permute-done.20.refs_6_.refs_7_) | copy-start | bytes 393220
  115.9 6.7 %collective-permute-start.21 = (bf16[4,128,128]{2,1,0:T(8,128)(2,1)S(1)}, bf16[4,128,128]{2,1,0:T(8,128)(2,1)S(1)}, u32[]{:S(2)}, u32[]{:S(2)}) collective-permute-start(bf16[4,128,128]{2,1,0:T(8,128)(2,1)S(1)} %collective-permute-done.20.refs_6_.refs_7_), channel_id=1, source_target_pairs={{0,224},{32,0},{64,32},{96,64},{128,96},{160,128},{192,160},{224,1... | collective-permute-start | bytes 393224 | tf_op jit(solution)/shard_map/ppermute | solution.py:406
  122.6 10.7 %copy-start.6 = (bf16[4,128,128]{2,1,0:T(8,128)(2,1)}, bf16[4,128,128]{2,1,0:T(8,128)(2,1)S(1)}, u32[]{:S(2)}) copy-start(bf16[4,128,128]{2,1,0:T(8,128)(2,1)S(1)} %collective-permute-done.17.refs_3_.refs_4_) | copy-start | bytes 393220
  122.6 6.2 %collective-permute-start.18 = (bf16[4,128,128]{2,1,0:T(8,128)(2,1)S(1)}, bf16[4,128,128]{2,1,0:T(8,128)(2,1)S(1)}, u32[]{:S(2)}, u32[]{:S(2)}) collective-permute-start(bf16[4,128,128]{2,1,0:T(8,128)(2,1)S(1)} %collective-permute-done.17.refs_3_.refs_4_), channel_id=1, source_target_pairs={{0,32},{32,64},{64,96},{96,128},{128,160},{160,192},{192,224},{224... | collective-permute-start | bytes 393224 | tf_op jit(solution)/shard_map/ppermute | solution.py:406
  122.6 10.7 %copy-start.7 = (bf16[4,128,128]{2,1,0:T(8,128)(2,1)}, bf16[4,128,128]{2,1,0:T(8,128)(2,1)S(1)}, u32[]{:S(2)}) copy-start(bf16[4,128,128]{2,1,0:T(8,128)(2,1)S(1)} %collective-permute-done.21.refs_7_.refs_8_) | copy-start | bytes 393220
  128.8 4.5 %copy-start.8 = (bf16[4,128,128]{2,1,0:T(8,128)(2,1)}, bf16[4,128,128]{2,1,0:T(8,128)(2,1)S(1)}, u32[]{:S(2)}) copy-start(bf16[4,128,128]{2,1,0:T(8,128)(2,1)S(1)} %collective-permute-done.18.refs_4_.refs_5_) | copy-start | bytes 393220
  128.8 1.3 copy-start
  131.6 8.4 %collective-permute-start.23 = (bf16[2,8,2,128,128]{4,3,2,1,0:T(8,128)(2,1)S(1)}, bf16[2,8,2,128,128]{4,3,2,1,0:T(8,128)(2,1)}, u32[]{:S(2)}, u32[]{:S(2)}) collective-permute-start(bf16[2,8,2,128,128]{4,3,2,1,0:T(8,128)(2,1)S(1)} %shard_map.45), channel_id=1, source_target_pairs={{0,0},{1,1},{2,2},{3,3},{4,4},{5,5},{6,6},{7,7},{8,8},{9,9},{10,10... | collective-permute-start | bytes 3145736 | tf_op jit(solution)/shard_map/ppermute | solution.py:461
  140.0 58.3 %collective-permute-start.24 = (bf16[2,8,2,128,128]{4,3,2,1,0:T(8,128)(2,1)}, bf16[2,8,2,128,128]{4,3,2,1,0:T(8,128)(2,1)S(1)}, u32[]{:S(2)}, u32[]{:S(2)}) collective-permute-start(bf16[2,8,2,128,128]{4,3,2,1,0:T(8,128)(2,1)} %collective-permute-done.23), channel_id=1, source_target_pairs={{0,0},{1,1},{2,34},{3,35},{4,68},{5,69},{6,102},{7,103},{8,136},{9... | collective-permute-start | bytes 3145736 | tf_op jit(solution)/shard_map/ppermute | solution.py:464
  158.5 39.9 %all-to-all-start.2 = ((f32[8,64,1024]{2,1,0:T(8,128)}), f32[8,64,1024]{2,1,0:T(8,128)S(1)}, u32[]{:S(2)}, u32[]{:S(2)}) async-start(f32[8,64,1024]{2,1,0:T(8,128)} %bitcast.4), calls=%async_computation.2 | async-start | bytes 4194304 | tf_op jit(solution)/shard_map/all_to_all | solution.py:465
  198.4 2.8 %collective-permute-start.25 = (bf16[2,8,2,128,128]{4,3,2,1,0:T(8,128)(2,1)S(1)}, bf16[2,8,2,128,128]{4,3,2,1,0:T(8,128)(2,1)}, u32[]{:S(2)}, u32[]{:S(2)}) collective-permute-start(bf16[2,8,2,128,128]{4,3,2,1,0:T(8,128)(2,1)S(1)} %collective-permute-done.24.near), channel_id=1, source_target_pairs={{0,1},{1,0},{2,3},{3,2},{4,5},{5,4},{6,7},{7,6},{8,9},{9,8},{10,11... | collective-permute-start | bytes 3145736 | tf_op jit(solution)/shard_map/ppermute | solution.py:402
Sparse Core Ops, SparseCore 0:
  75.2 40.8 all-gather.2
